TPU v7x, 32 devices: a whole 2x2x4 slice. The times are simulated.
32 devices in a mesh: grp: 2 (over y), sp: 8 (over z, x), ch: 2 (over core).
Axes of the slice: x: 2, y: 2, z: 4, core: 2. Of those that a mesh axis runs over, the one named last changes fastest.
Arguments:
- fine_state: float32 [2048, 4, 256], P('sp', ('grp', 'ch')), parts along dimension 1, may hold values from -6 to 6
- coarse_state: float32 [512, 4, 256], P('sp', ('grp', 'ch')), parts along dimension 1, may hold values from -6 to 6
- fine_senders: int32 [8192], P('sp'), may hold values from 0 to 511
- up_owner: int32 [2048, 1], P('sp'), may hold values from 0 to 7; in each aligned block of 256 rows (0 to 255, 256 to 511, ...) at most 64 rows name the same one
- up_local: int32 [2048], P('sp'), may hold values from 0 to 63
- coarse_owner: int32 [2048, 1], P('sp'), may hold values from 0 to 7; in each aligned block of 256 rows (0 to 255, 256 to 511, ...) at most 64 rows name the same one
- coarse_local: int32 [2048], P('sp'), may hold values from 0 to 63
- fine_w_send: float32 [2, 256, 256], replicated, may hold values from -0.375 to 0.375
- fine_w_recv: float32 [2, 256, 256], replicated, may hold values from -0.375 to 0.375
- fine_bias: float32 [2, 256], replicated, may hold values from -3 to 3
- fine_w_out: float32 [2, 256, 256], replicated, may hold values from -0.1875 to 0.1875
- up_w_in: float32 [256, 256], replicated, may hold values from -0.375 to 0.375
- up_bias: float32 [256], replicated, may hold values from -3 to 3
- up_w_out: float32 [256, 256], replicated, may hold values from -0.125 to 0.125
- coarse_w_send: float32 [256, 256], replicated, may hold values from -0.375 to 0.375
- coarse_w_recv: float32 [256, 256], replicated, may hold values from -0.375 to 0.375
- coarse_bias: float32 [256], replicated, may hold values from -3 to 3
- coarse_w_out: float32 [256, 256], replicated, may hold values from -0.1875 to 0.1875
- down_w_in: float32 [256, 256], replicated, may hold values from -0.375 to 0.375
- down_bias: float32 [256], replicated, may hold values from -3 to 3
- down_w_out: float32 [256, 256], replicated, may hold values from -0.375 to 0.375
Outputs:
- fine_out: float32 [2048, 4, 256], P('sp', ('grp', 'ch')), parts along dimension 1
- coarse_out: float32 [512, 4, 256], P('sp', ('grp', 'ch')), parts along dimension 1
There are 2 independent parts, one for each index of `grp`. A program takes and returns all parts, laid end to end along the dimension named above; an argument that names none is the same for every part. Nothing has to cross between parts.
Inputs may be any that keep to these rules, and one draw needn't show every extreme that they name: `up_owner`: within the rows of one device, at most 64 fine nodes name the same dealt set; some dealt set is named exactly 64 times by one device's rows. `coarse_owner`: within the rows of one device, at most 64 coarse edges name the same dealt set; some dealt set is named exactly 64 times by one device's rows.
All inputs are finite; a program needn't handle non-finite values.
Results may differ from a plain program's by a relative error of at most 0.0001.
Values sent between devices are 32-bit elements; how exact they have to be, the bound alone decides.
No kernel may reach another device: no remote copies, remote signals or barrier semaphores. Data moves between devices by JAX's collectives and lax.ppermute only.
A program may use at most 64 MiB of HBM per device.

v0:
```python
import jax
import jax.numpy as jnp
from jax import lax
from jax.sharding import PartitionSpec as P

HALO = 128


epsilon = 1e-05
highest = lax.Precision.HIGHEST


def extended_2(cells, sides, width):
    for axis, dim in sides:
        count = lax.axis_size(axis)
        head = lax.slice_in_dim(cells, 0, width, axis=dim)
        tail = lax.slice_in_dim(cells, cells.shape[dim] - width, cells.shape[dim], axis=dim)
        cells = jnp.concatenate(
            [
                lax.ppermute(tail, axis, [(i, (i + 1) % count) for i in range(count)]),
                cells,
                lax.ppermute(head, axis, [((i + 1) % count, i) for i in range(count)]),
            ],
            axis=dim,
        )
    return cells


def layer_norm(values):
    average = jnp.mean(values, axis=-1, keepdims=True)
    centered = values - average
    spread = jnp.mean(centered * centered, axis=-1, keepdims=True)
    return centered / jnp.sqrt(spread + epsilon)


def project(values, matrix):
    return jnp.einsum(
        "nsd,dh->nsh", values, matrix, precision=highest, preferred_element_type=jnp.float32
    )


def slot_ranks(owners, peer_count):
    matches = (owners[:, None] == jnp.arange(peer_count, dtype=jnp.int32)[None, :]).astype(
        jnp.int32
    )
    ranking = jnp.cumsum(matches, axis=0) - 1
    return jnp.sum(ranking * matches, axis=1)


def shards(
    fine_state,
    coarse_state,
    fine_senders,
    up_owner,
    up_local,
    coarse_owner,
    coarse_local,
    fine_w_send,
    fine_w_recv,
    fine_bias,
    fine_w_out,
    up_w_in,
    up_bias,
    up_w_out,
    coarse_w_send,
    coarse_w_recv,
    coarse_bias,
    coarse_w_out,
    down_w_in,
    down_bias,
    down_w_out,
):
    peer_count = lax.axis_size("sp")
    fine_rows = fine_state.shape[0]
    coarse_rows = coarse_state.shape[0]
    samples = fine_state.shape[1]
    feature_width = fine_state.shape[2]
    degree_fine = fine_senders.shape[0] // fine_rows
    degree_coarse = coarse_owner.shape[0] // coarse_rows
    hidden_state = fine_state
    for layer_index in range(fine_w_send.shape[0]):
        normed = layer_norm(hidden_state)
        outward = project(normed, fine_w_send[layer_index])
        inward = project(normed, fine_w_recv[layer_index]) + fine_bias[layer_index]
        extended = extended_2(outward, (("sp", 0),), HALO)
        gathered = extended[fine_senders].reshape(fine_rows, degree_fine, samples, -1)
        summed = jnp.sum(jax.nn.silu(gathered + inward[:, None]), axis=1)
        hidden_state = hidden_state + project(summed, fine_w_out[layer_index])
    capacity = max(4, 2 * fine_rows // peer_count)
    owners = up_owner[:, 0]
    places = owners * capacity + slot_ranks(owners, peer_count)
    targets = (
        jnp.full((peer_count * capacity,), -1.0, jnp.float32)
        .at[places]
        .set(up_local.astype(jnp.float32))
        .reshape(peer_count, capacity)
    )
    activated = jax.nn.silu(project(layer_norm(hidden_state), up_w_in) + up_bias)
    coarse_ids = jnp.arange(coarse_rows, dtype=jnp.float32)[:, None]
    messages = project(activated, up_w_out)
    outgoing = (
        jnp.zeros((peer_count * capacity, samples, feature_width), jnp.float32)
        .at[places]
        .set(messages)
        .reshape(peer_count, capacity, samples, feature_width)
    )
    arrived, sources = (
        lax.all_to_all(outgoing, "sp", split_axis=0, concat_axis=0, tiled=True),
        lax.all_to_all(targets, "sp", split_axis=0, concat_axis=0, tiled=True),
    )
    selector = (sources.reshape(1, -1) == coarse_ids).astype(jnp.float32)
    gained = jnp.einsum(
        "cr,rsd->csd",
        selector,
        arrived.reshape(peer_count * capacity, samples, feature_width),
        precision=highest,
        preferred_element_type=jnp.float32,
    )
    coarse = coarse_state + gained
    normed = layer_norm(coarse)
    outward = project(normed, coarse_w_send)
    inward = project(normed, coarse_w_recv) + coarse_bias
    anchor_owner = coarse_owner[:, 0]
    everything = lax.all_gather(outward, "sp", axis=0, tiled=True)
    picked = everything[anchor_owner * coarse_rows + coarse_local]
    edge_terms = picked.reshape(coarse_rows, degree_coarse, samples, -1)
    summed = jnp.sum(jax.nn.silu(edge_terms + inward[:, None]), axis=1)
    coarse_out = coarse + project(summed, coarse_w_out)
    downward = project(
        jax.nn.silu(project(layer_norm(coarse_out), down_w_in) + down_bias), down_w_out
    )
    wanted = jnp.maximum(sources.reshape(-1), 0.0).astype(jnp.int32)
    replies = downward[wanted].reshape(peer_count, capacity, samples, feature_width)
    answered = lax.all_to_all(replies, "sp", split_axis=0, concat_axis=0, tiled=True)
    fine_out = (
        hidden_state + answered.reshape(peer_count * capacity, samples, feature_width)[places]
    )
    return (fine_out, coarse_out)


def solution(mesh):
    in_specs = (
        P("sp", ("grp", "ch"), None),
        P("sp", ("grp", "ch"), None),
        P("sp"),
        P("sp", None),
        P("sp"),
        P("sp", None),
        P("sp"),
        P(),
        P(),
        P(),
        P(),
        P(),
        P(),
        P(),
        P(),
        P(),
        P(),
        P(),
        P(),
        P(),
        P(),
    )
    out_specs = (P("sp", ("grp", "ch"), None), P("sp", ("grp", "ch"), None))
    return jax.shard_map(shards, mesh=mesh, in_specs=in_specs, out_specs=out_specs, check_vma=False)
```

profile of v0, /device:TPU:0, one launch (start us, length us, event | category | flops | bytes accessed | tf_op | source)
XLA Modules:
  0.0 122.9 jit_solution(1076265548420080681)
XLA Ops:
  0.7 2.1 %reduce_sum.128 = f32[256]{0:T(256)S(1)} reduce(f32[256,1,256]{2,1,0:T(1,128)} %param.21, f32[]{:T(128)} %constant.21.clone.1), dimensions={1,2}, to_apply=%region_0.0 | reduce | flops 65280 | bytes 263172 | tf_op jit(solution)/shard_map/reduce_sum | solution.py:30
  2.7 3.6 %multiply_reduce_fusion.2 = f32[256]{0:T(256)S(1)} fusion(f32[256,1,256]{2,1,0:T(1,128)S(1)} %copy-done.1, f32[256]{0:T(256)S(1)} %broadcast_multiply_fusion.3), kind=kLoop, calls=%fused_computation.58 | loop fusion | flops 196352 | bytes 264192 | tf_op jit(solution)/shard_map/reduce_sum | solution.py:32
  6.3 1.2 subtract_divide_fusion.1
  8.0 3.0 %collective-permute-start = (f32[128,1,256]{2,0,1:T(8,128)S(1)}, f32[128,1,256]{2,0,1:T(8,128)S(1)}, u32[]{:S(2)}, u32[]{:S(2)}) collective-permute-start(f32[128,1,256]{2,0,1:T(8,128)S(1)} %get-tuple-element.10), channel_id=1, source_target_pairs={{0,2},{2,4},{4,6},{6,8},{8,10},{10,12},{12,14},{14,0},{1,3},{3,5},... | collective-permute-start | bytes 393224 | tf_op jit(solution)/shard_map/ppermute | solution.py:20
  11.0 3.1 %collective-permute-start.1 = (f32[128,1,256]{2,0,1:T(8,128)S(1)}, f32[128,1,256]{2,0,1:T(8,128)S(1)}, u32[]{:S(2)}, u32[]{:S(2)}) collective-permute-start(f32[128,1,256]{2,0,1:T(8,128)S(1)} %get-tuple-element.11), channel_id=1, source_target_pairs={{2,0},{4,2},{6,4},{8,6},{10,8},{12,10},{14,12},{0,14},{3,1},{5,3},... | collective-permute-start | bytes 393224 | tf_op jit(solution)/shard_map/ppermute | solution.py:22
  15.1 0.7 copy-done.20
  15.7 1.4 %scatter_custom_fusion = f32[512]{0:T(512)S(1)} fusion(s32[256]{0:T(256)S(1)} %bitcast.114, f32[256]{0:T(256)S(1)} %convert_element_type.23, f32[]{:T(128)} %constant.47.clone.1), kind=kCustom, calls=%fused_computation.108 | custom fusion | bytes 2052 | tf_op jit(solution)/shard_map/scatter | solution.py:95
  17.1 0.7 all_to_all.12
  17.8 3.3 %all-to-all-start = ((f32[8,1,64]{2,1,0:T(1,128)}), f32[8,1,64]{2,1,0:T(1,128)S(1)}, u32[]{:S(2)}, u32[]{:S(2)}) async-start(f32[8,1,64]{2,1,0:T(1,128)} %all_to_all.12), calls=%async_computation | async-start | bytes 8192 | tf_op jit(solution)/shard_map/all_to_all | solution.py:109
  22.6 3.5 %gather_fusion = f32[1024,256]{1,0:T(8,128)S(1)} fusion(f32[512,256]{1,0:T(8,128)S(1)} %maximum_bitcast_fusion, s32[1024]{0:T(1024)S(1)} %fusion.59), kind=kCustom, calls=%fused_computation | custom fusion | bytes 2101248 | tf_op jit(solution)/shard_map/gather | solution.py:86
  26.4 1.2 fusion.4
  29.3 2.0 %collective-permute-start.2 = (f32[128,1,256]{2,0,1:T(8,128)S(1)}, f32[128,1,256]{2,0,1:T(8,128)S(1)}, u32[]{:S(2)}, u32[]{:S(2)}) collective-permute-start(f32[128,1,256]{2,0,1:T(8,128)S(1)} %get-tuple-element.8), channel_id=1, source_target_pairs={{0,2},{2,4},{4,6},{6,8},{8,10},{10,12},{12,14},{14,0},{1,3},{3,5},... | collective-permute-start | bytes 393224 | tf_op jit(solution)/shard_map/ppermute | solution.py:20
  31.3 3.0 %collective-permute-start.3 = (f32[128,1,256]{2,0,1:T(8,128)S(1)}, f32[128,1,256]{2,0,1:T(8,128)S(1)}, u32[]{:S(2)}, u32[]{:S(2)}) collective-permute-start(f32[128,1,256]{2,0,1:T(8,128)S(1)} %get-tuple-element.9), channel_id=1, source_target_pairs={{2,0},{4,2},{6,4},{8,6},{10,8},{12,10},{14,12},{0,14},{3,1},{5,3},... | collective-permute-start | bytes 393224 | tf_op jit(solution)/shard_map/ppermute | solution.py:22
  34.9 2.2 %collective-permute-done.2 = f32[128,1,256]{2,0,1:T(8,128)S(1)} collective-permute-done((f32[128,1,256]{2,0,1:T(8,128)S(1)}, f32[128,1,256]{2,0,1:T(8,128)S(1)}, u32[]{:S(2)}, u32[]{:S(2)}) %collective-permute-start.2) | collective-permute-done | bytes 131104 | tf_op jit(solution)/shard_map/ppermute | solution.py:20
  37.1 1.4 %collective-permute-done.3 = f32[128,1,256]{2,0,1:T(8,128)S(1)} collective-permute-done((f32[128,1,256]{2,0,1:T(8,128)S(1)}, f32[128,1,256]{2,0,1:T(8,128)S(1)}, u32[]{:S(2)}, u32[]{:S(2)}) %collective-permute-start.3) | collective-permute-done | bytes 131104 | tf_op jit(solution)/shard_map/ppermute | solution.py:22
  38.5 3.5 %gather_fusion.1 = f32[1024,256]{1,0:T(8,128)S(1)} fusion(f32[512,256]{1,0:T(8,128)S(1)} %maximum_bitcast_fusion.1, s32[1024]{0:T(1024)S(1)} %fusion.59), kind=kCustom, calls=%fused_computation.1 | custom fusion | bytes 2101248 | tf_op jit(solution)/shard_map/gather | solution.py:86
  42.3 1.2 fusion.5
  46.3 2.2 %scatter_custom_fusion.1 = f32[512,256]{1,0:T(8,128)} fusion(s32[256]{0:T(256)S(1)} %bitcast.115, f32[256,256]{1,0:T(8,128)S(1)} %fusion.21, f32[]{:T(128)} %constant.21.clone.1), kind=kCustom, calls=%fused_computation.41 | custom fusion | bytes 524292 | tf_op jit(solution)/shard_map/scatter | solution.py:104
  48.5 4.8 %all-to-all-start.1 = ((f32[8,64,1,256]{3,1,2,0:T(8,128)}), f32[8,64,1,256]{3,1,2,0:T(8,128)S(1)}, u32[]{:S(2)}, u32[]{:S(2)}) async-start(f32[8,64,1,256]{3,1,2,0:T(8,128)} %bitcast.26), calls=%async_computation.1 | async-start | bytes 1048576 | tf_op jit(solution)/shard_map/all_to_all | solution.py:108
  53.3 0.7 copy-done.19
  54.5 0.7 reduce.22
  55.4 12.0 %all-to-all-done.1 = f32[8,64,1,256]{3,1,2,0:T(8,128)S(1)} async-done(((f32[8,64,1,256]{3,1,2,0:T(8,128)}), f32[8,64,1,256]{3,1,2,0:T(8,128)S(1)}, u32[]{:S(2)}, u32[]{:S(2)}) %all-to-all-start.1) | async-done | bytes 524320 | tf_op jit(solution)/shard_map/all_to_all | solution.py:108
  68.6 31.6 %all-gather = f32[512,256]{1,0:T(8,128)S(1)} all-gather(f32[64,256]{1,0:T(8,128)S(1)} %fusion.43), channel_id=2, replica_groups=mesh['grp'=2,'sp'=8,'ch'=2] {'sp'}, dimensions={0}, use_global_device_ids=true | all-gather | bytes 589824 | tf_op jit(solution)/shard_map/all_gather | solution.py:124
  100.2 1.0 gather_fusion.2
  101.3 0.8 copy-done.5
  102.7 0.7 copy-done.8
  105.0 2.2 %gather_fusion.3 = f32[512,256]{1,0:T(8,128)} fusion(f32[64,256]{1,0:T(8,128)S(1)} %fusion.45, s32[1024]{0:T(1024)S(1)} %pad_clamp_fusion.1), kind=kCustom, calls=%fused_computation.3 | custom fusion | bytes 1050624 | tf_op jit(solution)/shard_map/gather | solution.py:133
  107.2 3.5 %all-to-all-start.2 = ((f32[8,64,1,256]{3,1,2,0:T(8,128)}), f32[8,64,1,256]{3,1,2,0:T(8,128)S(1)}, u32[]{:S(2)}, u32[]{:S(2)}) async-start(f32[8,64,1,256]{3,1,2,0:T(8,128)} %bitcast.35), calls=%async_computation.2 | async-start | bytes 1048576 | tf_op jit(solution)/shard_map/all_to_all | solution.py:134
  110.7 0.7 copy.38
  111.4 9.5 %all-to-all-done.2 = f32[8,64,1,256]{3,1,2,0:T(8,128)S(1)} async-done(((f32[8,64,1,256]{3,1,2,0:T(8,128)}), f32[8,64,1,256]{3,1,2,0:T(8,128)S(1)}, u32[]{:S(2)}, u32[]{:S(2)}) %all-to-all-start.2) | async-done | bytes 524320 | tf_op jit(solution)/shard_map/all_to_all | solution.py:134
  120.9 1.0 gather_fusion.4
  122.1 0.8 copy.37
  (106 shorter events, 12.8 us)
Async XLA Ops:
  0.6 43.6 %copy-start = (f32[256,256]{1,0:T(8,128)S(1)}, f32[256,256]{1,0:T(8,128)}, u32[]{:S(2)}) copy-start(f32[256,256]{1,0:T(8,128)} %param.32) | copy-start | bytes 786436
  0.6 2.1 %copy-start.1 = (f32[256,1,256]{2,1,0:T(1,128)S(1)}, f32[256,1,256]{2,1,0:T(1,128)}, u32[]{:S(2)}) copy-start(f32[256,1,256]{2,1,0:T(1,128)} %param.21) | copy-start | bytes 786436
  0.7 6.9 %copy-start.9 = (f32[2,256,256]{2,1,0:T(8,128)S(1)}, f32[2,256,256]{2,1,0:T(8,128)}, u32[]{:S(2)}) copy-start(f32[2,256,256]{2,1,0:T(8,128)} %param.28) | copy-start | bytes 1572868
  7.9 13.9 %copy-start.11 = (f32[2,256,256]{2,1,0:T(8,128)S(1)}, f32[2,256,256]{2,1,0:T(8,128)}, u32[]{:S(2)}) copy-start(f32[2,256,256]{2,1,0:T(8,128)} %param.29) | copy-start | bytes 1572868
  8.0 14.5 %collective-permute-start = (f32[128,1,256]{2,0,1:T(8,128)S(1)}, f32[128,1,256]{2,0,1:T(8,128)S(1)}, u32[]{:S(2)}, u32[]{:S(2)}) collective-permute-start(f32[128,1,256]{2,0,1:T(8,128)S(1)} %get-tuple-element.10), channel_id=1, source_target_pairs={{0,2},{2,4},{4,6},{6,8},{8,10},{10,12},{12,14},{14,0},{1,3},{3,5},... | collective-permute-start | bytes 393224 | tf_op jit(solution)/shard_map/ppermute | solution.py:20
  11.0 3.1 %copy-start.14 = (s32[256,1]{0,1:T(1,128)S(1)}, s32[256,1]{0,1:T(1,128)}, u32[]{:S(2)}) copy-start(s32[256,1]{0,1:T(1,128)} %param.24) | copy-start | bytes 3076
  11.0 11.5 %collective-permute-start.1 = (f32[128,1,256]{2,0,1:T(8,128)S(1)}, f32[128,1,256]{2,0,1:T(8,128)S(1)}, u32[]{:S(2)}, u32[]{:S(2)}) collective-permute-start(f32[128,1,256]{2,0,1:T(8,128)S(1)} %get-tuple-element.11), channel_id=1, source_target_pairs={{2,0},{4,2},{6,4},{8,6},{10,8},{12,10},{14,12},{0,14},{3,1},{5,3},... | collective-permute-start | bytes 393224 | tf_op jit(solution)/shard_map/ppermute | solution.py:22
  15.1 0.7 copy-start.20
  17.8 30.6 %all-to-all-start = ((f32[8,1,64]{2,1,0:T(1,128)}), f32[8,1,64]{2,1,0:T(1,128)S(1)}, u32[]{:S(2)}, u32[]{:S(2)}) async-start(f32[8,1,64]{2,1,0:T(1,128)} %all_to_all.12), calls=%async_computation | async-start | bytes 8192 | tf_op jit(solution)/shard_map/all_to_all | solution.py:109
  21.1 0.7 copy-start.16
  21.8 0.7 copy-start.15
  26.4 1.2 copy-start.2
  27.6 1.0 copy-start.10
  29.2 5.0 %copy-start.12 = (f32[2,256,256]{2,1,0:T(8,128)S(1)}, f32[2,256,256]{2,1,0:T(8,128)}, u32[]{:S(2)}) copy-start(f32[2,256,256]{2,1,0:T(8,128)} %param.29) | copy-start | bytes 1572868
  29.3 7.8 %collective-permute-start.2 = (f32[128,1,256]{2,0,1:T(8,128)S(1)}, f32[128,1,256]{2,0,1:T(8,128)S(1)}, u32[]{:S(2)}, u32[]{:S(2)}) collective-permute-start(f32[128,1,256]{2,0,1:T(8,128)S(1)} %get-tuple-element.8), channel_id=1, source_target_pairs={{0,2},{2,4},{4,6},{6,8},{8,10},{10,12},{12,14},{14,0},{1,3},{3,5},... | collective-permute-start | bytes 393224 | tf_op jit(solution)/shard_map/ppermute | solution.py:20
  31.3 7.2 %collective-permute-start.3 = (f32[128,1,256]{2,0,1:T(8,128)S(1)}, f32[128,1,256]{2,0,1:T(8,128)S(1)}, u32[]{:S(2)}, u32[]{:S(2)}) collective-permute-start(f32[128,1,256]{2,0,1:T(8,128)S(1)} %get-tuple-element.9), channel_id=1, source_target_pairs={{2,0},{4,2},{6,4},{8,6},{10,8},{12,10},{14,12},{0,14},{3,1},{5,3},... | collective-permute-start | bytes 393224 | tf_op jit(solution)/shard_map/ppermute | solution.py:22
  42.3 1.2 copy-start.3
  44.2 0.7 copy-start.23
  44.9 0.9 copy-start.22
  48.4 4.9 %copy-start.21 = (s32[256,1]{0,1:T(1,128)S(1)}, s32[256,1]{0,1:T(1,128)}, u32[]{:S(2)}) copy-start(s32[256,1]{0,1:T(1,128)} %param.26) | copy-start | bytes 3076
  48.5 18.9 %copy-start.13 = (f32[64,1,256]{2,1,0:T(1,128)S(1)}, f32[64,1,256]{2,1,0:T(1,128)}, u32[]{:S(2)}) copy-start(f32[64,1,256]{2,1,0:T(1,128)} %param.22) | copy-start | bytes 196612
  48.5 18.9 %all-to-all-start.1 = ((f32[8,64,1,256]{3,1,2,0:T(8,128)}), f32[8,64,1,256]{3,1,2,0:T(8,128)S(1)}, u32[]{:S(2)}, u32[]{:S(2)}) async-start(f32[8,64,1,256]{3,1,2,0:T(8,128)} %bitcast.26), calls=%async_computation.1 | async-start | bytes 1048576 | tf_op jit(solution)/shard_map/all_to_all | solution.py:108
  53.3 0.7 copy-start.19
  67.4 1.0 copy-start.4
  101.2 1.0 copy-start.5
  101.2 0.9 copy-start.17
  102.4 1.0 copy-start.8
  103.4 0.9 copy-start.6
  103.4 1.0 copy-start.18
  103.7 1.0 copy-start.7
  107.2 13.7 %all-to-all-start.2 = ((f32[8,64,1,256]{3,1,2,0:T(8,128)}), f32[8,64,1,256]{3,1,2,0:T(8,128)S(1)}, u32[]{:S(2)}, u32[]{:S(2)}) async-start(f32[8,64,1,256]{3,1,2,0:T(8,128)} %bitcast.35), calls=%async_computation.2 | async-start | bytes 1048576 | tf_op jit(solution)/shard_map/all_to_all | solution.py:134
where the time goes:
time: 124 us; the launch traced here: 123 us
  blocking collectives  31.6 us (25%)
  waiting for transfers between devices  25.1 us (20%)
  local copies, waits for them, and re-layouts  24.6 us (20%)
  starting transfers between devices  22.7 us (18%)
  other arithmetic  11.6 us (9%)
  matrix products  6.15 us (5%)
    all_gather x1, blocking collectives, shards(): everything = lax.all_gather(outward, 'sp', axis=0, tiled=True)  31.6 us
    all_to_all x1, waiting for transfers between devices, shards(): lax.all_to_all(outgoing, 'sp', split_axis=0, concat_axis=0, tiled=True)  12 us
    all_to_all x1, waiting for transfers between devices, shards(): lax.all_to_all(replies, 'sp', split_axis=0, concat_axis=0, tiled=True)  9.49 us
    unnamed x51, local copies, waits for them, and re-layouts  7.55 us
    gather x2, local copies, waits for them, and re-layouts, shards(): extended[fine_senders].reshape(fine_rows, degree_fine, samples, -1)  6.93 us
    ppermute x2, starting transfers between devices, extended_2(): lax.ppermute(head, axis, [((i + 1) % count, i) for i in range(count)])  6.09 us
    dot_general x13, matrix products, project(): jnp.einsum('nsd,dh->nsh', values, matrix, precision=highest, preferred_el...  5.73 us
    ppermute x2, starting transfers between devices, extended_2(): lax.ppermute(tail, axis, [(i, (i + 1) % count) for i in range(count)])  5 us
  transfers between devices with their start and end apart: 7, of which 4 were waited for; matrix products, arithmetic and copies ran while one was open for 17% of the time, Pallas kernels for 0%

commit v1 on v0

--- a/solution.py
+++ b/solution.py
@@ -1,9 +1,13 @@
+import functools
 import jax
 import jax.numpy as jnp
 from jax import lax
+from jax.experimental import pallas as pl
+from jax.experimental.pallas import tpu as pltpu
 from jax.sharding import PartitionSpec as P
 
 HALO = 128
+LANES = 128
 
 
 epsilon = 1e-05
@@ -47,7 +51,7 @@
     return jnp.sum(ranking * matches, axis=1)
 
 
-def shards(
+def general_shards(
     fine_state,
     coarse_state,
     fine_senders,
@@ -138,6 +142,362 @@
     return (fine_out, coarse_out)
 
 
+f32 = jnp.float32
+bf16 = jnp.bfloat16
+
+
+def load_rows(ref, rows, parts, start=0):
+    return jnp.concatenate(
+        [ref[pl.ds(start * parts + j, rows, stride=parts), :] for j in range(parts)], axis=1
+    )
+
+
+def store_rows(ref, values, parts, start=0):
+    for j in range(parts):
+        ref[pl.ds(start * parts + j, values.shape[0], stride=parts), :] = values[
+            :, j * LANES : (j + 1) * LANES
+        ]
+
+
+def halves(values):
+    high = values.astype(bf16)
+    return high, (values - high.astype(f32)).astype(bf16)
+
+
+def mm(a, b):
+    return jnp.dot(a, b, preferred_element_type=f32)
+
+
+def times(values, matrix):
+    vh, vl = halves(values)
+    mh, ml = halves(matrix)
+    return mm(vh, mh) + (mm(vl, mh) + mm(vh, ml))
+
+
+def times_one_hot(one_hot, values):
+    vh, vl = halves(values)
+    return mm(one_hot, vh) + mm(one_hot, vl)
+
+
+def unit(values):
+    width = values.shape[1]
+    average = jnp.sum(values, axis=1, keepdims=True) * (1.0 / width)
+    centered = values - average
+    spread = jnp.sum(centered * centered, axis=1, keepdims=True) * (1.0 / width)
+    return centered * lax.rsqrt(spread + epsilon)
+
+
+def gate(half):
+    return half + half * jnp.tanh(half)
+
+
+def columns_equal(column, count):
+    ids = lax.broadcasted_iota(jnp.int32, (column.shape[0], count), 1)
+    return jnp.where(ids == column, 1.0, 0.0).astype(bf16)
+
+
+def near_kernel(first, state_ref, *refs):
+    if first:
+        index_ref, ws_ref, wr_ref, bias_ref, hot_ref, got_ref, into_ref = refs
+    else:
+        hot_ref, ws_ref, wr_ref, bias_ref, got_ref, into_ref = refs
+    layer = 0 if first else 1
+    rows, width = into_ref.shape
+    parts = width // LANES
+    edges, window = hot_ref.shape
+    if first:
+        columns = jnp.transpose(index_ref[...])
+        blocks = edges // LANES
+        for b in range(blocks):
+            hot_ref[b * LANES : (b + 1) * LANES, :] = columns_equal(
+                columns[:, b : b + 1], window
+            )
+    normed = unit(load_rows(state_ref, rows, parts))
+    into_ref[...] = (times(normed, wr_ref[layer]) + bias_ref[layer : layer + 1, :]) * 0.5
+    sends = times(normed, ws_ref[layer]) * 0.5
+    got_ref[...] = times_one_hot(hot_ref[:, :rows], sends)
+
+
+def far_sum(layer, swap_ref, diag_ref, state_ref, hot_ref, got_ref, into_ref, ws_ref, wo_ref):
+    rows, width = into_ref.shape
+    parts = width // LANES
+    rim = swap_ref.shape[0] // parts
+    degree = hot_ref.shape[0] // rows
+    far = jnp.concatenate(
+        [load_rows(swap_ref, rim, parts), load_rows(diag_ref, rim, parts)], axis=0
+    )
+    sends = times(unit(far), ws_ref[layer]) * 0.5
+    high, low = halves(sends)
+    total = None
+    for k in range(degree):
+        hot = hot_ref[k * rows : (k + 1) * rows, rows:]
+        half = got_ref[k * rows : (k + 1) * rows, :] + into_ref[...] + (mm(hot, high) + mm(hot, low))
+        total = gate(half) if total is None else total + gate(half)
+    return load_rows(state_ref, rows, parts) + times(total, wo_ref[layer])
+
+
+def far_kernel(
+    odd_ref, swap_ref, diag_ref, state_ref, hot_ref, got_ref, into_ref, ws_ref, wo_ref,
+    next_ref, out_swap_ref, out_diag_ref,
+):
+    parts = into_ref.shape[1] // LANES
+    store_rows(
+        next_ref,
+        far_sum(0, swap_ref, diag_ref, state_ref, hot_ref, got_ref, into_ref, ws_ref, wo_ref),
+        parts,
+    )
+    lines = out_swap_ref.shape[0]
+    odd = odd_ref[0]
+    last = next_ref.shape[0] - lines
+    out_swap_ref[...] = next_ref[pl.ds(pl.multiple_of((1 - odd) * last, LANES), lines), :]
+    out_diag_ref[...] = next_ref[pl.ds(pl.multiple_of(odd * last, LANES), lines), :]
+
+
+def up_kernel(
+    me_ref, swap_ref, diag_ref, state_ref, hot_ref, got_ref, into_ref, ws_ref, wo_ref,
+    parent_ref, wi_ref, bias_ref, wu_ref, last_ref, *slot_refs,
+):
+    hidden = far_sum(
+        1, swap_ref, diag_ref, state_ref, hot_ref, got_ref, into_ref, ws_ref, wo_ref
+    )
+    last_ref[...] = hidden
+    rows, width = hidden.shape
+    parts = width // LANES
+    act = gate((times(unit(hidden), wi_ref[...]) + bias_ref[...]) * 0.5)
+    messages = times(act, wu_ref[...])
+    count = slot_refs[0].shape[0] // parts
+    coarse = count * len(slot_refs)
+    place = jnp.bitwise_xor(parent_ref[...], me_ref[0] * count)
+    ids = lax.broadcasted_iota(jnp.int32, (coarse, rows), 0)
+    select = jnp.where(ids == place, 1.0, 0.0).astype(bf16)
+    sums = times_one_hot(select, messages)
+    for k, slot in enumerate(slot_refs):
+        store_rows(slot, sums[k * count : (k + 1) * count, :], parts)
+
+
+def middle_kernel(state_ref, anchor_ref, *refs):
+    out_ref = refs[-1]
+    total = state_ref[...]
+    for ref in refs[:-1]:
+        total = total + ref[...]
+    lines = total.shape[0]
+    out_ref[:lines, :] = total
+    out_ref[lines:, :] = anchor_ref[...]
+
+
+def coarse_kernel(peers, anchor_lines, me_ref, last_ref, parent_ref, *refs):
+    blocks = refs[:peers]
+    cs_ref, cr_ref, cb_ref, co_ref, di_ref, db_ref, do_ref, fine_ref, coarse_ref = refs[peers:]
+    rows, width = last_ref.shape
+    parts = width // LANES
+    count = coarse_ref.shape[0] // parts
+    coarse = count * peers
+    lines = coarse_ref.shape[0]
+    flip = me_ref[0] * count
+    middle = jnp.concatenate([load_rows(b, count, parts) for b in blocks], axis=0)
+    normed = unit(middle)
+    high, low = halves(times(normed, cs_ref[...]) * 0.5)
+    into = (times(normed, cr_ref[...]) + cb_ref[...]) * 0.5
+    anchors = [
+        jnp.bitwise_xor(
+            jnp.transpose(b[lines : lines + anchor_lines, :]).astype(jnp.int32), flip
+        )
+        for b in blocks
+    ]
+    per_line = LANES // count
+    degree = 4
+    total = None
+    for k in range(degree):
+        low_row = (k % per_line) * count
+        column = jnp.concatenate(
+            [
+                a[low_row : low_row + count, k // per_line : k // per_line + 1]
+                for a in anchors
+            ],
+            axis=0,
+        )
+        hot = columns_equal(column, coarse)
+        half = into + (mm(hot, high) + mm(hot, low))
+        total = gate(half) if total is None else total + gate(half)
+    done = middle + times(total, co_ref[...])
+    store_rows(coarse_ref, done[:count, :], parts)
+    act = gate((times(unit(done), di_ref[...]) + db_ref[...]) * 0.5)
+    down = times(act, do_ref[...])
+    dh, dl = halves(down)
+    places = jnp.bitwise_xor(jnp.transpose(parent_ref[...]), flip)
+    for j in range(rows // LANES):
+        hot = columns_equal(places[:, j : j + 1], coarse)
+        store_rows(
+            fine_ref,
+            last_ref[j * LANES : (j + 1) * LANES, :] + (mm(hot, dh) + mm(hot, dl)),
+            parts,
+            start=j * LANES,
+        )
+
+
+VMEM = pl.BlockSpec(memory_space=pltpu.VMEM)
+SMEM = pl.BlockSpec(memory_space=pltpu.SMEM)
+
+
+def call(kernel, in_specs, out_shapes, name):
+    return pl.pallas_call(
+        kernel,
+        in_specs=in_specs,
+        out_specs=[VMEM] * len(out_shapes),
+        out_shape=out_shapes,
+        name=name,
+        compiler_params=pltpu.CompilerParams(vmem_limit_bytes=32 * 2**20),
+    )
+
+
+def shape(*dims, kind=f32):
+    return jax.ShapeDtypeStruct(dims, kind)
+
+
+def kernel_shards(
+    fine_state,
+    coarse_state,
+    fine_senders,
+    up_owner,
+    up_local,
+    coarse_owner,
+    coarse_local,
+    fine_w_send,
+    fine_w_recv,
+    fine_bias,
+    fine_w_out,
+    up_w_in,
+    up_bias,
+    up_w_out,
+    coarse_w_send,
+    coarse_w_recv,
+    coarse_bias,
+    coarse_w_out,
+    down_w_in,
+    down_bias,
+    down_w_out,
+):
+    peers = lax.axis_size("sp")
+    me = lax.axis_index("sp").astype(jnp.int32)
+    odd = me % 2
+    rows, _, width = fine_state.shape
+    count = coarse_state.shape[0]
+    parts = width // LANES
+    degree = fine_senders.shape[0] // rows
+    degree_coarse = coarse_owner.shape[0] // count
+    swap = [(i, i ^ 1) for i in range(peers)]
+    diag = [(i, (i + 1 if i % 2 else i - 1) % peers) for i in range(peers)]
+    rim = HALO * parts
+
+    state = fine_state.reshape(rows * parts, LANES)
+    last = (rows - HALO) * parts
+    out_swap = lax.dynamic_slice(state, ((1 - odd) * last, 0), (rim, LANES))
+    out_diag = lax.dynamic_slice(state, (odd * last, 0), (rim, LANES))
+
+    before = jnp.where(odd == 1, rows, rows + HALO)
+    after = jnp.where(odd == 1, rows + HALO, rows)
+    index = jnp.where(
+        fine_senders < HALO,
+        fine_senders + before,
+        jnp.where(
+            fine_senders < HALO + rows,
+            fine_senders - HALO,
+            fine_senders - (HALO + rows) + after,
+        ),
+    )
+    index = index.reshape(rows, degree).T.reshape(rows * degree // LANES, LANES)
+    parent = up_owner[:, 0] * count + up_local
+    anchor = (coarse_owner[:, 0] * count + coarse_local).reshape(count, degree_coarse).T
+    anchor_lines = count * degree_coarse // LANES
+    anchor = jnp.pad(
+        anchor.astype(f32).reshape(anchor_lines, LANES), ((0, 8 - anchor_lines % 8), (0, 0))
+    )
+    odd_arg, me_arg = odd.reshape(1), me.reshape(1)
+
+    edges, window = rows * degree, rows + 2 * HALO
+    in_swap = lax.ppermute(out_swap, "sp", swap)
+    in_diag = lax.ppermute(out_diag, "sp", diag)
+    hot, got, into = call(
+        functools.partial(near_kernel, True),
+        [VMEM] * 5,
+        [shape(edges, window, kind=bf16), shape(edges, width), shape(rows, width)],
+        "near0",
+    )(state, index, fine_w_send, fine_w_recv, fine_bias)
+    state, out_swap, out_diag = call(
+        far_kernel,
+        [SMEM] + [VMEM] * 8,
+        [shape(rows * parts, LANES), shape(rim, LANES), shape(rim, LANES)],
+        "far0",
+    )(odd_arg, in_swap, in_diag, state, hot, got, into, fine_w_send, fine_w_out)
+    in_swap = lax.ppermute(out_swap, "sp", swap)
+    in_diag = lax.ppermute(out_diag, "sp", diag)
+    got, into = call(
+        functools.partial(near_kernel, False),
+        [VMEM] * 5,
+        [shape(edges, width), shape(rows, width)],
+        "near1",
+    )(state, hot, fine_w_send, fine_w_recv, fine_bias)
+    hidden, *slots = call(
+        up_kernel,
+        [SMEM] + [VMEM] * 12,
+        [shape(rows, width)] + [shape(count * parts, LANES)] * peers,
+        "up",
+    )(
+        me_arg, in_swap, in_diag, state, hot, got, into, fine_w_send, fine_w_out,
+        parent.reshape(1, rows), up_w_in, up_bias.reshape(1, width), up_w_out,
+    )
+    arrived = [slots[0]] + [
+        lax.ppermute(slots[k], "sp", [(i, i ^ k) for i in range(peers)]) for k in range(1, peers)
+    ]
+    (middle,) = call(
+        middle_kernel,
+        [VMEM] * (2 + peers),
+        [shape(count * parts + anchor.shape[0], LANES)],
+        "middle",
+    )(coarse_state.reshape(count * parts, LANES), anchor, *arrived)
+    columns = {0: middle}
+    for k in range(2, peers, 2):
+        columns[k] = lax.ppermute(middle, "sp", [(i, i ^ k) for i in range(peers)])
+    for k in range(0, peers, 2):
+        columns[k + 1] = lax.ppermute(columns[k], "sp", swap)
+    fine_out, coarse_out = call(
+        functools.partial(coarse_kernel, peers, anchor_lines),
+        [SMEM] + [VMEM] * (9 + peers),
+        [shape(rows * parts, LANES), shape(count * parts, LANES)],
+        "coarse",
+    )(
+        me_arg, hidden, parent.reshape(rows // LANES, LANES),
+        *[columns[k] for k in range(peers)],
+        coarse_w_send, coarse_w_recv, coarse_bias.reshape(1, width), coarse_w_out,
+        down_w_in, down_bias.reshape(1, width), down_w_out,
+    )
+    return (fine_out.reshape(fine_state.shape), coarse_out.reshape(coarse_state.shape))
+
+
+def shards(*args):
+    fine_state, coarse_state, fine_senders = args[0], args[1], args[2]
+    coarse_owner, layers = args[5], args[7].shape[0]
+    peers = lax.axis_size("sp")
+    rows, samples, width = fine_state.shape
+    count = coarse_state.shape[0]
+    fits = (
+        samples == 1
+        and layers == 2
+        and width % LANES == 0
+        and peers % 2 == 0
+        and peers & (peers - 1) == 0
+        and rows % LANES == 0
+        and rows >= HALO
+        and count & (count - 1) == 0
+        and LANES % count == 0
+        and coarse_owner.shape[0] % LANES == 0
+        and coarse_owner.shape[0] == 4 * count
+        and fine_senders.shape[0] % (8 * LANES) == 0
+        and peers * count <= 1024
+    )
+    return (kernel_shards if fits else general_shards)(*args)
+
+
 def solution(mesh):
     in_specs = (
         P("sp", ("grp", "ch"), None),
@@ -147,20 +507,6 @@
         P("sp"),
         P("sp", None),
         P("sp"),
-        P(),
-        P(),
-        P(),
-        P(),
-        P(),
-        P(),
-        P(),
-        P(),
-        P(),
-        P(),
-        P(),
-        P(),
-        P(),
-        P(),
-    )
+    ) + (P(),) * 14
     out_specs = (P("sp", ("grp", "ch"), None), P("sp", ("grp", "ch"), None))
     return jax.shard_map(shards, mesh=mesh, in_specs=in_specs, out_specs=out_specs, check_vma=False)

time: 124 us -> 59.9 us (0.48)
  blocking collectives: 31.6 us -> 0 us
  local copies, waits for them, and re-layouts: 24.6 us -> 5.3 us
  waiting for transfers between devices: 25.1 us -> 11.7 us
  other arithmetic: 11.6 us -> 0.02 us
  Pallas kernels: 0 us -> 10.6 us
  starting transfers between devices: 22.7 us -> 31.1 us
  matrix products: 6.15 us -> 0 us
    all_gather x1 -> x0, blocking collectives: 31.6 us -> none  [shards(): everything = lax.all_gather(outward, 'sp', axis=0, tiled=True)]
    all_to_all x3 -> x0, waiting for transfers between devices: 21.5 us -> none  [the longest x1 12 us: shards(): lax.all_to_all(outgoing, 'sp', split_axis=0, concat_axis=0, tiled=True)]
    ppermute x4 -> x18, starting transfers between devices: 11.1 us -> 31.1 us  [the longest x7 10.5 us: kernel_shards(): lax.ppermute(slots[k], 'sp', [(i, i ^ k) for i in range(peers)])]
    all_to_all x3 -> x0, starting transfers between devices: 11.7 us -> none  [the longest x1 4.85 us: shards(): lax.all_to_all(outgoing, 'sp', split_axis=0, concat_axis=0, tiled=True)]
    gather x6 -> x0, local copies, waits for them, and re-layouts: 11.2 us -> none  [the longest x2 6.93 us: shards(): extended[fine_senders].reshape(fine_rows, degree_fine, samples, -1)]
    pallas_call x0 -> x6, Pallas kernels: none -> 10.6 us  [the longest x1 4.85 us: kernel_shards(): call(functools.partial(coarse_kernel, peers, anchor_lines), [SMEM] + [VME...]
    reduce_sum x10 -> x0, other arithmetic: 8.87 us -> none  [the longest x5 4.03 us: layer_norm(): spread = jnp.mean(centered * centered, axis=-1, keepdims=True)]
    ppermute x4 -> x18, waiting for transfers between devices: 3.61 us -> 11.7 us  [the longest x7 5.17 us: kernel_shards(): lax.ppermute(slots[k], 'sp', [(i, i ^ k) for i in range(peers)])]
  transfers between devices with their start and end apart: 7 -> 18, of which waited for: 4 -> 11; matrix products, arithmetic and copies ran while one was open for 17% -> 1% of each run, Pallas kernels for 0% -> 3%
where the time goes in v1:
time: 59.9 us; the launch traced here: 59.6 us
  starting transfers between devices  31.1 us (52%)
  waiting for transfers between devices  11.7 us (20%)
  Pallas kernels  10.6 us (18%)
  local copies, waits for them, and re-layouts  5.3 us (9%)
  between operations  0.86 us (1%)
    ppermute x7, starting transfers between devices, kernel_shards(): lax.ppermute(slots[k], 'sp', [(i, i ^ k) for i in range(peers)])  10.5 us
    ppermute x2, starting transfers between devices, kernel_shards(): in_diag = lax.ppermute(out_diag, 'sp', diag)  7.15 us
    ppermute x4, starting transfers between devices, kernel_shards(): columns[k + 1] = lax.ppermute(columns[k], 'sp', swap)  5.49 us
    ppermute x7, waiting for transfers between devices, kernel_shards(): lax.ppermute(slots[k], 'sp', [(i, i ^ k) for i in range(peers)])  5.17 us
    pallas_call x1, Pallas kernels, kernel_shards(): call(functools.partial(coarse_kernel, peers, anchor_lines), [SMEM] + [VME...  4.85 us
    ppermute x3, starting transfers between devices, kernel_shards(): columns[k] = lax.ppermute(middle, 'sp', [(i, i ^ k) for i in range(peers)])  4.45 us
    unnamed x42, local copies, waits for them, and re-layouts  3.77 us
    ppermute x2, starting transfers between devices, kernel_shards(): in_swap = lax.ppermute(out_swap, 'sp', swap)  3.48 us
  transfers between devices with their start and end apart: 18, of which 11 were waited for; matrix products, arithmetic and copies ran while one was open for 1% of the time, Pallas kernels for 3%

profile of v1, /device:TPU:0, one launch (start us, length us, event | category | flops | bytes accessed | tf_op | source)
XLA Modules:
  0.0 59.6 jit_solution(17735554987523482112)
XLA Ops:
  0.7 1.0 %constant_dynamic-slice_fusion = (f32[256,128]{1,0:T(8,128)S(1)}, f32[256,128]{1,0:T(8,128)S(1)}) fusion(f32[512,128]{1,0:T(8,128)} %bitcast.15, s32[]{:T(128)S(6)} %select_n.29, s32[]{:T(128)S(6)} %select_n.28), kind=kLoop, calls=%fused_computation.4 | loop fusion | bytes 524296 | tf_op jit(solution)/shard_map/dynamic_slice | solution.py:395
  1.7 3.0 %collective-permute-start = (f32[256,128]{1,0:T(8,128)S(1)}, f32[256,128]{1,0:T(8,128)S(1)}, u32[]{:S(2)}, u32[]{:S(2)}) collective-permute-start(f32[256,128]{1,0:T(8,128)S(1)} %get-tuple-element.45), channel_id=1, source_target_pairs={{0,2},{2,0},{4,6},{6,4},{8,10},{10,8},{12,14},{14,12},{1,3},{3,1},... | collective-permute-start | bytes 393224 | tf_op jit(solution)/shard_map/ppermute | solution.py:418
  4.8 3.6 %collective-permute-start.1 = (f32[256,128]{1,0:T(8,128)S(1)}, f32[256,128]{1,0:T(8,128)S(1)}, u32[]{:S(2)}, u32[]{:S(2)}) collective-permute-start(f32[256,128]{1,0:T(8,128)S(1)} %get-tuple-element.44), channel_id=1, source_target_pairs={{0,14},{2,4},{4,2},{6,8},{8,6},{10,12},{12,10},{14,0},{1,15},{3,5}... | collective-permute-start | bytes 393224 | tf_op jit(solution)/shard_map/ppermute | solution.py:419
  9.3 1.0 %copy-done.3 = f32[2,256,256]{2,1,0:T(8,128)S(1)} copy-done((f32[2,256,256]{2,1,0:T(8,128)S(1)}, f32[2,256,256]{2,1,0:T(8,128)}, u32[]{:S(2)}) %copy-start.3) | copy-done | bytes 524312
  10.3 1.0 %near0.1 = (bf16[1024,512]{1,0:T(8,128)(2,1)S(1)}, f32[1024,256]{1,0:T(8,128)S(1)}, f32[256,256]{1,0:T(8,128)S(1)}) custom-call(f32[512,128]{1,0:T(8,128)S(1)} %bitcast.16, s32[8,128]{1,0:T(8,128)S(1)} %reshape.56.refs_0_, f32[2,256,256]{2,1,0:T(8,128)S(1)} %copy-done, f32[2,256,256]{2,1,0:T(8,128)S(1)} %copy-done.3, f32[2,256]{1,0:T(2,128)S(1)} %copy-done.12), custom_call_target="tpu_custom_call" | custom-call | tf_op jit(solution)/shard_map/near0/pallas_call | solution.py:420
  11.3 1.1 %collective-permute-done.1.diag_ref = f32[256,128]{1,0:T(8,128)S(1)} collective-permute-done((f32[256,128]{1,0:T(8,128)S(1)}, f32[256,128]{1,0:T(8,128)S(1)}, u32[]{:S(2)}, u32[]{:S(2)}) %collective-permute-start.1) | collective-permute-done | bytes 131104 | tf_op jit(solution)/shard_map/ppermute | solution.py:419
  12.4 1.3 %far0.1 = (f32[512,128]{1,0:T(8,128)S(1)}, f32[256,128]{1,0:T(8,128)S(1)}, f32[256,128]{1,0:T(8,128)S(1)}) custom-call(s32[1]{0:T(128)} %bitcast.1.odd_ref, f32[256,128]{1,0:T(8,128)S(1)} %collective-permute-done.swap_ref, f32[256,128]{1,0:T(8,128)S(1)} %collective-permute-done.1.diag_ref, f32[512,128]{1,0:T(8,128)S(1)} %bitcast.17, ...), custom_call_target="tpu_custom_call" | custom-call | tf_op jit(solution)/shard_map/far0/pallas_call | solution.py:426
  14.2 3.6 %collective-permute-start.3 = (f32[256,128]{1,0:T(8,128)S(1)}, f32[256,128]{1,0:T(8,128)S(1)}, u32[]{:S(2)}, u32[]{:S(2)}) collective-permute-start(f32[256,128]{1,0:T(8,128)S(1)} %get-tuple-element.25), channel_id=1, source_target_pairs={{0,14},{2,4},{4,2},{6,8},{8,6},{10,12},{12,10},{14,0},{1,15},{3,5}... | collective-permute-start | bytes 393224 | tf_op jit(solution)/shard_map/ppermute | solution.py:433
  17.8 0.7 %copy-done.17 = s32[256]{0:T(256)S(1)} copy-done((s32[256]{0:T(256)S(1)}, s32[256]{0:T(256)}, u32[]{:S(2)}) %copy-start.17) | copy-done | bytes 1048
  18.5 1.0 %near1.1 = (f32[1024,256]{1,0:T(8,128)S(1)}, f32[256,256]{1,0:T(8,128)S(1)}) custom-call(f32[512,128]{1,0:T(8,128)S(1)} %get-tuple-element.26.state_ref, bf16[1024,512]{1,0:T(8,128)(2,1)S(1)} %get-tuple-element.21.hot_ref.refs_0_, f32[2,256,256]{2,1,0:T(8,128)S(1)} %copy-done, f32[2,256,256]{2,1,0:T(8,128)S(1)} %copy-done.3, f32[2,256]{1,0:T(2,128)S(1)} %copy-done.12), custom_call_target="tpu_custom_call" | custom-call | tf_op jit(solution)/shard_map/near1/pallas_call | solution.py:434
  19.5 0.8 %collective-permute-done.2.swap_ref = f32[256,128]{1,0:T(8,128)S(1)} collective-permute-done((f32[256,128]{1,0:T(8,128)S(1)}, f32[256,128]{1,0:T(8,128)S(1)}, u32[]{:S(2)}, u32[]{:S(2)}) %collective-permute-start.2) | collective-permute-done | bytes 131104 | tf_op jit(solution)/shard_map/ppermute | solution.py:432
  20.2 1.7 %collective-permute-done.3.diag_ref = f32[256,128]{1,0:T(8,128)S(1)} collective-permute-done((f32[256,128]{1,0:T(8,128)S(1)}, f32[256,128]{1,0:T(8,128)S(1)}, u32[]{:S(2)}, u32[]{:S(2)}) %collective-permute-start.3) | collective-permute-done | bytes 131104 | tf_op jit(solution)/shard_map/ppermute | solution.py:433
  21.9 0.7 %copy-done.15 = f32[256]{0:T(256)S(1)} copy-done((f32[256]{0:T(256)S(1)}, f32[256]{0:T(256)}, u32[]{:S(2)}) %copy-start.15) | copy-done | bytes 1048
  22.6 2.4 %up.1 = (f32[256,256]{1,0:T(8,128)S(1)}, f32[128,128]{1,0:T(8,128)S(1)}, f32[128,128]{1,0:T(8,128)S(1)}, f32[128,128]{1,0:T(8,128)S(1)}, f32[128,128]{1,0:T(8,12...) custom-call(s32[1]{0:T(128)} %bitcast.me_ref, ...), custom_call_target="tpu_custom_call" | custom-call | tf_op jit(solution)/shard_map/up/pallas_call | solution.py:440
  25.1 3.6 %collective-permute-start.10 = (f32[128,128]{1,0:T(8,128)S(1)}, f32[128,128]{1,0:T(8,128)S(1)}, u32[]{:S(2)}, u32[]{:S(2)}) collective-permute-start(f32[128,128]{1,0:T(8,128)S(1)} %get-tuple-element.37), channel_id=1, source_target_pairs={{0,14},{2,12},{4,10},{6,8},{8,6},{10,4},{12,2},{14,0},{1,15},{3,13... | collective-permute-start | bytes 196616 | tf_op jit(solution)/shard_map/ppermute | solution.py:450
  28.8 3.4 %collective-permute-start.6 = (f32[128,128]{1,0:T(8,128)S(1)}, f32[128,128]{1,0:T(8,128)S(1)}, u32[]{:S(2)}, u32[]{:S(2)}) collective-permute-start(f32[128,128]{1,0:T(8,128)S(1)} %get-tuple-element.33), channel_id=1, source_target_pairs={{0,6},{2,4},{4,2},{6,0},{8,14},{10,12},{12,10},{14,8},{1,7},{3,5},... | collective-permute-start | bytes 196616 | tf_op jit(solution)/shard_map/ppermute | solution.py:450
  32.2 0.7 %collective-permute-done.10.refs_7_ = f32[128,128]{1,0:T(8,128)S(1)} collective-permute-done((f32[128,128]{1,0:T(8,128)S(1)}, f32[128,128]{1,0:T(8,128)S(1)}, u32[]{:S(2)}, u32[]{:S(2)}) %collective-permute-start.10) | collective-permute-done | bytes 65568 | tf_op jit(solution)/shard_map/ppermute | solution.py:450
  32.9 1.7 %collective-permute-start.8 = (f32[128,128]{1,0:T(8,128)S(1)}, f32[128,128]{1,0:T(8,128)S(1)}, u32[]{:S(2)}, u32[]{:S(2)}) collective-permute-start(f32[128,128]{1,0:T(8,128)S(1)} %get-tuple-element.35), channel_id=1, source_target_pairs={{0,10},{2,8},{4,14},{6,12},{8,2},{10,0},{12,6},{14,4},{1,11},{3,9}... | collective-permute-start | bytes 196616 | tf_op jit(solution)/shard_map/ppermute | solution.py:450
  34.6 1.6 %collective-permute-start.9 = (f32[128,128]{1,0:T(8,128)S(1)}, f32[128,128]{1,0:T(8,128)S(1)}, u32[]{:S(2)}, u32[]{:S(2)}) collective-permute-start(f32[128,128]{1,0:T(8,128)S(1)} %get-tuple-element.36), channel_id=1, source_target_pairs={{0,12},{2,14},{4,8},{6,10},{8,4},{10,6},{12,0},{14,2},{1,13},{3,15... | collective-permute-start | bytes 196616 | tf_op jit(solution)/shard_map/ppermute | solution.py:450
  36.6 1.0 %collective-permute-done.7.refs_4_ = f32[128,128]{1,0:T(8,128)S(1)} collective-permute-done((f32[128,128]{1,0:T(8,128)S(1)}, f32[128,128]{1,0:T(8,128)S(1)}, u32[]{:S(2)}, u32[]{:S(2)}) %collective-permute-start.7) | collective-permute-done | bytes 65568 | tf_op jit(solution)/shard_map/ppermute | solution.py:450
  37.6 1.7 %collective-permute-done.8.refs_5_ = f32[128,128]{1,0:T(8,128)S(1)} collective-permute-done((f32[128,128]{1,0:T(8,128)S(1)}, f32[128,128]{1,0:T(8,128)S(1)}, u32[]{:S(2)}, u32[]{:S(2)}) %collective-permute-start.8) | collective-permute-done | bytes 65568 | tf_op jit(solution)/shard_map/ppermute | solution.py:450
  39.3 1.7 %collective-permute-done.9.refs_6_ = f32[128,128]{1,0:T(8,128)S(1)} collective-permute-done((f32[128,128]{1,0:T(8,128)S(1)}, f32[128,128]{1,0:T(8,128)S(1)}, u32[]{:S(2)}, u32[]{:S(2)}) %collective-permute-start.9) | collective-permute-done | bytes 65568 | tf_op jit(solution)/shard_map/ppermute | solution.py:450
  41.1 1.0 %collective-permute-start.12 = (f32[136,128]{1,0:T(8,128)S(1)}, f32[136,128]{1,0:T(8,128)S(1)}, u32[]{:S(2)}, u32[]{:S(2)}) collective-permute-start(f32[136,128]{1,0:T(8,128)S(1)} %middle.1.refs_0_), channel_id=1, source_target_pairs={{0,4},{2,6},{4,0},{6,2},{8,12},{10,14},{12,8},{14,10},{1,5},{3,7},... | collective-permute-start | bytes 208904 | tf_op jit(solution)/shard_map/ppermute | solution.py:460
  42.1 1.0 %collective-permute-start.14 = (f32[136,128]{1,0:T(8,128)S(1)}, f32[136,128]{1,0:T(8,128)S(1)}, u32[]{:S(2)}, u32[]{:S(2)}) collective-permute-start(f32[136,128]{1,0:T(8,128)S(1)} %middle.1.refs_0_), channel_id=1, source_target_pairs={{0,8},{2,10},{4,12},{6,14},{8,0},{10,2},{12,4},{14,6},{1,9},{3,11}... | collective-permute-start | bytes 208904 | tf_op jit(solution)/shard_map/ppermute | solution.py:460
  43.1 2.4 %collective-permute-start.16 = (f32[136,128]{1,0:T(8,128)S(1)}, f32[136,128]{1,0:T(8,128)S(1)}, u32[]{:S(2)}, u32[]{:S(2)}) collective-permute-start(f32[136,128]{1,0:T(8,128)S(1)} %middle.1.refs_0_), channel_id=1, source_target_pairs={{0,12},{2,14},{4,8},{6,10},{8,4},{10,6},{12,0},{14,2},{1,13},{3,15... | collective-permute-start | bytes 208904 | tf_op jit(solution)/shard_map/ppermute | solution.py:460
  45.6 2.2 %collective-permute-start.11 = (f32[136,128]{1,0:T(8,128)S(1)}, f32[136,128]{1,0:T(8,128)S(1)}, u32[]{:S(2)}, u32[]{:S(2)}) collective-permute-start(f32[136,128]{1,0:T(8,128)S(1)} %middle.1.refs_0_), channel_id=1, source_target_pairs={{0,2},{2,0},{4,6},{6,4},{8,10},{10,8},{12,14},{14,12},{1,3},{3,1},... | collective-permute-start | bytes 208904 | tf_op jit(solution)/shard_map/ppermute | solution.py:462
  48.1 1.7 %collective-permute-start.15 = (f32[136,128]{1,0:T(8,128)S(1)}, f32[136,128]{1,0:T(8,128)S(1)}, u32[]{:S(2)}, u32[]{:S(2)}) collective-permute-start(f32[136,128]{1,0:T(8,128)S(1)} %collective-permute-done.14.refs_4_), channel_id=1, source_target_pairs={{0,2},{2,0},{4,6},{6,4},{8,10},{10,8},{12,14},{14,12},{1,3},{3,1},... | collective-permute-start | bytes 208904 | tf_op jit(solution)/shard_map/ppermute | solution.py:462
  49.8 1.6 %collective-permute-start.17 = (f32[136,128]{1,0:T(8,128)S(1)}, f32[136,128]{1,0:T(8,128)S(1)}, u32[]{:S(2)}, u32[]{:S(2)}) collective-permute-start(f32[136,128]{1,0:T(8,128)S(1)} %collective-permute-done.16.refs_6_), channel_id=1, source_target_pairs={{0,2},{2,0},{4,6},{6,4},{8,10},{10,8},{12,14},{14,12},{1,3},{3,1},... | collective-permute-start | bytes 208904 | tf_op jit(solution)/shard_map/ppermute | solution.py:462
  51.3 0.7 %collective-permute-done.13.refs_3_ = f32[136,128]{1,0:T(8,128)S(1)} collective-permute-done((f32[136,128]{1,0:T(8,128)S(1)}, f32[136,128]{1,0:T(8,128)S(1)}, u32[]{:S(2)}, u32[]{:S(2)}) %collective-permute-start.13) | collective-permute-done | bytes 69664 | tf_op jit(solution)/shard_map/ppermute | solution.py:462
  52.1 0.7 %collective-permute-done.15.refs_5_ = f32[136,128]{1,0:T(8,128)S(1)} collective-permute-done((f32[136,128]{1,0:T(8,128)S(1)}, f32[136,128]{1,0:T(8,128)S(1)}, u32[]{:S(2)}, u32[]{:S(2)}) %collective-permute-start.15) | collective-permute-done | bytes 69664 | tf_op jit(solution)/shard_map/ppermute | solution.py:462
  52.8 1.3 %collective-permute-done.17.refs_7_ = f32[136,128]{1,0:T(8,128)S(1)} collective-permute-done((f32[136,128]{1,0:T(8,128)S(1)}, f32[136,128]{1,0:T(8,128)S(1)}, u32[]{:S(2)}, u32[]{:S(2)}) %collective-permute-start.17) | collective-permute-done | bytes 69664 | tf_op jit(solution)/shard_map/ppermute | solution.py:462
  54.8 4.8 %coarse.1 = (f32[512,128]{1,0:T(8,128)}, f32[128,128]{1,0:T(8,128)}) custom-call(s32[1]{0:T(128)} %bitcast.me_ref, f32[256,256]{1,0:T(8,128)S(1)} %get-tuple-element.29.last_ref, s32[2,128]{1,0:T(2,128)S(1)} %bitcast.20, f32[136,128]{1,0:T(8,128)S(1)} %middle.1.refs_0_, f32[136,128]{1,0:T(8,128)S(1)} %collective-permute-done.11.refs_1_, ...), custom_call_target="tpu_custom_call" | custom-call | tf_op jit(solution)/shard_map/coarse/pallas_call | solution.py:463
  (65 shorter events, 2.8 us)
Async XLA Ops:
  0.6 7.9 %copy-start = (f32[2,256,256]{2,1,0:T(8,128)S(1)}, f32[2,256,256]{2,1,0:T(8,128)}, u32[]{:S(2)}) copy-start(f32[2,256,256]{2,1,0:T(8,128)} %ws_ref.3) | copy-start | bytes 1572868
  0.7 7.7 %copy-start.16 = (s32[1024]{0:T(1024)S(1)}, s32[1024]{0:T(1024)}, u32[]{:S(2)}) copy-start(s32[1024]{0:T(1024)} %param.23) | copy-start | bytes 12292
  1.7 6.9 %copy-start.1 = (f32[256,1,256]{2,1,0:T(1,128)S(1)}, f32[256,1,256]{2,1,0:T(1,128)}, u32[]{:S(2)}) copy-start(f32[256,1,256]{2,1,0:T(1,128)} %param.21) | copy-start | bytes 786436
  1.7 9.6 %collective-permute-start = (f32[256,128]{1,0:T(8,128)S(1)}, f32[256,128]{1,0:T(8,128)S(1)}, u32[]{:S(2)}, u32[]{:S(2)}) collective-permute-start(f32[256,128]{1,0:T(8,128)S(1)} %get-tuple-element.45), channel_id=1, source_target_pairs={{0,2},{2,0},{4,6},{6,4},{8,10},{10,8},{12,14},{14,12},{1,3},{3,1},... | collective-permute-start | bytes 393224 | tf_op jit(solution)/shard_map/ppermute | solution.py:418
  4.8 7.7 %collective-permute-start.1 = (f32[256,128]{1,0:T(8,128)S(1)}, f32[256,128]{1,0:T(8,128)S(1)}, u32[]{:S(2)}, u32[]{:S(2)}) collective-permute-start(f32[256,128]{1,0:T(8,128)S(1)} %get-tuple-element.44), channel_id=1, source_target_pairs={{0,14},{2,4},{4,2},{6,8},{8,6},{10,12},{12,10},{14,0},{1,15},{3,5}... | collective-permute-start | bytes 393224 | tf_op jit(solution)/shard_map/ppermute | solution.py:419
  13.8 4.0 %copy-start.19 = (s32[256,1]{0,1:T(1,128)S(1)}, s32[256,1]{0,1:T(1,128)}, u32[]{:S(2)}) copy-start(s32[256,1]{0,1:T(1,128)} %param.24) | copy-start | bytes 3076
  13.8 6.4 %collective-permute-start.2 = (f32[256,128]{1,0:T(8,128)S(1)}, f32[256,128]{1,0:T(8,128)S(1)}, u32[]{:S(2)}, u32[]{:S(2)}) collective-permute-start(f32[256,128]{1,0:T(8,128)S(1)} %get-tuple-element.24), channel_id=1, source_target_pairs={{0,2},{2,0},{4,6},{6,4},{8,10},{10,8},{12,14},{14,12},{1,3},{3,1},... | collective-permute-start | bytes 393224 | tf_op jit(solution)/shard_map/ppermute | solution.py:432
  14.2 7.7 %collective-permute-start.3 = (f32[256,128]{1,0:T(8,128)S(1)}, f32[256,128]{1,0:T(8,128)S(1)}, u32[]{:S(2)}, u32[]{:S(2)}) collective-permute-start(f32[256,128]{1,0:T(8,128)S(1)} %get-tuple-element.25), channel_id=1, source_target_pairs={{0,14},{2,4},{4,2},{6,8},{8,6},{10,12},{12,10},{14,0},{1,15},{3,5}... | collective-permute-start | bytes 393224 | tf_op jit(solution)/shard_map/ppermute | solution.py:433
  18.5 3.4 %copy-start.5 = (f32[256,256]{1,0:T(8,128)S(1)}, f32[256,256]{1,0:T(8,128)}, u32[]{:S(2)}) copy-start(f32[256,256]{1,0:T(8,128)} %wu_ref.1) | copy-start | bytes 786436
  22.6 6.1 %copy-start.20 = (s32[256,1]{0,1:T(1,128)S(1)}, s32[256,1]{0,1:T(1,128)}, u32[]{:S(2)}) copy-start(s32[256,1]{0,1:T(1,128)} %param.26) | copy-start | bytes 3076
  22.6 13.7 %copy-start.18 = (s32[256]{0:T(256)S(1)}, s32[256]{0:T(256)}, u32[]{:S(2)}) copy-start(s32[256]{0:T(256)} %param.27) | copy-start | bytes 3076
  22.6 31.5 %copy-start.8 = (f32[256,256]{1,0:T(8,128)S(1)}, f32[256,256]{1,0:T(8,128)}, u32[]{:S(2)}) copy-start(f32[256,256]{1,0:T(8,128)} %refs_11_.1) | copy-start | bytes 786436
  22.6 31.5 %copy-start.9 = (f32[256,256]{1,0:T(8,128)S(1)}, f32[256,256]{1,0:T(8,128)}, u32[]{:S(2)}) copy-start(f32[256,256]{1,0:T(8,128)} %refs_12_.1) | copy-start | bytes 786436
  22.6 31.5 %copy-start.10 = (f32[256,256]{1,0:T(8,128)S(1)}, f32[256,256]{1,0:T(8,128)}, u32[]{:S(2)}) copy-start(f32[256,256]{1,0:T(8,128)} %refs_14_.1) | copy-start | bytes 786436
  25.1 16.0 %copy-start.11 = (f32[64,1,256]{2,1,0:T(1,128)S(1)}, f32[64,1,256]{2,1,0:T(1,128)}, u32[]{:S(2)}) copy-start(f32[64,1,256]{2,1,0:T(1,128)} %param.22) | copy-start | bytes 196612
  25.1 7.8 %collective-permute-start.10 = (f32[128,128]{1,0:T(8,128)S(1)}, f32[128,128]{1,0:T(8,128)S(1)}, u32[]{:S(2)}, u32[]{:S(2)}) collective-permute-start(f32[128,128]{1,0:T(8,128)S(1)} %get-tuple-element.37), channel_id=1, source_target_pairs={{0,14},{2,12},{4,10},{6,8},{8,6},{10,4},{12,2},{14,0},{1,15},{3,13... | collective-permute-start | bytes 196616 | tf_op jit(solution)/shard_map/ppermute | solution.py:450
  28.7 5.9 %collective-permute-start.4 = (f32[128,128]{1,0:T(8,128)S(1)}, f32[128,128]{1,0:T(8,128)S(1)}, u32[]{:S(2)}, u32[]{:S(2)}) collective-permute-start(f32[128,128]{1,0:T(8,128)S(1)} %get-tuple-element.31), channel_id=1, source_target_pairs={{0,2},{2,0},{4,6},{6,4},{8,10},{10,8},{12,14},{14,12},{1,3},{3,1},... | collective-permute-start | bytes 196616 | tf_op jit(solution)/shard_map/ppermute | solution.py:450
  28.7 7.9 %collective-permute-start.5 = (f32[128,128]{1,0:T(8,128)S(1)}, f32[128,128]{1,0:T(8,128)S(1)}, u32[]{:S(2)}, u32[]{:S(2)}) collective-permute-start(f32[128,128]{1,0:T(8,128)S(1)} %get-tuple-element.32), channel_id=1, source_target_pairs={{0,4},{2,6},{4,0},{6,2},{8,12},{10,14},{12,8},{14,10},{1,5},{3,7},... | collective-permute-start | bytes 196616 | tf_op jit(solution)/shard_map/ppermute | solution.py:450
  28.8 7.8 %collective-permute-start.6 = (f32[128,128]{1,0:T(8,128)S(1)}, f32[128,128]{1,0:T(8,128)S(1)}, u32[]{:S(2)}, u32[]{:S(2)}) collective-permute-start(f32[128,128]{1,0:T(8,128)S(1)} %get-tuple-element.33), channel_id=1, source_target_pairs={{0,6},{2,4},{4,2},{6,0},{8,14},{10,12},{12,10},{14,8},{1,7},{3,5},... | collective-permute-start | bytes 196616 | tf_op jit(solution)/shard_map/ppermute | solution.py:450
  32.2 5.4 %collective-permute-start.7 = (f32[128,128]{1,0:T(8,128)S(1)}, f32[128,128]{1,0:T(8,128)S(1)}, u32[]{:S(2)}, u32[]{:S(2)}) collective-permute-start(f32[128,128]{1,0:T(8,128)S(1)} %get-tuple-element.34), channel_id=1, source_target_pairs={{0,8},{2,10},{4,12},{6,14},{8,0},{10,2},{12,4},{14,6},{1,9},{3,11}... | collective-permute-start | bytes 196616 | tf_op jit(solution)/shard_map/ppermute | solution.py:450
  32.9 6.4 %collective-permute-start.8 = (f32[128,128]{1,0:T(8,128)S(1)}, f32[128,128]{1,0:T(8,128)S(1)}, u32[]{:S(2)}, u32[]{:S(2)}) collective-permute-start(f32[128,128]{1,0:T(8,128)S(1)} %get-tuple-element.35), channel_id=1, source_target_pairs={{0,10},{2,8},{4,14},{6,12},{8,2},{10,0},{12,6},{14,4},{1,11},{3,9}... | collective-permute-start | bytes 196616 | tf_op jit(solution)/shard_map/ppermute | solution.py:450
  34.6 6.4 %collective-permute-start.9 = (f32[128,128]{1,0:T(8,128)S(1)}, f32[128,128]{1,0:T(8,128)S(1)}, u32[]{:S(2)}, u32[]{:S(2)}) collective-permute-start(f32[128,128]{1,0:T(8,128)S(1)} %get-tuple-element.36), channel_id=1, source_target_pairs={{0,12},{2,14},{4,8},{6,10},{8,4},{10,6},{12,0},{14,2},{1,13},{3,15... | collective-permute-start | bytes 196616 | tf_op jit(solution)/shard_map/ppermute | solution.py:450
  41.0 13.1 %copy-start.6 = (f32[256,256]{1,0:T(8,128)S(1)}, f32[256,256]{1,0:T(8,128)}, u32[]{:S(2)}) copy-start(f32[256,256]{1,0:T(8,128)} %refs_8_.1) | copy-start | bytes 786436
  41.0 13.1 %copy-start.7 = (f32[256,256]{1,0:T(8,128)S(1)}, f32[256,256]{1,0:T(8,128)}, u32[]{:S(2)}) copy-start(f32[256,256]{1,0:T(8,128)} %refs_9_.1) | copy-start | bytes 786436
  41.0 13.1 %copy-start.14 = (f32[256]{0:T(256)S(1)}, f32[256]{0:T(256)}, u32[]{:S(2)}) copy-start(f32[256]{0:T(256)} %param.40) | copy-start | bytes 3076
  41.1 6.6 %collective-permute-start.12 = (f32[136,128]{1,0:T(8,128)S(1)}, f32[136,128]{1,0:T(8,128)S(1)}, u32[]{:S(2)}, u32[]{:S(2)}) collective-permute-start(f32[136,128]{1,0:T(8,128)S(1)} %middle.1.refs_0_), channel_id=1, source_target_pairs={{0,4},{2,6},{4,0},{6,2},{8,12},{10,14},{12,8},{14,10},{1,5},{3,7},... | collective-permute-start | bytes 208904 | tf_op jit(solution)/shard_map/ppermute | solution.py:460
  42.1 6.0 %collective-permute-start.14 = (f32[136,128]{1,0:T(8,128)S(1)}, f32[136,128]{1,0:T(8,128)S(1)}, u32[]{:S(2)}, u32[]{:S(2)}) collective-permute-start(f32[136,128]{1,0:T(8,128)S(1)} %middle.1.refs_0_), channel_id=1, source_target_pairs={{0,8},{2,10},{4,12},{6,14},{8,0},{10,2},{12,4},{14,6},{1,9},{3,11}... | collective-permute-start | bytes 208904 | tf_op jit(solution)/shard_map/ppermute | solution.py:460
  43.1 6.6 %collective-permute-start.16 = (f32[136,128]{1,0:T(8,128)S(1)}, f32[136,128]{1,0:T(8,128)S(1)}, u32[]{:S(2)}, u32[]{:S(2)}) collective-permute-start(f32[136,128]{1,0:T(8,128)S(1)} %middle.1.refs_0_), channel_id=1, source_target_pairs={{0,12},{2,14},{4,8},{6,10},{8,4},{10,6},{12,0},{14,2},{1,13},{3,15... | collective-permute-start | bytes 208904 | tf_op jit(solution)/shard_map/ppermute | solution.py:460
  45.6 5.8 %collective-permute-start.11 = (f32[136,128]{1,0:T(8,128)S(1)}, f32[136,128]{1,0:T(8,128)S(1)}, u32[]{:S(2)}, u32[]{:S(2)}) collective-permute-start(f32[136,128]{1,0:T(8,128)S(1)} %middle.1.refs_0_), channel_id=1, source_target_pairs={{0,2},{2,0},{4,6},{6,4},{8,10},{10,8},{12,14},{14,12},{1,3},{3,1},... | collective-permute-start | bytes 208904 | tf_op jit(solution)/shard_map/ppermute | solution.py:462
  47.7 4.3 %collective-permute-start.13 = (f32[136,128]{1,0:T(8,128)S(1)}, f32[136,128]{1,0:T(8,128)S(1)}, u32[]{:S(2)}, u32[]{:S(2)}) collective-permute-start(f32[136,128]{1,0:T(8,128)S(1)} %collective-permute-done.12.refs_2_), channel_id=1, source_target_pairs={{0,2},{2,0},{4,6},{6,4},{8,10},{10,8},{12,14},{14,12},{1,3},{3,1},... | collective-permute-start | bytes 208904 | tf_op jit(solution)/shard_map/ppermute | solution.py:462
  48.1 4.7 %collective-permute-start.15 = (f32[136,128]{1,0:T(8,128)S(1)}, f32[136,128]{1,0:T(8,128)S(1)}, u32[]{:S(2)}, u32[]{:S(2)}) collective-permute-start(f32[136,128]{1,0:T(8,128)S(1)} %collective-permute-done.14.refs_4_), channel_id=1, source_target_pairs={{0,2},{2,0},{4,6},{6,4},{8,10},{10,8},{12,14},{14,12},{1,3},{3,1},... | collective-permute-start | bytes 208904 | tf_op jit(solution)/shard_map/ppermute | solution.py:462
  49.8 4.3 %collective-permute-start.17 = (f32[136,128]{1,0:T(8,128)S(1)}, f32[136,128]{1,0:T(8,128)S(1)}, u32[]{:S(2)}, u32[]{:S(2)}) collective-permute-start(f32[136,128]{1,0:T(8,128)S(1)} %collective-permute-done.16.refs_6_), channel_id=1, source_target_pairs={{0,2},{2,0},{4,6},{6,4},{8,10},{10,8},{12,14},{14,12},{1,3},{3,1},... | collective-permute-start | bytes 208904 | tf_op jit(solution)/shard_map/ppermute | solution.py:462
  (7 other events, 9.3 us)

commit v2 on v1

--- a/solution.py
+++ b/solution.py
@@ -198,27 +198,44 @@
 
 def near_kernel(first, state_ref, *refs):
     if first:
-        index_ref, ws_ref, wr_ref, bias_ref, hot_ref, got_ref, into_ref = refs
+        (
+            index_ref, ws_ref, wr_ref, bias_ref, up_ref, cb_ref, db_ref,
+            hot_ref, got_ref, into_ref, pack_ref,
+        ) = refs
+        bias = bias_ref[0:1, :]
     else:
-        hot_ref, ws_ref, wr_ref, bias_ref, got_ref, into_ref = refs
+        hot_ref, ws_ref, wr_ref, pack_ref, got_ref, into_ref, high_ref, low_ref = refs
+        bias = pack_ref[0:1, :]
     layer = 0 if first else 1
     rows, width = into_ref.shape
     parts = width // LANES
-    edges, window = hot_ref.shape
     if first:
-        columns = jnp.transpose(index_ref[...])
-        blocks = edges // LANES
-        for b in range(blocks):
-            hot_ref[b * LANES : (b + 1) * LANES, :] = columns_equal(
-                columns[:, b : b + 1], window
-            )
+        build_hot(hot_ref, jnp.transpose(index_ref[...]))
+        pack_ref[...] = jnp.concatenate(
+            [bias_ref[1:2, :], up_ref[...], cb_ref[...], db_ref[...]]
+            + [jnp.zeros_like(up_ref[...])] * 4,
+            axis=0,
+        )
     normed = unit(load_rows(state_ref, rows, parts))
-    into_ref[...] = (times(normed, wr_ref[layer]) + bias_ref[layer : layer + 1, :]) * 0.5
-    sends = times(normed, ws_ref[layer]) * 0.5
-    got_ref[...] = times_one_hot(hot_ref[:, :rows], sends)
-
-
-def far_sum(layer, swap_ref, diag_ref, state_ref, hot_ref, got_ref, into_ref, ws_ref, wo_ref):
+    into_ref[...] = (times(normed, wr_ref[layer]) + bias) * 0.5
+    high, low = halves(times(normed, ws_ref[layer]) * 0.5)
+    if not first:
+        high_ref[...] = high
+        low_ref[...] = low
+    hot = hot_ref[:, :rows]
+    got_ref[...] = mm(hot, high) + mm(hot, low)
+
+
+def build_hot(hot_ref, columns):
+    window = hot_ref.shape[1]
+    for b in range(hot_ref.shape[0] // LANES):
+        hot_ref[b * LANES : (b + 1) * LANES, :] = columns_equal(columns[:, b : b + 1], window)
+
+
+def far_kernel(
+    odd_ref, swap_ref, diag_ref, state_ref, hot_ref, got_ref, into_ref, ws_ref, wo_ref,
+    index_ref, parent_ref, out_full_ref, out_half_ref,
+):
     rows, width = into_ref.shape
     parts = width // LANES
     rim = swap_ref.shape[0] // parts
@@ -226,49 +243,85 @@
     far = jnp.concatenate(
         [load_rows(swap_ref, rim, parts), load_rows(diag_ref, rim, parts)], axis=0
     )
-    sends = times(unit(far), ws_ref[layer]) * 0.5
-    high, low = halves(sends)
+    high, low = halves(times(unit(far), ws_ref[0]) * 0.5)
     total = None
     for k in range(degree):
         hot = hot_ref[k * rows : (k + 1) * rows, rows:]
         half = got_ref[k * rows : (k + 1) * rows, :] + into_ref[...] + (mm(hot, high) + mm(hot, low))
         total = gate(half) if total is None else total + gate(half)
-    return load_rows(state_ref, rows, parts) + times(total, wo_ref[layer])
-
-
-def far_kernel(
-    odd_ref, swap_ref, diag_ref, state_ref, hot_ref, got_ref, into_ref, ws_ref, wo_ref,
-    next_ref, out_swap_ref, out_diag_ref,
+    store_rows(out_full_ref, load_rows(state_ref, rows, parts) + times(total, wo_ref[0]), parts)
+    lines = rows * parts
+    senders = index_ref.shape[0]
+    rest = out_full_ref.shape[0] - lines - senders
+    out_full_ref[lines : lines + senders, :] = index_ref[...].astype(f32)
+    out_full_ref[lines + senders :, :] = jnp.concatenate(
+        [parent_ref[...].astype(f32), jnp.zeros((rest - parent_ref.shape[0], LANES), f32)], axis=0
+    )
+    half_lines = out_half_ref.shape[0]
+    start = pl.multiple_of(odd_ref[0] * (lines - half_lines), LANES)
+    out_half_ref[...] = out_full_ref[pl.ds(start, half_lines), :]
+
+
+def up_kernel(
+    peers, odd_ref, me_ref, full_ref, swap_ref, pair_ref, diag_ref, hot_ref, got_ref, into_ref,
+    high_ref, low_ref, ws_ref, wr_ref, wo_ref, parent_ref, wi_ref, wu_ref, pack_ref,
+    last_ref, *refs,
 ):
-    parts = into_ref.shape[1] // LANES
-    store_rows(
-        next_ref,
-        far_sum(0, swap_ref, diag_ref, state_ref, hot_ref, got_ref, into_ref, ws_ref, wo_ref),
-        parts,
-    )
-    lines = out_swap_ref.shape[0]
+    slot_refs = refs[: peers // 2]
+    hot2_ref, mh_ref, ml_ref, th_ref, tl_ref = refs[peers // 2 :]
+    rows, width = into_ref.shape
+    parts = width // LANES
+    rim = diag_ref.shape[0] // parts
+    degree = hot_ref.shape[0] // rows
+    lines = rows * parts
+    senders = hot_ref.shape[0] // LANES
     odd = odd_ref[0]
-    last = next_ref.shape[0] - lines
-    out_swap_ref[...] = next_ref[pl.ds(pl.multiple_of((1 - odd) * last, LANES), lines), :]
-    out_diag_ref[...] = next_ref[pl.ds(pl.multiple_of(odd * last, LANES), lines), :]
-
-
-def up_kernel(
-    me_ref, swap_ref, diag_ref, state_ref, hot_ref, got_ref, into_ref, ws_ref, wo_ref,
-    parent_ref, wi_ref, bias_ref, wu_ref, last_ref, *slot_refs,
-):
-    hidden = far_sum(
-        1, swap_ref, diag_ref, state_ref, hot_ref, got_ref, into_ref, ws_ref, wo_ref
-    )
-    last_ref[...] = hidden
-    rows, width = hidden.shape
-    parts = width // LANES
-    act = gate((times(unit(hidden), wi_ref[...]) + bias_ref[...]) * 0.5)
+    mine_touch = pl.multiple_of((1 - odd) * (rows - rim), LANES)
+    other_touch = pl.multiple_of(odd * (rows - rim), LANES)
+
+    build_hot(
+        hot2_ref, jnp.transpose(swap_ref[lines : lines + senders, :]).astype(jnp.int32)
+    )
+    other = load_rows(swap_ref, rows, parts)
+    normed = unit(
+        jnp.concatenate(
+            [other, load_rows(pair_ref, rim, parts), load_rows(diag_ref, rim, parts)], axis=0
+        )
+    )
+    high, low = halves(times(normed, ws_ref[1]) * 0.5)
+    for src, t_ref, m_ref, own_ref in (
+        (high, th_ref, mh_ref, high_ref), (low, tl_ref, ml_ref, low_ref),
+    ):
+        t_ref[:rows, :] = src[:rows, :]
+        t_ref[rows : rows + rim, :] = own_ref[pl.ds(mine_touch, rim), :]
+        t_ref[rows + rim :, :] = src[rows : rows + rim, :]
+        m_ref[:rim, :] = t_ref[pl.ds(other_touch, rim), :]
+        m_ref[rim:, :] = src[rows + rim :, :]
+    into = (times(normed[:rows, :], wr_ref[1]) + pack_ref[0:1, :]) * 0.5
+    total, total2 = None, None
+    for k in range(degree):
+        part = slice(k * rows, (k + 1) * rows)
+        hot = hot_ref[part, rows:]
+        half = got_ref[part, :] + into_ref[...] + (mm(hot, mh_ref[...]) + mm(hot, ml_ref[...]))
+        total = gate(half) if total is None else total + gate(half)
+        hot = hot2_ref[part, :]
+        half = into + (mm(hot, th_ref[...]) + mm(hot, tl_ref[...]))
+        total2 = gate(half) if total2 is None else total2 + gate(half)
+    hidden = jnp.concatenate([load_rows(full_ref, rows, parts), other], axis=0) + times(
+        jnp.concatenate([total, total2], axis=0), wo_ref[1]
+    )
+    last_ref[...] = hidden[:rows, :]
+    act = gate((times(unit(hidden), wi_ref[...]) + pack_ref[1:2, :]) * 0.5)
     messages = times(act, wu_ref[...])
     count = slot_refs[0].shape[0] // parts
     coarse = count * len(slot_refs)
-    place = jnp.bitwise_xor(parent_ref[...], me_ref[0] * count)
-    ids = lax.broadcasted_iota(jnp.int32, (coarse, rows), 0)
+    first = lines + senders
+    parents = [parent_ref[j : j + 1, :] for j in range(rows // LANES)] + [
+        swap_ref[first + j : first + j + 1, :].astype(jnp.int32) for j in range(rows // LANES)
+    ]
+    place = jnp.bitwise_xor(jnp.concatenate(parents, axis=1), me_ref[0] * count)
+    ids = lax.broadcasted_iota(jnp.int32, (coarse, 2 * rows), 0)
+    ids = ids + jnp.bitwise_and(ids, -count)
     select = jnp.where(ids == place, 1.0, 0.0).astype(bf16)
     sums = times_one_hot(select, messages)
     for k, slot in enumerate(slot_refs):
@@ -287,7 +340,7 @@
 
 def coarse_kernel(peers, anchor_lines, me_ref, last_ref, parent_ref, *refs):
     blocks = refs[:peers]
-    cs_ref, cr_ref, cb_ref, co_ref, di_ref, db_ref, do_ref, fine_ref, coarse_ref = refs[peers:]
+    cs_ref, cr_ref, co_ref, di_ref, do_ref, pack_ref, fine_ref, coarse_ref = refs[peers:]
     rows, width = last_ref.shape
     parts = width // LANES
     count = coarse_ref.shape[0] // parts
@@ -297,7 +350,7 @@
     middle = jnp.concatenate([load_rows(b, count, parts) for b in blocks], axis=0)
     normed = unit(middle)
     high, low = halves(times(normed, cs_ref[...]) * 0.5)
-    into = (times(normed, cr_ref[...]) + cb_ref[...]) * 0.5
+    into = (times(normed, cr_ref[...]) + pack_ref[2:3, :]) * 0.5
     anchors = [
         jnp.bitwise_xor(
             jnp.transpose(b[lines : lines + anchor_lines, :]).astype(jnp.int32), flip
@@ -321,7 +374,7 @@
         total = gate(half) if total is None else total + gate(half)
     done = middle + times(total, co_ref[...])
     store_rows(coarse_ref, done[:count, :], parts)
-    act = gate((times(unit(done), di_ref[...]) + db_ref[...]) * 0.5)
+    act = gate((times(unit(done), di_ref[...]) + pack_ref[3:4, :]) * 0.5)
     down = times(act, do_ref[...])
     dh, dl = halves(down)
     places = jnp.bitwise_xor(jnp.transpose(parent_ref[...]), flip)
@@ -339,12 +392,13 @@
 SMEM = pl.BlockSpec(memory_space=pltpu.SMEM)
 
 
-def call(kernel, in_specs, out_shapes, name):
+def call(kernel, in_specs, out_shapes, name, scratch=()):
     return pl.pallas_call(
         kernel,
         in_specs=in_specs,
         out_specs=[VMEM] * len(out_shapes),
         out_shape=out_shapes,
+        scratch_shapes=scratch,
         name=name,
         compiler_params=pltpu.CompilerParams(vmem_limit_bytes=32 * 2**20),
     )
@@ -415,43 +469,58 @@
     odd_arg, me_arg = odd.reshape(1), me.reshape(1)
 
     edges, window = rows * degree, rows + 2 * HALO
+    parent = parent.reshape(rows // LANES, LANES)
+    row = lambda bias: bias.reshape(1, width)
+    pair = [(i, (i + 2 if i % 2 else i - 2) % peers) for i in range(peers)]
+    full = rows * parts + -(-(edges + rows) // LANES // 8) * 8
     in_swap = lax.ppermute(out_swap, "sp", swap)
     in_diag = lax.ppermute(out_diag, "sp", diag)
-    hot, got, into = call(
+    hot, got, into, pack = call(
         functools.partial(near_kernel, True),
-        [VMEM] * 5,
-        [shape(edges, window, kind=bf16), shape(edges, width), shape(rows, width)],
+        [VMEM] * 8,
+        [
+            shape(edges, window, kind=bf16), shape(edges, width), shape(rows, width),
+            shape(8, width),
+        ],
         "near0",
-    )(state, index, fine_w_send, fine_w_recv, fine_bias)
-    state, out_swap, out_diag = call(
+    )(
+        state, index, fine_w_send, fine_w_recv, fine_bias, row(up_bias), row(coarse_bias),
+        row(down_bias),
+    )
+    state, out_half = call(
         far_kernel,
-        [SMEM] + [VMEM] * 8,
-        [shape(rows * parts, LANES), shape(rim, LANES), shape(rim, LANES)],
+        [SMEM] + [VMEM] * 10,
+        [shape(full, LANES), shape(rim, LANES)],
         "far0",
-    )(odd_arg, in_swap, in_diag, state, hot, got, into, fine_w_send, fine_w_out)
-    in_swap = lax.ppermute(out_swap, "sp", swap)
-    in_diag = lax.ppermute(out_diag, "sp", diag)
-    got, into = call(
+    )(odd_arg, in_swap, in_diag, state, hot, got, into, fine_w_send, fine_w_out, index, parent)
+    in_swap = lax.ppermute(state, "sp", swap)
+    in_pair = lax.ppermute(out_half, "sp", pair)
+    in_diag = lax.ppermute(out_half, "sp", diag)
+    got, into, high, low = call(
         functools.partial(near_kernel, False),
         [VMEM] * 5,
-        [shape(edges, width), shape(rows, width)],
+        [shape(edges, width), shape(rows, width)] + [shape(rows, width, kind=bf16)] * 2,
         "near1",
-    )(state, hot, fine_w_send, fine_w_recv, fine_bias)
+    )(state, hot, fine_w_send, fine_w_recv, pack)
     hidden, *slots = call(
-        up_kernel,
-        [SMEM] + [VMEM] * 12,
-        [shape(rows, width)] + [shape(count * parts, LANES)] * peers,
+        functools.partial(up_kernel, peers),
+        [SMEM] * 2 + [VMEM] * 16,
+        [shape(rows, width)] + [shape(count * parts, LANES)] * (peers // 2),
         "up",
+        [pltpu.VMEM((edges, window), bf16)]
+        + [pltpu.VMEM((2 * HALO, width), bf16)] * 2
+        + [pltpu.VMEM((window, width), bf16)] * 2,
     )(
-        me_arg, in_swap, in_diag, state, hot, got, into, fine_w_send, fine_w_out,
-        parent.reshape(1, rows), up_w_in, up_bias.reshape(1, width), up_w_out,
+        odd_arg, me_arg, state, in_swap, in_pair, in_diag, hot, got, into, high, low,
+        fine_w_send, fine_w_recv, fine_w_out, parent, up_w_in, up_w_out, pack,
     )
     arrived = [slots[0]] + [
-        lax.ppermute(slots[k], "sp", [(i, i ^ k) for i in range(peers)]) for k in range(1, peers)
+        lax.ppermute(slots[k], "sp", [(i, i ^ (2 * k)) for i in range(peers)])
+        for k in range(1, peers // 2)
     ]
     (middle,) = call(
         middle_kernel,
-        [VMEM] * (2 + peers),
+        [VMEM] * (2 + peers // 2),
         [shape(count * parts + anchor.shape[0], LANES)],
         "middle",
     )(coarse_state.reshape(count * parts, LANES), anchor, *arrived)
@@ -462,14 +531,13 @@
         columns[k + 1] = lax.ppermute(columns[k], "sp", swap)
     fine_out, coarse_out = call(
         functools.partial(coarse_kernel, peers, anchor_lines),
-        [SMEM] + [VMEM] * (9 + peers),
+        [SMEM] + [VMEM] * (8 + peers),
         [shape(rows * parts, LANES), shape(count * parts, LANES)],
         "coarse",
     )(
-        me_arg, hidden, parent.reshape(rows // LANES, LANES),
+        me_arg, hidden, parent,
         *[columns[k] for k in range(peers)],
-        coarse_w_send, coarse_w_recv, coarse_bias.reshape(1, width), coarse_w_out,
-        down_w_in, down_bias.reshape(1, width), down_w_out,
+        coarse_w_send, coarse_w_recv, coarse_w_out, down_w_in, down_w_out, pack,
     )
     return (fine_out.reshape(fine_state.shape), coarse_out.reshape(coarse_state.shape))
 
@@ -494,6 +562,8 @@
         and coarse_owner.shape[0] == 4 * count
         and fine_senders.shape[0] % (8 * LANES) == 0
         and peers * count <= 1024
+        and peers >= 4
+        and rows >= 2 * HALO
     )
     return (kernel_shards if fits else general_shards)(*args)
 

time: 59.9 us -> 56.8 us (0.948)
  starting transfers between devices: 31.1 us -> 24.3 us
  waiting for transfers between devices: 11.7 us -> 14.6 us
  Pallas kernels: 10.6 us -> 12 us
  local copies, waits for them, and re-layouts: 5.3 us -> 4.65 us
    ppermute x2 -> x1, starting transfers between devices: 7.15 us -> 3.57 us  [kernel_shards(): in_diag = lax.ppermute(out_diag, 'sp', diag)]
    ppermute x7 -> x6, waiting for transfers between devices: 5.17 us -> 8 us  [the longest x1 4.56 us: kernel_shards(): in_diag = lax.ppermute(out_half, 'sp', diag)]
    ppermute x2 -> x1, waiting for transfers between devices: 2.76 us -> 0.01 us  [kernel_shards(): in_diag = lax.ppermute(out_diag, 'sp', diag)]
    ppermute x3, waiting for transfers between devices: 0.3 us -> 2.33 us  [kernel_shards(): columns[k] = lax.ppermute(middle, 'sp', [(i, i ^ k) for i in range(peers)])]
    ppermute x4, starting transfers between devices: 5.49 us -> 3.46 us  [kernel_shards(): columns[k + 1] = lax.ppermute(columns[k], 'sp', swap)]
    ppermute x4, waiting for transfers between devices: 2.74 us -> 4.3 us  [kernel_shards(): columns[k + 1] = lax.ppermute(columns[k], 'sp', swap)]
    pallas_call x4, Pallas kernels: 4.85 us -> 6.18 us  [the longest x1 3.78 us: kernel_shards(): call(functools.partial(up_kernel, peers), [SMEM] * 2 + [VMEM] * 16, [shap...]
    ppermute x2 -> x1, waiting for transfers between devices: 0.76 us -> 0.01 us  [kernel_shards(): in_swap = lax.ppermute(out_swap, 'sp', swap)]
  transfers between devices with their start and end apart: 18 -> 15, of which waited for: 11 -> 9; matrix products, arithmetic and copies ran while one was open for 1% -> 1% of each run, Pallas kernels for 3% -> 4%
where the time goes in v2:
time: 56.8 us; the launch traced here: 56.5 us
  starting transfers between devices  24.3 us (43%)
  waiting for transfers between devices  14.6 us (26%)
  Pallas kernels  12 us (21%)
  local copies, waits for them, and re-layouts  4.65 us (8%)
  between operations  0.91 us (2%)
    pallas_call x1, Pallas kernels, kernel_shards(): call(functools.partial(coarse_kernel, peers, anchor_lines), [SMEM] + [VME...  4.85 us
    ppermute x1, waiting for transfers between devices, kernel_shards(): in_diag = lax.ppermute(out_half, 'sp', diag)  4.56 us
    ppermute x3, starting transfers between devices, kernel_shards(): columns[k] = lax.ppermute(middle, 'sp', [(i, i ^ k) for i in range(peers)])  4.45 us
    ppermute x3, starting transfers between devices, kernel_shards(): lax.ppermute(slots[k], 'sp', [(i, i ^ 2 * k) for i in range(peers)])  4.44 us
    ppermute x4, waiting for transfers between devices, kernel_shards(): columns[k + 1] = lax.ppermute(columns[k], 'sp', swap)  4.3 us
    pallas_call x1, Pallas kernels, kernel_shards(): call(functools.partial(up_kernel, peers), [SMEM] * 2 + [VMEM] * 16, [shap...  3.78 us
    ppermute x1, starting transfers between devices, kernel_shards(): in_pair = lax.ppermute(out_half, 'sp', pair)  3.75 us
    ppermute x1, starting transfers between devices, kernel_shards(): in_diag = lax.ppermute(out_diag, 'sp', diag)  3.57 us
  transfers between devices with their start and end apart: 15, of which 9 were waited for; matrix products, arithmetic and copies ran while one was open for 1% of the time, Pallas kernels for 4%

profile of v2, /device:TPU:0, one launch (start us, length us, event | category | flops | bytes accessed | tf_op | source)
XLA Modules:
  0.0 56.5 jit_solution(18375878838129432301)
XLA Ops:
  0.7 1.0 %constant_dynamic-slice_fusion = (f32[256,128]{1,0:T(8,128)S(1)}, f32[256,128]{1,0:T(8,128)S(1)}) fusion(f32[512,128]{1,0:T(8,128)} %bitcast.15, s32[]{:T(128)S(6)} %select_n.29, s32[]{:T(128)S(6)} %select_n.28), kind=kLoop, calls=%fused_computation.5 | loop fusion | bytes 524296 | tf_op jit(solution)/shard_map/dynamic_slice | solution.py:449
  1.7 3.0 %collective-permute-start = (f32[256,128]{1,0:T(8,128)S(1)}, f32[256,128]{1,0:T(8,128)S(1)}, u32[]{:S(2)}, u32[]{:S(2)}) collective-permute-start(f32[256,128]{1,0:T(8,128)S(1)} %get-tuple-element.41), channel_id=1, source_target_pairs={{0,2},{2,0},{4,6},{6,4},{8,10},{10,8},{12,14},{14,12},{1,3},{3,1},... | collective-permute-start | bytes 393224 | tf_op jit(solution)/shard_map/ppermute | solution.py:476
  4.8 3.6 %collective-permute-start.1 = (f32[256,128]{1,0:T(8,128)S(1)}, f32[256,128]{1,0:T(8,128)S(1)}, u32[]{:S(2)}, u32[]{:S(2)}) collective-permute-start(f32[256,128]{1,0:T(8,128)S(1)} %get-tuple-element.40), channel_id=1, source_target_pairs={{0,14},{2,4},{4,2},{6,8},{8,6},{10,12},{12,10},{14,0},{1,15},{3,5}... | collective-permute-start | bytes 393224 | tf_op jit(solution)/shard_map/ppermute | solution.py:477
  8.3 0.1 reshape.52
  8.6 0.7 %copy-done.19 = s32[256,1]{0,1:T(1,128)S(1)} copy-done((s32[256,1]{0,1:T(1,128)S(1)}, s32[256,1]{0,1:T(1,128)}, u32[]{:S(2)}) %copy-start.19) | copy-done | bytes 1048
  9.3 0.6 %copy-done.12 = f32[2,256]{1,0:T(2,128)S(1)} copy-done((f32[2,256]{1,0:T(2,128)S(1)}, f32[2,256]{1,0:T(2,128)}, u32[]{:S(2)}) %copy-start.12) | copy-done | bytes 2072
  10.0 1.0 %copy-done.1 = f32[2,256,256]{2,1,0:T(8,128)S(1)} copy-done((f32[2,256,256]{2,1,0:T(8,128)S(1)}, f32[2,256,256]{2,1,0:T(8,128)}, u32[]{:S(2)}) %copy-start.1) | copy-done | bytes 524312
  11.0 1.0 %near0.1 = (bf16[1024,512]{1,0:T(8,128)(2,1)S(1)}, f32[1024,256]{1,0:T(8,128)S(1)}, f32[256,256]{1,0:T(8,128)S(1)}, f32[8,256]{1,0:T(8,128)S(1)}) custom-call(f32[512,128]{1,0:T(8,128)S(1)} %bitcast.16, s32[8,128]{1,0:T(8,128)S(1)} %reshape.53.refs_0_.index_ref, f32[2,256,256]{2,1,0:T(8,128)S(1)} %copy-done, f32[2,256,256]{2,1,0:T(8,128)S(1)} %copy-done.1, ...), custom_call_target="tpu_custom_call" | custom-call | tf_op jit(solution)/shard_map/near0/pallas_call | solution.py:478
  12.0 0.7 %copy-done.17 = s32[256]{0:T(256)S(1)} copy-done((s32[256]{0:T(256)S(1)}, s32[256]{0:T(256)}, u32[]{:S(2)}) %copy-start.17) | copy-done | bytes 1048
  12.7 1.3 %far0.1 = (f32[528,128]{1,0:T(8,128)S(1)}, f32[256,128]{1,0:T(8,128)S(1)}) custom-call(s32[1]{0:T(128)} %bitcast.1.odd_ref, f32[256,128]{1,0:T(8,128)S(1)} %collective-permute-done.swap_ref, f32[256,128]{1,0:T(8,128)S(1)} %collective-permute-done.1.diag_ref, f32[512,128]{1,0:T(8,128)S(1)} %bitcast.17, ...), custom_call_target="tpu_custom_call" | custom-call | tf_op jit(solution)/shard_map/far0/pallas_call | solution.py:490
  14.1 0.1 collective-permute-start.2
  14.2 3.8 %collective-permute-start.3 = (f32[256,128]{1,0:T(8,128)S(1)}, f32[256,128]{1,0:T(8,128)S(1)}, u32[]{:S(2)}, u32[]{:S(2)}) collective-permute-start(f32[256,128]{1,0:T(8,128)S(1)} %get-tuple-element.23), channel_id=1, source_target_pairs={{0,12},{2,6},{4,0},{6,10},{8,4},{10,14},{12,8},{14,2},{1,13},{3,7}... | collective-permute-start | bytes 393224 | tf_op jit(solution)/shard_map/ppermute | solution.py:497
  18.0 1.5 %collective-permute-start.4 = (f32[256,128]{1,0:T(8,128)S(1)}, f32[256,128]{1,0:T(8,128)S(1)}, u32[]{:S(2)}, u32[]{:S(2)}) collective-permute-start(f32[256,128]{1,0:T(8,128)S(1)} %get-tuple-element.23), channel_id=1, source_target_pairs={{0,14},{2,4},{4,2},{6,8},{8,6},{10,12},{12,10},{14,0},{1,15},{3,5}... | collective-permute-start | bytes 393224 | tf_op jit(solution)/shard_map/ppermute | solution.py:498
  19.5 1.0 %near1.1 = (f32[1024,256]{1,0:T(8,128)S(1)}, f32[256,256]{1,0:T(8,128)S(1)}, bf16[256,256]{1,0:T(8,128)(2,1)S(1)}, bf16[256,256]{1,0:T(8,128)(2,1)S(1)}) custom-call(f32[528,128]{1,0:T(8,128)S(1)} %get-tuple-element.22.state_ref.full_ref, bf16[1024,512]{1,0:T(8,128)(2,1)S(1)} %get-tuple-element.19.hot_ref.refs_0_, f32[2,256,256]{2,1,0:T(8,128)S(1)} %copy-done, ...), custom_call_target="tpu_custom_call" | custom-call | tf_op jit(solution)/shard_map/near1/pallas_call | solution.py:499
  20.4 0.7 %collective-permute-done.3.pair_ref = f32[256,128]{1,0:T(8,128)S(1)} collective-permute-done((f32[256,128]{1,0:T(8,128)S(1)}, f32[256,128]{1,0:T(8,128)S(1)}, u32[]{:S(2)}, u32[]{:S(2)}) %collective-permute-start.3) | collective-permute-done | bytes 131104 | tf_op jit(solution)/shard_map/ppermute | solution.py:497
  21.1 4.6 %collective-permute-done.4.diag_ref = f32[256,128]{1,0:T(8,128)S(1)} collective-permute-done((f32[256,128]{1,0:T(8,128)S(1)}, f32[256,128]{1,0:T(8,128)S(1)}, u32[]{:S(2)}, u32[]{:S(2)}) %collective-permute-start.4) | collective-permute-done | bytes 131104 | tf_op jit(solution)/shard_map/ppermute | solution.py:498
  25.7 3.8 %up.1 = (f32[256,256]{1,0:T(8,128)S(1)}, f32[128,128]{1,0:T(8,128)S(1)}, f32[128,128]{1,0:T(8,128)S(1)}, f32[128,128]{1,0:T(8,128)S(1)}, f32[128,128]{1,0:T(8,128)S(1)}) custom-call(s32[1]{0:T(128)} %bitcast.1.odd_ref, s32[1]{0:T(128)} %bitcast.me_ref, f32[528,128]{1,0:T(8,128)S(1)} %get-tuple-element.22.state_ref.full_ref, ...), custom_call_target="tpu_custom_call" | custom-call | tf_op jit(solution)/shard_map/up/pallas_call | solution.py:505
  29.6 0.7 %collective-permute-start.6 = (f32[128,128]{1,0:T(8,128)S(1)}, f32[128,128]{1,0:T(8,128)S(1)}, u32[]{:S(2)}, u32[]{:S(2)}) collective-permute-start(f32[128,128]{1,0:T(8,128)S(1)} %get-tuple-element.32), channel_id=1, source_target_pairs={{0,8},{2,10},{4,12},{6,14},{8,0},{10,2},{12,4},{14,6},{1,9},{3,11}... | collective-permute-start | bytes 196616 | tf_op jit(solution)/shard_map/ppermute | solution.py:518
  30.3 3.6 %collective-permute-start.7 = (f32[128,128]{1,0:T(8,128)S(1)}, f32[128,128]{1,0:T(8,128)S(1)}, u32[]{:S(2)}, u32[]{:S(2)}) collective-permute-start(f32[128,128]{1,0:T(8,128)S(1)} %get-tuple-element.33), channel_id=1, source_target_pairs={{0,12},{2,14},{4,8},{6,10},{8,4},{10,6},{12,0},{14,2},{1,13},{3,15... | collective-permute-start | bytes 196616 | tf_op jit(solution)/shard_map/ppermute | solution.py:518
  34.3 1.0 %collective-permute-done.5.refs_1_ = f32[128,128]{1,0:T(8,128)S(1)} collective-permute-done((f32[128,128]{1,0:T(8,128)S(1)}, f32[128,128]{1,0:T(8,128)S(1)}, u32[]{:S(2)}, u32[]{:S(2)}) %collective-permute-start.5) | collective-permute-done | bytes 65568 | tf_op jit(solution)/shard_map/ppermute | solution.py:518
  35.3 1.8 %collective-permute-done.7.refs_3_ = f32[128,128]{1,0:T(8,128)S(1)} collective-permute-done((f32[128,128]{1,0:T(8,128)S(1)}, f32[128,128]{1,0:T(8,128)S(1)}, u32[]{:S(2)}, u32[]{:S(2)}) %collective-permute-start.7) | collective-permute-done | bytes 65568 | tf_op jit(solution)/shard_map/ppermute | solution.py:518
  37.1 0.7 %collective-permute-start.9 = (f32[136,128]{1,0:T(8,128)S(1)}, f32[136,128]{1,0:T(8,128)S(1)}, u32[]{:S(2)}, u32[]{:S(2)}) collective-permute-start(f32[136,128]{1,0:T(8,128)S(1)} %middle.1.refs_0_), channel_id=1, source_target_pairs={{0,4},{2,6},{4,0},{6,2},{8,12},{10,14},{12,8},{14,10},{1,5},{3,7},... | collective-permute-start | bytes 208904 | tf_op jit(solution)/shard_map/ppermute | solution.py:529
  37.8 3.4 %collective-permute-start.11 = (f32[136,128]{1,0:T(8,128)S(1)}, f32[136,128]{1,0:T(8,128)S(1)}, u32[]{:S(2)}, u32[]{:S(2)}) collective-permute-start(f32[136,128]{1,0:T(8,128)S(1)} %middle.1.refs_0_), channel_id=1, source_target_pairs={{0,8},{2,10},{4,12},{6,14},{8,0},{10,2},{12,4},{14,6},{1,9},{3,11}... | collective-permute-start | bytes 208904 | tf_op jit(solution)/shard_map/ppermute | solution.py:529
  41.2 0.3 collective-permute-start.13
  41.5 2.1 %collective-permute-start.8 = (f32[136,128]{1,0:T(8,128)S(1)}, f32[136,128]{1,0:T(8,128)S(1)}, u32[]{:S(2)}, u32[]{:S(2)}) collective-permute-start(f32[136,128]{1,0:T(8,128)S(1)} %middle.1.refs_0_), channel_id=1, source_target_pairs={{0,2},{2,0},{4,6},{6,4},{8,10},{10,8},{12,14},{14,12},{1,3},{3,1},... | collective-permute-start | bytes 208904 | tf_op jit(solution)/shard_map/ppermute | solution.py:531
  43.6 0.6 %collective-permute-done.11.refs_4_ = f32[136,128]{1,0:T(8,128)S(1)} collective-permute-done((f32[136,128]{1,0:T(8,128)S(1)}, f32[136,128]{1,0:T(8,128)S(1)}, u32[]{:S(2)}, u32[]{:S(2)}) %collective-permute-start.11) | collective-permute-done | bytes 69664 | tf_op jit(solution)/shard_map/ppermute | solution.py:529
  44.2 1.4 %collective-permute-start.12 = (f32[136,128]{1,0:T(8,128)S(1)}, f32[136,128]{1,0:T(8,128)S(1)}, u32[]{:S(2)}, u32[]{:S(2)}) collective-permute-start(f32[136,128]{1,0:T(8,128)S(1)} %collective-permute-done.11.refs_4_), channel_id=1, source_target_pairs={{0,2},{2,0},{4,6},{6,4},{8,10},{10,8},{12,14},{14,12},{1,3},{3,1},... | collective-permute-start | bytes 208904 | tf_op jit(solution)/shard_map/ppermute | solution.py:531
  45.6 1.7 %collective-permute-done.13.refs_6_ = f32[136,128]{1,0:T(8,128)S(1)} collective-permute-done((f32[136,128]{1,0:T(8,128)S(1)}, f32[136,128]{1,0:T(8,128)S(1)}, u32[]{:S(2)}, u32[]{:S(2)}) %collective-permute-start.13) | collective-permute-done | bytes 69664 | tf_op jit(solution)/shard_map/ppermute | solution.py:529
  47.3 0.6 %collective-permute-done.10.refs_3_ = f32[136,128]{1,0:T(8,128)S(1)} collective-permute-done((f32[136,128]{1,0:T(8,128)S(1)}, f32[136,128]{1,0:T(8,128)S(1)}, u32[]{:S(2)}, u32[]{:S(2)}) %collective-permute-start.10) | collective-permute-done | bytes 69664 | tf_op jit(solution)/shard_map/ppermute | solution.py:531
  47.9 0.7 %collective-permute-done.12.refs_5_ = f32[136,128]{1,0:T(8,128)S(1)} collective-permute-done((f32[136,128]{1,0:T(8,128)S(1)}, f32[136,128]{1,0:T(8,128)S(1)}, u32[]{:S(2)}, u32[]{:S(2)}) %collective-permute-start.12) | collective-permute-done | bytes 69664 | tf_op jit(solution)/shard_map/ppermute | solution.py:531
  48.6 3.0 %collective-permute-done.14.refs_7_ = f32[136,128]{1,0:T(8,128)S(1)} collective-permute-done((f32[136,128]{1,0:T(8,128)S(1)}, f32[136,128]{1,0:T(8,128)S(1)}, u32[]{:S(2)}, u32[]{:S(2)}) %collective-permute-start.14) | collective-permute-done | bytes 69664 | tf_op jit(solution)/shard_map/ppermute | solution.py:531
  51.7 4.8 %coarse.1 = (f32[512,128]{1,0:T(8,128)}, f32[128,128]{1,0:T(8,128)}) custom-call(s32[1]{0:T(128)} %bitcast.me_ref, f32[256,256]{1,0:T(8,128)S(1)} %get-tuple-element.29.last_ref, s32[2,128]{1,0:T(2,128)S(1)} %add_bitcast_fusion.parent_ref, f32[136,128]{1,0:T(8,128)S(1)} %middle.1.refs_0_, f32[136,128]{1,0:T(8,128)S(1)} %collective-permute-done.8.refs_1_, ...), custom_call_target="tpu_custom_call" | custom-call | tf_op jit(solution)/shard_map/coarse/pallas_call | solution.py:532
  (59 shorter events, 0.6 us)
Async XLA Ops:
  0.6 8.6 %copy-start = (f32[2,256,256]{2,1,0:T(8,128)S(1)}, f32[2,256,256]{2,1,0:T(8,128)}, u32[]{:S(2)}) copy-start(f32[2,256,256]{2,1,0:T(8,128)} %ws_ref.3) | copy-start | bytes 1572868
  0.7 7.7 %copy-start.16 = (s32[1024]{0:T(1024)S(1)}, s32[1024]{0:T(1024)}, u32[]{:S(2)}) copy-start(s32[1024]{0:T(1024)} %param.23) | copy-start | bytes 12292
  1.7 7.5 %copy-start.2 = (f32[256,1,256]{2,1,0:T(1,128)S(1)}, f32[256,1,256]{2,1,0:T(1,128)}, u32[]{:S(2)}) copy-start(f32[256,1,256]{2,1,0:T(1,128)} %param.21) | copy-start | bytes 786436
  1.7 11.0 %collective-permute-start = (f32[256,128]{1,0:T(8,128)S(1)}, f32[256,128]{1,0:T(8,128)S(1)}, u32[]{:S(2)}, u32[]{:S(2)}) collective-permute-start(f32[256,128]{1,0:T(8,128)S(1)} %get-tuple-element.41), channel_id=1, source_target_pairs={{0,2},{2,0},{4,6},{6,4},{8,10},{10,8},{12,14},{14,12},{1,3},{3,1},... | collective-permute-start | bytes 393224 | tf_op jit(solution)/shard_map/ppermute | solution.py:476
  4.8 8.0 %collective-permute-start.1 = (f32[256,128]{1,0:T(8,128)S(1)}, f32[256,128]{1,0:T(8,128)S(1)}, u32[]{:S(2)}, u32[]{:S(2)}) collective-permute-start(f32[256,128]{1,0:T(8,128)S(1)} %get-tuple-element.40), channel_id=1, source_target_pairs={{0,14},{2,4},{4,2},{6,8},{8,6},{10,12},{12,10},{14,0},{1,15},{3,5}... | collective-permute-start | bytes 393224 | tf_op jit(solution)/shard_map/ppermute | solution.py:477
  8.6 0.7 %copy-start.14 = (f32[256]{0:T(256)S(1)}, f32[256]{0:T(256)}, u32[]{:S(2)}) copy-start(f32[256]{0:T(256)} %param.37) | copy-start | bytes 3076
  8.6 0.7 %copy-start.15 = (f32[256]{0:T(256)S(1)}, f32[256]{0:T(256)}, u32[]{:S(2)}) copy-start(f32[256]{0:T(256)} %param.40) | copy-start | bytes 3076
  10.0 1.0 %copy-start.1 = (f32[2,256,256]{2,1,0:T(8,128)S(1)}, f32[2,256,256]{2,1,0:T(8,128)}, u32[]{:S(2)}) copy-start(f32[2,256,256]{2,1,0:T(8,128)} %wr_ref.1) | copy-start | bytes 1572868
  11.0 1.7 %copy-start.3 = (f32[2,256,256]{2,1,0:T(8,128)S(1)}, f32[2,256,256]{2,1,0:T(8,128)}, u32[]{:S(2)}) copy-start(f32[2,256,256]{2,1,0:T(8,128)} %wo_ref.3) | copy-start | bytes 1572868
  14.1 5.4 %copy-start.20 = (s32[256,1]{0,1:T(1,128)S(1)}, s32[256,1]{0,1:T(1,128)}, u32[]{:S(2)}) copy-start(s32[256,1]{0,1:T(1,128)} %param.26) | copy-start | bytes 3076
  14.1 11.6 %collective-permute-start.2 = (f32[528,128]{1,0:T(8,128)S(1)}, f32[528,128]{1,0:T(8,128)S(1)}, u32[]{:S(2)}, u32[]{:S(2)}) collective-permute-start(f32[528,128]{1,0:T(8,128)S(1)} %get-tuple-element.22.state_ref.full_ref), channel_id=1, source_target_pairs={{0,2},{2,0},{4,6},{6,4},{8,10},{10,8},{12,14},{14,12},{1,3},{3,1},... | collective-permute-start | bytes 811016 | tf_op jit(solution)/shard_map/ppermute | solution.py:496
  14.2 6.9 %collective-permute-start.3 = (f32[256,128]{1,0:T(8,128)S(1)}, f32[256,128]{1,0:T(8,128)S(1)}, u32[]{:S(2)}, u32[]{:S(2)}) collective-permute-start(f32[256,128]{1,0:T(8,128)S(1)} %get-tuple-element.23), channel_id=1, source_target_pairs={{0,12},{2,6},{4,0},{6,10},{8,4},{10,14},{12,8},{14,2},{1,13},{3,7}... | collective-permute-start | bytes 393224 | tf_op jit(solution)/shard_map/ppermute | solution.py:497
  18.0 7.7 %collective-permute-start.4 = (f32[256,128]{1,0:T(8,128)S(1)}, f32[256,128]{1,0:T(8,128)S(1)}, u32[]{:S(2)}, u32[]{:S(2)}) collective-permute-start(f32[256,128]{1,0:T(8,128)S(1)} %get-tuple-element.23), channel_id=1, source_target_pairs={{0,14},{2,4},{4,2},{6,8},{8,6},{10,12},{12,10},{14,0},{1,15},{3,5}... | collective-permute-start | bytes 393224 | tf_op jit(solution)/shard_map/ppermute | solution.py:498
  19.5 6.2 %copy-start.4 = (f32[256,256]{1,0:T(8,128)S(1)}, f32[256,256]{1,0:T(8,128)}, u32[]{:S(2)}) copy-start(f32[256,256]{1,0:T(8,128)} %wi_ref.1) | copy-start | bytes 786436
  19.5 6.2 %copy-start.5 = (f32[256,256]{1,0:T(8,128)S(1)}, f32[256,256]{1,0:T(8,128)}, u32[]{:S(2)}) copy-start(f32[256,256]{1,0:T(8,128)} %wu_ref.1) | copy-start | bytes 786436
  25.7 8.3 %copy-start.18 = (s32[256]{0:T(256)S(1)}, s32[256]{0:T(256)}, u32[]{:S(2)}) copy-start(s32[256]{0:T(256)} %param.27) | copy-start | bytes 3076
  25.7 11.4 %copy-start.11 = (f32[64,1,256]{2,1,0:T(1,128)S(1)}, f32[64,1,256]{2,1,0:T(1,128)}, u32[]{:S(2)}) copy-start(f32[64,1,256]{2,1,0:T(1,128)} %param.22) | copy-start | bytes 196612
  25.7 25.9 %copy-start.7 = (f32[256,256]{1,0:T(8,128)S(1)}, f32[256,256]{1,0:T(8,128)}, u32[]{:S(2)}) copy-start(f32[256,256]{1,0:T(8,128)} %refs_9_.1) | copy-start | bytes 786436
  25.7 25.9 %copy-start.8 = (f32[256,256]{1,0:T(8,128)S(1)}, f32[256,256]{1,0:T(8,128)}, u32[]{:S(2)}) copy-start(f32[256,256]{1,0:T(8,128)} %refs_10_.1) | copy-start | bytes 786436
  25.7 25.9 %copy-start.9 = (f32[256,256]{1,0:T(8,128)S(1)}, f32[256,256]{1,0:T(8,128)}, u32[]{:S(2)}) copy-start(f32[256,256]{1,0:T(8,128)} %refs_11_.1) | copy-start | bytes 786436
  25.7 25.9 %copy-start.10 = (f32[256,256]{1,0:T(8,128)S(1)}, f32[256,256]{1,0:T(8,128)}, u32[]{:S(2)}) copy-start(f32[256,256]{1,0:T(8,128)} %refs_12_.1) | copy-start | bytes 786436
  29.5 22.1 %copy-start.6 = (f32[256,256]{1,0:T(8,128)S(1)}, f32[256,256]{1,0:T(8,128)}, u32[]{:S(2)}) copy-start(f32[256,256]{1,0:T(8,128)} %refs_8_.1) | copy-start | bytes 786436
  29.5 5.7 %collective-permute-start.5 = (f32[128,128]{1,0:T(8,128)S(1)}, f32[128,128]{1,0:T(8,128)S(1)}, u32[]{:S(2)}, u32[]{:S(2)}) collective-permute-start(f32[128,128]{1,0:T(8,128)S(1)} %get-tuple-element.31), channel_id=1, source_target_pairs={{0,4},{2,6},{4,0},{6,2},{8,12},{10,14},{12,8},{14,10},{1,5},{3,7},... | collective-permute-start | bytes 196616 | tf_op jit(solution)/shard_map/ppermute | solution.py:518
  29.6 5.7 %collective-permute-start.6 = (f32[128,128]{1,0:T(8,128)S(1)}, f32[128,128]{1,0:T(8,128)S(1)}, u32[]{:S(2)}, u32[]{:S(2)}) collective-permute-start(f32[128,128]{1,0:T(8,128)S(1)} %get-tuple-element.32), channel_id=1, source_target_pairs={{0,8},{2,10},{4,12},{6,14},{8,0},{10,2},{12,4},{14,6},{1,9},{3,11}... | collective-permute-start | bytes 196616 | tf_op jit(solution)/shard_map/ppermute | solution.py:518
  30.3 6.7 %collective-permute-start.7 = (f32[128,128]{1,0:T(8,128)S(1)}, f32[128,128]{1,0:T(8,128)S(1)}, u32[]{:S(2)}, u32[]{:S(2)}) collective-permute-start(f32[128,128]{1,0:T(8,128)S(1)} %get-tuple-element.33), channel_id=1, source_target_pairs={{0,12},{2,14},{4,8},{6,10},{8,4},{10,6},{12,0},{14,2},{1,13},{3,15... | collective-permute-start | bytes 196616 | tf_op jit(solution)/shard_map/ppermute | solution.py:518
  37.1 6.5 %collective-permute-start.9 = (f32[136,128]{1,0:T(8,128)S(1)}, f32[136,128]{1,0:T(8,128)S(1)}, u32[]{:S(2)}, u32[]{:S(2)}) collective-permute-start(f32[136,128]{1,0:T(8,128)S(1)} %middle.1.refs_0_), channel_id=1, source_target_pairs={{0,4},{2,6},{4,0},{6,2},{8,12},{10,14},{12,8},{14,10},{1,5},{3,7},... | collective-permute-start | bytes 208904 | tf_op jit(solution)/shard_map/ppermute | solution.py:529
  37.8 6.4 %collective-permute-start.11 = (f32[136,128]{1,0:T(8,128)S(1)}, f32[136,128]{1,0:T(8,128)S(1)}, u32[]{:S(2)}, u32[]{:S(2)}) collective-permute-start(f32[136,128]{1,0:T(8,128)S(1)} %middle.1.refs_0_), channel_id=1, source_target_pairs={{0,8},{2,10},{4,12},{6,14},{8,0},{10,2},{12,4},{14,6},{1,9},{3,11}... | collective-permute-start | bytes 208904 | tf_op jit(solution)/shard_map/ppermute | solution.py:529
  41.2 6.1 %collective-permute-start.13 = (f32[136,128]{1,0:T(8,128)S(1)}, f32[136,128]{1,0:T(8,128)S(1)}, u32[]{:S(2)}, u32[]{:S(2)}) collective-permute-start(f32[136,128]{1,0:T(8,128)S(1)} %middle.1.refs_0_), channel_id=1, source_target_pairs={{0,12},{2,14},{4,8},{6,10},{8,4},{10,6},{12,0},{14,2},{1,13},{3,15... | collective-permute-start | bytes 208904 | tf_op jit(solution)/shard_map/ppermute | solution.py:529
  41.5 5.8 %collective-permute-start.8 = (f32[136,128]{1,0:T(8,128)S(1)}, f32[136,128]{1,0:T(8,128)S(1)}, u32[]{:S(2)}, u32[]{:S(2)}) collective-permute-start(f32[136,128]{1,0:T(8,128)S(1)} %middle.1.refs_0_), channel_id=1, source_target_pairs={{0,2},{2,0},{4,6},{6,4},{8,10},{10,8},{12,14},{14,12},{1,3},{3,1},... | collective-permute-start | bytes 208904 | tf_op jit(solution)/shard_map/ppermute | solution.py:531
  43.6 4.3 %collective-permute-start.10 = (f32[136,128]{1,0:T(8,128)S(1)}, f32[136,128]{1,0:T(8,128)S(1)}, u32[]{:S(2)}, u32[]{:S(2)}) collective-permute-start(f32[136,128]{1,0:T(8,128)S(1)} %collective-permute-done.9.refs_2_), channel_id=1, source_target_pairs={{0,2},{2,0},{4,6},{6,4},{8,10},{10,8},{12,14},{14,12},{1,3},{3,1},... | collective-permute-start | bytes 208904 | tf_op jit(solution)/shard_map/ppermute | solution.py:531
  44.2 4.4 %collective-permute-start.12 = (f32[136,128]{1,0:T(8,128)S(1)}, f32[136,128]{1,0:T(8,128)S(1)}, u32[]{:S(2)}, u32[]{:S(2)}) collective-permute-start(f32[136,128]{1,0:T(8,128)S(1)} %collective-permute-done.11.refs_4_), channel_id=1, source_target_pairs={{0,2},{2,0},{4,6},{6,4},{8,10},{10,8},{12,14},{14,12},{1,3},{3,1},... | collective-permute-start | bytes 208904 | tf_op jit(solution)/shard_map/ppermute | solution.py:531
  47.3 4.3 %collective-permute-start.14 = (f32[136,128]{1,0:T(8,128)S(1)}, f32[136,128]{1,0:T(8,128)S(1)}, u32[]{:S(2)}, u32[]{:S(2)}) collective-permute-start(f32[136,128]{1,0:T(8,128)S(1)} %collective-permute-done.13.refs_6_), channel_id=1, source_target_pairs={{0,2},{2,0},{4,6},{6,4},{8,10},{10,8},{12,14},{14,12},{1,3},{3,1},... | collective-permute-start | bytes 208904 | tf_op jit(solution)/shard_map/ppermute | solution.py:531
  (4 other events, 2.7 us)

commit v3 on v0

--- a/solution.py
+++ b/solution.py
@@ -1,9 +1,13 @@
+import functools
 import jax
 import jax.numpy as jnp
 from jax import lax
+from jax.experimental import pallas as pl
+from jax.experimental.pallas import tpu as pltpu
 from jax.sharding import PartitionSpec as P
 
 HALO = 128
+LANES = 128
 
 
 epsilon = 1e-05
@@ -47,7 +51,7 @@
     return jnp.sum(ranking * matches, axis=1)
 
 
-def shards(
+def general_shards(
     fine_state,
     coarse_state,
     fine_senders,
@@ -138,6 +142,548 @@
     return (fine_out, coarse_out)
 
 
+f32 = jnp.float32
+bf16 = jnp.bfloat16
+
+
+def load_rows(ref, rows, parts, start=0):
+    return jnp.concatenate(
+        [ref[pl.ds(start * parts + j, rows, stride=parts), :] for j in range(parts)], axis=1
+    )
+
+
+def store_rows(ref, values, parts, start=0):
+    for j in range(parts):
+        ref[pl.ds(start * parts + j, values.shape[0], stride=parts), :] = values[
+            :, j * LANES : (j + 1) * LANES
+        ]
+
+
+def halves(values):
+    high = values.astype(bf16)
+    return high, (values - high.astype(f32)).astype(bf16)
+
+
+def mm(a, b):
+    return jnp.dot(a, b, preferred_element_type=f32)
+
+
+def times(values, high, low):
+    vh, vl = halves(values)
+    return mm(vh, high) + (mm(vl, high) + mm(vh, low))
+
+
+def take(one_hot, high, low):
+    return mm(one_hot, high) + mm(one_hot, low)
+
+
+def unit(values):
+    width = values.shape[1]
+    average = jnp.sum(values, axis=1, keepdims=True) * (1.0 / width)
+    centered = values - average
+    spread = jnp.sum(centered * centered, axis=1, keepdims=True) * (1.0 / width)
+    return centered * lax.rsqrt(spread + epsilon)
+
+
+def gate(half):
+    return half + half * jnp.tanh(half)
+
+
+def equal(column, count):
+    ids = lax.broadcasted_iota(jnp.int32, (column.shape[0], count), 1).astype(f32)
+    return jnp.where(ids == column, 1.0, 0.0).astype(bf16)
+
+
+def turned(lines):
+    pad = jnp.zeros((LANES - lines.shape[0], LANES), f32)
+    return jnp.transpose(jnp.concatenate([lines, pad], axis=0))
+
+
+def edge_hot(hot_ref, turn_ref, lines, degree, nodes, flip=None):
+    turn_ref[...] = turned(lines)
+    step = LANES // degree
+    for k in range(degree):
+        spread = turn_ref[pl.ds(k, step, stride=degree), :]
+        if flip is not None:
+            spread = jnp.bitwise_xor(spread.astype(jnp.int32), flip).astype(f32)
+        for line in range(lines.shape[0]):
+            start = k * nodes + line * step
+            hot_ref[start : start + step, :] = equal(
+                spread[:, line : line + 1], hot_ref.shape[1]
+            )
+
+
+def split_into(high_ref, low_ref, *matrices):
+    for j, matrix in enumerate(matrices):
+        size = matrix.shape[0]
+        high_ref[j * size : (j + 1) * size, :], low_ref[j * size : (j + 1) * size, :] = halves(
+            matrix
+        )
+
+
+def weights(high_ref, low_ref, j):
+    size = high_ref.shape[1]
+    return high_ref[j * size : (j + 1) * size, :], low_ref[j * size : (j + 1) * size, :]
+
+
+def start_kernel(
+    count, place_ref, state_hbm, coarse_hbm, sender_hbm, owner_hbm, local_hbm, cowner_hbm,
+    clocal_hbm, fb_hbm, ub_hbm, cb_hbm, db_hbm,
+    state_ref, ints_ref, pack_ref, swap_ref, diag_ref,
+    sender_ref, owner_ref, local_ref, cowner_ref, clocal_ref, fb_ref, ub_ref, cb_ref, db_ref,
+    sems,
+):
+    odd = place_ref[0]
+    rim = diag_ref.shape[0]
+    far = state_hbm.shape[0] - rim
+    own = coarse_hbm.shape[0]
+    pairs = [
+        (sender_hbm, sender_ref),
+        (owner_hbm, owner_ref),
+        (local_hbm, local_ref),
+        (cowner_hbm, cowner_ref),
+        (clocal_hbm, clocal_ref),
+        (fb_hbm, fb_ref),
+        (ub_hbm, ub_ref),
+        (cb_hbm, cb_ref),
+        (db_hbm, db_ref),
+        (state_hbm.at[pl.ds(pl.multiple_of((1 - odd) * far, LANES), rim), :], swap_ref.at[0:rim, :]),
+        (state_hbm.at[pl.ds(pl.multiple_of(odd * far, LANES), rim), :], diag_ref),
+        (coarse_hbm, swap_ref.at[rim : rim + own, :]),
+        (state_hbm, state_ref),
+    ]
+    copies = [pltpu.make_async_copy(a, b, sems.at[j]) for j, (a, b) in enumerate(pairs)]
+    for copy in copies:
+        copy.start()
+    for copy in copies[:9]:
+        copy.wait()
+    parts = fb_ref.shape[1] // LANES
+    rows = state_hbm.shape[0] // parts
+    halo = rim // parts
+    sender = sender_ref[...]
+    before = rows + (1 - odd) * halo
+    after = rows + odd * halo
+    index = jnp.where(
+        sender < halo,
+        sender + before,
+        jnp.where(sender < halo + rows, sender - halo, sender - (halo + rows) + after),
+    )
+    lines = [
+        index.astype(f32),
+        (owner_ref[...] * count + local_ref[...]).astype(f32),
+        (cowner_ref[...] * count + clocal_ref[...]).astype(f32),
+    ]
+    rest = ints_ref.shape[0] - sum(x.shape[0] for x in lines)
+    ints = jnp.concatenate(lines + [jnp.zeros((rest, LANES), f32)], axis=0)
+    ints_ref[...] = ints
+    swap_ref[rim + own :, :] = ints
+    pack_ref[...] = jnp.concatenate(
+        [fb_ref[...], ub_ref[...], cb_ref[...], db_ref[...]]
+        + [jnp.zeros((3, fb_ref.shape[1]), f32)],
+        axis=0,
+    )
+    for copy in copies[9:]:
+        copy.wait()
+
+
+def near_kernel(
+    edges, state_ref, ints_ref, ws_ref, wr_ref, wo_ref, pack_ref,
+    hot_ref, got_ref, into_ref, high_ref, low_ref, turn_ref,
+):
+    rows, width = into_ref.shape
+    parts = width // LANES
+    split_into(high_ref, low_ref, ws_ref[0], wo_ref[0])
+    edge_hot(
+        hot_ref, turn_ref, ints_ref[: edges // LANES, :], edges // rows, rows
+    )
+    normed = unit(load_rows(state_ref, rows, parts))
+    into_ref[...] = (times(normed, *halves(wr_ref[0])) + pack_ref[0:1, :]) * 0.5
+    high, low = halves(times(normed, *weights(high_ref, low_ref, 0)) * 0.5)
+    got_ref[...] = take(hot_ref[:, :rows], high, low)
+
+
+def far_kernel(
+    place_ref, swap_ref, diag_ref, state_ref, hot_ref, got_ref, into_ref, high_ref, low_ref,
+    out_full_ref, out_half_ref,
+):
+    rows, width = into_ref.shape
+    parts = width // LANES
+    rim = diag_ref.shape[0] // parts
+    degree = hot_ref.shape[0] // rows
+    far = jnp.concatenate(
+        [load_rows(swap_ref, rim, parts), load_rows(diag_ref, rim, parts)], axis=0
+    )
+    high, low = halves(times(unit(far), *weights(high_ref, low_ref, 0)) * 0.5)
+    total = None
+    for k in range(degree):
+        part = slice(k * rows, (k + 1) * rows)
+        half = got_ref[part, :] + into_ref[...] + take(hot_ref[part, rows:], high, low)
+        total = gate(half) if total is None else total + gate(half)
+    store_rows(
+        out_full_ref,
+        load_rows(state_ref, rows, parts) + times(total, *weights(high_ref, low_ref, 1)),
+        parts,
+    )
+    lines = out_half_ref.shape[0]
+    start = pl.multiple_of(place_ref[0] * (rows * parts - lines), LANES)
+    out_half_ref[...] = out_full_ref[pl.ds(start, lines), :]
+
+
+def near2_kernel(
+    edges, place_ref, state_ref, ints_ref, swap_ref, hot_ref, ws_ref, wr_ref, wo_ref, wi_ref,
+    wu_ref, pack_ref,
+    got_ref, into_ref, own_high_ref, own_low_ref, hot2_ref, select_ref, high_ref, low_ref,
+    turn_ref,
+):
+    rows, width = into_ref.shape
+    parts = width // LANES
+    senders = edges // LANES
+    first = swap_ref.shape[0] - ints_ref.shape[0]
+    split_into(
+        high_ref, low_ref, ws_ref[1], wr_ref[1], wo_ref[1], wi_ref[...], wu_ref[...]
+    )
+    normed = unit(load_rows(state_ref, rows, parts))
+    into_ref[...] = (times(normed, *weights(high_ref, low_ref, 1)) + pack_ref[1:2, :]) * 0.5
+    high, low = halves(times(normed, *weights(high_ref, low_ref, 0)) * 0.5)
+    own_high_ref[...] = high
+    own_low_ref[...] = low
+    got_ref[...] = take(hot_ref[:, :rows], high, low)
+    edge_hot(hot2_ref, turn_ref, swap_ref[first : first + senders, :], edges // rows, rows)
+    flip = place_ref[1]
+    line = senders
+    for half, ref, base in ((0, ints_ref, 0), (1, swap_ref, first)):
+        for j in range(rows // LANES):
+            parent = ref[base + line + j : base + line + j + 1, :].astype(jnp.int32)
+            parent = jnp.bitwise_xor(parent, flip)
+            ids = lax.broadcasted_iota(jnp.int32, (select_ref.shape[0], LANES), 0)
+            start = half * rows + j * LANES
+            select_ref[:, start : start + LANES] = jnp.where(ids == parent, 1.0, 0.0).astype(
+                bf16
+            )
+
+
+def messages(hidden, high_ref, low_ref, pack_ref):
+    act = gate((times(unit(hidden), *weights(high_ref, low_ref, 3)) + pack_ref[2:3, :]) * 0.5)
+    return halves(times(act, *weights(high_ref, low_ref, 4)))
+
+
+def other_kernel(
+    place_ref, swap_ref, pair_ref, own_high_ref, own_low_ref, hot_ref, select_ref, high_ref,
+    low_ref, pack_ref,
+    sums_ref, touch_high_ref, touch_low_ref, th_ref, tl_ref,
+):
+    rim, width = touch_high_ref.shape
+    rows = own_high_ref.shape[0]
+    parts = width // LANES
+    degree = hot_ref.shape[0] // rows
+    odd = place_ref[0]
+    mine = pl.multiple_of((1 - odd) * (rows - rim), LANES)
+    theirs = pl.multiple_of(odd * (rows - rim), LANES)
+    other = load_rows(swap_ref, rows, parts)
+    normed = unit(jnp.concatenate([other, load_rows(pair_ref, rim, parts)], axis=0))
+    sends = halves(times(normed, *weights(high_ref, low_ref, 0)) * 0.5)
+    for src, t_ref, own_ref, touch_ref in (
+        (sends[0], th_ref, own_high_ref, touch_high_ref),
+        (sends[1], tl_ref, own_low_ref, touch_low_ref),
+    ):
+        t_ref[:rows, :] = src[:rows, :]
+        t_ref[rows : rows + rim, :] = own_ref[pl.ds(mine, rim), :]
+        t_ref[rows + rim :, :] = src[rows:, :]
+        touch_ref[...] = t_ref[pl.ds(theirs, rim), :]
+    into = (times(normed[:rows, :], *weights(high_ref, low_ref, 1)) + pack_ref[1:2, :]) * 0.5
+    total = None
+    for k in range(degree):
+        half = into + take(hot_ref[k * rows : (k + 1) * rows, :], th_ref[...], tl_ref[...])
+        total = gate(half) if total is None else total + gate(half)
+    hidden = other + times(total, *weights(high_ref, low_ref, 2))
+    sums_ref[...] = take(select_ref[:, rows:], *messages(hidden, high_ref, low_ref, pack_ref))
+
+
+def own_kernel(
+    diag_ref, state_ref, hot_ref, got_ref, into_ref, touch_high_ref, touch_low_ref, sums_ref,
+    select_ref, ints_ref, swap_ref, high_ref, low_ref, pack_ref,
+    last_ref, *slot_refs,
+):
+    rows, width = into_ref.shape
+    parts = width // LANES
+    rim = diag_ref.shape[0] // parts
+    degree = hot_ref.shape[0] // rows
+    high, low = halves(
+        times(unit(load_rows(diag_ref, rim, parts)), *weights(high_ref, low_ref, 0)) * 0.5
+    )
+    high = jnp.concatenate([touch_high_ref[...], high], axis=0)
+    low = jnp.concatenate([touch_low_ref[...], low], axis=0)
+    total = None
+    for k in range(degree):
+        part = slice(k * rows, (k + 1) * rows)
+        half = got_ref[part, :] + into_ref[...] + take(hot_ref[part, rows:], high, low)
+        total = gate(half) if total is None else total + gate(half)
+    hidden = load_rows(state_ref, rows, parts) + times(total, *weights(high_ref, low_ref, 2))
+    last_ref[...] = hidden
+    sums = sums_ref[...] + take(
+        select_ref[:, :rows], *messages(hidden, high_ref, low_ref, pack_ref)
+    )
+    size = sums.shape[0] // len(slot_refs)
+    first = hot_ref.shape[0] // LANES + rows // LANES
+    base = swap_ref.shape[0] - ints_ref.shape[0]
+    anchor = (slot_refs[0].shape[0] - size * parts) // 4
+    for j, slot in enumerate(slot_refs):
+        store_rows(slot, sums[j * size : (j + 1) * size, :], parts)
+        slot[size * parts :, :] = jnp.concatenate(
+            [
+                ints_ref[first : first + anchor, :],
+                swap_ref[base + first : base + first + anchor, :],
+                jnp.zeros((2 * anchor, LANES), f32),
+            ],
+            axis=0,
+        )
+
+
+def middle_kernel(state_ref, swap_ref, *refs):
+    out_ref = refs[-1]
+    own = state_ref.shape[0]
+    lines = out_ref.shape[0]
+    rim = swap_ref.shape[0] - own - 16
+    total = jnp.concatenate([state_ref[...], swap_ref[rim : rim + own, :]], axis=0)
+    for ref in refs[:-1]:
+        total = total + ref[:lines, :]
+    out_ref[...] = total
+
+
+def edges_kernel(
+    degree, rows, place_ref, ints_ref, cs_ref, cr_ref, co_ref, di_ref, do_ref, *refs
+):
+    *slot_refs, hot_ref, parent_ref, high_ref, low_ref, turn_ref = refs
+    coarse = hot_ref.shape[1]
+    flip = place_ref[1]
+    split_into(
+        high_ref, low_ref, cs_ref[...], cr_ref[...], co_ref[...], di_ref[...], do_ref[...]
+    )
+    count = coarse * degree // LANES // len(slot_refs)
+    lines = jnp.concatenate(
+        [ref[ref.shape[0] - 2 * count : ref.shape[0] - count, :] for ref in slot_refs], axis=0
+    )
+    edge_hot(hot_ref, turn_ref, lines, degree, coarse, flip)
+    columns = turned(ints_ref[...])
+    first = ints_ref.shape[0] // 2
+    for j in range(rows // LANES):
+        column = jnp.bitwise_xor(
+            columns[:, first + j : first + j + 1].astype(jnp.int32), flip
+        ).astype(f32)
+        parent_ref[j * LANES : (j + 1) * LANES, :] = equal(column, coarse)
+
+
+def coarse_kernel(last_ref, hot_ref, parent_ref, high_ref, low_ref, pack_ref, *refs):
+    *blocks, fine_ref, coarse_ref = refs
+    rows, width = last_ref.shape
+    parts = width // LANES
+    coarse = hot_ref.shape[1]
+    each = coarse // len(blocks)
+    middle = jnp.concatenate([load_rows(b, each, parts) for b in blocks], axis=0)
+    normed = unit(middle)
+    high, low = halves(times(normed, *weights(high_ref, low_ref, 0)) * 0.5)
+    into = (times(normed, *weights(high_ref, low_ref, 1)) + pack_ref[3:4, :]) * 0.5
+    total = None
+    for k in range(hot_ref.shape[0] // coarse):
+        half = into + take(hot_ref[k * coarse : (k + 1) * coarse, :], high, low)
+        total = gate(half) if total is None else total + gate(half)
+    done = middle + times(total, *weights(high_ref, low_ref, 2))
+    store_rows(coarse_ref, done[: coarse_ref.shape[0] // parts, :], parts)
+    act = gate((times(unit(done), *weights(high_ref, low_ref, 3)) + pack_ref[4:5, :]) * 0.5)
+    down = halves(times(act, *weights(high_ref, low_ref, 4)))
+    store_rows(fine_ref, last_ref[...] + take(parent_ref[...], *down), parts)
+
+
+VMEM = pl.BlockSpec(memory_space=pltpu.VMEM)
+SMEM = pl.BlockSpec(memory_space=pltpu.SMEM)
+HBM = pl.BlockSpec(memory_space=pltpu.HBM)
+
+
+def call(kernel, in_specs, out_shapes, name, scratch=()):
+    return pl.pallas_call(
+        kernel,
+        in_specs=in_specs,
+        out_specs=[VMEM] * len(out_shapes),
+        out_shape=out_shapes,
+        scratch_shapes=scratch,
+        name=name,
+        compiler_params=pltpu.CompilerParams(vmem_limit_bytes=32 * 2**20),
+    )
+
+
+def shape(*dims, kind=f32):
+    return jax.ShapeDtypeStruct(dims, kind)
+
+
+def kernel_shards(
+    fine_state,
+    coarse_state,
+    fine_senders,
+    up_owner,
+    up_local,
+    coarse_owner,
+    coarse_local,
+    fine_w_send,
+    fine_w_recv,
+    fine_bias,
+    fine_w_out,
+    up_w_in,
+    up_bias,
+    up_w_out,
+    coarse_w_send,
+    coarse_w_recv,
+    coarse_bias,
+    coarse_w_out,
+    down_w_in,
+    down_bias,
+    down_w_out,
+):
+    peers = lax.axis_size("sp")
+    me = lax.axis_index("sp").astype(jnp.int32)
+    rows, _, width = fine_state.shape
+    count = coarse_state.shape[0]
+    parts = width // LANES
+    edges = fine_senders.shape[0]
+    coarse_edges = coarse_owner.shape[0]
+    coarse = peers * count
+    window = rows + 2 * HALO
+    rim, own, full = HALO * parts, count * parts, rows * parts
+    size = width
+    swap = [(i, i ^ 1) for i in range(peers)]
+    diag = [(i, (i + 1 if i % 2 else i - 1) % peers) for i in range(peers)]
+    pair = [(i, (i + 2 if i % 2 else i - 2) % peers) for i in range(peers)]
+    flips = [[(i, i ^ (2 * j)) for i in range(peers)] for j in range(peers // 2)]
+    place = jnp.stack([me % 2, me * count])
+    lines = lambda x: x.reshape(-1, LANES)
+    row = lambda x: x.reshape(1, width)
+    turn = pltpu.VMEM((LANES, LANES), f32)
+    hot_shape = shape(edges, window, kind=bf16)
+    small = lambda ref: pltpu.VMEM(ref.shape, ref.dtype)
+
+    small_args = [
+        lines(fine_senders), lines(up_owner), lines(up_local), lines(coarse_owner),
+        lines(coarse_local), fine_bias, row(up_bias), row(coarse_bias), row(down_bias),
+    ]
+    state, ints, pack, out_swap, out_diag = call(
+        functools.partial(start_kernel, count),
+        [SMEM] + [HBM] * 11,
+        [
+            shape(full, LANES), shape(16, LANES), shape(8, width),
+            shape(rim + own + 16, LANES), shape(rim, LANES),
+        ],
+        "start",
+        [small(x) for x in small_args] + [pltpu.SemaphoreType.DMA((13,))],
+    )(place, lines(fine_state), lines(coarse_state), *small_args)
+    swap0 = lax.ppermute(out_swap, "sp", swap)
+    diag0 = lax.ppermute(out_diag, "sp", diag)
+    hot, got, into, high, low = call(
+        functools.partial(near_kernel, edges),
+        [VMEM] * 6,
+        [hot_shape, shape(edges, width), shape(rows, width)]
+        + [shape(2 * size, width, kind=bf16)] * 2,
+        "near0",
+        [turn],
+    )(state, ints, fine_w_send, fine_w_recv, fine_w_out, pack)
+    state, out_half = call(
+        far_kernel,
+        [SMEM] + [VMEM] * 8,
+        [shape(full, LANES), shape(rim, LANES)],
+        "far0",
+    )(place, swap0, diag0, state, hot, got, into, high, low)
+    swap1 = lax.ppermute(state, "sp", swap)
+    diag1 = lax.ppermute(out_half, "sp", diag)
+    pair1 = lax.ppermute(out_half, "sp", pair)
+    got, into, own_high, own_low, hot2, select, high, low = call(
+        functools.partial(near2_kernel, edges),
+        [SMEM] + [VMEM] * 10,
+        [shape(edges, width), shape(rows, width)]
+        + [shape(rows, width, kind=bf16)] * 2
+        + [hot_shape, shape(coarse, 2 * rows, kind=bf16)]
+        + [shape(5 * size, width, kind=bf16)] * 2,
+        "near1",
+        [turn],
+    )(
+        place, state, ints, swap0, hot, fine_w_send, fine_w_recv, fine_w_out, up_w_in, up_w_out,
+        pack,
+    )
+    sums, touch_high, touch_low = call(
+        other_kernel,
+        [SMEM] + [VMEM] * 9,
+        [shape(coarse, width)] + [shape(HALO, width, kind=bf16)] * 2,
+        "other",
+        [pltpu.VMEM((window, width), bf16)] * 2,
+    )(place, swap1, pair1, own_high, own_low, hot2, select, high, low, pack)
+    hidden, *slots = call(
+        own_kernel,
+        [VMEM] * 14,
+        [shape(rows, width)]
+        + [shape(2 * own + 8 * coarse_edges // 256, LANES)] * (peers // 2),
+        "own",
+    )(
+        diag1, state, hot, got, into, touch_high, touch_low, sums, select, ints, swap0, high,
+        low, pack,
+    )
+    arrived = [slots[0]] + [
+        lax.ppermute(slots[j], "sp", flips[j]) for j in range(1, peers // 2)
+    ]
+    (middle,) = call(
+        middle_kernel,
+        [VMEM] * (2 + peers // 2),
+        [shape(2 * own, LANES)],
+        "middle",
+    )(lines(coarse_state), swap0, *arrived)
+    blocks = [middle] + [lax.ppermute(middle, "sp", flips[j]) for j in range(1, peers // 2)]
+    coarse_hot, parent_hot, high, low = call(
+        functools.partial(edges_kernel, coarse_edges // count, rows),
+        [SMEM] + [VMEM] * (6 + peers // 2),
+        [
+            shape(coarse_edges // count * coarse, coarse, kind=bf16),
+            shape(rows, coarse, kind=bf16),
+        ]
+        + [shape(5 * size, width, kind=bf16)] * 2,
+        "edges",
+        [turn],
+    )(
+        place, ints, coarse_w_send, coarse_w_recv, coarse_w_out, down_w_in, down_w_out, *arrived
+    )
+    fine_out, coarse_out = call(
+        coarse_kernel,
+        [VMEM] * (6 + peers // 2),
+        [shape(full, LANES), shape(own, LANES)],
+        "coarse",
+    )(hidden, coarse_hot, parent_hot, high, low, pack, *blocks)
+    return (fine_out.reshape(fine_state.shape), coarse_out.reshape(coarse_state.shape))
+
+
+def shards(*args):
+    fine_state, coarse_state, fine_senders = args[0], args[1], args[2]
+    coarse_owner, layers = args[5], args[7].shape[0]
+    peers = lax.axis_size("sp")
+    rows, samples, width = fine_state.shape
+    count = coarse_state.shape[0]
+    fits = (
+        samples == 1
+        and layers == 2
+        and width % LANES == 0
+        and peers % 2 == 0
+        and peers & (peers - 1) == 0
+        and rows % LANES == 0
+        and rows >= HALO
+        and count & (count - 1) == 0
+        and LANES % count == 0
+        and coarse_owner.shape[0] % LANES == 0
+        and coarse_owner.shape[0] == 4 * count
+        and fine_senders.shape[0] == 8 * LANES
+        and rows == 2 * LANES
+        and coarse_owner.shape[0] == 2 * LANES
+        and width == args[7].shape[2]
+        and peers * count <= 1024
+        and peers >= 4
+        and rows >= 2 * HALO
+    )
+    return (kernel_shards if fits else general_shards)(*args)
+
+
 def solution(mesh):
     in_specs = (
         P("sp", ("grp", "ch"), None),
@@ -147,20 +693,6 @@
         P("sp"),
         P("sp", None),
         P("sp"),
-        P(),
-        P(),
-        P(),
-        P(),
-        P(),
-        P(),
-        P(),
-        P(),
-        P(),
-        P(),
-        P(),
-        P(),
-        P(),
-        P(),
-    )
+    ) + (P(),) * 14
     out_specs = (P("sp", ("grp", "ch"), None), P("sp", ("grp", "ch"), None))
     return jax.shard_map(shards, mesh=mesh, in_specs=in_specs, out_specs=out_specs, check_vma=False)

time: 124 us -> 68.6 us (0.55)
  blocking collectives: 31.6 us -> 0 us
  Pallas kernels: 0 us -> 17.4 us
  local copies, waits for them, and re-layouts: 24.6 us -> 11.1 us
  other arithmetic: 11.6 us -> 0.08 us
  waiting for transfers between devices: 25.1 us -> 17.4 us
  matrix products: 6.15 us -> 0 us
  starting transfers between devices: 22.7 us -> 21.2 us
    all_gather x1 -> x0, blocking collectives: 31.6 us -> none  [shards(): everything = lax.all_gather(outward, 'sp', axis=0, tiled=True)]
    all_to_all x3 -> x0, waiting for transfers between devices: 21.5 us -> none  [the longest x1 12 us: shards(): lax.all_to_all(outgoing, 'sp', split_axis=0, concat_axis=0, tiled=True)]
    pallas_call x0 -> x9, Pallas kernels: none -> 17.4 us  [the longest x1 4.61 us: kernel_shards(): call(coarse_kernel, [VMEM] * (6 + peers // 2), [shape(full, LANES), shape...]
    ppermute x4 -> x11, waiting for transfers between devices: 3.61 us -> 17.4 us  [the longest x3 8.88 us: kernel_shards(): lax.ppermute(slots[j], 'sp', flips[j])]
    all_to_all x3 -> x0, starting transfers between devices: 11.7 us -> none  [the longest x1 4.85 us: shards(): lax.all_to_all(outgoing, 'sp', split_axis=0, concat_axis=0, tiled=True)]
    gather x6 -> x0, local copies, waits for them, and re-layouts: 11.2 us -> none  [the longest x2 6.93 us: shards(): extended[fine_senders].reshape(fine_rows, degree_fine, samples, -1)]
    ppermute x4 -> x11, starting transfers between devices: 11.1 us -> 21.2 us  [the longest x3 4.78 us: kernel_shards(): lax.ppermute(slots[j], 'sp', flips[j])]
    reduce_sum x10 -> x0, other arithmetic: 8.87 us -> none  [the longest x5 4.03 us: layer_norm(): spread = jnp.mean(centered * centered, axis=-1, keepdims=True)]
  transfers between devices with their start and end apart: 7 -> 11, of which waited for: 4 -> 8; matrix products, arithmetic and copies ran while one was open for 17% -> 0% of each run, Pallas kernels for 0% -> 11%
where the time goes in v3:
time: 68.6 us; the launch traced here: 68 us
  starting transfers between devices  21.2 us (31%)
  Pallas kernels  17.4 us (25%)
  waiting for transfers between devices  17.4 us (25%)
  local copies, waits for them, and re-layouts  11.1 us (16%)
  between operations  0.83 us (1%)
    unnamed x50, local copies, waits for them, and re-layouts  11.1 us
    ppermute x3, waiting for transfers between devices, kernel_shards(): lax.ppermute(slots[j], 'sp', flips[j])  8.88 us
    ppermute x3, waiting for transfers between devices, kernel_shards(): lax.ppermute(middle, 'sp', flips[j])  5.96 us
    ppermute x3, starting transfers between devices, kernel_shards(): lax.ppermute(slots[j], 'sp', flips[j])  4.78 us
    pallas_call x1, Pallas kernels, kernel_shards(): call(coarse_kernel, [VMEM] * (6 + peers // 2), [shape(full, LANES), shape...  4.61 us
    ppermute x3, starting transfers between devices, kernel_shards(): lax.ppermute(middle, 'sp', flips[j])  4.45 us
    ppermute x1, starting transfers between devices, kernel_shards(): pair1 = lax.ppermute(out_half, 'sp', pair)  3.6 us
    ppermute x1, starting transfers between devices, kernel_shards(): diag0 = lax.ppermute(out_diag, 'sp', diag)  3.57 us
  transfers between devices with their start and end apart: 11, of which 8 were waited for; matrix products, arithmetic and copies ran while one was open for 0% of the time, Pallas kernels for 11%

profile of v3, /device:TPU:0, one launch (start us, length us, event | category | flops | bytes accessed | tf_op | source)
XLA Modules:
  0.0 68.0 jit_solution(14699493770946464212)
XLA Ops:
  0.7 0.8 %copy-done.6 = f32[64,1,256]{2,1,0:T(1,128)S(1)} copy-done((f32[64,1,256]{2,1,0:T(1,128)S(1)}, f32[64,1,256]{2,1,0:T(1,128)}, u32[]{:S(2)}) %copy-start.6) | copy-done | bytes 65560
  1.6 0.9 %copy-done.8 = f32[256,1,256]{2,1,0:T(1,128)S(1)} copy-done((f32[256,1,256]{2,1,0:T(1,128)S(1)}, f32[256,1,256]{2,1,0:T(1,128)}, u32[]{:S(2)}) %copy-start.8) | copy-done | bytes 262168
  2.5 0.7 %copy-done.16 = s32[1024]{0:T(1024)S(1)} copy-done((s32[1024]{0:T(1024)S(1)}, s32[1024]{0:T(1024)}, u32[]{:S(2)}) %copy-start.16) | copy-done | bytes 4120
  3.2 0.7 copy-done.17
  3.9 0.7 copy-done.18
  4.6 0.7 copy-done.19
  8.6 1.1 %start.1 = (f32[512,128]{1,0:T(8,128)S(1)}, f32[16,128]{1,0:T(8,128)S(1)}, f32[8,256]{1,0:T(8,128)S(1)}, f32[400,128]{1,0:T(8,128)S(1)}, f32[256,128]{1,0:T(8,128)S(1)}) custom-call(s32[2]{0:T(128)S(1)} %pad_add_fusion.place_ref, f32[512,128]{1,0:T(8,128)S(1)} %bitcast.16, f32[128,128]{1,0:T(8,128)S(1)} %bitcast.14, s32[8,128]{1,0:T(8,128)S(1)} %bitcast.17, ...), custom_call_target="tpu_custom_call" | custom-call | tf_op jit(solution)/shard_map/start/pallas_call | solution.py:567
  9.8 3.0 %collective-permute-start = (f32[400,128]{1,0:T(8,128)S(1)}, f32[400,128]{1,0:T(8,128)S(1)}, u32[]{:S(2)}, u32[]{:S(2)}) collective-permute-start(f32[400,128]{1,0:T(8,128)S(1)} %get-tuple-element.36), channel_id=1, source_target_pairs={{0,2},{2,0},{4,6},{6,4},{8,10},{10,8},{12,14},{14,12},{1,3},{3,1},... | collective-permute-start | bytes 614408 | tf_op jit(solution)/shard_map/ppermute | solution.py:577
  12.8 3.6 %collective-permute-start.1 = (f32[256,128]{1,0:T(8,128)S(1)}, f32[256,128]{1,0:T(8,128)S(1)}, u32[]{:S(2)}, u32[]{:S(2)}) collective-permute-start(f32[256,128]{1,0:T(8,128)S(1)} %get-tuple-element.37), channel_id=1, source_target_pairs={{0,14},{2,4},{4,2},{6,8},{8,6},{10,12},{12,10},{14,0},{1,15},{3,5}... | collective-permute-start | bytes 393224 | tf_op jit(solution)/shard_map/ppermute | solution.py:578
  16.4 1.0 %copy-done = f32[2,256,256]{2,1,0:T(8,128)S(1)} copy-done((f32[2,256,256]{2,1,0:T(8,128)S(1)}, f32[2,256,256]{2,1,0:T(8,128)}, u32[]{:S(2)}) %copy-start) | copy-done | bytes 524312
  17.4 1.0 %copy-done.2 = f32[2,256,256]{2,1,0:T(8,128)S(1)} copy-done((f32[2,256,256]{2,1,0:T(8,128)S(1)}, f32[2,256,256]{2,1,0:T(8,128)}, u32[]{:S(2)}) %copy-start.2) | copy-done | bytes 524312
  18.5 1.0 %copy-done.4 = f32[2,256,256]{2,1,0:T(8,128)S(1)} copy-done((f32[2,256,256]{2,1,0:T(8,128)S(1)}, f32[2,256,256]{2,1,0:T(8,128)}, u32[]{:S(2)}) %copy-start.4) | copy-done | bytes 524312
  19.5 1.0 %near0.1 = (bf16[1024,512]{1,0:T(8,128)(2,1)S(1)}, f32[1024,256]{1,0:T(8,128)S(1)}, f32[256,256]{1,0:T(8,128)S(1)}, bf16[512,256]{1,0:T(8,128)(2,1)S(1)}, bf16[512,256]{1,0:T(8,128)(2,1)S(1)}) custom-call(f32[512,128]{1,0:T(8,128)S(1)} %get-tuple-element.38.state_ref, f32[16,128]{1,0:T(8,128)S(1)} %get-tuple-element.39.ints_ref, f32[2,256,256]{2,1,0:T(8,128)S(1)} %copy-done, ...), custom_call_target="tpu_custom_call" | custom-call | tf_op jit(solution)/shard_map/near0/pallas_call | solution.py:579
  20.7 1.9 %far0.1 = (f32[512,128]{1,0:T(8,128)S(1)}, f32[256,128]{1,0:T(8,128)S(1)}) custom-call(s32[2]{0:T(128)S(1)} %pad_add_fusion.place_ref, f32[400,128]{1,0:T(8,128)S(1)} %collective-permute-done.swap_ref, f32[256,128]{1,0:T(8,128)S(1)} %collective-permute-done.1.diag_ref, f32[512,128]{1,0:T(8,128)S(1)} %get-tuple-element.38.state_ref, ...), custom_call_target="tpu_custom_call" | custom-call | tf_op jit(solution)/shard_map/far0/pallas_call | solution.py:587
  22.6 1.8 %collective-permute-start.3 = (f32[512,128]{1,0:T(8,128)S(1)}, f32[512,128]{1,0:T(8,128)S(1)}, u32[]{:S(2)}, u32[]{:S(2)}) collective-permute-start(f32[512,128]{1,0:T(8,128)S(1)} %get-tuple-element.47.state_ref), channel_id=1, source_target_pairs={{0,2},{2,0},{4,6},{6,4},{8,10},{10,8},{12,14},{14,12},{1,3},{3,1},... | collective-permute-start | bytes 786440 | tf_op jit(solution)/shard_map/ppermute | solution.py:593
  24.4 3.6 %collective-permute-start.4 = (f32[256,128]{1,0:T(8,128)S(1)}, f32[256,128]{1,0:T(8,128)S(1)}, u32[]{:S(2)}, u32[]{:S(2)}) collective-permute-start(f32[256,128]{1,0:T(8,128)S(1)} %get-tuple-element.46), channel_id=1, source_target_pairs={{0,12},{2,6},{4,0},{6,10},{8,4},{10,14},{12,8},{14,2},{1,13},{3,7}... | collective-permute-start | bytes 393224 | tf_op jit(solution)/shard_map/ppermute | solution.py:595
  28.0 1.9 %near1.1 = (f32[1024,256]{1,0:T(8,128)S(1)}, f32[256,256]{1,0:T(8,128)S(1)}, bf16[256,256]{1,0:T(8,128)(2,1)S(1)}, bf16[256,256]{1,0:T(8,128)(2,1)S(1)}, bf16[10...) custom-call(s32[2]{0:T(128)S(1)} %pad_add_fusion.place_ref, ...), custom_call_target="tpu_custom_call" | custom-call | tf_op jit(solution)/shard_map/near1/pallas_call | solution.py:596
  29.9 1.1 %collective-permute-done.4.pair_ref = f32[256,128]{1,0:T(8,128)S(1)} collective-permute-done((f32[256,128]{1,0:T(8,128)S(1)}, f32[256,128]{1,0:T(8,128)S(1)}, u32[]{:S(2)}, u32[]{:S(2)}) %collective-permute-start.4) | collective-permute-done | bytes 131104 | tf_op jit(solution)/shard_map/ppermute | solution.py:595
  31.0 0.9 %collective-permute-done.3.swap_ref = f32[512,128]{1,0:T(8,128)S(1)} collective-permute-done((f32[512,128]{1,0:T(8,128)S(1)}, f32[512,128]{1,0:T(8,128)S(1)}, u32[]{:S(2)}, u32[]{:S(2)}) %collective-permute-start.3) | collective-permute-done | bytes 262176 | tf_op jit(solution)/shard_map/ppermute | solution.py:593
  31.9 3.3 %other.1 = (f32[512,256]{1,0:T(8,128)S(1)}, bf16[128,256]{1,0:T(8,128)(2,1)S(1)}, bf16[128,256]{1,0:T(8,128)(2,1)S(1)}) custom-call(s32[2]{0:T(128)S(1)} %pad_add_fusion.place_ref, f32[512,128]{1,0:T(8,128)S(1)} %collective-permute-done.3.swap_ref, f32[256,128]{1,0:T(8,128)S(1)} %collective-permute-done.4.pair_ref, ...), custom_call_target="tpu_custom_call" | custom-call | tf_op jit(solution)/shard_map/other/pallas_call | solution.py:609
  35.7 2.2 %own.1 = (f32[256,256]{1,0:T(8,128)S(1)}, f32[264,128]{1,0:T(8,128)S(1)}, f32[264,128]{1,0:T(8,128)S(1)}, f32[264,128]{1,0:T(8,128)S(1)}, f32[264,128]{1,0:T(8,128)S(1)}) custom-call(f32[256,128]{1,0:T(8,128)S(1)} %collective-permute-done.2.diag_ref, f32[512,128]{1,0:T(8,128)S(1)} %get-tuple-element.47.state_ref, ...), custom_call_target="tpu_custom_call" | custom-call | tf_op jit(solution)/shard_map/own/pallas_call | solution.py:616
  37.9 2.2 %collective-permute-start.5 = (f32[264,128]{1,0:T(8,128)S(1)}, f32[264,128]{1,0:T(8,128)S(1)}, u32[]{:S(2)}, u32[]{:S(2)}) collective-permute-start(f32[264,128]{1,0:T(8,128)S(1)} %get-tuple-element.61), channel_id=1, source_target_pairs={{0,4},{2,6},{4,0},{6,2},{8,12},{10,14},{12,8},{14,10},{1,5},{3,7},... | collective-permute-start | bytes 405512 | tf_op jit(solution)/shard_map/ppermute | solution.py:627
  40.1 2.6 %collective-permute-start.6 = (f32[264,128]{1,0:T(8,128)S(1)}, f32[264,128]{1,0:T(8,128)S(1)}, u32[]{:S(2)}, u32[]{:S(2)}) collective-permute-start(f32[264,128]{1,0:T(8,128)S(1)} %get-tuple-element.62), channel_id=1, source_target_pairs={{0,8},{2,10},{4,12},{6,14},{8,0},{10,2},{12,4},{14,6},{1,9},{3,11}... | collective-permute-start | bytes 405512 | tf_op jit(solution)/shard_map/ppermute | solution.py:627
  42.7 0.9 %collective-permute-done.5.refs_1_ = f32[264,128]{1,0:T(8,128)S(1)} collective-permute-done((f32[264,128]{1,0:T(8,128)S(1)}, f32[264,128]{1,0:T(8,128)S(1)}, u32[]{:S(2)}, u32[]{:S(2)}) %collective-permute-start.5) | collective-permute-done | bytes 135200 | tf_op jit(solution)/shard_map/ppermute | solution.py:627
  43.6 7.9 %collective-permute-done.6.refs_2_ = f32[264,128]{1,0:T(8,128)S(1)} collective-permute-done((f32[264,128]{1,0:T(8,128)S(1)}, f32[264,128]{1,0:T(8,128)S(1)}, u32[]{:S(2)}, u32[]{:S(2)}) %collective-permute-start.6) | collective-permute-done | bytes 135200 | tf_op jit(solution)/shard_map/ppermute | solution.py:627
  51.6 2.6 %collective-permute-start.10 = (f32[256,128]{1,0:T(8,128)S(1)}, f32[256,128]{1,0:T(8,128)S(1)}, u32[]{:S(2)}, u32[]{:S(2)}) collective-permute-start(f32[256,128]{1,0:T(8,128)S(1)} %middle.1.refs_0_), channel_id=1, source_target_pairs={{0,12},{2,14},{4,8},{6,10},{8,4},{10,6},{12,0},{14,2},{1,13},{3,15... | collective-permute-start | bytes 393224 | tf_op jit(solution)/shard_map/ppermute | solution.py:635
  54.2 0.9 %collective-permute-start.9 = (f32[256,128]{1,0:T(8,128)S(1)}, f32[256,128]{1,0:T(8,128)S(1)}, u32[]{:S(2)}, u32[]{:S(2)}) collective-permute-start(f32[256,128]{1,0:T(8,128)S(1)} %middle.1.refs_0_), channel_id=1, source_target_pairs={{0,8},{2,10},{4,12},{6,14},{8,0},{10,2},{12,4},{14,6},{1,9},{3,11}... | collective-permute-start | bytes 393224 | tf_op jit(solution)/shard_map/ppermute | solution.py:635
  55.1 0.9 %collective-permute-start.8 = (f32[256,128]{1,0:T(8,128)S(1)}, f32[256,128]{1,0:T(8,128)S(1)}, u32[]{:S(2)}, u32[]{:S(2)}) collective-permute-start(f32[256,128]{1,0:T(8,128)S(1)} %middle.1.refs_0_), channel_id=1, source_target_pairs={{0,4},{2,6},{4,0},{6,2},{8,12},{10,14},{12,8},{14,10},{1,5},{3,7},... | collective-permute-start | bytes 393224 | tf_op jit(solution)/shard_map/ppermute | solution.py:635
  56.1 1.4 %edges.1 = (bf16[2048,512]{1,0:T(8,128)(2,1)S(1)}, bf16[256,512]{1,0:T(8,128)(2,1)S(1)}, bf16[1280,256]{1,0:T(8,128)(2,1)S(1)}, bf16[1280,256]{1,0:T(8,128)(2,1)S(1)}) custom-call(s32[2]{0:T(128)S(1)} %pad_add_fusion.place_ref, f32[16,128]{1,0:T(8,128)S(1)} %get-tuple-element.39.ints_ref, f32[256,256]{1,0:T(8,128)S(1)} %copy-done.9, ...), custom_call_target="tpu_custom_call" | custom-call | tf_op jit(solution)/shard_map/edges/pallas_call | solution.py:636
  57.5 2.4 %collective-permute-done.10.refs_3_ = f32[256,128]{1,0:T(8,128)S(1)} collective-permute-done((f32[256,128]{1,0:T(8,128)S(1)}, f32[256,128]{1,0:T(8,128)S(1)}, u32[]{:S(2)}, u32[]{:S(2)}) %collective-permute-start.10) | collective-permute-done | bytes 131104 | tf_op jit(solution)/shard_map/ppermute | solution.py:635
  59.8 3.6 %collective-permute-done.9.refs_2_ = f32[256,128]{1,0:T(8,128)S(1)} collective-permute-done((f32[256,128]{1,0:T(8,128)S(1)}, f32[256,128]{1,0:T(8,128)S(1)}, u32[]{:S(2)}, u32[]{:S(2)}) %collective-permute-start.9) | collective-permute-done | bytes 131104 | tf_op jit(solution)/shard_map/ppermute | solution.py:635
  63.4 4.6 %coarse.1 = (f32[512,128]{1,0:T(8,128)}, f32[128,128]{1,0:T(8,128)}) custom-call(f32[256,256]{1,0:T(8,128)S(1)} %get-tuple-element.59.last_ref, bf16[2048,512]{1,0:T(8,128)(2,1)S(1)} %get-tuple-element.64.hot_ref, bf16[256,512]{1,0:T(8,128)(2,1)S(1)} %get-tuple-element.65.parent_ref, bf16[1280,256]{1,0:T(8,128)(2,1)S(1)} %get-tuple-element.66.high_ref, ...), custom_call_target="tpu_custom_call" | custom-call | tf_op jit(solution)/shard_map/coarse/pallas_call | solution.py:649
  (50 shorter events, 4.2 us)
Async XLA Ops:
  0.7 0.8 %copy-start.6 = (f32[64,1,256]{2,1,0:T(1,128)S(1)}, f32[64,1,256]{2,1,0:T(1,128)}, u32[]{:S(2)}) copy-start(f32[64,1,256]{2,1,0:T(1,128)} %param.22) | copy-start | bytes 196612
  1.6 0.9 %copy-start.8 = (f32[256,1,256]{2,1,0:T(1,128)S(1)}, f32[256,1,256]{2,1,0:T(1,128)}, u32[]{:S(2)}) copy-start(f32[256,1,256]{2,1,0:T(1,128)} %param.21) | copy-start | bytes 786436
  2.5 0.7 %copy-start.16 = (s32[1024]{0:T(1024)S(1)}, s32[1024]{0:T(1024)}, u32[]{:S(2)}) copy-start(s32[1024]{0:T(1024)} %param.23) | copy-start | bytes 12292
  3.2 0.7 %copy-start.17 = (f32[2,256]{1,0:T(2,128)S(1)}, f32[2,256]{1,0:T(2,128)}, u32[]{:S(2)}) copy-start(f32[2,256]{1,0:T(2,128)} %fb_hbm.1) | copy-start | bytes 6148
  3.9 0.7 copy-start.18
  5.9 0.7 copy-start.21
  8.0 0.7 copy-start.24
  9.8 10.9 %collective-permute-start = (f32[400,128]{1,0:T(8,128)S(1)}, f32[400,128]{1,0:T(8,128)S(1)}, u32[]{:S(2)}, u32[]{:S(2)}) collective-permute-start(f32[400,128]{1,0:T(8,128)S(1)} %get-tuple-element.36), channel_id=1, source_target_pairs={{0,2},{2,0},{4,6},{6,4},{8,10},{10,8},{12,14},{14,12},{1,3},{3,1},... | collective-permute-start | bytes 614408 | tf_op jit(solution)/shard_map/ppermute | solution.py:577
  12.8 7.8 %collective-permute-start.1 = (f32[256,128]{1,0:T(8,128)S(1)}, f32[256,128]{1,0:T(8,128)S(1)}, u32[]{:S(2)}, u32[]{:S(2)}) collective-permute-start(f32[256,128]{1,0:T(8,128)S(1)} %get-tuple-element.37), channel_id=1, source_target_pairs={{0,14},{2,4},{4,2},{6,8},{8,6},{10,12},{12,10},{14,0},{1,15},{3,5}... | collective-permute-start | bytes 393224 | tf_op jit(solution)/shard_map/ppermute | solution.py:578
  16.4 1.0 %copy-start = (f32[2,256,256]{2,1,0:T(8,128)S(1)}, f32[2,256,256]{2,1,0:T(8,128)}, u32[]{:S(2)}) copy-start(f32[2,256,256]{2,1,0:T(8,128)} %ws_ref.3) | copy-start | bytes 1572868
  17.4 1.0 %copy-start.2 = (f32[2,256,256]{2,1,0:T(8,128)S(1)}, f32[2,256,256]{2,1,0:T(8,128)}, u32[]{:S(2)}) copy-start(f32[2,256,256]{2,1,0:T(8,128)} %wr_ref.3) | copy-start | bytes 1572868
  18.5 1.0 %copy-start.4 = (f32[2,256,256]{2,1,0:T(8,128)S(1)}, f32[2,256,256]{2,1,0:T(8,128)}, u32[]{:S(2)}) copy-start(f32[2,256,256]{2,1,0:T(8,128)} %wo_ref.3) | copy-start | bytes 1572868
  20.6 7.4 %copy-start.1 = (f32[2,256,256]{2,1,0:T(8,128)S(1)}, f32[2,256,256]{2,1,0:T(8,128)}, u32[]{:S(2)}) copy-start(f32[2,256,256]{2,1,0:T(8,128)} %ws_ref.3) | copy-start | bytes 1572868
  20.6 7.4 %copy-start.3 = (f32[2,256,256]{2,1,0:T(8,128)S(1)}, f32[2,256,256]{2,1,0:T(8,128)}, u32[]{:S(2)}) copy-start(f32[2,256,256]{2,1,0:T(8,128)} %wr_ref.3) | copy-start | bytes 1572868
  20.6 7.4 %copy-start.5 = (f32[2,256,256]{2,1,0:T(8,128)S(1)}, f32[2,256,256]{2,1,0:T(8,128)}, u32[]{:S(2)}) copy-start(f32[2,256,256]{2,1,0:T(8,128)} %wo_ref.3) | copy-start | bytes 1572868
  20.6 7.4 %copy-start.14 = (f32[256,256]{1,0:T(8,128)S(1)}, f32[256,256]{1,0:T(8,128)}, u32[]{:S(2)}) copy-start(f32[256,256]{1,0:T(8,128)} %wi_ref.1) | copy-start | bytes 786436
  20.6 7.4 %copy-start.15 = (f32[256,256]{1,0:T(8,128)S(1)}, f32[256,256]{1,0:T(8,128)}, u32[]{:S(2)}) copy-start(f32[256,256]{1,0:T(8,128)} %wu_ref.1) | copy-start | bytes 786436
  22.6 9.3 %collective-permute-start.3 = (f32[512,128]{1,0:T(8,128)S(1)}, f32[512,128]{1,0:T(8,128)S(1)}, u32[]{:S(2)}, u32[]{:S(2)}) collective-permute-start(f32[512,128]{1,0:T(8,128)S(1)} %get-tuple-element.47.state_ref), channel_id=1, source_target_pairs={{0,2},{2,0},{4,6},{6,4},{8,10},{10,8},{12,14},{14,12},{1,3},{3,1},... | collective-permute-start | bytes 786440 | tf_op jit(solution)/shard_map/ppermute | solution.py:593
  24.4 6.6 %collective-permute-start.4 = (f32[256,128]{1,0:T(8,128)S(1)}, f32[256,128]{1,0:T(8,128)S(1)}, u32[]{:S(2)}, u32[]{:S(2)}) collective-permute-start(f32[256,128]{1,0:T(8,128)S(1)} %get-tuple-element.46), channel_id=1, source_target_pairs={{0,12},{2,6},{4,0},{6,10},{8,4},{10,14},{12,8},{14,2},{1,13},{3,7}... | collective-permute-start | bytes 393224 | tf_op jit(solution)/shard_map/ppermute | solution.py:595
  28.0 7.7 %collective-permute-start.2 = (f32[256,128]{1,0:T(8,128)S(1)}, f32[256,128]{1,0:T(8,128)S(1)}, u32[]{:S(2)}, u32[]{:S(2)}) collective-permute-start(f32[256,128]{1,0:T(8,128)S(1)} %get-tuple-element.46), channel_id=1, source_target_pairs={{0,14},{2,4},{4,2},{6,8},{8,6},{10,12},{12,10},{14,0},{1,15},{3,5}... | collective-permute-start | bytes 393224 | tf_op jit(solution)/shard_map/ppermute | solution.py:594
  35.7 15.9 %copy-start.7 = (f32[64,1,256]{2,1,0:T(1,128)S(1)}, f32[64,1,256]{2,1,0:T(1,128)}, u32[]{:S(2)}) copy-start(f32[64,1,256]{2,1,0:T(1,128)} %param.22) | copy-start | bytes 196612
  35.7 20.4 %copy-start.9 = (f32[256,256]{1,0:T(8,128)S(1)}, f32[256,256]{1,0:T(8,128)}, u32[]{:S(2)}) copy-start(f32[256,256]{1,0:T(8,128)} %cs_ref.1) | copy-start | bytes 786436
  35.7 20.4 %copy-start.10 = (f32[256,256]{1,0:T(8,128)S(1)}, f32[256,256]{1,0:T(8,128)}, u32[]{:S(2)}) copy-start(f32[256,256]{1,0:T(8,128)} %cr_ref.1) | copy-start | bytes 786436
  35.7 20.4 %copy-start.11 = (f32[256,256]{1,0:T(8,128)S(1)}, f32[256,256]{1,0:T(8,128)}, u32[]{:S(2)}) copy-start(f32[256,256]{1,0:T(8,128)} %co_ref.1) | copy-start | bytes 786436
  35.7 20.4 %copy-start.12 = (f32[256,256]{1,0:T(8,128)S(1)}, f32[256,256]{1,0:T(8,128)}, u32[]{:S(2)}) copy-start(f32[256,256]{1,0:T(8,128)} %di_ref.1) | copy-start | bytes 786436
  35.7 20.4 %copy-start.13 = (f32[256,256]{1,0:T(8,128)S(1)}, f32[256,256]{1,0:T(8,128)}, u32[]{:S(2)}) copy-start(f32[256,256]{1,0:T(8,128)} %do_ref.1) | copy-start | bytes 786436
  37.9 5.7 %collective-permute-start.5 = (f32[264,128]{1,0:T(8,128)S(1)}, f32[264,128]{1,0:T(8,128)S(1)}, u32[]{:S(2)}, u32[]{:S(2)}) collective-permute-start(f32[264,128]{1,0:T(8,128)S(1)} %get-tuple-element.61), channel_id=1, source_target_pairs={{0,4},{2,6},{4,0},{6,2},{8,12},{10,14},{12,8},{14,10},{1,5},{3,7},... | collective-permute-start | bytes 405512 | tf_op jit(solution)/shard_map/ppermute | solution.py:627
  40.1 11.5 %collective-permute-start.6 = (f32[264,128]{1,0:T(8,128)S(1)}, f32[264,128]{1,0:T(8,128)S(1)}, u32[]{:S(2)}, u32[]{:S(2)}) collective-permute-start(f32[264,128]{1,0:T(8,128)S(1)} %get-tuple-element.62), channel_id=1, source_target_pairs={{0,8},{2,10},{4,12},{6,14},{8,0},{10,2},{12,4},{14,6},{1,9},{3,11}... | collective-permute-start | bytes 405512 | tf_op jit(solution)/shard_map/ppermute | solution.py:627
  42.7 8.9 %collective-permute-start.7 = (f32[264,128]{1,0:T(8,128)S(1)}, f32[264,128]{1,0:T(8,128)S(1)}, u32[]{:S(2)}, u32[]{:S(2)}) collective-permute-start(f32[264,128]{1,0:T(8,128)S(1)} %get-tuple-element.63), channel_id=1, source_target_pairs={{0,12},{2,14},{4,8},{6,10},{8,4},{10,6},{12,0},{14,2},{1,13},{3,15... | collective-permute-start | bytes 405512 | tf_op jit(solution)/shard_map/ppermute | solution.py:627
  51.6 8.2 %collective-permute-start.10 = (f32[256,128]{1,0:T(8,128)S(1)}, f32[256,128]{1,0:T(8,128)S(1)}, u32[]{:S(2)}, u32[]{:S(2)}) collective-permute-start(f32[256,128]{1,0:T(8,128)S(1)} %middle.1.refs_0_), channel_id=1, source_target_pairs={{0,12},{2,14},{4,8},{6,10},{8,4},{10,6},{12,0},{14,2},{1,13},{3,15... | collective-permute-start | bytes 393224 | tf_op jit(solution)/shard_map/ppermute | solution.py:635
  54.2 9.2 %collective-permute-start.9 = (f32[256,128]{1,0:T(8,128)S(1)}, f32[256,128]{1,0:T(8,128)S(1)}, u32[]{:S(2)}, u32[]{:S(2)}) collective-permute-start(f32[256,128]{1,0:T(8,128)S(1)} %middle.1.refs_0_), channel_id=1, source_target_pairs={{0,8},{2,10},{4,12},{6,14},{8,0},{10,2},{12,4},{14,6},{1,9},{3,11}... | collective-permute-start | bytes 393224 | tf_op jit(solution)/shard_map/ppermute | solution.py:635
  55.1 8.3 %collective-permute-start.8 = (f32[256,128]{1,0:T(8,128)S(1)}, f32[256,128]{1,0:T(8,128)S(1)}, u32[]{:S(2)}, u32[]{:S(2)}) collective-permute-start(f32[256,128]{1,0:T(8,128)S(1)} %middle.1.refs_0_), channel_id=1, source_target_pairs={{0,4},{2,6},{4,0},{6,2},{8,12},{10,14},{12,8},{14,10},{1,5},{3,7},... | collective-permute-start | bytes 393224 | tf_op jit(solution)/shard_map/ppermute | solution.py:635
  (4 other events, 2.7 us)

commit v4 on v3

--- a/solution.py
+++ b/solution.py
@@ -227,7 +227,7 @@
 
 
 def start_kernel(
-    count, place_ref, state_hbm, coarse_hbm, sender_hbm, owner_hbm, local_hbm, cowner_hbm,
+    count, place_ref, state_hbm, sender_hbm, owner_hbm, local_hbm, cowner_hbm,
     clocal_hbm, fb_hbm, ub_hbm, cb_hbm, db_hbm,
     state_ref, ints_ref, pack_ref, swap_ref, diag_ref,
     sender_ref, owner_ref, local_ref, cowner_ref, clocal_ref, fb_ref, ub_ref, cb_ref, db_ref,
@@ -236,7 +236,6 @@
     odd = place_ref[0]
     rim = diag_ref.shape[0]
     far = state_hbm.shape[0] - rim
-    own = coarse_hbm.shape[0]
     pairs = [
         (sender_hbm, sender_ref),
         (owner_hbm, owner_ref),
@@ -249,7 +248,6 @@
         (db_hbm, db_ref),
         (state_hbm.at[pl.ds(pl.multiple_of((1 - odd) * far, LANES), rim), :], swap_ref.at[0:rim, :]),
         (state_hbm.at[pl.ds(pl.multiple_of(odd * far, LANES), rim), :], diag_ref),
-        (coarse_hbm, swap_ref.at[rim : rim + own, :]),
         (state_hbm, state_ref),
     ]
     copies = [pltpu.make_async_copy(a, b, sems.at[j]) for j, (a, b) in enumerate(pairs)]
@@ -276,7 +274,7 @@
     rest = ints_ref.shape[0] - sum(x.shape[0] for x in lines)
     ints = jnp.concatenate(lines + [jnp.zeros((rest, LANES), f32)], axis=0)
     ints_ref[...] = ints
-    swap_ref[rim + own :, :] = ints
+    swap_ref[rim:, :] = ints
     pack_ref[...] = jnp.concatenate(
         [fb_ref[...], ub_ref[...], cb_ref[...], db_ref[...]]
         + [jnp.zeros((3, fb_ref.shape[1]), f32)],
@@ -287,17 +285,23 @@
 
 
 def near_kernel(
-    edges, state_ref, ints_ref, ws_ref, wr_ref, wo_ref, pack_ref,
-    hot_ref, got_ref, into_ref, high_ref, low_ref, turn_ref,
+    edges, state_ref, ints_ref, ws_hbm, wr_hbm, wo_hbm, pack_ref,
+    hot_ref, got_ref, into_ref, high_ref, low_ref, turn_ref, ws_ref, wr_ref, wo_ref, sems,
 ):
     rows, width = into_ref.shape
     parts = width // LANES
-    split_into(high_ref, low_ref, ws_ref[0], wo_ref[0])
-    edge_hot(
-        hot_ref, turn_ref, ints_ref[: edges // LANES, :], edges // rows, rows
-    )
+    pairs = ((ws_hbm, ws_ref), (wr_hbm, wr_ref), (wo_hbm, wo_ref))
+    copies = [
+        pltpu.make_async_copy(a.at[0], b, sems.at[j]) for j, (a, b) in enumerate(pairs)
+    ]
+    for copy in copies:
+        copy.start()
+    edge_hot(hot_ref, turn_ref, ints_ref[: edges // LANES, :], edges // rows, rows)
     normed = unit(load_rows(state_ref, rows, parts))
-    into_ref[...] = (times(normed, *halves(wr_ref[0])) + pack_ref[0:1, :]) * 0.5
+    for copy in copies:
+        copy.wait()
+    split_into(high_ref, low_ref, ws_ref[...], wo_ref[...])
+    into_ref[...] = (times(normed, *halves(wr_ref[...])) + pack_ref[0:1, :]) * 0.5
     high, low = halves(times(normed, *weights(high_ref, low_ref, 0)) * 0.5)
     got_ref[...] = take(hot_ref[:, :rows], high, low)
 
@@ -330,7 +334,7 @@
 
 
 def near2_kernel(
-    edges, place_ref, state_ref, ints_ref, swap_ref, hot_ref, ws_ref, wr_ref, wo_ref, wi_ref,
+    edges, count, place_ref, state_ref, ints_ref, swap_ref, hot_ref, ws_ref, wr_ref, wo_ref, wi_ref,
     wu_ref, pack_ref,
     got_ref, into_ref, own_high_ref, own_low_ref, hot2_ref, select_ref, high_ref, low_ref,
     turn_ref,
@@ -356,114 +360,90 @@
             parent = ref[base + line + j : base + line + j + 1, :].astype(jnp.int32)
             parent = jnp.bitwise_xor(parent, flip)
             ids = lax.broadcasted_iota(jnp.int32, (select_ref.shape[0], LANES), 0)
+            ids = ids + jnp.bitwise_and(ids, -count)
             start = half * rows + j * LANES
             select_ref[:, start : start + LANES] = jnp.where(ids == parent, 1.0, 0.0).astype(
                 bf16
             )
 
 
-def messages(hidden, high_ref, low_ref, pack_ref):
-    act = gate((times(unit(hidden), *weights(high_ref, low_ref, 3)) + pack_ref[2:3, :]) * 0.5)
-    return halves(times(act, *weights(high_ref, low_ref, 4)))
-
-
-def other_kernel(
-    place_ref, swap_ref, pair_ref, own_high_ref, own_low_ref, hot_ref, select_ref, high_ref,
-    low_ref, pack_ref,
-    sums_ref, touch_high_ref, touch_low_ref, th_ref, tl_ref,
+def up_kernel(
+    place_ref, swap_ref, pair_ref, diag_ref, state_ref, hot_ref, got_ref, into_ref, own_high_ref,
+    own_low_ref, hot2_ref, select_ref, ints_ref, swap0_ref, high_ref, low_ref, pack_ref,
+    last_ref, *refs,
 ):
-    rim, width = touch_high_ref.shape
-    rows = own_high_ref.shape[0]
+    *slot_refs, th_ref, tl_ref = refs
+    rows, width = into_ref.shape
     parts = width // LANES
+    rim = diag_ref.shape[0] // parts
     degree = hot_ref.shape[0] // rows
     odd = place_ref[0]
     mine = pl.multiple_of((1 - odd) * (rows - rim), LANES)
     theirs = pl.multiple_of(odd * (rows - rim), LANES)
     other = load_rows(swap_ref, rows, parts)
-    normed = unit(jnp.concatenate([other, load_rows(pair_ref, rim, parts)], axis=0))
+    normed = unit(
+        jnp.concatenate(
+            [other, load_rows(pair_ref, rim, parts), load_rows(diag_ref, rim, parts)], axis=0
+        )
+    )
     sends = halves(times(normed, *weights(high_ref, low_ref, 0)) * 0.5)
-    for src, t_ref, own_ref, touch_ref in (
-        (sends[0], th_ref, own_high_ref, touch_high_ref),
-        (sends[1], tl_ref, own_low_ref, touch_low_ref),
+    near = []
+    for src, t_ref, own_ref in (
+        (sends[0], th_ref, own_high_ref), (sends[1], tl_ref, own_low_ref),
     ):
         t_ref[:rows, :] = src[:rows, :]
         t_ref[rows : rows + rim, :] = own_ref[pl.ds(mine, rim), :]
-        t_ref[rows + rim :, :] = src[rows:, :]
-        touch_ref[...] = t_ref[pl.ds(theirs, rim), :]
+        t_ref[rows + rim :, :] = src[rows : rows + rim, :]
+        near.append(
+            jnp.concatenate([t_ref[pl.ds(theirs, rim), :], src[rows + rim :, :]], axis=0)
+        )
     into = (times(normed[:rows, :], *weights(high_ref, low_ref, 1)) + pack_ref[1:2, :]) * 0.5
-    total = None
-    for k in range(degree):
-        half = into + take(hot_ref[k * rows : (k + 1) * rows, :], th_ref[...], tl_ref[...])
-        total = gate(half) if total is None else total + gate(half)
-    hidden = other + times(total, *weights(high_ref, low_ref, 2))
-    sums_ref[...] = take(select_ref[:, rows:], *messages(hidden, high_ref, low_ref, pack_ref))
-
-
-def own_kernel(
-    diag_ref, state_ref, hot_ref, got_ref, into_ref, touch_high_ref, touch_low_ref, sums_ref,
-    select_ref, ints_ref, swap_ref, high_ref, low_ref, pack_ref,
-    last_ref, *slot_refs,
-):
-    rows, width = into_ref.shape
-    parts = width // LANES
-    rim = diag_ref.shape[0] // parts
-    degree = hot_ref.shape[0] // rows
-    high, low = halves(
-        times(unit(load_rows(diag_ref, rim, parts)), *weights(high_ref, low_ref, 0)) * 0.5
-    )
-    high = jnp.concatenate([touch_high_ref[...], high], axis=0)
-    low = jnp.concatenate([touch_low_ref[...], low], axis=0)
-    total = None
+    total, total2 = None, None
     for k in range(degree):
         part = slice(k * rows, (k + 1) * rows)
-        half = got_ref[part, :] + into_ref[...] + take(hot_ref[part, rows:], high, low)
+        half = got_ref[part, :] + into_ref[...] + take(hot_ref[part, rows:], *near)
         total = gate(half) if total is None else total + gate(half)
-    hidden = load_rows(state_ref, rows, parts) + times(total, *weights(high_ref, low_ref, 2))
-    last_ref[...] = hidden
-    sums = sums_ref[...] + take(
-        select_ref[:, :rows], *messages(hidden, high_ref, low_ref, pack_ref)
-    )
+        half = into + take(hot2_ref[part, :], th_ref[...], tl_ref[...])
+        total2 = gate(half) if total2 is None else total2 + gate(half)
+    hidden = jnp.concatenate([load_rows(state_ref, rows, parts), other], axis=0) + times(
+        jnp.concatenate([total, total2], axis=0), *weights(high_ref, low_ref, 2)
+    )
+    last_ref[...] = hidden[:rows, :]
+    act = gate((times(unit(hidden), *weights(high_ref, low_ref, 3)) + pack_ref[2:3, :]) * 0.5)
+    sums = take(select_ref[...], *halves(times(act, *weights(high_ref, low_ref, 4))))
     size = sums.shape[0] // len(slot_refs)
     first = hot_ref.shape[0] // LANES + rows // LANES
-    base = swap_ref.shape[0] - ints_ref.shape[0]
+    base = swap0_ref.shape[0] - ints_ref.shape[0]
     anchor = (slot_refs[0].shape[0] - size * parts) // 4
     for j, slot in enumerate(slot_refs):
         store_rows(slot, sums[j * size : (j + 1) * size, :], parts)
         slot[size * parts :, :] = jnp.concatenate(
             [
                 ints_ref[first : first + anchor, :],
-                swap_ref[base + first : base + first + anchor, :],
+                swap0_ref[base + first : base + first + anchor, :],
                 jnp.zeros((2 * anchor, LANES), f32),
             ],
             axis=0,
         )
 
 
-def middle_kernel(state_ref, swap_ref, *refs):
+def middle_kernel(state_ref, *refs):
     out_ref = refs[-1]
-    own = state_ref.shape[0]
-    lines = out_ref.shape[0]
-    rim = swap_ref.shape[0] - own - 16
-    total = jnp.concatenate([state_ref[...], swap_ref[rim : rim + own, :]], axis=0)
+    total = state_ref[...]
     for ref in refs[:-1]:
-        total = total + ref[:lines, :]
+        total = total + ref[: out_ref.shape[0], :]
     out_ref[...] = total
 
 
 def edges_kernel(
-    degree, rows, place_ref, ints_ref, cs_ref, cr_ref, co_ref, di_ref, do_ref, *refs
+    degree, count, place_ref, ints_ref, cs_ref, cr_ref, co_ref, di_ref, do_ref, *refs
 ):
     *slot_refs, hot_ref, parent_ref, high_ref, low_ref, turn_ref = refs
-    coarse = hot_ref.shape[1]
+    rows, coarse = parent_ref.shape
     flip = place_ref[1]
     split_into(
         high_ref, low_ref, cs_ref[...], cr_ref[...], co_ref[...], di_ref[...], do_ref[...]
     )
-    count = coarse * degree // LANES // len(slot_refs)
-    lines = jnp.concatenate(
-        [ref[ref.shape[0] - 2 * count : ref.shape[0] - count, :] for ref in slot_refs], axis=0
-    )
-    edge_hot(hot_ref, turn_ref, lines, degree, coarse, flip)
     columns = turned(ints_ref[...])
     first = ints_ref.shape[0] // 2
     for j in range(rows // LANES):
@@ -471,27 +451,52 @@
             columns[:, first + j : first + j + 1].astype(jnp.int32), flip
         ).astype(f32)
         parent_ref[j * LANES : (j + 1) * LANES, :] = equal(column, coarse)
+    here = coarse * degree // LANES // len(slot_refs)
+    lines = jnp.concatenate(
+        [ref[ref.shape[0] - 2 * here : ref.shape[0] - here, :] for ref in slot_refs], axis=0
+    )
+    turn_ref[...] = turned(lines)
+    step = LANES // degree
+    lane = lax.broadcasted_iota(jnp.int32, (coarse, LANES), 1)
+    table = jnp.zeros((coarse, LANES), f32)
+    each = hot_ref.shape[0] // degree
+    for k in range(degree):
+        spread = jnp.bitwise_xor(
+            turn_ref[pl.ds(k, step, stride=degree), :].astype(jnp.int32), flip
+        )
+        column = jnp.concatenate([spread[:, j : j + 1] for j in range(lines.shape[0])], axis=0)
+        hot_ref[k * each : k * each + count, :] = equal(column[:count, :].astype(f32), coarse)
+        high = jnp.right_shift(column, 8).astype(f32)
+        low = jnp.bitwise_and(column, 255).astype(f32)
+        table = jnp.where(lane == k, high, jnp.where(lane == degree + k, low, table))
+    found = mm(parent_ref[...], table.astype(bf16))
+    for k in range(degree):
+        column = found[:, k : k + 1] * 256.0 + found[:, degree + k : degree + k + 1]
+        hot_ref[k * each + count : (k + 1) * each, :] = equal(column, coarse)
 
 
 def coarse_kernel(last_ref, hot_ref, parent_ref, high_ref, low_ref, pack_ref, *refs):
     *blocks, fine_ref, coarse_ref = refs
     rows, width = last_ref.shape
     parts = width // LANES
-    coarse = hot_ref.shape[1]
-    each = coarse // len(blocks)
-    middle = jnp.concatenate([load_rows(b, each, parts) for b in blocks], axis=0)
-    normed = unit(middle)
-    high, low = halves(times(normed, *weights(high_ref, low_ref, 0)) * 0.5)
-    into = (times(normed, *weights(high_ref, low_ref, 1)) + pack_ref[3:4, :]) * 0.5
+    count = coarse_ref.shape[0] // parts
+    need = count + rows
+    middle = jnp.concatenate([load_rows(b, count, parts) for b in blocks], axis=0)
+    sends = halves(times(unit(middle), *weights(high_ref, low_ref, 0)) * 0.5)
+    wanted = jnp.concatenate(
+        [middle[:count, :], take(parent_ref[...], *halves(middle))], axis=0
+    )
+    into = (times(unit(wanted), *weights(high_ref, low_ref, 1)) + pack_ref[3:4, :]) * 0.5
     total = None
-    for k in range(hot_ref.shape[0] // coarse):
-        half = into + take(hot_ref[k * coarse : (k + 1) * coarse, :], high, low)
+    for k in range(hot_ref.shape[0] // need):
+        half = into + take(hot_ref[k * need : (k + 1) * need, :], *sends)
         total = gate(half) if total is None else total + gate(half)
-    done = middle + times(total, *weights(high_ref, low_ref, 2))
-    store_rows(coarse_ref, done[: coarse_ref.shape[0] // parts, :], parts)
-    act = gate((times(unit(done), *weights(high_ref, low_ref, 3)) + pack_ref[4:5, :]) * 0.5)
-    down = halves(times(act, *weights(high_ref, low_ref, 4)))
-    store_rows(fine_ref, last_ref[...] + take(parent_ref[...], *down), parts)
+    done = wanted + times(total, *weights(high_ref, low_ref, 2))
+    store_rows(coarse_ref, done[:count, :], parts)
+    act = gate(
+        (times(unit(done[count:, :]), *weights(high_ref, low_ref, 3)) + pack_ref[4:5, :]) * 0.5
+    )
+    store_rows(fine_ref, last_ref[...] + times(act, *weights(high_ref, low_ref, 4)), parts)
 
 
 VMEM = pl.BlockSpec(memory_space=pltpu.VMEM)
@@ -564,26 +569,27 @@
         lines(fine_senders), lines(up_owner), lines(up_local), lines(coarse_owner),
         lines(coarse_local), fine_bias, row(up_bias), row(coarse_bias), row(down_bias),
     ]
+    here = lambda *xs: [pltpu.with_memory_space_constraint(x, pltpu.HBM) for x in xs]
     state, ints, pack, out_swap, out_diag = call(
         functools.partial(start_kernel, count),
-        [SMEM] + [HBM] * 11,
+        [SMEM] + [HBM] * 10,
         [
             shape(full, LANES), shape(16, LANES), shape(8, width),
-            shape(rim + own + 16, LANES), shape(rim, LANES),
+            shape(rim + 16, LANES), shape(rim, LANES),
         ],
         "start",
-        [small(x) for x in small_args] + [pltpu.SemaphoreType.DMA((13,))],
-    )(place, lines(fine_state), lines(coarse_state), *small_args)
+        [small(x) for x in small_args] + [pltpu.SemaphoreType.DMA((12,))],
+    )(place, *here(lines(fine_state), *small_args))
     swap0 = lax.ppermute(out_swap, "sp", swap)
     diag0 = lax.ppermute(out_diag, "sp", diag)
     hot, got, into, high, low = call(
         functools.partial(near_kernel, edges),
-        [VMEM] * 6,
+        [VMEM] * 2 + [HBM] * 3 + [VMEM],
         [hot_shape, shape(edges, width), shape(rows, width)]
         + [shape(2 * size, width, kind=bf16)] * 2,
         "near0",
-        [turn],
-    )(state, ints, fine_w_send, fine_w_recv, fine_w_out, pack)
+        [turn] + [pltpu.VMEM((size, width), f32)] * 3 + [pltpu.SemaphoreType.DMA((3,))],
+    )(state, ints, *here(fine_w_send, fine_w_recv, fine_w_out), pack)
     state, out_half = call(
         far_kernel,
         [SMEM] + [VMEM] * 8,
@@ -594,11 +600,11 @@
     diag1 = lax.ppermute(out_half, "sp", diag)
     pair1 = lax.ppermute(out_half, "sp", pair)
     got, into, own_high, own_low, hot2, select, high, low = call(
-        functools.partial(near2_kernel, edges),
+        functools.partial(near2_kernel, edges, count),
         [SMEM] + [VMEM] * 10,
         [shape(edges, width), shape(rows, width)]
         + [shape(rows, width, kind=bf16)] * 2
-        + [hot_shape, shape(coarse, 2 * rows, kind=bf16)]
+        + [hot_shape, shape(coarse // 2, 2 * rows, kind=bf16)]
         + [shape(5 * size, width, kind=bf16)] * 2,
         "near1",
         [turn],
@@ -606,38 +612,36 @@
         place, state, ints, swap0, hot, fine_w_send, fine_w_recv, fine_w_out, up_w_in, up_w_out,
         pack,
     )
-    sums, touch_high, touch_low = call(
-        other_kernel,
-        [SMEM] + [VMEM] * 9,
-        [shape(coarse, width)] + [shape(HALO, width, kind=bf16)] * 2,
-        "other",
+    hidden, *slots = call(
+        up_kernel,
+        [SMEM] + [VMEM] * 16,
+        [shape(rows, width)]
+        + [shape(own + 8 * coarse_edges // 256, LANES)] * (peers // 2),
+        "up",
         [pltpu.VMEM((window, width), bf16)] * 2,
-    )(place, swap1, pair1, own_high, own_low, hot2, select, high, low, pack)
-    hidden, *slots = call(
-        own_kernel,
-        [VMEM] * 14,
-        [shape(rows, width)]
-        + [shape(2 * own + 8 * coarse_edges // 256, LANES)] * (peers // 2),
-        "own",
     )(
-        diag1, state, hot, got, into, touch_high, touch_low, sums, select, ints, swap0, high,
-        low, pack,
+        place, swap1, pair1, diag1, state, hot, got, into, own_high, own_low, hot2, select, ints,
+        swap0, high, low, pack,
     )
     arrived = [slots[0]] + [
         lax.ppermute(slots[j], "sp", flips[j]) for j in range(1, peers // 2)
     ]
     (middle,) = call(
         middle_kernel,
-        [VMEM] * (2 + peers // 2),
-        [shape(2 * own, LANES)],
+        [VMEM] * (1 + peers // 2),
+        [shape(own, LANES)],
         "middle",
-    )(lines(coarse_state), swap0, *arrived)
-    blocks = [middle] + [lax.ppermute(middle, "sp", flips[j]) for j in range(1, peers // 2)]
+    )(lines(coarse_state), *arrived)
+    columns = [middle] + [lax.ppermute(middle, "sp", flips[j]) for j in range(1, peers // 2)]
+    blocks = []
+    for block in columns:
+        blocks += [block, lax.ppermute(block, "sp", swap)]
+    degree = coarse_edges // count
     coarse_hot, parent_hot, high, low = call(
-        functools.partial(edges_kernel, coarse_edges // count, rows),
+        functools.partial(edges_kernel, degree, count),
         [SMEM] + [VMEM] * (6 + peers // 2),
         [
-            shape(coarse_edges // count * coarse, coarse, kind=bf16),
+            shape(degree * (count + rows), coarse, kind=bf16),
             shape(rows, coarse, kind=bf16),
         ]
         + [shape(5 * size, width, kind=bf16)] * 2,
@@ -648,7 +652,7 @@
     )
     fine_out, coarse_out = call(
         coarse_kernel,
-        [VMEM] * (6 + peers // 2),
+        [VMEM] * (6 + peers),
         [shape(full, LANES), shape(own, LANES)],
         "coarse",
     )(hidden, coarse_hot, parent_hot, high, low, pack, *blocks)

time: 68.6 us -> 55.5 us (0.81)
  local copies, waits for them, and re-layouts: 11.1 us -> 0.05 us
  waiting for transfers between devices: 17.4 us -> 12 us
  starting transfers between devices: 21.2 us -> 24.6 us
    unnamed x50 -> x22, local copies, waits for them, and re-layouts: 11.1 us -> 0.05 us
    ppermute x3, waiting for transfers between devices: 5.96 us -> 0.59 us  [kernel_shards(): lax.ppermute(middle, 'sp', flips[j])]
    ppermute x0 -> x4, starting transfers between devices: none -> 4.51 us  [kernel_shards(): blocks += [block, lax.ppermute(block, 'sp', swap)]]
    ppermute x3, waiting for transfers between devices: 8.88 us -> 5.2 us  [kernel_shards(): lax.ppermute(slots[j], 'sp', flips[j])]
    ppermute x1, starting transfers between devices: 0.01 us -> 3.57 us  [kernel_shards(): diag1 = lax.ppermute(out_half, 'sp', diag)]
    ppermute x1, starting transfers between devices: 3.6 us -> 0.45 us  [kernel_shards(): pair1 = lax.ppermute(out_half, 'sp', pair)]
    ppermute x1, waiting for transfers between devices: 0.47 us -> 2.63 us  [kernel_shards(): diag1 = lax.ppermute(out_half, 'sp', diag)]
    ppermute x1, waiting for transfers between devices: 0.01 us -> 1.68 us  [kernel_shards(): diag0 = lax.ppermute(out_diag, 'sp', diag)]
  transfers between devices with their start and end apart: 11 -> 15, of which waited for: 8 -> 10; matrix products, arithmetic and copies ran while one was open for 0% -> 0% of each run, Pallas kernels for 11% -> 11%
where the time goes in v4:
time: 55.5 us; the launch traced here: 55.3 us
  starting transfers between devices  24.6 us (44%)
  Pallas kernels  17.8 us (32%)
  waiting for transfers between devices  12 us (22%)
  between operations  0.79 us (1%)
    ppermute x3, waiting for transfers between devices, kernel_shards(): lax.ppermute(slots[j], 'sp', flips[j])  5.2 us
    ppermute x4, starting transfers between devices, kernel_shards(): blocks += [block, lax.ppermute(block, 'sp', swap)]  4.51 us
    ppermute x3, starting transfers between devices, kernel_shards(): lax.ppermute(slots[j], 'sp', flips[j])  4.45 us
    ppermute x3, starting transfers between devices, kernel_shards(): lax.ppermute(middle, 'sp', flips[j])  4.45 us
    pallas_call x1, Pallas kernels, kernel_shards(): call(up_kernel, [SMEM] + [VMEM] * 16, [shape(rows, width)] + [shape(own +...  4.17 us
    pallas_call x1, Pallas kernels, kernel_shards(): call(coarse_kernel, [VMEM] * (6 + peers), [shape(full, LANES), shape(own,...  3.66 us
    ppermute x1, starting transfers between devices, kernel_shards(): diag1 = lax.ppermute(out_half, 'sp', diag)  3.57 us
    ppermute x1, starting transfers between devices, kernel_shards(): diag0 = lax.ppermute(out_diag, 'sp', diag)  3.57 us
  transfers between devices with their start and end apart: 15, of which 10 were waited for; matrix products, arithmetic and copies ran while one was open for 0% of the time, Pallas kernels for 11%

profile of v4, /device:TPU:0, one launch (start us, length us, event | category | flops | bytes accessed | tf_op | source)
XLA Modules:
  0.0 55.3 jit_solution(10905222183710920532)
XLA Ops:
  0.6 0.1 pad_add_fusion.place_ref
  0.7 1.9 %start.1 = (f32[512,128]{1,0:T(8,128)S(1)}, f32[16,128]{1,0:T(8,128)S(1)}, f32[8,256]{1,0:T(8,128)S(1)}, f32[272,128]{1,0:T(8,128)S(1)}, f32[256,128]{1,0:T(8,128)S(1)}) custom-call(s32[2]{0:T(128)S(1)} %pad_add_fusion.place_ref, f32[512,128]{1,0:T(8,128)} %bitcast.15, s32[8,128]{1,0:T(8,128)} %bitcast.16, s32[2,128]{1,0:T(2,128)} %bitcast.17, ...), custom_call_target="tpu_custom_call" | custom-call | tf_op jit(solution)/shard_map/start/pallas_call | solution.py:573
  2.6 3.0 %collective-permute-start = (f32[272,128]{1,0:T(8,128)S(1)}, f32[272,128]{1,0:T(8,128)S(1)}, u32[]{:S(2)}, u32[]{:S(2)}) collective-permute-start(f32[272,128]{1,0:T(8,128)S(1)} %get-tuple-element.33), channel_id=1, source_target_pairs={{0,2},{2,0},{4,6},{6,4},{8,10},{10,8},{12,14},{14,12},{1,3},{3,1},... | collective-permute-start | bytes 417800 | tf_op jit(solution)/shard_map/ppermute | solution.py:583
  5.6 3.6 %collective-permute-start.1 = (f32[256,128]{1,0:T(8,128)S(1)}, f32[256,128]{1,0:T(8,128)S(1)}, u32[]{:S(2)}, u32[]{:S(2)}) collective-permute-start(f32[256,128]{1,0:T(8,128)S(1)} %get-tuple-element.34), channel_id=1, source_target_pairs={{0,14},{2,4},{4,2},{6,8},{8,6},{10,12},{12,10},{14,0},{1,15},{3,5}... | collective-permute-start | bytes 393224 | tf_op jit(solution)/shard_map/ppermute | solution.py:584
  9.2 2.4 %near0.1 = (bf16[1024,512]{1,0:T(8,128)(2,1)S(1)}, f32[1024,256]{1,0:T(8,128)S(1)}, f32[256,256]{1,0:T(8,128)S(1)}, bf16[512,256]{1,0:T(8,128)(2,1)S(1)}, bf16[512,256]{1,0:T(8,128)(2,1)S(1)}) custom-call(f32[512,128]{1,0:T(8,128)S(1)} %get-tuple-element.35.state_ref, f32[16,128]{1,0:T(8,128)S(1)} %get-tuple-element.36.ints_ref, f32[2,256,256]{2,1,0:T(8,128)} %ws_ref.1, ...), custom_call_target="tpu_custom_call" | custom-call | tf_op jit(solution)/shard_map/near0/pallas_call | solution.py:585
  11.6 1.7 %collective-permute-done.1.diag_ref = f32[256,128]{1,0:T(8,128)S(1)} collective-permute-done((f32[256,128]{1,0:T(8,128)S(1)}, f32[256,128]{1,0:T(8,128)S(1)}, u32[]{:S(2)}, u32[]{:S(2)}) %collective-permute-start.1) | collective-permute-done | bytes 131104 | tf_op jit(solution)/shard_map/ppermute | solution.py:584
  13.3 1.9 %far0.1 = (f32[512,128]{1,0:T(8,128)S(1)}, f32[256,128]{1,0:T(8,128)S(1)}) custom-call(s32[2]{0:T(128)S(1)} %pad_add_fusion.place_ref, f32[272,128]{1,0:T(8,128)S(1)} %collective-permute-done.swap_ref.swap0_ref, f32[256,128]{1,0:T(8,128)S(1)} %collective-permute-done.1.diag_ref, f32[512,128]{1,0:T(8,128)S(1)} %get-tuple-element.35.state_ref, ...), custom_call_target="tpu_custom_call" | custom-call | tf_op jit(solution)/shard_map/far0/pallas_call | solution.py:593
  15.2 0.6 %collective-permute-start.2 = (f32[512,128]{1,0:T(8,128)S(1)}, f32[512,128]{1,0:T(8,128)S(1)}, u32[]{:S(2)}, u32[]{:S(2)}) collective-permute-start(f32[512,128]{1,0:T(8,128)S(1)} %get-tuple-element.43.state_ref), channel_id=1, source_target_pairs={{0,2},{2,0},{4,6},{6,4},{8,10},{10,8},{12,14},{14,12},{1,3},{3,1},... | collective-permute-start | bytes 786440 | tf_op jit(solution)/shard_map/ppermute | solution.py:599
  15.8 3.6 %collective-permute-start.4 = (f32[256,128]{1,0:T(8,128)S(1)}, f32[256,128]{1,0:T(8,128)S(1)}, u32[]{:S(2)}, u32[]{:S(2)}) collective-permute-start(f32[256,128]{1,0:T(8,128)S(1)} %get-tuple-element.44), channel_id=1, source_target_pairs={{0,14},{2,4},{4,2},{6,8},{8,6},{10,12},{12,10},{14,0},{1,15},{3,5}... | collective-permute-start | bytes 393224 | tf_op jit(solution)/shard_map/ppermute | solution.py:600
  19.4 0.4 collective-permute-start.3
  19.9 1.7 %near1.1 = (f32[1024,256]{1,0:T(8,128)S(1)}, f32[256,256]{1,0:T(8,128)S(1)}, bf16[256,256]{1,0:T(8,128)(2,1)S(1)}, bf16[256,256]{1,0:T(8,128)(2,1)S(1)}, bf16[10...) custom-call(s32[2]{0:T(128)S(1)} %pad_add_fusion.place_ref, ...), custom_call_target="tpu_custom_call" | custom-call | tf_op jit(solution)/shard_map/near1/pallas_call | solution.py:602
  21.5 2.6 %collective-permute-done.4.diag_ref = f32[256,128]{1,0:T(8,128)S(1)} collective-permute-done((f32[256,128]{1,0:T(8,128)S(1)}, f32[256,128]{1,0:T(8,128)S(1)}, u32[]{:S(2)}, u32[]{:S(2)}) %collective-permute-start.4) | collective-permute-done | bytes 131104 | tf_op jit(solution)/shard_map/ppermute | solution.py:600
  24.2 0.2 collective-permute-done.3.pair_ref
  24.4 0.3 collective-permute-done.2.swap_ref
  24.7 4.2 %up.1 = (f32[256,256]{1,0:T(8,128)S(1)}, f32[136,128]{1,0:T(8,128)S(1)}, f32[136,128]{1,0:T(8,128)S(1)}, f32[136,128]{1,0:T(8,128)S(1)}, f32[136,128]{1,0:T(8,128)S(1)}) custom-call(s32[2]{0:T(128)S(1)} %pad_add_fusion.place_ref, f32[512,128]{1,0:T(8,128)S(1)} %collective-permute-done.2.swap_ref, f32[256,128]{1,0:T(8,128)S(1)} %collective-permute-done.3.pair_ref, ...), custom_call_target="tpu_custom_call" | custom-call | tf_op jit(solution)/shard_map/up/pallas_call | solution.py:615
  28.9 1.0 %collective-permute-start.5 = (f32[136,128]{1,0:T(8,128)S(1)}, f32[136,128]{1,0:T(8,128)S(1)}, u32[]{:S(2)}, u32[]{:S(2)}) collective-permute-start(f32[136,128]{1,0:T(8,128)S(1)} %get-tuple-element.55), channel_id=1, source_target_pairs={{0,4},{2,6},{4,0},{6,2},{8,12},{10,14},{12,8},{14,10},{1,5},{3,7},... | collective-permute-start | bytes 208904 | tf_op jit(solution)/shard_map/ppermute | solution.py:627
  29.9 2.5 %collective-permute-start.6 = (f32[136,128]{1,0:T(8,128)S(1)}, f32[136,128]{1,0:T(8,128)S(1)}, u32[]{:S(2)}, u32[]{:S(2)}) collective-permute-start(f32[136,128]{1,0:T(8,128)S(1)} %get-tuple-element.56), channel_id=1, source_target_pairs={{0,8},{2,10},{4,12},{6,14},{8,0},{10,2},{12,4},{14,6},{1,9},{3,11}... | collective-permute-start | bytes 208904 | tf_op jit(solution)/shard_map/ppermute | solution.py:627
  32.5 0.9 %collective-permute-start.7 = (f32[136,128]{1,0:T(8,128)S(1)}, f32[136,128]{1,0:T(8,128)S(1)}, u32[]{:S(2)}, u32[]{:S(2)}) collective-permute-start(f32[136,128]{1,0:T(8,128)S(1)} %get-tuple-element.57), channel_id=1, source_target_pairs={{0,12},{2,14},{4,8},{6,10},{8,4},{10,6},{12,0},{14,2},{1,13},{3,15... | collective-permute-start | bytes 208904 | tf_op jit(solution)/shard_map/ppermute | solution.py:627
  33.4 2.5 %collective-permute-done.6.refs_2_ = f32[136,128]{1,0:T(8,128)S(1)} collective-permute-done((f32[136,128]{1,0:T(8,128)S(1)}, f32[136,128]{1,0:T(8,128)S(1)}, u32[]{:S(2)}, u32[]{:S(2)}) %collective-permute-start.6) | collective-permute-done | bytes 69664 | tf_op jit(solution)/shard_map/ppermute | solution.py:627
  35.9 2.7 %collective-permute-done.7.refs_3_ = f32[136,128]{1,0:T(8,128)S(1)} collective-permute-done((f32[136,128]{1,0:T(8,128)S(1)}, f32[136,128]{1,0:T(8,128)S(1)}, u32[]{:S(2)}, u32[]{:S(2)}) %collective-permute-start.7) | collective-permute-done | bytes 69664 | tf_op jit(solution)/shard_map/ppermute | solution.py:627
  38.6 1.0 %collective-permute-start.13 = (f32[128,128]{1,0:T(8,128)S(1)}, f32[128,128]{1,0:T(8,128)S(1)}, u32[]{:S(2)}, u32[]{:S(2)}) collective-permute-start(f32[128,128]{1,0:T(8,128)S(1)} %middle.1.refs_0_), channel_id=1, source_target_pairs={{0,12},{2,14},{4,8},{6,10},{8,4},{10,6},{12,0},{14,2},{1,13},{3,15... | collective-permute-start | bytes 196616 | tf_op jit(solution)/shard_map/ppermute | solution.py:635
  39.6 3.5 %collective-permute-start.9 = (f32[128,128]{1,0:T(8,128)S(1)}, f32[128,128]{1,0:T(8,128)S(1)}, u32[]{:S(2)}, u32[]{:S(2)}) collective-permute-start(f32[128,128]{1,0:T(8,128)S(1)} %middle.1.refs_0_), channel_id=1, source_target_pairs={{0,4},{2,6},{4,0},{6,2},{8,12},{10,14},{12,8},{14,10},{1,5},{3,7},... | collective-permute-start | bytes 196616 | tf_op jit(solution)/shard_map/ppermute | solution.py:635
  43.0 1.3 %collective-permute-start.8 = (f32[128,128]{1,0:T(8,128)S(1)}, f32[128,128]{1,0:T(8,128)S(1)}, u32[]{:S(2)}, u32[]{:S(2)}) collective-permute-start(f32[128,128]{1,0:T(8,128)S(1)} %middle.1.refs_0_), channel_id=1, source_target_pairs={{0,2},{2,0},{4,6},{6,4},{8,10},{10,8},{12,14},{14,12},{1,3},{3,1},... | collective-permute-start | bytes 196616 | tf_op jit(solution)/shard_map/ppermute | solution.py:638
  44.3 0.5 collective-permute-done.13.refs_6_
  44.8 1.2 %collective-permute-start.14 = (f32[128,128]{1,0:T(8,128)S(1)}, f32[128,128]{1,0:T(8,128)S(1)}, u32[]{:S(2)}, u32[]{:S(2)}) collective-permute-start(f32[128,128]{1,0:T(8,128)S(1)} %collective-permute-done.13.refs_6_), channel_id=1, source_target_pairs={{0,2},{2,0},{4,6},{6,4},{8,10},{10,8},{12,14},{14,12},{1,3},{3,1},... | collective-permute-start | bytes 196616 | tf_op jit(solution)/shard_map/ppermute | solution.py:638
  46.0 0.1 collective-permute-done.11.refs_4_
  46.1 1.3 %collective-permute-start.12 = (f32[128,128]{1,0:T(8,128)S(1)}, f32[128,128]{1,0:T(8,128)S(1)}, u32[]{:S(2)}, u32[]{:S(2)}) collective-permute-start(f32[128,128]{1,0:T(8,128)S(1)} %collective-permute-done.11.refs_4_), channel_id=1, source_target_pairs={{0,2},{2,0},{4,6},{6,4},{8,10},{10,8},{12,14},{14,12},{1,3},{3,1},... | collective-permute-start | bytes 196616 | tf_op jit(solution)/shard_map/ppermute | solution.py:638
  47.4 0.7 %collective-permute-start.10 = (f32[128,128]{1,0:T(8,128)S(1)}, f32[128,128]{1,0:T(8,128)S(1)}, u32[]{:S(2)}, u32[]{:S(2)}) collective-permute-start(f32[128,128]{1,0:T(8,128)S(1)} %collective-permute-done.9.refs_2_), channel_id=1, source_target_pairs={{0,2},{2,0},{4,6},{6,4},{8,10},{10,8},{12,14},{14,12},{1,3},{3,1},... | collective-permute-start | bytes 196616 | tf_op jit(solution)/shard_map/ppermute | solution.py:638
  48.2 2.1 %edges.1 = (bf16[1280,512]{1,0:T(8,128)(2,1)S(1)}, bf16[256,512]{1,0:T(8,128)(2,1)S(1)}, bf16[1280,256]{1,0:T(8,128)(2,1)S(1)}, bf16[1280,256]{1,0:T(8,128)(2,1)S(1)}) custom-call(s32[2]{0:T(128)S(1)} %pad_add_fusion.place_ref, f32[16,128]{1,0:T(8,128)S(1)} %get-tuple-element.36.ints_ref, f32[256,256]{1,0:T(8,128)S(1)} %copy-done.3, ...), custom_call_target="tpu_custom_call" | custom-call | tf_op jit(solution)/shard_map/edges/pallas_call | solution.py:640
  50.3 0.1 collective-permute-done.12.refs_5_
  50.4 1.3 %collective-permute-done.10.refs_3_ = f32[128,128]{1,0:T(8,128)S(1)} collective-permute-done((f32[128,128]{1,0:T(8,128)S(1)}, f32[128,128]{1,0:T(8,128)S(1)}, u32[]{:S(2)}, u32[]{:S(2)}) %collective-permute-start.10) | collective-permute-done | bytes 65568 | tf_op jit(solution)/shard_map/ppermute | solution.py:638
  51.7 3.7 %coarse.1 = (f32[512,128]{1,0:T(8,128)}, f32[128,128]{1,0:T(8,128)}) custom-call(f32[256,256]{1,0:T(8,128)S(1)} %get-tuple-element.53.last_ref, bf16[1280,512]{1,0:T(8,128)(2,1)S(1)} %get-tuple-element.58.hot_ref, bf16[256,512]{1,0:T(8,128)(2,1)S(1)} %get-tuple-element.59.parent_ref, bf16[1280,256]{1,0:T(8,128)(2,1)S(1)} %get-tuple-element.60.high_ref, ...), custom_call_target="tpu_custom_call" | custom-call | tf_op jit(solution)/shard_map/coarse/pallas_call | solution.py:653
  (29 shorter events, 0.1 us)
Async XLA Ops:
  2.6 10.7 %collective-permute-start = (f32[272,128]{1,0:T(8,128)S(1)}, f32[272,128]{1,0:T(8,128)S(1)}, u32[]{:S(2)}, u32[]{:S(2)}) collective-permute-start(f32[272,128]{1,0:T(8,128)S(1)} %get-tuple-element.33), channel_id=1, source_target_pairs={{0,2},{2,0},{4,6},{6,4},{8,10},{10,8},{12,14},{14,12},{1,3},{3,1},... | collective-permute-start | bytes 417800 | tf_op jit(solution)/shard_map/ppermute | solution.py:583
  5.6 7.7 %collective-permute-start.1 = (f32[256,128]{1,0:T(8,128)S(1)}, f32[256,128]{1,0:T(8,128)S(1)}, u32[]{:S(2)}, u32[]{:S(2)}) collective-permute-start(f32[256,128]{1,0:T(8,128)S(1)} %get-tuple-element.34), channel_id=1, source_target_pairs={{0,14},{2,4},{4,2},{6,8},{8,6},{10,12},{12,10},{14,0},{1,15},{3,5}... | collective-permute-start | bytes 393224 | tf_op jit(solution)/shard_map/ppermute | solution.py:584
  13.3 6.6 %copy-start = (f32[2,256,256]{2,1,0:T(8,128)S(1)}, f32[2,256,256]{2,1,0:T(8,128)}, u32[]{:S(2)}) copy-start(f32[2,256,256]{2,1,0:T(8,128)} %ws_ref.1) | copy-start | bytes 1572868
  13.3 6.6 %copy-start.1 = (f32[2,256,256]{2,1,0:T(8,128)S(1)}, f32[2,256,256]{2,1,0:T(8,128)}, u32[]{:S(2)}) copy-start(f32[2,256,256]{2,1,0:T(8,128)} %wr_ref.1) | copy-start | bytes 1572868
  13.3 6.6 %copy-start.2 = (f32[2,256,256]{2,1,0:T(8,128)S(1)}, f32[2,256,256]{2,1,0:T(8,128)}, u32[]{:S(2)}) copy-start(f32[2,256,256]{2,1,0:T(8,128)} %wo_ref.1) | copy-start | bytes 1572868
  13.3 6.6 %copy-start.8 = (f32[256,256]{1,0:T(8,128)S(1)}, f32[256,256]{1,0:T(8,128)}, u32[]{:S(2)}) copy-start(f32[256,256]{1,0:T(8,128)} %wi_ref.1) | copy-start | bytes 786436
  13.3 6.5 %copy-start.9 = (f32[256,256]{1,0:T(8,128)S(1)}, f32[256,256]{1,0:T(8,128)}, u32[]{:S(2)}) copy-start(f32[256,256]{1,0:T(8,128)} %wu_ref.1) | copy-start | bytes 786436
  15.2 9.5 %collective-permute-start.2 = (f32[512,128]{1,0:T(8,128)S(1)}, f32[512,128]{1,0:T(8,128)S(1)}, u32[]{:S(2)}, u32[]{:S(2)}) collective-permute-start(f32[512,128]{1,0:T(8,128)S(1)} %get-tuple-element.43.state_ref), channel_id=1, source_target_pairs={{0,2},{2,0},{4,6},{6,4},{8,10},{10,8},{12,14},{14,12},{1,3},{3,1},... | collective-permute-start | bytes 786440 | tf_op jit(solution)/shard_map/ppermute | solution.py:599
  15.8 8.4 %collective-permute-start.4 = (f32[256,128]{1,0:T(8,128)S(1)}, f32[256,128]{1,0:T(8,128)S(1)}, u32[]{:S(2)}, u32[]{:S(2)}) collective-permute-start(f32[256,128]{1,0:T(8,128)S(1)} %get-tuple-element.44), channel_id=1, source_target_pairs={{0,14},{2,4},{4,2},{6,8},{8,6},{10,12},{12,10},{14,0},{1,15},{3,5}... | collective-permute-start | bytes 393224 | tf_op jit(solution)/shard_map/ppermute | solution.py:600
  19.4 5.0 %collective-permute-start.3 = (f32[256,128]{1,0:T(8,128)S(1)}, f32[256,128]{1,0:T(8,128)S(1)}, u32[]{:S(2)}, u32[]{:S(2)}) collective-permute-start(f32[256,128]{1,0:T(8,128)S(1)} %get-tuple-element.44), channel_id=1, source_target_pairs={{0,12},{2,6},{4,0},{6,10},{8,4},{10,14},{12,8},{14,2},{1,13},{3,7}... | collective-permute-start | bytes 393224 | tf_op jit(solution)/shard_map/ppermute | solution.py:601
  24.7 13.9 %copy-start.10 = (f32[64,1,256]{2,1,0:T(1,128)S(1)}, f32[64,1,256]{2,1,0:T(1,128)}, u32[]{:S(2)}) copy-start(f32[64,1,256]{2,1,0:T(1,128)} %param.22) | copy-start | bytes 196612
  24.7 23.5 %copy-start.3 = (f32[256,256]{1,0:T(8,128)S(1)}, f32[256,256]{1,0:T(8,128)}, u32[]{:S(2)}) copy-start(f32[256,256]{1,0:T(8,128)} %cs_ref.1) | copy-start | bytes 786436
  24.7 23.5 %copy-start.4 = (f32[256,256]{1,0:T(8,128)S(1)}, f32[256,256]{1,0:T(8,128)}, u32[]{:S(2)}) copy-start(f32[256,256]{1,0:T(8,128)} %cr_ref.1) | copy-start | bytes 786436
  24.7 23.5 %copy-start.5 = (f32[256,256]{1,0:T(8,128)S(1)}, f32[256,256]{1,0:T(8,128)}, u32[]{:S(2)}) copy-start(f32[256,256]{1,0:T(8,128)} %co_ref.1) | copy-start | bytes 786436
  24.7 23.5 %copy-start.6 = (f32[256,256]{1,0:T(8,128)S(1)}, f32[256,256]{1,0:T(8,128)}, u32[]{:S(2)}) copy-start(f32[256,256]{1,0:T(8,128)} %di_ref.1) | copy-start | bytes 786436
  24.7 23.5 %copy-start.7 = (f32[256,256]{1,0:T(8,128)S(1)}, f32[256,256]{1,0:T(8,128)}, u32[]{:S(2)}) copy-start(f32[256,256]{1,0:T(8,128)} %do_ref.1) | copy-start | bytes 786436
  28.9 4.5 %collective-permute-start.5 = (f32[136,128]{1,0:T(8,128)S(1)}, f32[136,128]{1,0:T(8,128)S(1)}, u32[]{:S(2)}, u32[]{:S(2)}) collective-permute-start(f32[136,128]{1,0:T(8,128)S(1)} %get-tuple-element.55), channel_id=1, source_target_pairs={{0,4},{2,6},{4,0},{6,2},{8,12},{10,14},{12,8},{14,10},{1,5},{3,7},... | collective-permute-start | bytes 208904 | tf_op jit(solution)/shard_map/ppermute | solution.py:627
  29.9 6.0 %collective-permute-start.6 = (f32[136,128]{1,0:T(8,128)S(1)}, f32[136,128]{1,0:T(8,128)S(1)}, u32[]{:S(2)}, u32[]{:S(2)}) collective-permute-start(f32[136,128]{1,0:T(8,128)S(1)} %get-tuple-element.56), channel_id=1, source_target_pairs={{0,8},{2,10},{4,12},{6,14},{8,0},{10,2},{12,4},{14,6},{1,9},{3,11}... | collective-permute-start | bytes 208904 | tf_op jit(solution)/shard_map/ppermute | solution.py:627
  32.5 6.1 %collective-permute-start.7 = (f32[136,128]{1,0:T(8,128)S(1)}, f32[136,128]{1,0:T(8,128)S(1)}, u32[]{:S(2)}, u32[]{:S(2)}) collective-permute-start(f32[136,128]{1,0:T(8,128)S(1)} %get-tuple-element.57), channel_id=1, source_target_pairs={{0,12},{2,14},{4,8},{6,10},{8,4},{10,6},{12,0},{14,2},{1,13},{3,15... | collective-permute-start | bytes 208904 | tf_op jit(solution)/shard_map/ppermute | solution.py:627
  38.6 6.2 %collective-permute-start.13 = (f32[128,128]{1,0:T(8,128)S(1)}, f32[128,128]{1,0:T(8,128)S(1)}, u32[]{:S(2)}, u32[]{:S(2)}) collective-permute-start(f32[128,128]{1,0:T(8,128)S(1)} %middle.1.refs_0_), channel_id=1, source_target_pairs={{0,12},{2,14},{4,8},{6,10},{8,4},{10,6},{12,0},{14,2},{1,13},{3,15... | collective-permute-start | bytes 196616 | tf_op jit(solution)/shard_map/ppermute | solution.py:635
  39.6 6.6 %collective-permute-start.11 = (f32[128,128]{1,0:T(8,128)S(1)}, f32[128,128]{1,0:T(8,128)S(1)}, u32[]{:S(2)}, u32[]{:S(2)}) collective-permute-start(f32[128,128]{1,0:T(8,128)S(1)} %middle.1.refs_0_), channel_id=1, source_target_pairs={{0,8},{2,10},{4,12},{6,14},{8,0},{10,2},{12,4},{14,6},{1,9},{3,11}... | collective-permute-start | bytes 196616 | tf_op jit(solution)/shard_map/ppermute | solution.py:635
  39.6 7.8 %collective-permute-start.9 = (f32[128,128]{1,0:T(8,128)S(1)}, f32[128,128]{1,0:T(8,128)S(1)}, u32[]{:S(2)}, u32[]{:S(2)}) collective-permute-start(f32[128,128]{1,0:T(8,128)S(1)} %middle.1.refs_0_), channel_id=1, source_target_pairs={{0,4},{2,6},{4,0},{6,2},{8,12},{10,14},{12,8},{14,10},{1,5},{3,7},... | collective-permute-start | bytes 196616 | tf_op jit(solution)/shard_map/ppermute | solution.py:635
  43.0 7.3 %collective-permute-start.8 = (f32[128,128]{1,0:T(8,128)S(1)}, f32[128,128]{1,0:T(8,128)S(1)}, u32[]{:S(2)}, u32[]{:S(2)}) collective-permute-start(f32[128,128]{1,0:T(8,128)S(1)} %middle.1.refs_0_), channel_id=1, source_target_pairs={{0,2},{2,0},{4,6},{6,4},{8,10},{10,8},{12,14},{14,12},{1,3},{3,1},... | collective-permute-start | bytes 196616 | tf_op jit(solution)/shard_map/ppermute | solution.py:638
  44.8 5.5 %collective-permute-start.14 = (f32[128,128]{1,0:T(8,128)S(1)}, f32[128,128]{1,0:T(8,128)S(1)}, u32[]{:S(2)}, u32[]{:S(2)}) collective-permute-start(f32[128,128]{1,0:T(8,128)S(1)} %collective-permute-done.13.refs_6_), channel_id=1, source_target_pairs={{0,2},{2,0},{4,6},{6,4},{8,10},{10,8},{12,14},{14,12},{1,3},{3,1},... | collective-permute-start | bytes 196616 | tf_op jit(solution)/shard_map/ppermute | solution.py:638
  46.1 4.3 %collective-permute-start.12 = (f32[128,128]{1,0:T(8,128)S(1)}, f32[128,128]{1,0:T(8,128)S(1)}, u32[]{:S(2)}, u32[]{:S(2)}) collective-permute-start(f32[128,128]{1,0:T(8,128)S(1)} %collective-permute-done.11.refs_4_), channel_id=1, source_target_pairs={{0,2},{2,0},{4,6},{6,4},{8,10},{10,8},{12,14},{14,12},{1,3},{3,1},... | collective-permute-start | bytes 196616 | tf_op jit(solution)/shard_map/ppermute | solution.py:638
  47.4 4.3 %collective-permute-start.10 = (f32[128,128]{1,0:T(8,128)S(1)}, f32[128,128]{1,0:T(8,128)S(1)}, u32[]{:S(2)}, u32[]{:S(2)}) collective-permute-start(f32[128,128]{1,0:T(8,128)S(1)} %collective-permute-done.9.refs_2_), channel_id=1, source_target_pairs={{0,2},{2,0},{4,6},{6,4},{8,10},{10,8},{12,14},{14,12},{1,3},{3,1},... | collective-permute-start | bytes 196616 | tf_op jit(solution)/shard_map/ppermute | solution.py:638

commit v5 on v4

--- a/solution.py
+++ b/solution.py
@@ -227,15 +227,13 @@
 
 
 def start_kernel(
-    count, place_ref, state_hbm, sender_hbm, owner_hbm, local_hbm, cowner_hbm,
+    count, halo, place_ref, state_hbm, sender_hbm, owner_hbm, local_hbm, cowner_hbm,
     clocal_hbm, fb_hbm, ub_hbm, cb_hbm, db_hbm,
-    state_ref, ints_ref, pack_ref, swap_ref, diag_ref,
+    state_ref, ints_ref, pack_ref,
     sender_ref, owner_ref, local_ref, cowner_ref, clocal_ref, fb_ref, ub_ref, cb_ref, db_ref,
     sems,
 ):
     odd = place_ref[0]
-    rim = diag_ref.shape[0]
-    far = state_hbm.shape[0] - rim
     pairs = [
         (sender_hbm, sender_ref),
         (owner_hbm, owner_ref),
@@ -246,18 +244,14 @@
         (ub_hbm, ub_ref),
         (cb_hbm, cb_ref),
         (db_hbm, db_ref),
-        (state_hbm.at[pl.ds(pl.multiple_of((1 - odd) * far, LANES), rim), :], swap_ref.at[0:rim, :]),
-        (state_hbm.at[pl.ds(pl.multiple_of(odd * far, LANES), rim), :], diag_ref),
         (state_hbm, state_ref),
     ]
     copies = [pltpu.make_async_copy(a, b, sems.at[j]) for j, (a, b) in enumerate(pairs)]
     for copy in copies:
         copy.start()
-    for copy in copies[:9]:
+    for copy in copies[:-1]:
         copy.wait()
-    parts = fb_ref.shape[1] // LANES
-    rows = state_hbm.shape[0] // parts
-    halo = rim // parts
+    rows = state_hbm.shape[0] * LANES // fb_ref.shape[1]
     sender = sender_ref[...]
     before = rows + (1 - odd) * halo
     after = rows + odd * halo
@@ -272,16 +266,13 @@
         (cowner_ref[...] * count + clocal_ref[...]).astype(f32),
     ]
     rest = ints_ref.shape[0] - sum(x.shape[0] for x in lines)
-    ints = jnp.concatenate(lines + [jnp.zeros((rest, LANES), f32)], axis=0)
-    ints_ref[...] = ints
-    swap_ref[rim:, :] = ints
+    ints_ref[...] = jnp.concatenate(lines + [jnp.zeros((rest, LANES), f32)], axis=0)
     pack_ref[...] = jnp.concatenate(
         [fb_ref[...], ub_ref[...], cb_ref[...], db_ref[...]]
         + [jnp.zeros((3, fb_ref.shape[1]), f32)],
         axis=0,
     )
-    for copy in copies[9:]:
-        copy.wait()
+    copies[-1].wait()
 
 
 def near_kernel(
@@ -334,7 +325,7 @@
 
 
 def near2_kernel(
-    edges, count, place_ref, state_ref, ints_ref, swap_ref, hot_ref, ws_ref, wr_ref, wo_ref, wi_ref,
+    edges, count, place_ref, state_ref, ints_ref, ints0_ref, hot_ref, ws_ref, wr_ref, wo_ref, wi_ref,
     wu_ref, pack_ref,
     got_ref, into_ref, own_high_ref, own_low_ref, hot2_ref, select_ref, high_ref, low_ref,
     turn_ref,
@@ -342,7 +333,6 @@
     rows, width = into_ref.shape
     parts = width // LANES
     senders = edges // LANES
-    first = swap_ref.shape[0] - ints_ref.shape[0]
     split_into(
         high_ref, low_ref, ws_ref[1], wr_ref[1], wo_ref[1], wi_ref[...], wu_ref[...]
     )
@@ -352,12 +342,12 @@
     own_high_ref[...] = high
     own_low_ref[...] = low
     got_ref[...] = take(hot_ref[:, :rows], high, low)
-    edge_hot(hot2_ref, turn_ref, swap_ref[first : first + senders, :], edges // rows, rows)
+    edge_hot(hot2_ref, turn_ref, ints0_ref[:senders, :], edges // rows, rows)
     flip = place_ref[1]
     line = senders
-    for half, ref, base in ((0, ints_ref, 0), (1, swap_ref, first)):
+    for half, ref in ((0, ints_ref), (1, ints0_ref)):
         for j in range(rows // LANES):
-            parent = ref[base + line + j : base + line + j + 1, :].astype(jnp.int32)
+            parent = ref[line + j : line + j + 1, :].astype(jnp.int32)
             parent = jnp.bitwise_xor(parent, flip)
             ids = lax.broadcasted_iota(jnp.int32, (select_ref.shape[0], LANES), 0)
             ids = ids + jnp.bitwise_and(ids, -count)
@@ -367,43 +357,56 @@
             )
 
 
+def halo_kernel(
+    place_ref, pair_ref, diag_ref, own_high_ref, own_low_ref, hot2_ref, high_ref, low_ref,
+    got2_ref, diag_high_ref, diag_low_ref,
+):
+    rim, width = diag_high_ref.shape
+    rows = own_high_ref.shape[0]
+    parts = width // LANES
+    mine = pl.multiple_of((1 - place_ref[0]) * (rows - rim), LANES)
+    normed = unit(
+        jnp.concatenate(
+            [load_rows(pair_ref, rim, parts), load_rows(diag_ref, rim, parts)], axis=0
+        )
+    )
+    high, low = halves(times(normed, *weights(high_ref, low_ref, 0)) * 0.5)
+    diag_high_ref[...] = high[rim:, :]
+    diag_low_ref[...] = low[rim:, :]
+    got2_ref[...] = take(
+        hot2_ref[:, rows:],
+        jnp.concatenate([own_high_ref[pl.ds(mine, rim), :], high[:rim, :]], axis=0),
+        jnp.concatenate([own_low_ref[pl.ds(mine, rim), :], low[:rim, :]], axis=0),
+    )
+
+
 def up_kernel(
-    place_ref, swap_ref, pair_ref, diag_ref, state_ref, hot_ref, got_ref, into_ref, own_high_ref,
-    own_low_ref, hot2_ref, select_ref, ints_ref, swap0_ref, high_ref, low_ref, pack_ref,
+    place_ref, swap_ref, diag_high_ref, diag_low_ref, state_ref, hot_ref, got_ref, into_ref,
+    hot2_ref, got2_ref, select_ref, ints_ref, ints0_ref, high_ref, low_ref, pack_ref,
     last_ref, *refs,
 ):
     *slot_refs, th_ref, tl_ref = refs
     rows, width = into_ref.shape
     parts = width // LANES
-    rim = diag_ref.shape[0] // parts
+    rim = diag_high_ref.shape[0]
     degree = hot_ref.shape[0] // rows
-    odd = place_ref[0]
-    mine = pl.multiple_of((1 - odd) * (rows - rim), LANES)
-    theirs = pl.multiple_of(odd * (rows - rim), LANES)
+    theirs = pl.multiple_of(place_ref[0] * (rows - rim), LANES)
     other = load_rows(swap_ref, rows, parts)
-    normed = unit(
-        jnp.concatenate(
-            [other, load_rows(pair_ref, rim, parts), load_rows(diag_ref, rim, parts)], axis=0
-        )
-    )
-    sends = halves(times(normed, *weights(high_ref, low_ref, 0)) * 0.5)
-    near = []
-    for src, t_ref, own_ref in (
-        (sends[0], th_ref, own_high_ref), (sends[1], tl_ref, own_low_ref),
-    ):
-        t_ref[:rows, :] = src[:rows, :]
-        t_ref[rows : rows + rim, :] = own_ref[pl.ds(mine, rim), :]
-        t_ref[rows + rim :, :] = src[rows : rows + rim, :]
-        near.append(
-            jnp.concatenate([t_ref[pl.ds(theirs, rim), :], src[rows + rim :, :]], axis=0)
-        )
-    into = (times(normed[:rows, :], *weights(high_ref, low_ref, 1)) + pack_ref[1:2, :]) * 0.5
+    normed = unit(other)
+    high, low = halves(times(normed, *weights(high_ref, low_ref, 0)) * 0.5)
+    th_ref[...] = high
+    tl_ref[...] = low
+    near = (
+        jnp.concatenate([th_ref[pl.ds(theirs, rim), :], diag_high_ref[...]], axis=0),
+        jnp.concatenate([tl_ref[pl.ds(theirs, rim), :], diag_low_ref[...]], axis=0),
+    )
+    into = (times(normed, *weights(high_ref, low_ref, 1)) + pack_ref[1:2, :]) * 0.5
     total, total2 = None, None
     for k in range(degree):
         part = slice(k * rows, (k + 1) * rows)
         half = got_ref[part, :] + into_ref[...] + take(hot_ref[part, rows:], *near)
         total = gate(half) if total is None else total + gate(half)
-        half = into + take(hot2_ref[part, :], th_ref[...], tl_ref[...])
+        half = got2_ref[part, :] + into + take(hot2_ref[part, :rows], high, low)
         total2 = gate(half) if total2 is None else total2 + gate(half)
     hidden = jnp.concatenate([load_rows(state_ref, rows, parts), other], axis=0) + times(
         jnp.concatenate([total, total2], axis=0), *weights(high_ref, low_ref, 2)
@@ -413,14 +416,13 @@
     sums = take(select_ref[...], *halves(times(act, *weights(high_ref, low_ref, 4))))
     size = sums.shape[0] // len(slot_refs)
     first = hot_ref.shape[0] // LANES + rows // LANES
-    base = swap0_ref.shape[0] - ints_ref.shape[0]
     anchor = (slot_refs[0].shape[0] - size * parts) // 4
     for j, slot in enumerate(slot_refs):
         store_rows(slot, sums[j * size : (j + 1) * size, :], parts)
         slot[size * parts :, :] = jnp.concatenate(
             [
                 ints_ref[first : first + anchor, :],
-                swap0_ref[base + first : base + first + anchor, :],
+                ints0_ref[first : first + anchor, :],
                 jnp.zeros((2 * anchor, LANES), f32),
             ],
             axis=0,
@@ -435,6 +437,16 @@
     out_ref[...] = total
 
 
+def position(ids, flip, count, coarse):
+    ids = jnp.bitwise_xor(ids.astype(jnp.int32), flip)
+    slot = jnp.right_shift(ids, count.bit_length() - 1)
+    return (
+        jnp.bitwise_and(ids, count - 1)
+        + jnp.right_shift(slot, 1) * count
+        + jnp.bitwise_and(slot, 1) * (coarse // 2)
+    )
+
+
 def edges_kernel(
     degree, count, place_ref, ints_ref, cs_ref, cr_ref, co_ref, di_ref, do_ref, *refs
 ):
@@ -447,13 +459,17 @@
     columns = turned(ints_ref[...])
     first = ints_ref.shape[0] // 2
     for j in range(rows // LANES):
-        column = jnp.bitwise_xor(
-            columns[:, first + j : first + j + 1].astype(jnp.int32), flip
-        ).astype(f32)
+        column = position(columns[:, first + j : first + j + 1], flip, count, coarse).astype(f32)
         parent_ref[j * LANES : (j + 1) * LANES, :] = equal(column, coarse)
     here = coarse * degree // LANES // len(slot_refs)
+    line = here // 2
     lines = jnp.concatenate(
-        [ref[ref.shape[0] - 2 * here : ref.shape[0] - here, :] for ref in slot_refs], axis=0
+        [
+            ref[ref.shape[0] - 2 * here + side * line : ref.shape[0] - 2 * here + (side + 1) * line, :]
+            for side in range(2)
+            for ref in slot_refs
+        ],
+        axis=0,
     )
     turn_ref[...] = turned(lines)
     step = LANES // degree
@@ -461,9 +477,7 @@
     table = jnp.zeros((coarse, LANES), f32)
     each = hot_ref.shape[0] // degree
     for k in range(degree):
-        spread = jnp.bitwise_xor(
-            turn_ref[pl.ds(k, step, stride=degree), :].astype(jnp.int32), flip
-        )
+        spread = position(turn_ref[pl.ds(k, step, stride=degree), :], flip, count, coarse)
         column = jnp.concatenate([spread[:, j : j + 1] for j in range(lines.shape[0])], axis=0)
         hot_ref[k * each : k * each + count, :] = equal(column[:count, :].astype(f32), coarse)
         high = jnp.right_shift(column, 8).astype(f32)
@@ -475,22 +489,43 @@
         hot_ref[k * each + count : (k + 1) * each, :] = equal(column, coarse)
 
 
-def coarse_kernel(last_ref, hot_ref, parent_ref, high_ref, low_ref, pack_ref, *refs):
+def column_kernel(hot_ref, parent_ref, high_ref, low_ref, *refs):
+    *blocks, got_ref, wanted_ref = refs
+    rows, width = wanted_ref.shape
+    parts = width // LANES
+    count = blocks[0].shape[0] // parts
+    middle = jnp.concatenate([load_rows(b, count, parts) for b in blocks], axis=0)
+    half = count * len(blocks)
+    sends = halves(times(unit(middle), *weights(high_ref, low_ref, 0)) * 0.5)
+    got_ref[...] = take(hot_ref[:, :half], *sends)
+    wanted_ref[:count, :] = middle[:count, :]
+    wanted_ref[count:, :] = take(parent_ref[:, :half], *halves(middle))
+
+
+def coarse_kernel(
+    last_ref, hot_ref, parent_ref, got_ref, wanted_ref, high_ref, low_ref, pack_ref, *refs
+):
     *blocks, fine_ref, coarse_ref = refs
     rows, width = last_ref.shape
     parts = width // LANES
     count = coarse_ref.shape[0] // parts
     need = count + rows
     middle = jnp.concatenate([load_rows(b, count, parts) for b in blocks], axis=0)
+    half = count * len(blocks)
     sends = halves(times(unit(middle), *weights(high_ref, low_ref, 0)) * 0.5)
     wanted = jnp.concatenate(
-        [middle[:count, :], take(parent_ref[...], *halves(middle))], axis=0
+        [
+            wanted_ref[:count, :],
+            wanted_ref[count:, :] + take(parent_ref[:, half:], *halves(middle)),
+        ],
+        axis=0,
     )
     into = (times(unit(wanted), *weights(high_ref, low_ref, 1)) + pack_ref[3:4, :]) * 0.5
     total = None
     for k in range(hot_ref.shape[0] // need):
-        half = into + take(hot_ref[k * need : (k + 1) * need, :], *sends)
-        total = gate(half) if total is None else total + gate(half)
+        part = slice(k * need, (k + 1) * need)
+        term = gate(got_ref[part, :] + into + take(hot_ref[part, half:], *sends))
+        total = term if total is None else total + term
     done = wanted + times(total, *weights(high_ref, low_ref, 2))
     store_rows(coarse_ref, done[:count, :], parts)
     act = gate(
@@ -562,6 +597,7 @@
     lines = lambda x: x.reshape(-1, LANES)
     row = lambda x: x.reshape(1, width)
     turn = pltpu.VMEM((LANES, LANES), f32)
+    here = lambda *xs: [pltpu.with_memory_space_constraint(x, pltpu.HBM) for x in xs]
     hot_shape = shape(edges, window, kind=bf16)
     small = lambda ref: pltpu.VMEM(ref.shape, ref.dtype)
 
@@ -569,19 +605,19 @@
         lines(fine_senders), lines(up_owner), lines(up_local), lines(coarse_owner),
         lines(coarse_local), fine_bias, row(up_bias), row(coarse_bias), row(down_bias),
     ]
-    here = lambda *xs: [pltpu.with_memory_space_constraint(x, pltpu.HBM) for x in xs]
-    state, ints, pack, out_swap, out_diag = call(
-        functools.partial(start_kernel, count),
-        [SMEM] + [HBM] * 10,
-        [
-            shape(full, LANES), shape(16, LANES), shape(8, width),
-            shape(rim + 16, LANES), shape(rim, LANES),
-        ],
-        "start",
-        [small(x) for x in small_args] + [pltpu.SemaphoreType.DMA((12,))],
-    )(place, *here(lines(fine_state), *small_args))
+    flat = lines(fine_state)
+    out_swap = lax.dynamic_slice(flat, ((1 - me % 2) * (full - rim), 0), (rim, LANES))
+    out_diag = lax.dynamic_slice(flat, (me % 2 * (full - rim), 0), (rim, LANES))
     swap0 = lax.ppermute(out_swap, "sp", swap)
     diag0 = lax.ppermute(out_diag, "sp", diag)
+    state, ints, pack = call(
+        functools.partial(start_kernel, count, HALO),
+        [SMEM] + [HBM] * 10,
+        [shape(full, LANES), shape(16, LANES), shape(8, width)],
+        "start",
+        [small(x) for x in small_args] + [pltpu.SemaphoreType.DMA((10,))],
+    )(place, *here(flat, *small_args))
+    ints0 = lax.ppermute(ints, "sp", swap)
     hot, got, into, high, low = call(
         functools.partial(near_kernel, edges),
         [VMEM] * 2 + [HBM] * 3 + [VMEM],
@@ -609,19 +645,25 @@
         "near1",
         [turn],
     )(
-        place, state, ints, swap0, hot, fine_w_send, fine_w_recv, fine_w_out, up_w_in, up_w_out,
+        place, state, ints, ints0, hot, fine_w_send, fine_w_recv, fine_w_out, up_w_in, up_w_out,
         pack,
     )
+    got2, diag_high, diag_low = call(
+        halo_kernel,
+        [SMEM] + [VMEM] * 7,
+        [shape(edges, width)] + [shape(HALO, width, kind=bf16)] * 2,
+        "halo",
+    )(place, pair1, diag1, own_high, own_low, hot2, high, low)
     hidden, *slots = call(
         up_kernel,
-        [SMEM] + [VMEM] * 16,
+        [SMEM] + [VMEM] * 15,
         [shape(rows, width)]
         + [shape(own + 8 * coarse_edges // 256, LANES)] * (peers // 2),
         "up",
-        [pltpu.VMEM((window, width), bf16)] * 2,
+        [pltpu.VMEM((rows, width), bf16)] * 2,
     )(
-        place, swap1, pair1, diag1, state, hot, got, into, own_high, own_low, hot2, select, ints,
-        swap0, high, low, pack,
+        place, swap1, diag_high, diag_low, state, hot, got, into, hot2, got2, select, ints, ints0,
+        high, low, pack,
     )
     arrived = [slots[0]] + [
         lax.ppermute(slots[j], "sp", flips[j]) for j in range(1, peers // 2)
@@ -633,9 +675,7 @@
         "middle",
     )(lines(coarse_state), *arrived)
     columns = [middle] + [lax.ppermute(middle, "sp", flips[j]) for j in range(1, peers // 2)]
-    blocks = []
-    for block in columns:
-        blocks += [block, lax.ppermute(block, "sp", swap)]
+    across = [lax.ppermute(block, "sp", swap) for block in columns]
     degree = coarse_edges // count
     coarse_hot, parent_hot, high, low = call(
         functools.partial(edges_kernel, degree, count),
@@ -650,12 +690,18 @@
     )(
         place, ints, coarse_w_send, coarse_w_recv, coarse_w_out, down_w_in, down_w_out, *arrived
     )
+    got, wanted = call(
+        column_kernel,
+        [VMEM] * (4 + peers // 2),
+        [shape(degree * (count + rows), width), shape(count + rows, width)],
+        "column",
+    )(coarse_hot, parent_hot, high, low, *columns)
     fine_out, coarse_out = call(
         coarse_kernel,
-        [VMEM] * (6 + peers),
+        [VMEM] * (8 + peers // 2),
         [shape(full, LANES), shape(own, LANES)],
         "coarse",
-    )(hidden, coarse_hot, parent_hot, high, low, pack, *blocks)
+    )(hidden, coarse_hot, parent_hot, got, wanted, high, low, pack, *across)
     return (fine_out.reshape(fine_state.shape), coarse_out.reshape(coarse_state.shape))
 
 

time: 55.5 us -> 59.2 us (1.067)
  waiting for transfers between devices: 12 us -> 15.3 us
  starting transfers between devices: 24.6 us -> 22.3 us
  Pallas kernels: 17.8 us -> 19.4 us
  local copies, waits for them, and re-layouts: 0.05 us -> 1.05 us
    ppermute x4 -> x5, waiting for transfers between devices: 1.36 us -> 7.01 us  [the longest x1 6.99 us: kernel_shards(): ints0 = lax.ppermute(ints, 'sp', swap)]
    ppermute x1, starting transfers between devices: 3.03 us -> 0.01 us  [kernel_shards(): swap0 = lax.ppermute(out_swap, 'sp', swap)]
    ppermute x1, waiting for transfers between devices: 2.63 us -> 0.01 us  [kernel_shards(): diag1 = lax.ppermute(out_half, 'sp', diag)]
    ppermute x1, starting transfers between devices: 3.57 us -> 6.07 us  [kernel_shards(): diag0 = lax.ppermute(out_diag, 'sp', diag)]
    ppermute x1, waiting for transfers between devices: 0.01 us -> 2.08 us  [kernel_shards(): swap0 = lax.ppermute(out_swap, 'sp', swap)]
    ppermute x1, waiting for transfers between devices: 1.68 us -> 0.01 us  [kernel_shards(): diag0 = lax.ppermute(out_diag, 'sp', diag)]
    pallas_call x3 -> x5, Pallas kernels: 9.68 us -> 11.3 us  [the longest x1 3.89 us: kernel_shards(): call(up_kernel, [SMEM] + [VMEM] * 15, [shape(rows, width)] + [shape(own +...]
    ppermute x3, waiting for transfers between devices: 0.59 us -> 2.09 us  [kernel_shards(): lax.ppermute(middle, 'sp', flips[j])]
  transfers between devices with their start and end apart: 15 -> 16, of which waited for: 10 -> 6; matrix products, arithmetic and copies ran while one was open for 0% -> 0% of each run, Pallas kernels for 11% -> 18%
where the time goes in v5:
time: 59.2 us; the launch traced here: 59 us
  starting transfers between devices  22.3 us (38%)
  Pallas kernels  19.4 us (33%)
  waiting for transfers between devices  15.3 us (26%)
  local copies, waits for them, and re-layouts  1.05 us (2%)
  between operations  0.89 us (2%)
    ppermute x1, waiting for transfers between devices, kernel_shards(): ints0 = lax.ppermute(ints, 'sp', swap)  6.99 us
    ppermute x1, starting transfers between devices, kernel_shards(): diag0 = lax.ppermute(out_diag, 'sp', diag)  6.07 us
    ppermute x3, starting transfers between devices, kernel_shards(): lax.ppermute(middle, 'sp', flips[j])  4.45 us
    ppermute x3, starting transfers between devices, kernel_shards(): lax.ppermute(slots[j], 'sp', flips[j])  4.44 us
    ppermute x3, waiting for transfers between devices, kernel_shards(): lax.ppermute(slots[j], 'sp', flips[j])  4.09 us
    pallas_call x1, Pallas kernels, kernel_shards(): call(up_kernel, [SMEM] + [VMEM] * 15, [shape(rows, width)] + [shape(own +...  3.89 us
    ppermute x1, starting transfers between devices, kernel_shards(): diag1 = lax.ppermute(out_half, 'sp', diag)  3.16 us
    ppermute x4, starting transfers between devices, kernel_shards(): across = [lax.ppermute(block, 'sp', swap) for block in columns]  3.01 us
  transfers between devices with their start and end apart: 16, of which 6 were waited for; matrix products, arithmetic and copies ran while one was open for 0% of the time, Pallas kernels for 18%

profile of v5, /device:TPU:0, one launch (start us, length us, event | category | flops | bytes accessed | tf_op | source)
XLA Modules:
  0.0 59.0 jit_solution(9647744749689519580)
XLA Ops:
  0.7 1.0 %constant_dynamic-slice_fusion = (f32[256,128]{1,0:T(8,128)S(1)}, f32[256,128]{1,0:T(8,128)S(1)}) fusion(f32[512,128]{1,0:T(8,128)} %bitcast.15, s32[]{:T(128)S(6)} %select_n.19, s32[]{:T(128)S(6)} %select_n.18), kind=kLoop, calls=%fused_computation.1 | loop fusion | bytes 524296 | tf_op jit(solution)/shard_map/dynamic_slice | solution.py:610
  1.6 6.1 %collective-permute-start.1 = (f32[256,128]{1,0:T(8,128)S(1)}, f32[256,128]{1,0:T(8,128)S(1)}, u32[]{:S(2)}, u32[]{:S(2)}) collective-permute-start(f32[256,128]{1,0:T(8,128)S(1)} %get-tuple-element.72), channel_id=1, source_target_pairs={{0,14},{2,4},{4,2},{6,8},{8,6},{10,12},{12,10},{14,0},{1,15},{3,5}... | collective-permute-start | bytes 393224 | tf_op jit(solution)/shard_map/ppermute | solution.py:612
  7.7 0.1 pad_add_fusion.place_ref
  7.8 1.7 %start.1 = (f32[512,128]{1,0:T(8,128)S(1)}, f32[16,128]{1,0:T(8,128)S(1)}, f32[8,256]{1,0:T(8,128)S(1)}) custom-call(s32[2]{0:T(128)S(1)} %pad_add_fusion.place_ref, f32[512,128]{1,0:T(8,128)} %bitcast.16, s32[8,128]{1,0:T(8,128)} %bitcast.17, s32[2,128]{1,0:T(2,128)} %bitcast.18, s32[2,128]{1,0:T(2,128)} %bitcast.19, s32[2,128]{1,0:T(2,128)} %bitcast.20, ...), custom_call_target="tpu_custom_call" | custom-call | tf_op jit(solution)/shard_map/start/pallas_call | solution.py:613
  9.5 2.4 %near0.1 = (bf16[1024,512]{1,0:T(8,128)(2,1)S(1)}, f32[1024,256]{1,0:T(8,128)S(1)}, f32[256,256]{1,0:T(8,128)S(1)}, bf16[512,256]{1,0:T(8,128)(2,1)S(1)}, bf16[512,256]{1,0:T(8,128)(2,1)S(1)}) custom-call(f32[512,128]{1,0:T(8,128)S(1)} %get-tuple-element.36.state_ref, f32[16,128]{1,0:T(8,128)S(1)} %get-tuple-element.37.ints_ref, f32[2,256,256]{2,1,0:T(8,128)} %ws_ref.1, ...), custom_call_target="tpu_custom_call" | custom-call | tf_op jit(solution)/shard_map/near0/pallas_call | solution.py:621
  11.9 2.1 %collective-permute-done.swap_ref = f32[256,128]{1,0:T(8,128)S(1)} collective-permute-done((f32[256,128]{1,0:T(8,128)S(1)}, f32[256,128]{1,0:T(8,128)S(1)}, u32[]{:S(2)}, u32[]{:S(2)}) %collective-permute-start) | collective-permute-done | bytes 131104 | tf_op jit(solution)/shard_map/ppermute | solution.py:611
  14.0 1.9 %far0.1 = (f32[512,128]{1,0:T(8,128)S(1)}, f32[256,128]{1,0:T(8,128)S(1)}) custom-call(s32[2]{0:T(128)S(1)} %pad_add_fusion.place_ref, f32[256,128]{1,0:T(8,128)S(1)} %collective-permute-done.swap_ref, f32[256,128]{1,0:T(8,128)S(1)} %collective-permute-done.1.diag_ref, f32[512,128]{1,0:T(8,128)S(1)} %get-tuple-element.36.state_ref, ...), custom_call_target="tpu_custom_call" | custom-call | tf_op jit(solution)/shard_map/far0/pallas_call | solution.py:629
  15.9 0.1 collective-permute-start.2
  16.0 3.2 %collective-permute-start.4 = (f32[256,128]{1,0:T(8,128)S(1)}, f32[256,128]{1,0:T(8,128)S(1)}, u32[]{:S(2)}, u32[]{:S(2)}) collective-permute-start(f32[256,128]{1,0:T(8,128)S(1)} %get-tuple-element.45), channel_id=1, source_target_pairs={{0,14},{2,4},{4,2},{6,8},{8,6},{10,12},{12,10},{14,0},{1,15},{3,5}... | collective-permute-start | bytes 393224 | tf_op jit(solution)/shard_map/ppermute | solution.py:636
  19.2 0.4 collective-permute-start.3
  19.6 0.6 %collective-permute-start.5 = (f32[16,128]{1,0:T(8,128)S(1)}, f32[16,128]{1,0:T(8,128)S(1)}, u32[]{:S(2)}, u32[]{:S(2)}) collective-permute-start(f32[16,128]{1,0:T(8,128)S(1)} %get-tuple-element.37.ints_ref), channel_id=1, source_target_pairs={{0,2},{2,0},{4,6},{6,4},{8,10},{10,8},{12,14},{14,12},{1,3},{3,1},... | collective-permute-start | bytes 24584 | tf_op jit(solution)/shard_map/ppermute | solution.py:620
  20.2 7.0 %collective-permute-done.5.ints0_ref = f32[16,128]{1,0:T(8,128)S(1)} collective-permute-done((f32[16,128]{1,0:T(8,128)S(1)}, f32[16,128]{1,0:T(8,128)S(1)}, u32[]{:S(2)}, u32[]{:S(2)}) %collective-permute-start.5) | collective-permute-done | bytes 8224 | tf_op jit(solution)/shard_map/ppermute | solution.py:620
  27.3 1.7 %near1.1 = (f32[1024,256]{1,0:T(8,128)S(1)}, f32[256,256]{1,0:T(8,128)S(1)}, bf16[256,256]{1,0:T(8,128)(2,1)S(1)}, bf16[256,256]{1,0:T(8,128)(2,1)S(1)}, bf16[10...) custom-call(s32[2]{0:T(128)S(1)} %pad_add_fusion.place_ref, ...), custom_call_target="tpu_custom_call" | custom-call | tf_op jit(solution)/shard_map/near1/pallas_call | solution.py:638
  29.0 1.5 %halo.1 = (f32[1024,256]{1,0:T(8,128)S(1)}, bf16[128,256]{1,0:T(8,128)(2,1)S(1)}, bf16[128,256]{1,0:T(8,128)(2,1)S(1)}) custom-call(s32[2]{0:T(128)S(1)} %pad_add_fusion.place_ref, f32[256,128]{1,0:T(8,128)S(1)} %collective-permute-done.3.pair_ref, f32[256,128]{1,0:T(8,128)S(1)} %collective-permute-done.4.diag_ref, ...), custom_call_target="tpu_custom_call" | custom-call | tf_op jit(solution)/shard_map/halo/pallas_call | solution.py:651
  30.6 3.9 %up.1 = (f32[256,256]{1,0:T(8,128)S(1)}, f32[136,128]{1,0:T(8,128)S(1)}, f32[136,128]{1,0:T(8,128)S(1)}, f32[136,128]{1,0:T(8,128)S(1)}, f32[136,128]{1,0:T(8,128)S(1)}) custom-call(s32[2]{0:T(128)S(1)} %pad_add_fusion.place_ref, f32[512,128]{1,0:T(8,128)S(1)} %collective-permute-done.2.swap_ref, bf16[128,256]{1,0:T(8,128)(2,1)S(1)} %get-tuple-element.51.diag_high_ref, ...), custom_call_target="tpu_custom_call" | custom-call | tf_op jit(solution)/shard_map/up/pallas_call | solution.py:657
  34.5 0.1 collective-permute-start.6
  34.6 2.3 %collective-permute-start.7 = (f32[136,128]{1,0:T(8,128)S(1)}, f32[136,128]{1,0:T(8,128)S(1)}, u32[]{:S(2)}, u32[]{:S(2)}) collective-permute-start(f32[136,128]{1,0:T(8,128)S(1)} %get-tuple-element.60), channel_id=1, source_target_pairs={{0,8},{2,10},{4,12},{6,14},{8,0},{10,2},{12,4},{14,6},{1,9},{3,11}... | collective-permute-start | bytes 208904 | tf_op jit(solution)/shard_map/ppermute | solution.py:669
  36.8 2.1 %collective-permute-start.8 = (f32[136,128]{1,0:T(8,128)S(1)}, f32[136,128]{1,0:T(8,128)S(1)}, u32[]{:S(2)}, u32[]{:S(2)}) collective-permute-start(f32[136,128]{1,0:T(8,128)S(1)} %get-tuple-element.61), channel_id=1, source_target_pairs={{0,12},{2,14},{4,8},{6,10},{8,4},{10,6},{12,0},{14,2},{1,13},{3,15... | collective-permute-start | bytes 208904 | tf_op jit(solution)/shard_map/ppermute | solution.py:669
  38.9 2.8 %collective-permute-done.7.refs_2_ = f32[136,128]{1,0:T(8,128)S(1)} collective-permute-done((f32[136,128]{1,0:T(8,128)S(1)}, f32[136,128]{1,0:T(8,128)S(1)}, u32[]{:S(2)}, u32[]{:S(2)}) %collective-permute-start.7) | collective-permute-done | bytes 69664 | tf_op jit(solution)/shard_map/ppermute | solution.py:669
  41.8 1.3 %collective-permute-done.8.refs_3_ = f32[136,128]{1,0:T(8,128)S(1)} collective-permute-done((f32[136,128]{1,0:T(8,128)S(1)}, f32[136,128]{1,0:T(8,128)S(1)}, u32[]{:S(2)}, u32[]{:S(2)}) %collective-permute-start.8) | collective-permute-done | bytes 69664 | tf_op jit(solution)/shard_map/ppermute | solution.py:669
  43.1 2.2 %collective-permute-start.11 = (f32[128,128]{1,0:T(8,128)S(1)}, f32[128,128]{1,0:T(8,128)S(1)}, u32[]{:S(2)}, u32[]{:S(2)}) collective-permute-start(f32[128,128]{1,0:T(8,128)S(1)} %middle.1.refs_0_), channel_id=1, source_target_pairs={{0,12},{2,14},{4,8},{6,10},{8,4},{10,6},{12,0},{14,2},{1,13},{3,15... | collective-permute-start | bytes 196616 | tf_op jit(solution)/shard_map/ppermute | solution.py:677
  45.2 0.4 collective-permute-start.10
  45.6 1.9 %collective-permute-start.9 = (f32[128,128]{1,0:T(8,128)S(1)}, f32[128,128]{1,0:T(8,128)S(1)}, u32[]{:S(2)}, u32[]{:S(2)}) collective-permute-start(f32[128,128]{1,0:T(8,128)S(1)} %middle.1.refs_0_), channel_id=1, source_target_pairs={{0,4},{2,6},{4,0},{6,2},{8,12},{10,14},{12,8},{14,10},{1,5},{3,7},... | collective-permute-start | bytes 196616 | tf_op jit(solution)/shard_map/ppermute | solution.py:677
  47.5 0.4 collective-permute-start.12
  47.9 1.3 %collective-permute-done.11.refs_3_ = f32[128,128]{1,0:T(8,128)S(1)} collective-permute-done((f32[128,128]{1,0:T(8,128)S(1)}, f32[128,128]{1,0:T(8,128)S(1)}, u32[]{:S(2)}, u32[]{:S(2)}) %collective-permute-start.11) | collective-permute-done | bytes 65568 | tf_op jit(solution)/shard_map/ppermute | solution.py:677
  49.2 0.6 %collective-permute-start.15 = (f32[128,128]{1,0:T(8,128)S(1)}, f32[128,128]{1,0:T(8,128)S(1)}, u32[]{:S(2)}, u32[]{:S(2)}) collective-permute-start(f32[128,128]{1,0:T(8,128)S(1)} %collective-permute-done.11.refs_3_), channel_id=1, source_target_pairs={{0,2},{2,0},{4,6},{6,4},{8,10},{10,8},{12,14},{14,12},{1,3},{3,1},... | collective-permute-start | bytes 196616 | tf_op jit(solution)/shard_map/ppermute | solution.py:678
  49.8 0.8 %collective-permute-done.10.refs_2_ = f32[128,128]{1,0:T(8,128)S(1)} collective-permute-done((f32[128,128]{1,0:T(8,128)S(1)}, f32[128,128]{1,0:T(8,128)S(1)}, u32[]{:S(2)}, u32[]{:S(2)}) %collective-permute-start.10) | collective-permute-done | bytes 65568 | tf_op jit(solution)/shard_map/ppermute | solution.py:677
  50.6 0.8 %collective-permute-start.14 = (f32[128,128]{1,0:T(8,128)S(1)}, f32[128,128]{1,0:T(8,128)S(1)}, u32[]{:S(2)}, u32[]{:S(2)}) collective-permute-start(f32[128,128]{1,0:T(8,128)S(1)} %collective-permute-done.10.refs_2_), channel_id=1, source_target_pairs={{0,2},{2,0},{4,6},{6,4},{8,10},{10,8},{12,14},{14,12},{1,3},{3,1},... | collective-permute-start | bytes 196616 | tf_op jit(solution)/shard_map/ppermute | solution.py:678
  51.4 1.2 %collective-permute-start.13 = (f32[128,128]{1,0:T(8,128)S(1)}, f32[128,128]{1,0:T(8,128)S(1)}, u32[]{:S(2)}, u32[]{:S(2)}) collective-permute-start(f32[128,128]{1,0:T(8,128)S(1)} %collective-permute-done.9.refs_1_), channel_id=1, source_target_pairs={{0,2},{2,0},{4,6},{6,4},{8,10},{10,8},{12,14},{14,12},{1,3},{3,1},... | collective-permute-start | bytes 196616 | tf_op jit(solution)/shard_map/ppermute | solution.py:678
  52.6 2.1 %edges.1 = (bf16[1280,512]{1,0:T(8,128)(2,1)S(1)}, bf16[256,512]{1,0:T(8,128)(2,1)S(1)}, bf16[1280,256]{1,0:T(8,128)(2,1)S(1)}, bf16[1280,256]{1,0:T(8,128)(2,1)S(1)}) custom-call(s32[2]{0:T(128)S(1)} %pad_add_fusion.place_ref, f32[16,128]{1,0:T(8,128)S(1)} %get-tuple-element.37.ints_ref, f32[256,256]{1,0:T(8,128)S(1)} %copy-done.5, ...), custom_call_target="tpu_custom_call" | custom-call | tf_op jit(solution)/shard_map/edges/pallas_call | solution.py:680
  54.8 1.2 %column.1 = (f32[1280,256]{1,0:T(8,128)S(1)}, f32[320,256]{1,0:T(8,128)S(1)}) custom-call(bf16[1280,512]{1,0:T(8,128)(2,1)S(1)} %get-tuple-element.62.hot_ref, bf16[256,512]{1,0:T(8,128)(2,1)S(1)} %get-tuple-element.63.parent_ref, bf16[1280,256]{1,0:T(8,128)(2,1)S(1)} %get-tuple-element.64.high_ref, bf16[1280,256]{1,0:T(8,128)(2,1)S(1)} %get-tuple-element.65.low_ref, ...), custom_call_target="tpu_custom_call" | custom-call | tf_op jit(solution)/shard_map/column/pallas_call | solution.py:693
  56.0 3.0 %coarse.1 = (f32[512,128]{1,0:T(8,128)}, f32[128,128]{1,0:T(8,128)}) custom-call(f32[256,256]{1,0:T(8,128)S(1)} %get-tuple-element.57.last_ref, bf16[1280,512]{1,0:T(8,128)(2,1)S(1)} %get-tuple-element.62.hot_ref, bf16[256,512]{1,0:T(8,128)(2,1)S(1)} %get-tuple-element.63.parent_ref, f32[1280,256]{1,0:T(8,128)S(1)} %get-tuple-element.66.got_ref, ...), custom_call_target="tpu_custom_call" | custom-call | tf_op jit(solution)/shard_map/coarse/pallas_call | solution.py:699
  (34 shorter events, 0.1 us)
Async XLA Ops:
  1.6 10.3 %collective-permute-start.1 = (f32[256,128]{1,0:T(8,128)S(1)}, f32[256,128]{1,0:T(8,128)S(1)}, u32[]{:S(2)}, u32[]{:S(2)}) collective-permute-start(f32[256,128]{1,0:T(8,128)S(1)} %get-tuple-element.72), channel_id=1, source_target_pairs={{0,14},{2,4},{4,2},{6,8},{8,6},{10,12},{12,10},{14,0},{1,15},{3,5}... | collective-permute-start | bytes 393224 | tf_op jit(solution)/shard_map/ppermute | solution.py:612
  7.7 6.3 %collective-permute-start = (f32[256,128]{1,0:T(8,128)S(1)}, f32[256,128]{1,0:T(8,128)S(1)}, u32[]{:S(2)}, u32[]{:S(2)}) collective-permute-start(f32[256,128]{1,0:T(8,128)S(1)} %get-tuple-element.73), channel_id=1, source_target_pairs={{0,2},{2,0},{4,6},{6,4},{8,10},{10,8},{12,14},{14,12},{1,3},{3,1},... | collective-permute-start | bytes 393224 | tf_op jit(solution)/shard_map/ppermute | solution.py:611
  14.0 13.2 %copy-start = (f32[2,256,256]{2,1,0:T(8,128)S(1)}, f32[2,256,256]{2,1,0:T(8,128)}, u32[]{:S(2)}) copy-start(f32[2,256,256]{2,1,0:T(8,128)} %ws_ref.1) | copy-start | bytes 1572868
  14.0 13.2 %copy-start.1 = (f32[2,256,256]{2,1,0:T(8,128)S(1)}, f32[2,256,256]{2,1,0:T(8,128)}, u32[]{:S(2)}) copy-start(f32[2,256,256]{2,1,0:T(8,128)} %wr_ref.1) | copy-start | bytes 1572868
  14.0 13.2 %copy-start.2 = (f32[2,256,256]{2,1,0:T(8,128)S(1)}, f32[2,256,256]{2,1,0:T(8,128)}, u32[]{:S(2)}) copy-start(f32[2,256,256]{2,1,0:T(8,128)} %wo_ref.1) | copy-start | bytes 1572868
  14.0 13.2 %copy-start.3 = (f32[256,256]{1,0:T(8,128)S(1)}, f32[256,256]{1,0:T(8,128)}, u32[]{:S(2)}) copy-start(f32[256,256]{1,0:T(8,128)} %wi_ref.1) | copy-start | bytes 786436
  14.0 13.2 %copy-start.4 = (f32[256,256]{1,0:T(8,128)S(1)}, f32[256,256]{1,0:T(8,128)}, u32[]{:S(2)}) copy-start(f32[256,256]{1,0:T(8,128)} %wu_ref.1) | copy-start | bytes 786436
  15.9 14.6 %collective-permute-start.2 = (f32[512,128]{1,0:T(8,128)S(1)}, f32[512,128]{1,0:T(8,128)S(1)}, u32[]{:S(2)}, u32[]{:S(2)}) collective-permute-start(f32[512,128]{1,0:T(8,128)S(1)} %get-tuple-element.44.state_ref), channel_id=1, source_target_pairs={{0,2},{2,0},{4,6},{6,4},{8,10},{10,8},{12,14},{14,12},{1,3},{3,1},... | collective-permute-start | bytes 786440 | tf_op jit(solution)/shard_map/ppermute | solution.py:635
  16.0 12.9 %collective-permute-start.4 = (f32[256,128]{1,0:T(8,128)S(1)}, f32[256,128]{1,0:T(8,128)S(1)}, u32[]{:S(2)}, u32[]{:S(2)}) collective-permute-start(f32[256,128]{1,0:T(8,128)S(1)} %get-tuple-element.45), channel_id=1, source_target_pairs={{0,14},{2,4},{4,2},{6,8},{8,6},{10,12},{12,10},{14,0},{1,15},{3,5}... | collective-permute-start | bytes 393224 | tf_op jit(solution)/shard_map/ppermute | solution.py:636
  19.2 9.8 %collective-permute-start.3 = (f32[256,128]{1,0:T(8,128)S(1)}, f32[256,128]{1,0:T(8,128)S(1)}, u32[]{:S(2)}, u32[]{:S(2)}) collective-permute-start(f32[256,128]{1,0:T(8,128)S(1)} %get-tuple-element.45), channel_id=1, source_target_pairs={{0,12},{2,6},{4,0},{6,10},{8,4},{10,14},{12,8},{14,2},{1,13},{3,7}... | collective-permute-start | bytes 393224 | tf_op jit(solution)/shard_map/ppermute | solution.py:637
  19.6 7.6 %collective-permute-start.5 = (f32[16,128]{1,0:T(8,128)S(1)}, f32[16,128]{1,0:T(8,128)S(1)}, u32[]{:S(2)}, u32[]{:S(2)}) collective-permute-start(f32[16,128]{1,0:T(8,128)S(1)} %get-tuple-element.37.ints_ref), channel_id=1, source_target_pairs={{0,2},{2,0},{4,6},{6,4},{8,10},{10,8},{12,14},{14,12},{1,3},{3,1},... | collective-permute-start | bytes 24584 | tf_op jit(solution)/shard_map/ppermute | solution.py:620
  30.5 12.5 %copy-start.10 = (f32[64,1,256]{2,1,0:T(1,128)S(1)}, f32[64,1,256]{2,1,0:T(1,128)}, u32[]{:S(2)}) copy-start(f32[64,1,256]{2,1,0:T(1,128)} %param.22) | copy-start | bytes 196612
  30.5 22.1 %copy-start.5 = (f32[256,256]{1,0:T(8,128)S(1)}, f32[256,256]{1,0:T(8,128)}, u32[]{:S(2)}) copy-start(f32[256,256]{1,0:T(8,128)} %cs_ref.1) | copy-start | bytes 786436
  30.5 22.1 %copy-start.6 = (f32[256,256]{1,0:T(8,128)S(1)}, f32[256,256]{1,0:T(8,128)}, u32[]{:S(2)}) copy-start(f32[256,256]{1,0:T(8,128)} %cr_ref.1) | copy-start | bytes 786436
  30.5 22.1 %copy-start.7 = (f32[256,256]{1,0:T(8,128)S(1)}, f32[256,256]{1,0:T(8,128)}, u32[]{:S(2)}) copy-start(f32[256,256]{1,0:T(8,128)} %co_ref.1) | copy-start | bytes 786436
  30.6 22.1 %copy-start.8 = (f32[256,256]{1,0:T(8,128)S(1)}, f32[256,256]{1,0:T(8,128)}, u32[]{:S(2)}) copy-start(f32[256,256]{1,0:T(8,128)} %di_ref.1) | copy-start | bytes 786436
  30.6 22.1 %copy-start.9 = (f32[256,256]{1,0:T(8,128)S(1)}, f32[256,256]{1,0:T(8,128)}, u32[]{:S(2)}) copy-start(f32[256,256]{1,0:T(8,128)} %do_ref.1) | copy-start | bytes 786436
  34.5 4.5 %collective-permute-start.6 = (f32[136,128]{1,0:T(8,128)S(1)}, f32[136,128]{1,0:T(8,128)S(1)}, u32[]{:S(2)}, u32[]{:S(2)}) collective-permute-start(f32[136,128]{1,0:T(8,128)S(1)} %get-tuple-element.59), channel_id=1, source_target_pairs={{0,4},{2,6},{4,0},{6,2},{8,12},{10,14},{12,8},{14,10},{1,5},{3,7},... | collective-permute-start | bytes 208904 | tf_op jit(solution)/shard_map/ppermute | solution.py:669
  34.6 7.2 %collective-permute-start.7 = (f32[136,128]{1,0:T(8,128)S(1)}, f32[136,128]{1,0:T(8,128)S(1)}, u32[]{:S(2)}, u32[]{:S(2)}) collective-permute-start(f32[136,128]{1,0:T(8,128)S(1)} %get-tuple-element.60), channel_id=1, source_target_pairs={{0,8},{2,10},{4,12},{6,14},{8,0},{10,2},{12,4},{14,6},{1,9},{3,11}... | collective-permute-start | bytes 208904 | tf_op jit(solution)/shard_map/ppermute | solution.py:669
  36.8 6.2 %collective-permute-start.8 = (f32[136,128]{1,0:T(8,128)S(1)}, f32[136,128]{1,0:T(8,128)S(1)}, u32[]{:S(2)}, u32[]{:S(2)}) collective-permute-start(f32[136,128]{1,0:T(8,128)S(1)} %get-tuple-element.61), channel_id=1, source_target_pairs={{0,12},{2,14},{4,8},{6,10},{8,4},{10,6},{12,0},{14,2},{1,13},{3,15... | collective-permute-start | bytes 208904 | tf_op jit(solution)/shard_map/ppermute | solution.py:669
  43.1 6.1 %collective-permute-start.11 = (f32[128,128]{1,0:T(8,128)S(1)}, f32[128,128]{1,0:T(8,128)S(1)}, u32[]{:S(2)}, u32[]{:S(2)}) collective-permute-start(f32[128,128]{1,0:T(8,128)S(1)} %middle.1.refs_0_), channel_id=1, source_target_pairs={{0,12},{2,14},{4,8},{6,10},{8,4},{10,6},{12,0},{14,2},{1,13},{3,15... | collective-permute-start | bytes 196616 | tf_op jit(solution)/shard_map/ppermute | solution.py:677
  45.2 5.4 %collective-permute-start.10 = (f32[128,128]{1,0:T(8,128)S(1)}, f32[128,128]{1,0:T(8,128)S(1)}, u32[]{:S(2)}, u32[]{:S(2)}) collective-permute-start(f32[128,128]{1,0:T(8,128)S(1)} %middle.1.refs_0_), channel_id=1, source_target_pairs={{0,8},{2,10},{4,12},{6,14},{8,0},{10,2},{12,4},{14,6},{1,9},{3,11}... | collective-permute-start | bytes 196616 | tf_op jit(solution)/shard_map/ppermute | solution.py:677
  45.6 5.8 %collective-permute-start.9 = (f32[128,128]{1,0:T(8,128)S(1)}, f32[128,128]{1,0:T(8,128)S(1)}, u32[]{:S(2)}, u32[]{:S(2)}) collective-permute-start(f32[128,128]{1,0:T(8,128)S(1)} %middle.1.refs_0_), channel_id=1, source_target_pairs={{0,4},{2,6},{4,0},{6,2},{8,12},{10,14},{12,8},{14,10},{1,5},{3,7},... | collective-permute-start | bytes 196616 | tf_op jit(solution)/shard_map/ppermute | solution.py:677
  47.5 8.4 %collective-permute-start.12 = (f32[128,128]{1,0:T(8,128)S(1)}, f32[128,128]{1,0:T(8,128)S(1)}, u32[]{:S(2)}, u32[]{:S(2)}) collective-permute-start(f32[128,128]{1,0:T(8,128)S(1)} %middle.1.refs_0_), channel_id=1, source_target_pairs={{0,2},{2,0},{4,6},{6,4},{8,10},{10,8},{12,14},{14,12},{1,3},{3,1},... | collective-permute-start | bytes 196616 | tf_op jit(solution)/shard_map/ppermute | solution.py:678
  49.2 6.8 %collective-permute-start.15 = (f32[128,128]{1,0:T(8,128)S(1)}, f32[128,128]{1,0:T(8,128)S(1)}, u32[]{:S(2)}, u32[]{:S(2)}) collective-permute-start(f32[128,128]{1,0:T(8,128)S(1)} %collective-permute-done.11.refs_3_), channel_id=1, source_target_pairs={{0,2},{2,0},{4,6},{6,4},{8,10},{10,8},{12,14},{14,12},{1,3},{3,1},... | collective-permute-start | bytes 196616 | tf_op jit(solution)/shard_map/ppermute | solution.py:678
  50.6 5.4 %collective-permute-start.14 = (f32[128,128]{1,0:T(8,128)S(1)}, f32[128,128]{1,0:T(8,128)S(1)}, u32[]{:S(2)}, u32[]{:S(2)}) collective-permute-start(f32[128,128]{1,0:T(8,128)S(1)} %collective-permute-done.10.refs_2_), channel_id=1, source_target_pairs={{0,2},{2,0},{4,6},{6,4},{8,10},{10,8},{12,14},{14,12},{1,3},{3,1},... | collective-permute-start | bytes 196616 | tf_op jit(solution)/shard_map/ppermute | solution.py:678
  51.4 4.6 %collective-permute-start.13 = (f32[128,128]{1,0:T(8,128)S(1)}, f32[128,128]{1,0:T(8,128)S(1)}, u32[]{:S(2)}, u32[]{:S(2)}) collective-permute-start(f32[128,128]{1,0:T(8,128)S(1)} %collective-permute-done.9.refs_1_), channel_id=1, source_target_pairs={{0,2},{2,0},{4,6},{6,4},{8,10},{10,8},{12,14},{14,12},{1,3},{3,1},... | collective-permute-start | bytes 196616 | tf_op jit(solution)/shard_map/ppermute | solution.py:678

commit v6 on v5

--- a/solution.py
+++ b/solution.py
@@ -447,15 +447,16 @@
     )
 
 
-def edges_kernel(
-    degree, count, place_ref, ints_ref, cs_ref, cr_ref, co_ref, di_ref, do_ref, *refs
-):
-    *slot_refs, hot_ref, parent_ref, high_ref, low_ref, turn_ref = refs
+def split_kernel(cs_ref, cr_ref, co_ref, di_ref, do_ref, high_ref, low_ref):
+    split_into(
+        high_ref, low_ref, cs_ref[...], cr_ref[...], co_ref[...], di_ref[...], do_ref[...]
+    )
+
+
+def edges_kernel(degree, count, place_ref, ints_ref, *refs):
+    *slot_refs, hot_ref, parent_ref, turn_ref = refs
     rows, coarse = parent_ref.shape
     flip = place_ref[1]
-    split_into(
-        high_ref, low_ref, cs_ref[...], cr_ref[...], co_ref[...], di_ref[...], do_ref[...]
-    )
     columns = turned(ints_ref[...])
     first = ints_ref.shape[0] // 2
     for j in range(rows // LANES):
@@ -491,7 +492,7 @@
 
 def column_kernel(hot_ref, parent_ref, high_ref, low_ref, *refs):
     *blocks, got_ref, wanted_ref = refs
-    rows, width = wanted_ref.shape
+    _, width = wanted_ref.shape
     parts = width // LANES
     count = blocks[0].shape[0] // parts
     middle = jnp.concatenate([load_rows(b, count, parts) for b in blocks], axis=0)
@@ -539,16 +540,19 @@
 HBM = pl.BlockSpec(memory_space=pltpu.HBM)
 
 
-def call(kernel, in_specs, out_shapes, name, scratch=()):
+def call(kernel, in_specs, out_shapes, scratch=()):
     return pl.pallas_call(
         kernel,
         in_specs=in_specs,
         out_specs=[VMEM] * len(out_shapes),
         out_shape=out_shapes,
         scratch_shapes=scratch,
-        name=name,
         compiler_params=pltpu.CompilerParams(vmem_limit_bytes=32 * 2**20),
     )
+
+
+def move(values, pairs):
+    return lax.ppermute(values, "sp", pairs)
 
 
 def shape(*dims, kind=f32):
@@ -608,33 +612,28 @@
     flat = lines(fine_state)
     out_swap = lax.dynamic_slice(flat, ((1 - me % 2) * (full - rim), 0), (rim, LANES))
     out_diag = lax.dynamic_slice(flat, (me % 2 * (full - rim), 0), (rim, LANES))
-    swap0 = lax.ppermute(out_swap, "sp", swap)
-    diag0 = lax.ppermute(out_diag, "sp", diag)
+    swap0 = move(out_swap, swap)
+    diag0 = move(out_diag, diag)
     state, ints, pack = call(
         functools.partial(start_kernel, count, HALO),
         [SMEM] + [HBM] * 10,
         [shape(full, LANES), shape(16, LANES), shape(8, width)],
-        "start",
         [small(x) for x in small_args] + [pltpu.SemaphoreType.DMA((10,))],
     )(place, *here(flat, *small_args))
-    ints0 = lax.ppermute(ints, "sp", swap)
+    ints0 = move(ints, swap)
     hot, got, into, high, low = call(
         functools.partial(near_kernel, edges),
         [VMEM] * 2 + [HBM] * 3 + [VMEM],
         [hot_shape, shape(edges, width), shape(rows, width)]
         + [shape(2 * size, width, kind=bf16)] * 2,
-        "near0",
         [turn] + [pltpu.VMEM((size, width), f32)] * 3 + [pltpu.SemaphoreType.DMA((3,))],
     )(state, ints, *here(fine_w_send, fine_w_recv, fine_w_out), pack)
     state, out_half = call(
-        far_kernel,
-        [SMEM] + [VMEM] * 8,
-        [shape(full, LANES), shape(rim, LANES)],
-        "far0",
+        far_kernel, [SMEM] + [VMEM] * 8, [shape(full, LANES), shape(rim, LANES)]
     )(place, swap0, diag0, state, hot, got, into, high, low)
-    swap1 = lax.ppermute(state, "sp", swap)
-    diag1 = lax.ppermute(out_half, "sp", diag)
-    pair1 = lax.ppermute(out_half, "sp", pair)
+    swap1 = move(state, swap)
+    diag1 = move(out_half, diag)
+    pair1 = move(out_half, pair)
     got, into, own_high, own_low, hot2, select, high, low = call(
         functools.partial(near2_kernel, edges, count),
         [SMEM] + [VMEM] * 10,
@@ -642,7 +641,6 @@
         + [shape(rows, width, kind=bf16)] * 2
         + [hot_shape, shape(coarse // 2, 2 * rows, kind=bf16)]
         + [shape(5 * size, width, kind=bf16)] * 2,
-        "near1",
         [turn],
     )(
         place, state, ints, ints0, hot, fine_w_send, fine_w_recv, fine_w_out, up_w_in, up_w_out,
@@ -652,55 +650,43 @@
         halo_kernel,
         [SMEM] + [VMEM] * 7,
         [shape(edges, width)] + [shape(HALO, width, kind=bf16)] * 2,
-        "halo",
     )(place, pair1, diag1, own_high, own_low, hot2, high, low)
     hidden, *slots = call(
         up_kernel,
         [SMEM] + [VMEM] * 15,
         [shape(rows, width)]
         + [shape(own + 8 * coarse_edges // 256, LANES)] * (peers // 2),
-        "up",
         [pltpu.VMEM((rows, width), bf16)] * 2,
     )(
         place, swap1, diag_high, diag_low, state, hot, got, into, hot2, got2, select, ints, ints0,
         high, low, pack,
     )
-    arrived = [slots[0]] + [
-        lax.ppermute(slots[j], "sp", flips[j]) for j in range(1, peers // 2)
-    ]
+    arrived = [slots[0]] + [move(slots[j], flips[j]) for j in range(1, peers // 2)]
     (middle,) = call(
-        middle_kernel,
-        [VMEM] * (1 + peers // 2),
-        [shape(own, LANES)],
-        "middle",
+        middle_kernel, [VMEM] * (1 + peers // 2), [shape(own, LANES)]
     )(lines(coarse_state), *arrived)
-    columns = [middle] + [lax.ppermute(middle, "sp", flips[j]) for j in range(1, peers // 2)]
-    across = [lax.ppermute(block, "sp", swap) for block in columns]
+    columns = [middle] + [move(middle, flips[j]) for j in range(1, peers // 2)]
+    across = [move(block, swap) for block in columns]
     degree = coarse_edges // count
-    coarse_hot, parent_hot, high, low = call(
+    coarse_hot, parent_hot = call(
         functools.partial(edges_kernel, degree, count),
-        [SMEM] + [VMEM] * (6 + peers // 2),
+        [SMEM] + [VMEM] * (1 + peers // 2),
         [
             shape(degree * (count + rows), coarse, kind=bf16),
             shape(rows, coarse, kind=bf16),
-        ]
-        + [shape(5 * size, width, kind=bf16)] * 2,
-        "edges",
+        ],
         [turn],
-    )(
-        place, ints, coarse_w_send, coarse_w_recv, coarse_w_out, down_w_in, down_w_out, *arrived
-    )
+    )(place, ints, *arrived)
+    high, low = call(
+        split_kernel, [VMEM] * 5, [shape(5 * size, width, kind=bf16)] * 2
+    )(coarse_w_send, coarse_w_recv, coarse_w_out, down_w_in, down_w_out)
     got, wanted = call(
         column_kernel,
         [VMEM] * (4 + peers // 2),
         [shape(degree * (count + rows), width), shape(count + rows, width)],
-        "column",
     )(coarse_hot, parent_hot, high, low, *columns)
     fine_out, coarse_out = call(
-        coarse_kernel,
-        [VMEM] * (8 + peers // 2),
-        [shape(full, LANES), shape(own, LANES)],
-        "coarse",
+        coarse_kernel, [VMEM] * (8 + peers // 2), [shape(full, LANES), shape(own, LANES)]
     )(hidden, coarse_hot, parent_hot, got, wanted, high, low, pack, *across)
     return (fine_out.reshape(fine_state.shape), coarse_out.reshape(coarse_state.shape))
 
@@ -731,7 +717,9 @@
         and peers >= 4
         and rows >= 2 * HALO
     )
-    return (kernel_shards if fits else general_shards)(*args)
+    if not fits:
+        return general_shards(*args)
+    return kernel_shards(*args)
 
 
 def solution(mesh):

time: 59.2 us -> 57.1 us (0.965)
  waiting for transfers between devices: 15.3 us -> 9.64 us
  starting transfers between devices: 22.3 us -> 25.8 us
    ppermute x16, waiting for transfers between devices: 15.3 us -> 9.64 us  [move(): return lax.ppermute(values, 'sp', pairs)]
    ppermute x16, starting transfers between devices: 22.3 us -> 25.8 us  [move(): return lax.ppermute(values, 'sp', pairs)]
    pallas_call x2 -> x3, Pallas kernels: 2.16 us -> 2.13 us  [the longest x1 1.9 us: kernel_shards(): call(functools.partial(edges_kernel, degree, count), [SMEM] + [VMEM] * (1...]
  transfers between devices with their start and end apart: 16 -> 16, of which waited for: 6 -> 7; matrix products, arithmetic and copies ran while one was open for 0% -> 0% of each run, Pallas kernels for 18% -> 19%
where the time goes in v6:
time: 57.1 us; the launch traced here: 56.9 us
  starting transfers between devices  25.8 us (45%)
  Pallas kernels  19.4 us (34%)
  waiting for transfers between devices  9.64 us (17%)
  local copies, waits for them, and re-layouts  1.06 us (2%)
  between operations  0.91 us (2%)
    ppermute x16, starting transfers between devices, move(): return lax.ppermute(values, 'sp', pairs)  25.8 us
    ppermute x16, waiting for transfers between devices, move(): return lax.ppermute(values, 'sp', pairs)  9.64 us
    pallas_call x1, Pallas kernels, kernel_shards(): call(up_kernel, [SMEM] + [VMEM] * 15, [shape(rows, width)] + [shape(own +...  3.89 us
    pallas_call x1, Pallas kernels, kernel_shards(): call(coarse_kernel, [VMEM] * (8 + peers // 2), [shape(full, LANES), shape...  3 us
    pallas_call x1, Pallas kernels, kernel_shards(): call(functools.partial(near_kernel, edges), [VMEM] * 2 + [HBM] * 3 + [VME...  2.4 us
    pallas_call x1, Pallas kernels, kernel_shards(): call(functools.partial(edges_kernel, degree, count), [SMEM] + [VMEM] * (1...  1.9 us
    pallas_call x1, Pallas kernels, kernel_shards(): call(far_kernel, [SMEM] + [VMEM] * 8, [shape(full, LANES), shape(rim, LAN...  1.89 us
    pallas_call x1, Pallas kernels, kernel_shards(): call(functools.partial(start_kernel, count, HALO), [SMEM] + [HBM] * 10, [...  1.71 us
  transfers between devices with their start and end apart: 16, of which 7 were waited for; matrix products, arithmetic and copies ran while one was open for 0% of the time, Pallas kernels for 19%

profile of v6, /device:TPU:0, one launch (start us, length us, event | category | flops | bytes accessed | tf_op | source)
XLA Modules:
  0.0 56.9 jit_solution(9292119819929008992)
XLA Ops:
  0.7 1.0 %constant_dynamic-slice_fusion = (f32[256,128]{1,0:T(8,128)S(1)}, f32[256,128]{1,0:T(8,128)S(1)}) fusion(f32[512,128]{1,0:T(8,128)} %bitcast.15, s32[]{:T(128)S(6)} %select_n.19, s32[]{:T(128)S(6)} %select_n.18), kind=kLoop, calls=%fused_computation.1 | loop fusion | bytes 524296 | tf_op jit(solution)/shard_map/dynamic_slice | solution.py:614
  1.6 3.0 %collective-permute-start = (f32[256,128]{1,0:T(8,128)S(1)}, f32[256,128]{1,0:T(8,128)S(1)}, u32[]{:S(2)}, u32[]{:S(2)}) collective-permute-start(f32[256,128]{1,0:T(8,128)S(1)} %get-tuple-element.73), channel_id=1, source_target_pairs={{0,2},{2,0},{4,6},{6,4},{8,10},{10,8},{12,14},{14,12},{1,3},{3,1},... | collective-permute-start | bytes 393224 | tf_op jit(solution)/shard_map/ppermute | solution.py:555
  4.7 3.6 %collective-permute-start.1 = (f32[256,128]{1,0:T(8,128)S(1)}, f32[256,128]{1,0:T(8,128)S(1)}, u32[]{:S(2)}, u32[]{:S(2)}) collective-permute-start(f32[256,128]{1,0:T(8,128)S(1)} %get-tuple-element.72), channel_id=1, source_target_pairs={{0,14},{2,4},{4,2},{6,8},{8,6},{10,12},{12,10},{14,0},{1,15},{3,5}... | collective-permute-start | bytes 393224 | tf_op jit(solution)/shard_map/ppermute | solution.py:555
  8.3 0.1 pad_add_fusion.place_ref
  8.3 1.7 %shard_map.212 = (f32[512,128]{1,0:T(8,128)S(1)}, f32[16,128]{1,0:T(8,128)S(1)}, f32[8,256]{1,0:T(8,128)S(1)}) custom-call(s32[2]{0:T(128)S(1)} %pad_add_fusion.place_ref, f32[512,128]{1,0:T(8,128)} %bitcast.16, s32[8,128]{1,0:T(8,128)} %bitcast.17, s32[2,128]{1,0:T(2,128)} %bitcast.18, s32[2,128]{1,0:T(2,128)} %bitcast.19, s32[2,128]{1,0:T(2,128)} %bitcast.20, ...), custom_call_target="tpu_custom_call" | custom-call | tf_op jit(solution)/shard_map/pallas_call | solution.py:617
  10.0 2.4 %shard_map.213 = (bf16[1024,512]{1,0:T(8,128)(2,1)S(1)}, f32[1024,256]{1,0:T(8,128)S(1)}, f32[256,256]{1,0:T(8,128)S(1)}, bf16[512,256]{1,0:T(8,128)(2,1)S(1)}, bf16[512,256]{1,0:T(8,128)(2,1)S(1)}) custom-call(f32[512,128]{1,0:T(8,128)S(1)} %get-tuple-element.36.state_ref, f32[16,128]{1,0:T(8,128)S(1)} %get-tuple-element.37.ints_ref, ...), custom_call_target="tpu_custom_call" | custom-call | tf_op jit(solution)/shard_map/pallas_call | solution.py:624
  12.5 1.9 %shard_map.214 = (f32[512,128]{1,0:T(8,128)S(1)}, f32[256,128]{1,0:T(8,128)S(1)}) custom-call(s32[2]{0:T(128)S(1)} %pad_add_fusion.place_ref, f32[256,128]{1,0:T(8,128)S(1)} %collective-permute-done.swap_ref, f32[256,128]{1,0:T(8,128)S(1)} %collective-permute-done.1.diag_ref, f32[512,128]{1,0:T(8,128)S(1)} %get-tuple-element.36.state_ref, ...), custom_call_target="tpu_custom_call" | custom-call | tf_op jit(solution)/shard_map/pallas_call | solution.py:631
  14.4 0.3 collective-permute-start.2
  14.7 3.7 %collective-permute-start.3 = (f32[256,128]{1,0:T(8,128)S(1)}, f32[256,128]{1,0:T(8,128)S(1)}, u32[]{:S(2)}, u32[]{:S(2)}) collective-permute-start(f32[256,128]{1,0:T(8,128)S(1)} %get-tuple-element.45), channel_id=1, source_target_pairs={{0,12},{2,6},{4,0},{6,10},{8,4},{10,14},{12,8},{14,2},{1,13},{3,7}... | collective-permute-start | bytes 393224 | tf_op jit(solution)/shard_map/ppermute | solution.py:555
  18.5 1.3 %collective-permute-start.4 = (f32[256,128]{1,0:T(8,128)S(1)}, f32[256,128]{1,0:T(8,128)S(1)}, u32[]{:S(2)}, u32[]{:S(2)}) collective-permute-start(f32[256,128]{1,0:T(8,128)S(1)} %get-tuple-element.45), channel_id=1, source_target_pairs={{0,14},{2,4},{4,2},{6,8},{8,6},{10,12},{12,10},{14,0},{1,15},{3,5}... | collective-permute-start | bytes 393224 | tf_op jit(solution)/shard_map/ppermute | solution.py:555
  19.8 3.7 %collective-permute-done.5.ints0_ref = f32[16,128]{1,0:T(8,128)S(1)} collective-permute-done((f32[16,128]{1,0:T(8,128)S(1)}, f32[16,128]{1,0:T(8,128)S(1)}, u32[]{:S(2)}, u32[]{:S(2)}) %collective-permute-start.5) | collective-permute-done | bytes 8224 | tf_op jit(solution)/shard_map/ppermute | solution.py:555
  23.6 1.7 %shard_map.215 = (f32[1024,256]{1,0:T(8,128)S(1)}, f32[256,256]{1,0:T(8,128)S(1)}, bf16[256,256]{1,0:T(8,128)(2,1)S(1)}, bf16[256,256]{1,0:T(8,128)(2,1)S(1)}, b...) custom-call(s32[2]{0:T(128)S(1)} %pad_add_fusion.place_ref, ...), custom_call_target="tpu_custom_call" | custom-call | tf_op jit(solution)/shard_map/pallas_call | solution.py:637
  25.3 0.9 %collective-permute-done.4.diag_ref = f32[256,128]{1,0:T(8,128)S(1)} collective-permute-done((f32[256,128]{1,0:T(8,128)S(1)}, f32[256,128]{1,0:T(8,128)S(1)}, u32[]{:S(2)}, u32[]{:S(2)}) %collective-permute-start.4) | collective-permute-done | bytes 131104 | tf_op jit(solution)/shard_map/ppermute | solution.py:555
  26.1 1.5 %shard_map.216 = (f32[1024,256]{1,0:T(8,128)S(1)}, bf16[128,256]{1,0:T(8,128)(2,1)S(1)}, bf16[128,256]{1,0:T(8,128)(2,1)S(1)}) custom-call(s32[2]{0:T(128)S(1)} %pad_add_fusion.place_ref, f32[256,128]{1,0:T(8,128)S(1)} %collective-permute-done.3.pair_ref, f32[256,128]{1,0:T(8,128)S(1)} %collective-permute-done.4.diag_ref, ...), custom_call_target="tpu_custom_call" | custom-call | tf_op jit(solution)/shard_map/pallas_call | solution.py:649
  27.7 3.9 %shard_map.217 = (f32[256,256]{1,0:T(8,128)S(1)}, f32[136,128]{1,0:T(8,128)S(1)}, f32[136,128]{1,0:T(8,128)S(1)}, f32[136,128]{1,0:T(8,128)S(1)}, f32[136,128]{1,0:T(8,128)S(1)}) custom-call(s32[2]{0:T(128)S(1)} %pad_add_fusion.place_ref, f32[512,128]{1,0:T(8,128)S(1)} %collective-permute-done.2.swap_ref, ...), custom_call_target="tpu_custom_call" | custom-call | tf_op jit(solution)/shard_map/pallas_call | solution.py:654
  31.6 0.4 collective-permute-start.6
  32.1 2.2 %collective-permute-start.7 = (f32[136,128]{1,0:T(8,128)S(1)}, f32[136,128]{1,0:T(8,128)S(1)}, u32[]{:S(2)}, u32[]{:S(2)}) collective-permute-start(f32[136,128]{1,0:T(8,128)S(1)} %get-tuple-element.60), channel_id=1, source_target_pairs={{0,8},{2,10},{4,12},{6,14},{8,0},{10,2},{12,4},{14,6},{1,9},{3,11}... | collective-permute-start | bytes 208904 | tf_op jit(solution)/shard_map/ppermute | solution.py:555
  34.2 1.9 %collective-permute-start.8 = (f32[136,128]{1,0:T(8,128)S(1)}, f32[136,128]{1,0:T(8,128)S(1)}, u32[]{:S(2)}, u32[]{:S(2)}) collective-permute-start(f32[136,128]{1,0:T(8,128)S(1)} %get-tuple-element.61), channel_id=1, source_target_pairs={{0,12},{2,14},{4,8},{6,10},{8,4},{10,6},{12,0},{14,2},{1,13},{3,15... | collective-permute-start | bytes 208904 | tf_op jit(solution)/shard_map/ppermute | solution.py:555
  36.1 0.5 collective-permute-done.6.refs_1_
  36.6 0.7 %collective-permute-done.7.refs_2_ = f32[136,128]{1,0:T(8,128)S(1)} collective-permute-done((f32[136,128]{1,0:T(8,128)S(1)}, f32[136,128]{1,0:T(8,128)S(1)}, u32[]{:S(2)}, u32[]{:S(2)}) %collective-permute-start.7) | collective-permute-done | bytes 69664 | tf_op jit(solution)/shard_map/ppermute | solution.py:555
  37.3 3.7 %collective-permute-done.8.refs_3_ = f32[136,128]{1,0:T(8,128)S(1)} collective-permute-done((f32[136,128]{1,0:T(8,128)S(1)}, f32[136,128]{1,0:T(8,128)S(1)}, u32[]{:S(2)}, u32[]{:S(2)}) %collective-permute-start.8) | collective-permute-done | bytes 69664 | tf_op jit(solution)/shard_map/ppermute | solution.py:555
  41.0 0.1 collective-permute-start.9
  41.1 2.5 %collective-permute-start.10 = (f32[128,128]{1,0:T(8,128)S(1)}, f32[128,128]{1,0:T(8,128)S(1)}, u32[]{:S(2)}, u32[]{:S(2)}) collective-permute-start(f32[128,128]{1,0:T(8,128)S(1)} %shard_map.220.refs_0_), channel_id=1, source_target_pairs={{0,8},{2,10},{4,12},{6,14},{8,0},{10,2},{12,4},{14,6},{1,9},{3,11}... | collective-permute-start | bytes 196616 | tf_op jit(solution)/shard_map/ppermute | solution.py:555
  43.6 1.9 %collective-permute-start.11 = (f32[128,128]{1,0:T(8,128)S(1)}, f32[128,128]{1,0:T(8,128)S(1)}, u32[]{:S(2)}, u32[]{:S(2)}) collective-permute-start(f32[128,128]{1,0:T(8,128)S(1)} %shard_map.220.refs_0_), channel_id=1, source_target_pairs={{0,12},{2,14},{4,8},{6,10},{8,4},{10,6},{12,0},{14,2},{1,13},{3,15... | collective-permute-start | bytes 196616 | tf_op jit(solution)/shard_map/ppermute | solution.py:555
  45.5 2.1 %collective-permute-start.12 = (f32[128,128]{1,0:T(8,128)S(1)}, f32[128,128]{1,0:T(8,128)S(1)}, u32[]{:S(2)}, u32[]{:S(2)}) collective-permute-start(f32[128,128]{1,0:T(8,128)S(1)} %shard_map.220.refs_0_), channel_id=1, source_target_pairs={{0,2},{2,0},{4,6},{6,4},{8,10},{10,8},{12,14},{14,12},{1,3},{3,1},... | collective-permute-start | bytes 196616 | tf_op jit(solution)/shard_map/ppermute | solution.py:555
  47.6 2.0 %collective-permute-start.14 = (f32[128,128]{1,0:T(8,128)S(1)}, f32[128,128]{1,0:T(8,128)S(1)}, u32[]{:S(2)}, u32[]{:S(2)}) collective-permute-start(f32[128,128]{1,0:T(8,128)S(1)} %collective-permute-done.10.refs_2_), channel_id=1, source_target_pairs={{0,2},{2,0},{4,6},{6,4},{8,10},{10,8},{12,14},{14,12},{1,3},{3,1},... | collective-permute-start | bytes 196616 | tf_op jit(solution)/shard_map/ppermute | solution.py:555
  49.6 0.9 %collective-permute-start.15 = (f32[128,128]{1,0:T(8,128)S(1)}, f32[128,128]{1,0:T(8,128)S(1)}, u32[]{:S(2)}, u32[]{:S(2)}) collective-permute-start(f32[128,128]{1,0:T(8,128)S(1)} %collective-permute-done.11.refs_3_), channel_id=1, source_target_pairs={{0,2},{2,0},{4,6},{6,4},{8,10},{10,8},{12,14},{14,12},{1,3},{3,1},... | collective-permute-start | bytes 196616 | tf_op jit(solution)/shard_map/ppermute | solution.py:555
  50.5 0.2 shard_map.219
  50.7 1.9 %shard_map.218 = (bf16[1280,512]{1,0:T(8,128)(2,1)S(1)}, bf16[256,512]{1,0:T(8,128)(2,1)S(1)}) custom-call(s32[2]{0:T(128)S(1)} %pad_add_fusion.place_ref, f32[16,128]{1,0:T(8,128)S(1)} %get-tuple-element.37.ints_ref, f32[136,128]{1,0:T(8,128)S(1)} %get-tuple-element.58.refs_0_, f32[136,128]{1,0:T(8,128)S(1)} %collective-permute-done.6.refs_1_, ...), custom_call_target="tpu_custom_call" | custom-call | tf_op jit(solution)/shard_map/pallas_call | solution.py:671
  52.6 1.2 %shard_map.221 = (f32[1280,256]{1,0:T(8,128)S(1)}, f32[320,256]{1,0:T(8,128)S(1)}) custom-call(bf16[1280,512]{1,0:T(8,128)(2,1)S(1)} %get-tuple-element.62.hot_ref, bf16[256,512]{1,0:T(8,128)(2,1)S(1)} %get-tuple-element.63.parent_ref, bf16[1280,256]{1,0:T(8,128)(2,1)S(1)} %get-tuple-element.64.high_ref, bf16[1280,256]{1,0:T(8,128)(2,1)S(1)} %get-tuple-element.65.low_ref, ...), custom_call_target="tpu_custom_call" | custom-call | tf_op jit(solution)/shard_map/pallas_call | solution.py:683
  53.8 0.1 collective-permute-done.15.refs_3_
  53.9 3.0 %shard_map.222 = (f32[512,128]{1,0:T(8,128)}, f32[128,128]{1,0:T(8,128)}) custom-call(f32[256,256]{1,0:T(8,128)S(1)} %get-tuple-element.57.last_ref, bf16[1280,512]{1,0:T(8,128)(2,1)S(1)} %get-tuple-element.62.hot_ref, bf16[256,512]{1,0:T(8,128)(2,1)S(1)} %get-tuple-element.63.parent_ref, f32[1280,256]{1,0:T(8,128)S(1)} %get-tuple-element.66.got_ref, ...), custom_call_target="tpu_custom_call" | custom-call | tf_op jit(solution)/shard_map/pallas_call | solution.py:688
  (35 shorter events, 0.2 us)
Async XLA Ops:
  1.6 10.8 %collective-permute-start = (f32[256,128]{1,0:T(8,128)S(1)}, f32[256,128]{1,0:T(8,128)S(1)}, u32[]{:S(2)}, u32[]{:S(2)}) collective-permute-start(f32[256,128]{1,0:T(8,128)S(1)} %get-tuple-element.73), channel_id=1, source_target_pairs={{0,2},{2,0},{4,6},{6,4},{8,10},{10,8},{12,14},{14,12},{1,3},{3,1},... | collective-permute-start | bytes 393224 | tf_op jit(solution)/shard_map/ppermute | solution.py:555
  4.7 7.8 %collective-permute-start.1 = (f32[256,128]{1,0:T(8,128)S(1)}, f32[256,128]{1,0:T(8,128)S(1)}, u32[]{:S(2)}, u32[]{:S(2)}) collective-permute-start(f32[256,128]{1,0:T(8,128)S(1)} %get-tuple-element.72), channel_id=1, source_target_pairs={{0,14},{2,4},{4,2},{6,8},{8,6},{10,12},{12,10},{14,0},{1,15},{3,5}... | collective-permute-start | bytes 393224 | tf_op jit(solution)/shard_map/ppermute | solution.py:555
  12.5 11.1 %copy-start = (f32[2,256,256]{2,1,0:T(8,128)S(1)}, f32[2,256,256]{2,1,0:T(8,128)}, u32[]{:S(2)}) copy-start(f32[2,256,256]{2,1,0:T(8,128)} %ws_ref.1) | copy-start | bytes 1572868
  12.5 11.0 %copy-start.1 = (f32[2,256,256]{2,1,0:T(8,128)S(1)}, f32[2,256,256]{2,1,0:T(8,128)}, u32[]{:S(2)}) copy-start(f32[2,256,256]{2,1,0:T(8,128)} %wr_ref.1) | copy-start | bytes 1572868
  12.5 11.0 %copy-start.2 = (f32[2,256,256]{2,1,0:T(8,128)S(1)}, f32[2,256,256]{2,1,0:T(8,128)}, u32[]{:S(2)}) copy-start(f32[2,256,256]{2,1,0:T(8,128)} %wo_ref.1) | copy-start | bytes 1572868
  12.5 11.0 %copy-start.3 = (f32[256,256]{1,0:T(8,128)S(1)}, f32[256,256]{1,0:T(8,128)}, u32[]{:S(2)}) copy-start(f32[256,256]{1,0:T(8,128)} %wi_ref.1) | copy-start | bytes 786436
  12.5 11.0 %copy-start.4 = (f32[256,256]{1,0:T(8,128)S(1)}, f32[256,256]{1,0:T(8,128)}, u32[]{:S(2)}) copy-start(f32[256,256]{1,0:T(8,128)} %wu_ref.1) | copy-start | bytes 786436
  14.4 13.2 %collective-permute-start.2 = (f32[512,128]{1,0:T(8,128)S(1)}, f32[512,128]{1,0:T(8,128)S(1)}, u32[]{:S(2)}, u32[]{:S(2)}) collective-permute-start(f32[512,128]{1,0:T(8,128)S(1)} %get-tuple-element.44.state_ref), channel_id=1, source_target_pairs={{0,2},{2,0},{4,6},{6,4},{8,10},{10,8},{12,14},{14,12},{1,3},{3,1},... | collective-permute-start | bytes 786440 | tf_op jit(solution)/shard_map/ppermute | solution.py:555
  14.7 10.5 %collective-permute-start.3 = (f32[256,128]{1,0:T(8,128)S(1)}, f32[256,128]{1,0:T(8,128)S(1)}, u32[]{:S(2)}, u32[]{:S(2)}) collective-permute-start(f32[256,128]{1,0:T(8,128)S(1)} %get-tuple-element.45), channel_id=1, source_target_pairs={{0,12},{2,6},{4,0},{6,10},{8,4},{10,14},{12,8},{14,2},{1,13},{3,7}... | collective-permute-start | bytes 393224 | tf_op jit(solution)/shard_map/ppermute | solution.py:555
  18.5 7.7 %collective-permute-start.4 = (f32[256,128]{1,0:T(8,128)S(1)}, f32[256,128]{1,0:T(8,128)S(1)}, u32[]{:S(2)}, u32[]{:S(2)}) collective-permute-start(f32[256,128]{1,0:T(8,128)S(1)} %get-tuple-element.45), channel_id=1, source_target_pairs={{0,14},{2,4},{4,2},{6,8},{8,6},{10,12},{12,10},{14,0},{1,15},{3,5}... | collective-permute-start | bytes 393224 | tf_op jit(solution)/shard_map/ppermute | solution.py:555
  19.8 3.7 %collective-permute-start.5 = (f32[16,128]{1,0:T(8,128)S(1)}, f32[16,128]{1,0:T(8,128)S(1)}, u32[]{:S(2)}, u32[]{:S(2)}) collective-permute-start(f32[16,128]{1,0:T(8,128)S(1)} %get-tuple-element.37.ints_ref), channel_id=1, source_target_pairs={{0,2},{2,0},{4,6},{6,4},{8,10},{10,8},{12,14},{14,12},{1,3},{3,1},... | collective-permute-start | bytes 24584 | tf_op jit(solution)/shard_map/ppermute | solution.py:555
  27.7 13.3 %copy-start.10 = (f32[64,1,256]{2,1,0:T(1,128)S(1)}, f32[64,1,256]{2,1,0:T(1,128)}, u32[]{:S(2)}) copy-start(f32[64,1,256]{2,1,0:T(1,128)} %param.22) | copy-start | bytes 196612
  27.7 22.8 %copy-start.5 = (f32[256,256]{1,0:T(8,128)S(1)}, f32[256,256]{1,0:T(8,128)}, u32[]{:S(2)}) copy-start(f32[256,256]{1,0:T(8,128)} %cs_ref.1) | copy-start | bytes 786436
  27.7 22.8 %copy-start.6 = (f32[256,256]{1,0:T(8,128)S(1)}, f32[256,256]{1,0:T(8,128)}, u32[]{:S(2)}) copy-start(f32[256,256]{1,0:T(8,128)} %cr_ref.1) | copy-start | bytes 786436
  27.7 22.8 %copy-start.7 = (f32[256,256]{1,0:T(8,128)S(1)}, f32[256,256]{1,0:T(8,128)}, u32[]{:S(2)}) copy-start(f32[256,256]{1,0:T(8,128)} %co_ref.1) | copy-start | bytes 786436
  27.7 22.8 %copy-start.8 = (f32[256,256]{1,0:T(8,128)S(1)}, f32[256,256]{1,0:T(8,128)}, u32[]{:S(2)}) copy-start(f32[256,256]{1,0:T(8,128)} %di_ref.1) | copy-start | bytes 786436
  27.7 22.8 %copy-start.9 = (f32[256,256]{1,0:T(8,128)S(1)}, f32[256,256]{1,0:T(8,128)}, u32[]{:S(2)}) copy-start(f32[256,256]{1,0:T(8,128)} %do_ref.1) | copy-start | bytes 786436
  31.6 4.9 %collective-permute-start.6 = (f32[136,128]{1,0:T(8,128)S(1)}, f32[136,128]{1,0:T(8,128)S(1)}, u32[]{:S(2)}, u32[]{:S(2)}) collective-permute-start(f32[136,128]{1,0:T(8,128)S(1)} %get-tuple-element.59), channel_id=1, source_target_pairs={{0,4},{2,6},{4,0},{6,2},{8,12},{10,14},{12,8},{14,10},{1,5},{3,7},... | collective-permute-start | bytes 208904 | tf_op jit(solution)/shard_map/ppermute | solution.py:555
  32.1 5.2 %collective-permute-start.7 = (f32[136,128]{1,0:T(8,128)S(1)}, f32[136,128]{1,0:T(8,128)S(1)}, u32[]{:S(2)}, u32[]{:S(2)}) collective-permute-start(f32[136,128]{1,0:T(8,128)S(1)} %get-tuple-element.60), channel_id=1, source_target_pairs={{0,8},{2,10},{4,12},{6,14},{8,0},{10,2},{12,4},{14,6},{1,9},{3,11}... | collective-permute-start | bytes 208904 | tf_op jit(solution)/shard_map/ppermute | solution.py:555
  34.2 6.7 %collective-permute-start.8 = (f32[136,128]{1,0:T(8,128)S(1)}, f32[136,128]{1,0:T(8,128)S(1)}, u32[]{:S(2)}, u32[]{:S(2)}) collective-permute-start(f32[136,128]{1,0:T(8,128)S(1)} %get-tuple-element.61), channel_id=1, source_target_pairs={{0,12},{2,14},{4,8},{6,10},{8,4},{10,6},{12,0},{14,2},{1,13},{3,15... | collective-permute-start | bytes 208904 | tf_op jit(solution)/shard_map/ppermute | solution.py:555
  41.0 6.5 %collective-permute-start.9 = (f32[128,128]{1,0:T(8,128)S(1)}, f32[128,128]{1,0:T(8,128)S(1)}, u32[]{:S(2)}, u32[]{:S(2)}) collective-permute-start(f32[128,128]{1,0:T(8,128)S(1)} %shard_map.220.refs_0_), channel_id=1, source_target_pairs={{0,4},{2,6},{4,0},{6,2},{8,12},{10,14},{12,8},{14,10},{1,5},{3,7},... | collective-permute-start | bytes 196616 | tf_op jit(solution)/shard_map/ppermute | solution.py:555
  41.1 6.5 %collective-permute-start.10 = (f32[128,128]{1,0:T(8,128)S(1)}, f32[128,128]{1,0:T(8,128)S(1)}, u32[]{:S(2)}, u32[]{:S(2)}) collective-permute-start(f32[128,128]{1,0:T(8,128)S(1)} %shard_map.220.refs_0_), channel_id=1, source_target_pairs={{0,8},{2,10},{4,12},{6,14},{8,0},{10,2},{12,4},{14,6},{1,9},{3,11}... | collective-permute-start | bytes 196616 | tf_op jit(solution)/shard_map/ppermute | solution.py:555
  43.6 6.1 %collective-permute-start.11 = (f32[128,128]{1,0:T(8,128)S(1)}, f32[128,128]{1,0:T(8,128)S(1)}, u32[]{:S(2)}, u32[]{:S(2)}) collective-permute-start(f32[128,128]{1,0:T(8,128)S(1)} %shard_map.220.refs_0_), channel_id=1, source_target_pairs={{0,12},{2,14},{4,8},{6,10},{8,4},{10,6},{12,0},{14,2},{1,13},{3,15... | collective-permute-start | bytes 196616 | tf_op jit(solution)/shard_map/ppermute | solution.py:555
  45.5 8.3 %collective-permute-start.12 = (f32[128,128]{1,0:T(8,128)S(1)}, f32[128,128]{1,0:T(8,128)S(1)}, u32[]{:S(2)}, u32[]{:S(2)}) collective-permute-start(f32[128,128]{1,0:T(8,128)S(1)} %shard_map.220.refs_0_), channel_id=1, source_target_pairs={{0,2},{2,0},{4,6},{6,4},{8,10},{10,8},{12,14},{14,12},{1,3},{3,1},... | collective-permute-start | bytes 196616 | tf_op jit(solution)/shard_map/ppermute | solution.py:555
  47.5 6.3 %collective-permute-start.13 = (f32[128,128]{1,0:T(8,128)S(1)}, f32[128,128]{1,0:T(8,128)S(1)}, u32[]{:S(2)}, u32[]{:S(2)}) collective-permute-start(f32[128,128]{1,0:T(8,128)S(1)} %collective-permute-done.9.refs_1_), channel_id=1, source_target_pairs={{0,2},{2,0},{4,6},{6,4},{8,10},{10,8},{12,14},{14,12},{1,3},{3,1},... | collective-permute-start | bytes 196616 | tf_op jit(solution)/shard_map/ppermute | solution.py:555
  47.6 6.3 %collective-permute-start.14 = (f32[128,128]{1,0:T(8,128)S(1)}, f32[128,128]{1,0:T(8,128)S(1)}, u32[]{:S(2)}, u32[]{:S(2)}) collective-permute-start(f32[128,128]{1,0:T(8,128)S(1)} %collective-permute-done.10.refs_2_), channel_id=1, source_target_pairs={{0,2},{2,0},{4,6},{6,4},{8,10},{10,8},{12,14},{14,12},{1,3},{3,1},... | collective-permute-start | bytes 196616 | tf_op jit(solution)/shard_map/ppermute | solution.py:555
  49.6 4.3 %collective-permute-start.15 = (f32[128,128]{1,0:T(8,128)S(1)}, f32[128,128]{1,0:T(8,128)S(1)}, u32[]{:S(2)}, u32[]{:S(2)}) collective-permute-start(f32[128,128]{1,0:T(8,128)S(1)} %collective-permute-done.11.refs_3_), channel_id=1, source_target_pairs={{0,2},{2,0},{4,6},{6,4},{8,10},{10,8},{12,14},{14,12},{1,3},{3,1},... | collective-permute-start | bytes 196616 | tf_op jit(solution)/shard_map/ppermute | solution.py:555

commit v7 on v6

--- a/solution.py
+++ b/solution.py
@@ -177,6 +177,10 @@
     return mm(one_hot, high) + mm(one_hot, low)
 
 
+def place():
+    return lax.axis_index("sp").astype(jnp.int32)
+
+
 def unit(values):
     width = values.shape[1]
     average = jnp.sum(values, axis=1, keepdims=True) * (1.0 / width)
@@ -227,13 +231,13 @@
 
 
 def start_kernel(
-    count, halo, place_ref, state_hbm, sender_hbm, owner_hbm, local_hbm, cowner_hbm,
+    count, halo, state_hbm, sender_hbm, owner_hbm, local_hbm, cowner_hbm,
     clocal_hbm, fb_hbm, ub_hbm, cb_hbm, db_hbm,
     state_ref, ints_ref, pack_ref,
     sender_ref, owner_ref, local_ref, cowner_ref, clocal_ref, fb_ref, ub_ref, cb_ref, db_ref,
     sems,
 ):
-    odd = place_ref[0]
+    odd = place() % 2
     pairs = [
         (sender_hbm, sender_ref),
         (owner_hbm, owner_ref),
@@ -298,7 +302,7 @@
 
 
 def far_kernel(
-    place_ref, swap_ref, diag_ref, state_ref, hot_ref, got_ref, into_ref, high_ref, low_ref,
+    swap_ref, diag_ref, ints0_ref, state_ref, hot_ref, got_ref, into_ref, high_ref, low_ref,
     out_full_ref, out_half_ref,
 ):
     rows, width = into_ref.shape
@@ -320,12 +324,12 @@
         parts,
     )
     lines = out_half_ref.shape[0]
-    start = pl.multiple_of(place_ref[0] * (rows * parts - lines), LANES)
+    start = pl.multiple_of(place() % 2 * (rows * parts - lines), LANES)
     out_half_ref[...] = out_full_ref[pl.ds(start, lines), :]
 
 
 def near2_kernel(
-    edges, count, place_ref, state_ref, ints_ref, ints0_ref, hot_ref, ws_ref, wr_ref, wo_ref, wi_ref,
+    edges, count, state_ref, ints_ref, ints0_ref, hot_ref, ws_ref, wr_ref, wo_ref, wi_ref,
     wu_ref, pack_ref,
     got_ref, into_ref, own_high_ref, own_low_ref, hot2_ref, select_ref, high_ref, low_ref,
     turn_ref,
@@ -343,7 +347,7 @@
     own_low_ref[...] = low
     got_ref[...] = take(hot_ref[:, :rows], high, low)
     edge_hot(hot2_ref, turn_ref, ints0_ref[:senders, :], edges // rows, rows)
-    flip = place_ref[1]
+    flip = place() * count
     line = senders
     for half, ref in ((0, ints_ref), (1, ints0_ref)):
         for j in range(rows // LANES):
@@ -357,56 +361,43 @@
             )
 
 
-def halo_kernel(
-    place_ref, pair_ref, diag_ref, own_high_ref, own_low_ref, hot2_ref, high_ref, low_ref,
-    got2_ref, diag_high_ref, diag_low_ref,
-):
-    rim, width = diag_high_ref.shape
-    rows = own_high_ref.shape[0]
-    parts = width // LANES
-    mine = pl.multiple_of((1 - place_ref[0]) * (rows - rim), LANES)
-    normed = unit(
-        jnp.concatenate(
-            [load_rows(pair_ref, rim, parts), load_rows(diag_ref, rim, parts)], axis=0
-        )
-    )
-    high, low = halves(times(normed, *weights(high_ref, low_ref, 0)) * 0.5)
-    diag_high_ref[...] = high[rim:, :]
-    diag_low_ref[...] = low[rim:, :]
-    got2_ref[...] = take(
-        hot2_ref[:, rows:],
-        jnp.concatenate([own_high_ref[pl.ds(mine, rim), :], high[:rim, :]], axis=0),
-        jnp.concatenate([own_low_ref[pl.ds(mine, rim), :], low[:rim, :]], axis=0),
-    )
-
-
 def up_kernel(
-    place_ref, swap_ref, diag_high_ref, diag_low_ref, state_ref, hot_ref, got_ref, into_ref,
-    hot2_ref, got2_ref, select_ref, ints_ref, ints0_ref, high_ref, low_ref, pack_ref,
+    swap_ref, pair_ref, diag_ref, state_ref, hot_ref, got_ref, into_ref, own_high_ref,
+    own_low_ref, hot2_ref, select_ref, ints_ref, ints0_ref, high_ref, low_ref, pack_ref,
     last_ref, *refs,
 ):
     *slot_refs, th_ref, tl_ref = refs
     rows, width = into_ref.shape
     parts = width // LANES
-    rim = diag_high_ref.shape[0]
+    rim = diag_ref.shape[0] // parts
     degree = hot_ref.shape[0] // rows
-    theirs = pl.multiple_of(place_ref[0] * (rows - rim), LANES)
+    odd = place() % 2
+    mine = pl.multiple_of((1 - odd) * (rows - rim), LANES)
+    theirs = pl.multiple_of(odd * (rows - rim), LANES)
     other = load_rows(swap_ref, rows, parts)
-    normed = unit(other)
-    high, low = halves(times(normed, *weights(high_ref, low_ref, 0)) * 0.5)
-    th_ref[...] = high
-    tl_ref[...] = low
-    near = (
-        jnp.concatenate([th_ref[pl.ds(theirs, rim), :], diag_high_ref[...]], axis=0),
-        jnp.concatenate([tl_ref[pl.ds(theirs, rim), :], diag_low_ref[...]], axis=0),
-    )
-    into = (times(normed, *weights(high_ref, low_ref, 1)) + pack_ref[1:2, :]) * 0.5
+    normed = unit(
+        jnp.concatenate(
+            [other, load_rows(pair_ref, rim, parts), load_rows(diag_ref, rim, parts)], axis=0
+        )
+    )
+    sends = halves(times(normed, *weights(high_ref, low_ref, 0)) * 0.5)
+    near = []
+    for src, t_ref, own_ref in (
+        (sends[0], th_ref, own_high_ref), (sends[1], tl_ref, own_low_ref),
+    ):
+        t_ref[:rows, :] = src[:rows, :]
+        t_ref[rows : rows + rim, :] = own_ref[pl.ds(mine, rim), :]
+        t_ref[rows + rim :, :] = src[rows : rows + rim, :]
+        near.append(
+            jnp.concatenate([t_ref[pl.ds(theirs, rim), :], src[rows + rim :, :]], axis=0)
+        )
+    into = (times(normed[:rows, :], *weights(high_ref, low_ref, 1)) + pack_ref[1:2, :]) * 0.5
     total, total2 = None, None
     for k in range(degree):
         part = slice(k * rows, (k + 1) * rows)
         half = got_ref[part, :] + into_ref[...] + take(hot_ref[part, rows:], *near)
         total = gate(half) if total is None else total + gate(half)
-        half = got2_ref[part, :] + into + take(hot2_ref[part, :rows], high, low)
+        half = into + take(hot2_ref[part, :], th_ref[...], tl_ref[...])
         total2 = gate(half) if total2 is None else total2 + gate(half)
     hidden = jnp.concatenate([load_rows(state_ref, rows, parts), other], axis=0) + times(
         jnp.concatenate([total, total2], axis=0), *weights(high_ref, low_ref, 2)
@@ -453,10 +444,10 @@
     )
 
 
-def edges_kernel(degree, count, place_ref, ints_ref, *refs):
+def edges_kernel(degree, count, ints_ref, *refs):
     *slot_refs, hot_ref, parent_ref, turn_ref = refs
     rows, coarse = parent_ref.shape
-    flip = place_ref[1]
+    flip = place() * count
     columns = turned(ints_ref[...])
     first = ints_ref.shape[0] // 2
     for j in range(rows // LANES):
@@ -506,7 +497,7 @@
 def coarse_kernel(
     last_ref, hot_ref, parent_ref, got_ref, wanted_ref, high_ref, low_ref, pack_ref, *refs
 ):
-    *blocks, fine_ref, coarse_ref = refs
+    *blocks, fine_hbm, coarse_hbm, fine_ref, coarse_ref, sems = refs
     rows, width = last_ref.shape
     parts = width // LANES
     count = coarse_ref.shape[0] // parts
@@ -529,10 +520,22 @@
         total = term if total is None else total + term
     done = wanted + times(total, *weights(high_ref, low_ref, 2))
     store_rows(coarse_ref, done[:count, :], parts)
+    copies = [pltpu.make_async_copy(coarse_ref, coarse_hbm, sems.at[0])]
+    copies[0].start()
     act = gate(
         (times(unit(done[count:, :]), *weights(high_ref, low_ref, 3)) + pack_ref[4:5, :]) * 0.5
     )
-    store_rows(fine_ref, last_ref[...] + times(act, *weights(high_ref, low_ref, 4)), parts)
+    size = rows // 2
+    for j in range(2):
+        down = times(act[j * size : (j + 1) * size, :], *weights(high_ref, low_ref, 4))
+        store_rows(fine_ref, last_ref[j * size : (j + 1) * size, :] + down, parts, j * size)
+        piece = pl.ds(j * size * parts, size * parts)
+        copies.append(
+            pltpu.make_async_copy(fine_ref.at[piece, :], fine_hbm.at[piece, :], sems.at[j + 1])
+        )
+        copies[-1].start()
+    for copy in copies:
+        copy.wait()
 
 
 VMEM = pl.BlockSpec(memory_space=pltpu.VMEM)
@@ -540,11 +543,11 @@
 HBM = pl.BlockSpec(memory_space=pltpu.HBM)
 
 
-def call(kernel, in_specs, out_shapes, scratch=()):
+def call(kernel, in_specs, out_shapes, scratch=(), out_spec=VMEM):
     return pl.pallas_call(
         kernel,
         in_specs=in_specs,
-        out_specs=[VMEM] * len(out_shapes),
+        out_specs=[out_spec] * len(out_shapes),
         out_shape=out_shapes,
         scratch_shapes=scratch,
         compiler_params=pltpu.CompilerParams(vmem_limit_bytes=32 * 2**20),
@@ -597,7 +600,6 @@
     diag = [(i, (i + 1 if i % 2 else i - 1) % peers) for i in range(peers)]
     pair = [(i, (i + 2 if i % 2 else i - 2) % peers) for i in range(peers)]
     flips = [[(i, i ^ (2 * j)) for i in range(peers)] for j in range(peers // 2)]
-    place = jnp.stack([me % 2, me * count])
     lines = lambda x: x.reshape(-1, LANES)
     row = lambda x: x.reshape(1, width)
     turn = pltpu.VMEM((LANES, LANES), f32)
@@ -616,10 +618,10 @@
     diag0 = move(out_diag, diag)
     state, ints, pack = call(
         functools.partial(start_kernel, count, HALO),
-        [SMEM] + [HBM] * 10,
+        [HBM] * 10,
         [shape(full, LANES), shape(16, LANES), shape(8, width)],
         [small(x) for x in small_args] + [pltpu.SemaphoreType.DMA((10,))],
-    )(place, *here(flat, *small_args))
+    )(*here(flat, *small_args))
     ints0 = move(ints, swap)
     hot, got, into, high, low = call(
         functools.partial(near_kernel, edges),
@@ -629,36 +631,31 @@
         [turn] + [pltpu.VMEM((size, width), f32)] * 3 + [pltpu.SemaphoreType.DMA((3,))],
     )(state, ints, *here(fine_w_send, fine_w_recv, fine_w_out), pack)
     state, out_half = call(
-        far_kernel, [SMEM] + [VMEM] * 8, [shape(full, LANES), shape(rim, LANES)]
-    )(place, swap0, diag0, state, hot, got, into, high, low)
+        far_kernel, [VMEM] * 9, [shape(full, LANES), shape(rim, LANES)]
+    )(swap0, diag0, ints0, state, hot, got, into, high, low)
     swap1 = move(state, swap)
     diag1 = move(out_half, diag)
     pair1 = move(out_half, pair)
     got, into, own_high, own_low, hot2, select, high, low = call(
         functools.partial(near2_kernel, edges, count),
-        [SMEM] + [VMEM] * 10,
+        [VMEM] * 10,
         [shape(edges, width), shape(rows, width)]
         + [shape(rows, width, kind=bf16)] * 2
         + [hot_shape, shape(coarse // 2, 2 * rows, kind=bf16)]
         + [shape(5 * size, width, kind=bf16)] * 2,
         [turn],
     )(
-        place, state, ints, ints0, hot, fine_w_send, fine_w_recv, fine_w_out, up_w_in, up_w_out,
+        state, ints, ints0, hot, fine_w_send, fine_w_recv, fine_w_out, up_w_in, up_w_out,
         pack,
     )
-    got2, diag_high, diag_low = call(
-        halo_kernel,
-        [SMEM] + [VMEM] * 7,
-        [shape(edges, width)] + [shape(HALO, width, kind=bf16)] * 2,
-    )(place, pair1, diag1, own_high, own_low, hot2, high, low)
     hidden, *slots = call(
         up_kernel,
-        [SMEM] + [VMEM] * 15,
+        [VMEM] * 16,
         [shape(rows, width)]
         + [shape(own + 8 * coarse_edges // 256, LANES)] * (peers // 2),
-        [pltpu.VMEM((rows, width), bf16)] * 2,
+        [pltpu.VMEM((window, width), bf16)] * 2,
     )(
-        place, swap1, diag_high, diag_low, state, hot, got, into, hot2, got2, select, ints, ints0,
+        swap1, pair1, diag1, state, hot, got, into, own_high, own_low, hot2, select, ints, ints0,
         high, low, pack,
     )
     arrived = [slots[0]] + [move(slots[j], flips[j]) for j in range(1, peers // 2)]
@@ -670,13 +667,13 @@
     degree = coarse_edges // count
     coarse_hot, parent_hot = call(
         functools.partial(edges_kernel, degree, count),
-        [SMEM] + [VMEM] * (1 + peers // 2),
+        [VMEM] * (1 + peers // 2),
         [
             shape(degree * (count + rows), coarse, kind=bf16),
             shape(rows, coarse, kind=bf16),
         ],
         [turn],
-    )(place, ints, *arrived)
+    )(ints, *arrived)
     high, low = call(
         split_kernel, [VMEM] * 5, [shape(5 * size, width, kind=bf16)] * 2
     )(coarse_w_send, coarse_w_recv, coarse_w_out, down_w_in, down_w_out)
@@ -686,7 +683,14 @@
         [shape(degree * (count + rows), width), shape(count + rows, width)],
     )(coarse_hot, parent_hot, high, low, *columns)
     fine_out, coarse_out = call(
-        coarse_kernel, [VMEM] * (8 + peers // 2), [shape(full, LANES), shape(own, LANES)]
+        coarse_kernel,
+        [VMEM] * (8 + peers // 2),
+        [shape(full, LANES), shape(own, LANES)],
+        [
+            pltpu.VMEM((full, LANES), f32), pltpu.VMEM((own, LANES), f32),
+            pltpu.SemaphoreType.DMA((3,)),
+        ],
+        HBM,
     )(hidden, coarse_hot, parent_hot, got, wanted, high, low, pack, *across)
     return (fine_out.reshape(fine_state.shape), coarse_out.reshape(coarse_state.shape))
 

time: 57.1 us -> 54.6 us (0.956)
  Pallas kernels: 19.4 us -> 15.2 us
  waiting for transfers between devices: 9.64 us -> 12.3 us
  starting transfers between devices: 25.8 us -> 25 us
    pallas_call x6 -> x5, Pallas kernels: 12.6 us -> 8.55 us  [the longest x1 3.58 us: kernel_shards(): call(up_kernel, [VMEM] * 16, [shape(rows, width)] + [shape(own + 8 * coar...]
    ppermute x16, waiting for transfers between devices: 9.64 us -> 12.3 us  [move(): return lax.ppermute(values, 'sp', pairs)]
    ppermute x16, starting transfers between devices: 25.8 us -> 25 us  [move(): return lax.ppermute(values, 'sp', pairs)]
  transfers between devices with their start and end apart: 16 -> 16, of which waited for: 7 -> 7; matrix products, arithmetic and copies ran while one was open for 0% -> 0% of each run, Pallas kernels for 19% -> 14%
where the time goes in v7:
time: 54.6 us; the launch traced here: 54.4 us
  starting transfers between devices  25 us (46%)
  Pallas kernels  15.2 us (28%)
  waiting for transfers between devices  12.3 us (23%)
  local copies, waits for them, and re-layouts  1.05 us (2%)
  between operations  0.87 us (2%)
    ppermute x16, starting transfers between devices, move(): return lax.ppermute(values, 'sp', pairs)  25 us
    ppermute x16, waiting for transfers between devices, move(): return lax.ppermute(values, 'sp', pairs)  12.3 us
    pallas_call x1, Pallas kernels, kernel_shards(): call(up_kernel, [VMEM] * 16, [shape(rows, width)] + [shape(own + 8 * coar...  3.58 us
    pallas_call x1, Pallas kernels, kernel_shards(): call(coarse_kernel, [VMEM] * (8 + peers // 2), [shape(full, LANES), shape...  2.85 us
    pallas_call x1, Pallas kernels, kernel_shards(): call(functools.partial(near_kernel, edges), [VMEM] * 2 + [HBM] * 3 + [VME...  2.4 us
    pallas_call x1, Pallas kernels, kernel_shards(): call(functools.partial(edges_kernel, degree, count), [VMEM] * (1 + peers...  1.35 us
    pallas_call x1, Pallas kernels, kernel_shards(): call(far_kernel, [VMEM] * 9, [shape(full, LANES), shape(rim, LANES)])  1.3 us
    pallas_call x1, Pallas kernels, kernel_shards(): call(functools.partial(start_kernel, count, HALO), [HBM] * 10, [shape(ful...  1.17 us
  transfers between devices with their start and end apart: 16, of which 7 were waited for; matrix products, arithmetic and copies ran while one was open for 0% of the time, Pallas kernels for 14%

profile of v7, /device:TPU:0, one launch (start us, length us, event | category | flops | bytes accessed | tf_op | source)
XLA Modules:
  0.0 54.4 jit_solution(5314305751615621934)
XLA Ops:
  0.6 1.0 %constant_dynamic-slice_fusion = (f32[256,128]{1,0:T(8,128)S(1)}, f32[256,128]{1,0:T(8,128)S(1)}) fusion(f32[512,128]{1,0:T(8,128)} %bitcast.13, s32[]{:T(128)S(6)} %select_n.17, s32[]{:T(128)S(6)} %select_n.16), kind=kLoop, calls=%fused_computation | loop fusion | bytes 524296 | tf_op jit(solution)/shard_map/dynamic_slice | solution.py:616
  1.6 3.0 %collective-permute-start = (f32[256,128]{1,0:T(8,128)S(1)}, f32[256,128]{1,0:T(8,128)S(1)}, u32[]{:S(2)}, u32[]{:S(2)}) collective-permute-start(f32[256,128]{1,0:T(8,128)S(1)} %get-tuple-element.67), channel_id=1, source_target_pairs={{0,2},{2,0},{4,6},{6,4},{8,10},{10,8},{12,14},{14,12},{1,3},{3,1},... | collective-permute-start | bytes 393224 | tf_op jit(solution)/shard_map/ppermute | solution.py:558
  4.7 3.6 %collective-permute-start.1 = (f32[256,128]{1,0:T(8,128)S(1)}, f32[256,128]{1,0:T(8,128)S(1)}, u32[]{:S(2)}, u32[]{:S(2)}) collective-permute-start(f32[256,128]{1,0:T(8,128)S(1)} %get-tuple-element.66), channel_id=1, source_target_pairs={{0,14},{2,4},{4,2},{6,8},{8,6},{10,12},{12,10},{14,0},{1,15},{3,5}... | collective-permute-start | bytes 393224 | tf_op jit(solution)/shard_map/ppermute | solution.py:558
  8.2 1.2 %shard_map.212 = (f32[512,128]{1,0:T(8,128)S(1)}, f32[16,128]{1,0:T(8,128)S(1)}, f32[8,256]{1,0:T(8,128)S(1)}) custom-call(f32[512,128]{1,0:T(8,128)} %bitcast.14, s32[8,128]{1,0:T(8,128)} %bitcast.15, s32[2,128]{1,0:T(2,128)} %bitcast.16, s32[2,128]{1,0:T(2,128)} %bitcast.17, s32[2,128]{1,0:T(2,128)} %bitcast.18, s32[2,128]{1,0:T(2,128)} %bitcast.19, ...), custom_call_target="tpu_custom_call" | custom-call | tf_op jit(solution)/shard_map/pallas_call | solution.py:619
  9.4 0.1 collective-permute-start.2
  9.5 2.4 %shard_map.213 = (bf16[1024,512]{1,0:T(8,128)(2,1)S(1)}, f32[1024,256]{1,0:T(8,128)S(1)}, f32[256,256]{1,0:T(8,128)S(1)}, bf16[512,256]{1,0:T(8,128)(2,1)S(1)}, bf16[512,256]{1,0:T(8,128)(2,1)S(1)}) custom-call(f32[512,128]{1,0:T(8,128)S(1)} %get-tuple-element.34.state_ref, f32[16,128]{1,0:T(8,128)S(1)} %get-tuple-element.33.ints_ref, ...), custom_call_target="tpu_custom_call" | custom-call | tf_op jit(solution)/shard_map/pallas_call | solution.py:626
  11.9 1.2 %collective-permute-done.2.ints0_ref = f32[16,128]{1,0:T(8,128)S(1)} collective-permute-done((f32[16,128]{1,0:T(8,128)S(1)}, f32[16,128]{1,0:T(8,128)S(1)}, u32[]{:S(2)}, u32[]{:S(2)}) %collective-permute-start.2) | collective-permute-done | bytes 8224 | tf_op jit(solution)/shard_map/ppermute | solution.py:558
  13.2 1.3 %shard_map.214 = (f32[512,128]{1,0:T(8,128)S(1)}, f32[256,128]{1,0:T(8,128)S(1)}) custom-call(f32[256,128]{1,0:T(8,128)S(1)} %collective-permute-done.swap_ref, f32[256,128]{1,0:T(8,128)S(1)} %collective-permute-done.1.diag_ref, f32[16,128]{1,0:T(8,128)S(1)} %collective-permute-done.2.ints0_ref, f32[512,128]{1,0:T(8,128)S(1)} %get-tuple-element.34.state_ref, ...), custom_call_target="tpu_custom_call" | custom-call | tf_op jit(solution)/shard_map/pallas_call | solution.py:633
  14.5 0.9 %collective-permute-start.3 = (f32[512,128]{1,0:T(8,128)S(1)}, f32[512,128]{1,0:T(8,128)S(1)}, u32[]{:S(2)}, u32[]{:S(2)}) collective-permute-start(f32[512,128]{1,0:T(8,128)S(1)} %get-tuple-element.41.state_ref), channel_id=1, source_target_pairs={{0,2},{2,0},{4,6},{6,4},{8,10},{10,8},{12,14},{14,12},{1,3},{3,1},... | collective-permute-start | bytes 786440 | tf_op jit(solution)/shard_map/ppermute | solution.py:558
  15.4 2.6 %collective-permute-start.4 = (f32[256,128]{1,0:T(8,128)S(1)}, f32[256,128]{1,0:T(8,128)S(1)}, u32[]{:S(2)}, u32[]{:S(2)}) collective-permute-start(f32[256,128]{1,0:T(8,128)S(1)} %get-tuple-element.42), channel_id=1, source_target_pairs={{0,12},{2,6},{4,0},{6,10},{8,4},{10,14},{12,8},{14,2},{1,13},{3,7}... | collective-permute-start | bytes 393224 | tf_op jit(solution)/shard_map/ppermute | solution.py:558
  18.0 1.9 %collective-permute-start.5 = (f32[256,128]{1,0:T(8,128)S(1)}, f32[256,128]{1,0:T(8,128)S(1)}, u32[]{:S(2)}, u32[]{:S(2)}) collective-permute-start(f32[256,128]{1,0:T(8,128)S(1)} %get-tuple-element.42), channel_id=1, source_target_pairs={{0,14},{2,4},{4,2},{6,8},{8,6},{10,12},{12,10},{14,0},{1,15},{3,5}... | collective-permute-start | bytes 393224 | tf_op jit(solution)/shard_map/ppermute | solution.py:558
  19.9 1.1 %shard_map.215 = (f32[1024,256]{1,0:T(8,128)S(1)}, f32[256,256]{1,0:T(8,128)S(1)}, bf16[256,256]{1,0:T(8,128)(2,1)S(1)}, bf16[256,256]{1,0:T(8,128)(2,1)S(1)}, b...) custom-call(f32[512,128]{1,0:T(8,128)S(1)} %get-tuple-element.41.sta, ...), custom_call_target="tpu_custom_call" | custom-call | tf_op jit(solution)/shard_map/pallas_call | solution.py:639
  21.0 0.4 collective-permute-done.4.pair_ref
  21.4 4.2 %collective-permute-done.5.diag_ref = f32[256,128]{1,0:T(8,128)S(1)} collective-permute-done((f32[256,128]{1,0:T(8,128)S(1)}, f32[256,128]{1,0:T(8,128)S(1)}, u32[]{:S(2)}, u32[]{:S(2)}) %collective-permute-start.5) | collective-permute-done | bytes 131104 | tf_op jit(solution)/shard_map/ppermute | solution.py:558
  25.7 3.6 %shard_map.216 = (f32[256,256]{1,0:T(8,128)S(1)}, f32[136,128]{1,0:T(8,128)S(1)}, f32[136,128]{1,0:T(8,128)S(1)}, f32[136,128]{1,0:T(8,128)S(1)}, f32[136,128]{1,0:T(8,128)S(1)}) custom-call(f32[512,128]{1,0:T(8,128)S(1)} %collective-permute-done.3.swap_ref, f32[256,128]{1,0:T(8,128)S(1)} %collective-permute-done.4.pair_ref, ...), custom_call_target="tpu_custom_call" | custom-call | tf_op jit(solution)/shard_map/pallas_call | solution.py:651
  29.3 0.1 collective-permute-start.6
  29.3 1.9 %collective-permute-start.7 = (f32[136,128]{1,0:T(8,128)S(1)}, f32[136,128]{1,0:T(8,128)S(1)}, u32[]{:S(2)}, u32[]{:S(2)}) collective-permute-start(f32[136,128]{1,0:T(8,128)S(1)} %get-tuple-element.54), channel_id=1, source_target_pairs={{0,8},{2,10},{4,12},{6,14},{8,0},{10,2},{12,4},{14,6},{1,9},{3,11}... | collective-permute-start | bytes 208904 | tf_op jit(solution)/shard_map/ppermute | solution.py:558
  31.2 2.5 %collective-permute-start.8 = (f32[136,128]{1,0:T(8,128)S(1)}, f32[136,128]{1,0:T(8,128)S(1)}, u32[]{:S(2)}, u32[]{:S(2)}) collective-permute-start(f32[136,128]{1,0:T(8,128)S(1)} %get-tuple-element.55), channel_id=1, source_target_pairs={{0,12},{2,14},{4,8},{6,10},{8,4},{10,6},{12,0},{14,2},{1,13},{3,15... | collective-permute-start | bytes 208904 | tf_op jit(solution)/shard_map/ppermute | solution.py:558
  33.7 1.5 %collective-permute-done.7.refs_2_ = f32[136,128]{1,0:T(8,128)S(1)} collective-permute-done((f32[136,128]{1,0:T(8,128)S(1)}, f32[136,128]{1,0:T(8,128)S(1)}, u32[]{:S(2)}, u32[]{:S(2)}) %collective-permute-start.7) | collective-permute-done | bytes 69664 | tf_op jit(solution)/shard_map/ppermute | solution.py:558
  35.2 2.5 %collective-permute-done.8.refs_3_ = f32[136,128]{1,0:T(8,128)S(1)} collective-permute-done((f32[136,128]{1,0:T(8,128)S(1)}, f32[136,128]{1,0:T(8,128)S(1)}, u32[]{:S(2)}, u32[]{:S(2)}) %collective-permute-start.8) | collective-permute-done | bytes 69664 | tf_op jit(solution)/shard_map/ppermute | solution.py:558
  37.7 0.2 collective-permute-start.9
  37.9 3.3 %collective-permute-start.10 = (f32[128,128]{1,0:T(8,128)S(1)}, f32[128,128]{1,0:T(8,128)S(1)}, u32[]{:S(2)}, u32[]{:S(2)}) collective-permute-start(f32[128,128]{1,0:T(8,128)S(1)} %shard_map.219.refs_0_), channel_id=1, source_target_pairs={{0,8},{2,10},{4,12},{6,14},{8,0},{10,2},{12,4},{14,6},{1,9},{3,11}... | collective-permute-start | bytes 196616 | tf_op jit(solution)/shard_map/ppermute | solution.py:558
  41.2 1.0 %collective-permute-start.11 = (f32[128,128]{1,0:T(8,128)S(1)}, f32[128,128]{1,0:T(8,128)S(1)}, u32[]{:S(2)}, u32[]{:S(2)}) collective-permute-start(f32[128,128]{1,0:T(8,128)S(1)} %shard_map.219.refs_0_), channel_id=1, source_target_pairs={{0,12},{2,14},{4,8},{6,10},{8,4},{10,6},{12,0},{14,2},{1,13},{3,15... | collective-permute-start | bytes 196616 | tf_op jit(solution)/shard_map/ppermute | solution.py:558
  42.2 2.0 %collective-permute-start.12 = (f32[128,128]{1,0:T(8,128)S(1)}, f32[128,128]{1,0:T(8,128)S(1)}, u32[]{:S(2)}, u32[]{:S(2)}) collective-permute-start(f32[128,128]{1,0:T(8,128)S(1)} %shard_map.219.refs_0_), channel_id=1, source_target_pairs={{0,2},{2,0},{4,6},{6,4},{8,10},{10,8},{12,14},{14,12},{1,3},{3,1},... | collective-permute-start | bytes 196616 | tf_op jit(solution)/shard_map/ppermute | solution.py:558
  44.2 0.0 collective-permute-start.13
  44.2 2.0 %collective-permute-start.14 = (f32[128,128]{1,0:T(8,128)S(1)}, f32[128,128]{1,0:T(8,128)S(1)}, u32[]{:S(2)}, u32[]{:S(2)}) collective-permute-start(f32[128,128]{1,0:T(8,128)S(1)} %collective-permute-done.10.refs_2_), channel_id=1, source_target_pairs={{0,2},{2,0},{4,6},{6,4},{8,10},{10,8},{12,14},{14,12},{1,3},{3,1},... | collective-permute-start | bytes 196616 | tf_op jit(solution)/shard_map/ppermute | solution.py:558
  46.2 1.1 %collective-permute-done.11.refs_3_ = f32[128,128]{1,0:T(8,128)S(1)} collective-permute-done((f32[128,128]{1,0:T(8,128)S(1)}, f32[128,128]{1,0:T(8,128)S(1)}, u32[]{:S(2)}, u32[]{:S(2)}) %collective-permute-start.11) | collective-permute-done | bytes 65568 | tf_op jit(solution)/shard_map/ppermute | solution.py:558
  47.3 0.2 shard_map.218
  47.5 1.4 %shard_map.217 = (bf16[1280,512]{1,0:T(8,128)(2,1)S(1)}, bf16[256,512]{1,0:T(8,128)(2,1)S(1)}) custom-call(f32[16,128]{1,0:T(8,128)S(1)} %get-tuple-element.33.ints_ref, f32[136,128]{1,0:T(8,128)S(1)} %get-tuple-element.52.refs_0_, f32[136,128]{1,0:T(8,128)S(1)} %collective-permute-done.6.refs_1_, f32[136,128]{1,0:T(8,128)S(1)} %collective-permute-done.7.refs_2_, ...), custom_call_target="tpu_custom_call" | custom-call | tf_op jit(solution)/shard_map/pallas_call | solution.py:668
  48.9 1.2 %shard_map.220 = (f32[1280,256]{1,0:T(8,128)S(1)}, f32[320,256]{1,0:T(8,128)S(1)}) custom-call(bf16[1280,512]{1,0:T(8,128)(2,1)S(1)} %get-tuple-element.56.hot_ref, bf16[256,512]{1,0:T(8,128)(2,1)S(1)} %get-tuple-element.57.parent_ref, bf16[1280,256]{1,0:T(8,128)(2,1)S(1)} %get-tuple-element.58.high_ref, bf16[1280,256]{1,0:T(8,128)(2,1)S(1)} %get-tuple-element.59.low_ref, ...), custom_call_target="tpu_custom_call" | custom-call | tf_op jit(solution)/shard_map/pallas_call | solution.py:680
  50.1 1.5 %collective-permute-done.15.refs_3_ = f32[128,128]{1,0:T(8,128)S(1)} collective-permute-done((f32[128,128]{1,0:T(8,128)S(1)}, f32[128,128]{1,0:T(8,128)S(1)}, u32[]{:S(2)}, u32[]{:S(2)}) %collective-permute-start.15) | collective-permute-done | bytes 65568 | tf_op jit(solution)/shard_map/ppermute | solution.py:558
  51.5 2.9 %shard_map.221 = (f32[512,128]{1,0:T(8,128)}, f32[128,128]{1,0:T(8,128)}) custom-call(f32[256,256]{1,0:T(8,128)S(1)} %get-tuple-element.51.last_ref, bf16[1280,512]{1,0:T(8,128)(2,1)S(1)} %get-tuple-element.56.hot_ref, bf16[256,512]{1,0:T(8,128)(2,1)S(1)} %get-tuple-element.57.parent_ref, f32[1280,256]{1,0:T(8,128)S(1)} %get-tuple-element.60.got_ref, ...), custom_call_target="tpu_custom_call" | custom-call | tf_op jit(solution)/shard_map/pallas_call | solution.py:685
  (33 shorter events, 0.1 us)
Async XLA Ops:
  1.6 11.5 %collective-permute-start = (f32[256,128]{1,0:T(8,128)S(1)}, f32[256,128]{1,0:T(8,128)S(1)}, u32[]{:S(2)}, u32[]{:S(2)}) collective-permute-start(f32[256,128]{1,0:T(8,128)S(1)} %get-tuple-element.67), channel_id=1, source_target_pairs={{0,2},{2,0},{4,6},{6,4},{8,10},{10,8},{12,14},{14,12},{1,3},{3,1},... | collective-permute-start | bytes 393224 | tf_op jit(solution)/shard_map/ppermute | solution.py:558
  4.7 8.5 %collective-permute-start.1 = (f32[256,128]{1,0:T(8,128)S(1)}, f32[256,128]{1,0:T(8,128)S(1)}, u32[]{:S(2)}, u32[]{:S(2)}) collective-permute-start(f32[256,128]{1,0:T(8,128)S(1)} %get-tuple-element.66), channel_id=1, source_target_pairs={{0,14},{2,4},{4,2},{6,8},{8,6},{10,12},{12,10},{14,0},{1,15},{3,5}... | collective-permute-start | bytes 393224 | tf_op jit(solution)/shard_map/ppermute | solution.py:558
  9.4 3.7 %collective-permute-start.2 = (f32[16,128]{1,0:T(8,128)S(1)}, f32[16,128]{1,0:T(8,128)S(1)}, u32[]{:S(2)}, u32[]{:S(2)}) collective-permute-start(f32[16,128]{1,0:T(8,128)S(1)} %get-tuple-element.33.ints_ref), channel_id=1, source_target_pairs={{0,2},{2,0},{4,6},{6,4},{8,10},{10,8},{12,14},{14,12},{1,3},{3,1},... | collective-permute-start | bytes 24584 | tf_op jit(solution)/shard_map/ppermute | solution.py:558
  13.1 6.7 %copy-start = (f32[2,256,256]{2,1,0:T(8,128)S(1)}, f32[2,256,256]{2,1,0:T(8,128)}, u32[]{:S(2)}) copy-start(f32[2,256,256]{2,1,0:T(8,128)} %ws_ref.1) | copy-start | bytes 1572868
  13.2 6.7 %copy-start.1 = (f32[2,256,256]{2,1,0:T(8,128)S(1)}, f32[2,256,256]{2,1,0:T(8,128)}, u32[]{:S(2)}) copy-start(f32[2,256,256]{2,1,0:T(8,128)} %wr_ref.1) | copy-start | bytes 1572868
  13.2 6.7 %copy-start.2 = (f32[2,256,256]{2,1,0:T(8,128)S(1)}, f32[2,256,256]{2,1,0:T(8,128)}, u32[]{:S(2)}) copy-start(f32[2,256,256]{2,1,0:T(8,128)} %wo_ref.1) | copy-start | bytes 1572868
  13.2 6.7 %copy-start.8 = (f32[256,256]{1,0:T(8,128)S(1)}, f32[256,256]{1,0:T(8,128)}, u32[]{:S(2)}) copy-start(f32[256,256]{1,0:T(8,128)} %wi_ref.1) | copy-start | bytes 786436
  13.2 6.7 %copy-start.9 = (f32[256,256]{1,0:T(8,128)S(1)}, f32[256,256]{1,0:T(8,128)}, u32[]{:S(2)}) copy-start(f32[256,256]{1,0:T(8,128)} %wu_ref.1) | copy-start | bytes 786436
  14.5 11.1 %collective-permute-start.3 = (f32[512,128]{1,0:T(8,128)S(1)}, f32[512,128]{1,0:T(8,128)S(1)}, u32[]{:S(2)}, u32[]{:S(2)}) collective-permute-start(f32[512,128]{1,0:T(8,128)S(1)} %get-tuple-element.41.state_ref), channel_id=1, source_target_pairs={{0,2},{2,0},{4,6},{6,4},{8,10},{10,8},{12,14},{14,12},{1,3},{3,1},... | collective-permute-start | bytes 786440 | tf_op jit(solution)/shard_map/ppermute | solution.py:558
  15.4 6.0 %collective-permute-start.4 = (f32[256,128]{1,0:T(8,128)S(1)}, f32[256,128]{1,0:T(8,128)S(1)}, u32[]{:S(2)}, u32[]{:S(2)}) collective-permute-start(f32[256,128]{1,0:T(8,128)S(1)} %get-tuple-element.42), channel_id=1, source_target_pairs={{0,12},{2,6},{4,0},{6,10},{8,4},{10,14},{12,8},{14,2},{1,13},{3,7}... | collective-permute-start | bytes 393224 | tf_op jit(solution)/shard_map/ppermute | solution.py:558
  18.0 7.7 %collective-permute-start.5 = (f32[256,128]{1,0:T(8,128)S(1)}, f32[256,128]{1,0:T(8,128)S(1)}, u32[]{:S(2)}, u32[]{:S(2)}) collective-permute-start(f32[256,128]{1,0:T(8,128)S(1)} %get-tuple-element.42), channel_id=1, source_target_pairs={{0,14},{2,4},{4,2},{6,8},{8,6},{10,12},{12,10},{14,0},{1,15},{3,5}... | collective-permute-start | bytes 393224 | tf_op jit(solution)/shard_map/ppermute | solution.py:558
  25.6 12.0 %copy-start.10 = (f32[64,1,256]{2,1,0:T(1,128)S(1)}, f32[64,1,256]{2,1,0:T(1,128)}, u32[]{:S(2)}) copy-start(f32[64,1,256]{2,1,0:T(1,128)} %param.22) | copy-start | bytes 196612
  25.6 21.6 %copy-start.3 = (f32[256,256]{1,0:T(8,128)S(1)}, f32[256,256]{1,0:T(8,128)}, u32[]{:S(2)}) copy-start(f32[256,256]{1,0:T(8,128)} %cs_ref.1) | copy-start | bytes 786436
  25.6 21.6 %copy-start.4 = (f32[256,256]{1,0:T(8,128)S(1)}, f32[256,256]{1,0:T(8,128)}, u32[]{:S(2)}) copy-start(f32[256,256]{1,0:T(8,128)} %cr_ref.1) | copy-start | bytes 786436
  25.6 21.6 %copy-start.5 = (f32[256,256]{1,0:T(8,128)S(1)}, f32[256,256]{1,0:T(8,128)}, u32[]{:S(2)}) copy-start(f32[256,256]{1,0:T(8,128)} %co_ref.1) | copy-start | bytes 786436
  25.7 21.6 %copy-start.6 = (f32[256,256]{1,0:T(8,128)S(1)}, f32[256,256]{1,0:T(8,128)}, u32[]{:S(2)}) copy-start(f32[256,256]{1,0:T(8,128)} %di_ref.1) | copy-start | bytes 786436
  25.7 21.6 %copy-start.7 = (f32[256,256]{1,0:T(8,128)S(1)}, f32[256,256]{1,0:T(8,128)}, u32[]{:S(2)}) copy-start(f32[256,256]{1,0:T(8,128)} %do_ref.1) | copy-start | bytes 786436
  29.3 4.5 %collective-permute-start.6 = (f32[136,128]{1,0:T(8,128)S(1)}, f32[136,128]{1,0:T(8,128)S(1)}, u32[]{:S(2)}, u32[]{:S(2)}) collective-permute-start(f32[136,128]{1,0:T(8,128)S(1)} %get-tuple-element.53), channel_id=1, source_target_pairs={{0,4},{2,6},{4,0},{6,2},{8,12},{10,14},{12,8},{14,10},{1,5},{3,7},... | collective-permute-start | bytes 208904 | tf_op jit(solution)/shard_map/ppermute | solution.py:558
  29.3 5.9 %collective-permute-start.7 = (f32[136,128]{1,0:T(8,128)S(1)}, f32[136,128]{1,0:T(8,128)S(1)}, u32[]{:S(2)}, u32[]{:S(2)}) collective-permute-start(f32[136,128]{1,0:T(8,128)S(1)} %get-tuple-element.54), channel_id=1, source_target_pairs={{0,8},{2,10},{4,12},{6,14},{8,0},{10,2},{12,4},{14,6},{1,9},{3,11}... | collective-permute-start | bytes 208904 | tf_op jit(solution)/shard_map/ppermute | solution.py:558
  31.2 6.4 %collective-permute-start.8 = (f32[136,128]{1,0:T(8,128)S(1)}, f32[136,128]{1,0:T(8,128)S(1)}, u32[]{:S(2)}, u32[]{:S(2)}) collective-permute-start(f32[136,128]{1,0:T(8,128)S(1)} %get-tuple-element.55), channel_id=1, source_target_pairs={{0,12},{2,14},{4,8},{6,10},{8,4},{10,6},{12,0},{14,2},{1,13},{3,15... | collective-permute-start | bytes 208904 | tf_op jit(solution)/shard_map/ppermute | solution.py:558
  37.7 6.5 %collective-permute-start.9 = (f32[128,128]{1,0:T(8,128)S(1)}, f32[128,128]{1,0:T(8,128)S(1)}, u32[]{:S(2)}, u32[]{:S(2)}) collective-permute-start(f32[128,128]{1,0:T(8,128)S(1)} %shard_map.219.refs_0_), channel_id=1, source_target_pairs={{0,4},{2,6},{4,0},{6,2},{8,12},{10,14},{12,8},{14,10},{1,5},{3,7},... | collective-permute-start | bytes 196616 | tf_op jit(solution)/shard_map/ppermute | solution.py:558
  37.9 6.3 %collective-permute-start.10 = (f32[128,128]{1,0:T(8,128)S(1)}, f32[128,128]{1,0:T(8,128)S(1)}, u32[]{:S(2)}, u32[]{:S(2)}) collective-permute-start(f32[128,128]{1,0:T(8,128)S(1)} %shard_map.219.refs_0_), channel_id=1, source_target_pairs={{0,8},{2,10},{4,12},{6,14},{8,0},{10,2},{12,4},{14,6},{1,9},{3,11}... | collective-permute-start | bytes 196616 | tf_op jit(solution)/shard_map/ppermute | solution.py:558
  41.2 6.1 %collective-permute-start.11 = (f32[128,128]{1,0:T(8,128)S(1)}, f32[128,128]{1,0:T(8,128)S(1)}, u32[]{:S(2)}, u32[]{:S(2)}) collective-permute-start(f32[128,128]{1,0:T(8,128)S(1)} %shard_map.219.refs_0_), channel_id=1, source_target_pairs={{0,12},{2,14},{4,8},{6,10},{8,4},{10,6},{12,0},{14,2},{1,13},{3,15... | collective-permute-start | bytes 196616 | tf_op jit(solution)/shard_map/ppermute | solution.py:558
  42.2 7.9 %collective-permute-start.12 = (f32[128,128]{1,0:T(8,128)S(1)}, f32[128,128]{1,0:T(8,128)S(1)}, u32[]{:S(2)}, u32[]{:S(2)}) collective-permute-start(f32[128,128]{1,0:T(8,128)S(1)} %shard_map.219.refs_0_), channel_id=1, source_target_pairs={{0,2},{2,0},{4,6},{6,4},{8,10},{10,8},{12,14},{14,12},{1,3},{3,1},... | collective-permute-start | bytes 196616 | tf_op jit(solution)/shard_map/ppermute | solution.py:558
  44.2 5.9 %collective-permute-start.13 = (f32[128,128]{1,0:T(8,128)S(1)}, f32[128,128]{1,0:T(8,128)S(1)}, u32[]{:S(2)}, u32[]{:S(2)}) collective-permute-start(f32[128,128]{1,0:T(8,128)S(1)} %collective-permute-done.9.refs_1_), channel_id=1, source_target_pairs={{0,2},{2,0},{4,6},{6,4},{8,10},{10,8},{12,14},{14,12},{1,3},{3,1},... | collective-permute-start | bytes 196616 | tf_op jit(solution)/shard_map/ppermute | solution.py:558
  44.2 5.9 %collective-permute-start.14 = (f32[128,128]{1,0:T(8,128)S(1)}, f32[128,128]{1,0:T(8,128)S(1)}, u32[]{:S(2)}, u32[]{:S(2)}) collective-permute-start(f32[128,128]{1,0:T(8,128)S(1)} %collective-permute-done.10.refs_2_), channel_id=1, source_target_pairs={{0,2},{2,0},{4,6},{6,4},{8,10},{10,8},{12,14},{14,12},{1,3},{3,1},... | collective-permute-start | bytes 196616 | tf_op jit(solution)/shard_map/ppermute | solution.py:558
  47.3 4.3 %collective-permute-start.15 = (f32[128,128]{1,0:T(8,128)S(1)}, f32[128,128]{1,0:T(8,128)S(1)}, u32[]{:S(2)}, u32[]{:S(2)}) collective-permute-start(f32[128,128]{1,0:T(8,128)S(1)} %collective-permute-done.11.refs_3_), channel_id=1, source_target_pairs={{0,2},{2,0},{4,6},{6,4},{8,10},{10,8},{12,14},{14,12},{1,3},{3,1},... | collective-permute-start | bytes 196616 | tf_op jit(solution)/shard_map/ppermute | solution.py:558

commit v8 on v7

--- a/solution.py
+++ b/solution.py
@@ -233,11 +233,15 @@
 def start_kernel(
     count, halo, state_hbm, sender_hbm, owner_hbm, local_hbm, cowner_hbm,
     clocal_hbm, fb_hbm, ub_hbm, cb_hbm, db_hbm,
-    state_ref, ints_ref, pack_ref,
+    state_ref, ints_ref, pack_ref, swap_ref, diag_ref,
     sender_ref, owner_ref, local_ref, cowner_ref, clocal_ref, fb_ref, ub_ref, cb_ref, db_ref,
     sems,
 ):
     odd = place() % 2
+    rim = diag_ref.shape[0]
+    far = state_hbm.shape[0] - rim
+    mine = pl.ds(pl.multiple_of((1 - odd) * far, LANES), rim)
+    away = pl.ds(pl.multiple_of(odd * far, LANES), rim)
     pairs = [
         (sender_hbm, sender_ref),
         (owner_hbm, owner_ref),
@@ -248,12 +252,14 @@
         (ub_hbm, ub_ref),
         (cb_hbm, cb_ref),
         (db_hbm, db_ref),
+        (state_hbm.at[mine, :], swap_ref.at[0:rim, :]),
+        (state_hbm.at[away, :], diag_ref),
         (state_hbm, state_ref),
     ]
     copies = [pltpu.make_async_copy(a, b, sems.at[j]) for j, (a, b) in enumerate(pairs)]
     for copy in copies:
         copy.start()
-    for copy in copies[:-1]:
+    for copy in copies[:-3]:
         copy.wait()
     rows = state_hbm.shape[0] * LANES // fb_ref.shape[1]
     sender = sender_ref[...]
@@ -270,13 +276,16 @@
         (cowner_ref[...] * count + clocal_ref[...]).astype(f32),
     ]
     rest = ints_ref.shape[0] - sum(x.shape[0] for x in lines)
-    ints_ref[...] = jnp.concatenate(lines + [jnp.zeros((rest, LANES), f32)], axis=0)
+    ints = jnp.concatenate(lines + [jnp.zeros((rest, LANES), f32)], axis=0)
+    ints_ref[...] = ints
+    swap_ref[rim:, :] = ints
     pack_ref[...] = jnp.concatenate(
         [fb_ref[...], ub_ref[...], cb_ref[...], db_ref[...]]
         + [jnp.zeros((3, fb_ref.shape[1]), f32)],
         axis=0,
     )
-    copies[-1].wait()
+    for copy in copies[-3:]:
+        copy.wait()
 
 
 def near_kernel(
@@ -302,7 +311,7 @@
 
 
 def far_kernel(
-    swap_ref, diag_ref, ints0_ref, state_ref, hot_ref, got_ref, into_ref, high_ref, low_ref,
+    swap_ref, diag_ref, state_ref, hot_ref, got_ref, into_ref, high_ref, low_ref,
     out_full_ref, out_half_ref,
 ):
     rows, width = into_ref.shape
@@ -346,12 +355,13 @@
     own_high_ref[...] = high
     own_low_ref[...] = low
     got_ref[...] = take(hot_ref[:, :rows], high, low)
-    edge_hot(hot2_ref, turn_ref, ints0_ref[:senders, :], edges // rows, rows)
+    first = ints0_ref.shape[0] - ints_ref.shape[0]
+    edge_hot(hot2_ref, turn_ref, ints0_ref[first : first + senders, :], edges // rows, rows)
     flip = place() * count
     line = senders
-    for half, ref in ((0, ints_ref), (1, ints0_ref)):
+    for half, ref, base in ((0, ints_ref, 0), (1, ints0_ref, first)):
         for j in range(rows // LANES):
-            parent = ref[line + j : line + j + 1, :].astype(jnp.int32)
+            parent = ref[base + line + j : base + line + j + 1, :].astype(jnp.int32)
             parent = jnp.bitwise_xor(parent, flip)
             ids = lax.broadcasted_iota(jnp.int32, (select_ref.shape[0], LANES), 0)
             ids = ids + jnp.bitwise_and(ids, -count)
@@ -407,13 +417,14 @@
     sums = take(select_ref[...], *halves(times(act, *weights(high_ref, low_ref, 4))))
     size = sums.shape[0] // len(slot_refs)
     first = hot_ref.shape[0] // LANES + rows // LANES
+    base = ints0_ref.shape[0] - ints_ref.shape[0]
     anchor = (slot_refs[0].shape[0] - size * parts) // 4
     for j, slot in enumerate(slot_refs):
         store_rows(slot, sums[j * size : (j + 1) * size, :], parts)
         slot[size * parts :, :] = jnp.concatenate(
             [
                 ints_ref[first : first + anchor, :],
-                ints0_ref[first : first + anchor, :],
+                ints0_ref[base + first : base + first + anchor, :],
                 jnp.zeros((2 * anchor, LANES), f32),
             ],
             axis=0,
@@ -611,18 +622,17 @@
         lines(fine_senders), lines(up_owner), lines(up_local), lines(coarse_owner),
         lines(coarse_local), fine_bias, row(up_bias), row(coarse_bias), row(down_bias),
     ]
-    flat = lines(fine_state)
-    out_swap = lax.dynamic_slice(flat, ((1 - me % 2) * (full - rim), 0), (rim, LANES))
-    out_diag = lax.dynamic_slice(flat, (me % 2 * (full - rim), 0), (rim, LANES))
+    state, ints, pack, out_swap, out_diag = call(
+        functools.partial(start_kernel, count, HALO),
+        [HBM] * 10,
+        [
+            shape(full, LANES), shape(16, LANES), shape(8, width), shape(rim + 16, LANES),
+            shape(rim, LANES),
+        ],
+        [small(x) for x in small_args] + [pltpu.SemaphoreType.DMA((12,))],
+    )(*here(lines(fine_state), *small_args))
     swap0 = move(out_swap, swap)
     diag0 = move(out_diag, diag)
-    state, ints, pack = call(
-        functools.partial(start_kernel, count, HALO),
-        [HBM] * 10,
-        [shape(full, LANES), shape(16, LANES), shape(8, width)],
-        [small(x) for x in small_args] + [pltpu.SemaphoreType.DMA((10,))],
-    )(*here(flat, *small_args))
-    ints0 = move(ints, swap)
     hot, got, into, high, low = call(
         functools.partial(near_kernel, edges),
         [VMEM] * 2 + [HBM] * 3 + [VMEM],
@@ -631,8 +641,8 @@
         [turn] + [pltpu.VMEM((size, width), f32)] * 3 + [pltpu.SemaphoreType.DMA((3,))],
     )(state, ints, *here(fine_w_send, fine_w_recv, fine_w_out), pack)
     state, out_half = call(
-        far_kernel, [VMEM] * 9, [shape(full, LANES), shape(rim, LANES)]
-    )(swap0, diag0, ints0, state, hot, got, into, high, low)
+        far_kernel, [VMEM] * 8, [shape(full, LANES), shape(rim, LANES)]
+    )(swap0, diag0, state, hot, got, into, high, low)
     swap1 = move(state, swap)
     diag1 = move(out_half, diag)
     pair1 = move(out_half, pair)
@@ -645,7 +655,7 @@
         + [shape(5 * size, width, kind=bf16)] * 2,
         [turn],
     )(
-        state, ints, ints0, hot, fine_w_send, fine_w_recv, fine_w_out, up_w_in, up_w_out,
+        state, ints, swap0, hot, fine_w_send, fine_w_recv, fine_w_out, up_w_in, up_w_out,
         pack,
     )
     hidden, *slots = call(
@@ -655,7 +665,7 @@
         + [shape(own + 8 * coarse_edges // 256, LANES)] * (peers // 2),
         [pltpu.VMEM((window, width), bf16)] * 2,
     )(
-        swap1, pair1, diag1, state, hot, got, into, own_high, own_low, hot2, select, ints, ints0,
+        swap1, pair1, diag1, state, hot, got, into, own_high, own_low, hot2, select, ints, swap0,
         high, low, pack,
     )
     arrived = [slots[0]] + [move(slots[j], flips[j]) for j in range(1, peers // 2)]

time: 54.6 us -> 54.4 us (level)
  waiting for transfers between devices: 12.3 us -> 14.2 us
  starting transfers between devices: 25 us -> 23.8 us
  local copies, waits for them, and re-layouts: 1.05 us -> 0.05 us
    ppermute x16 -> x15, waiting for transfers between devices: 12.3 us -> 14.2 us  [move(): return lax.ppermute(values, 'sp', pairs)]
    ppermute x16 -> x15, starting transfers between devices: 25 us -> 23.8 us  [move(): return lax.ppermute(values, 'sp', pairs)]
    dynamic_slice x1 -> x0, local copies, waits for them, and re-layouts: 0.99 us -> none  [kernel_shards(): out_diag = lax.dynamic_slice(flat, (me % 2 * (full - rim), 0), (rim, LANES))]
  transfers between devices with their start and end apart: 16 -> 15, of which waited for: 7 -> 8; matrix products, arithmetic and copies ran while one was open for 0% -> 0% of each run, Pallas kernels for 14% -> 12%
where the time goes in v8:
time: 54.4 us; the launch traced here: 54.3 us
  starting transfers between devices  23.8 us (44%)
  Pallas kernels  15.4 us (28%)
  waiting for transfers between devices  14.2 us (26%)
  between operations  0.83 us (2%)
    ppermute x15, starting transfers between devices, move(): return lax.ppermute(values, 'sp', pairs)  23.8 us
    ppermute x15, waiting for transfers between devices, move(): return lax.ppermute(values, 'sp', pairs)  14.2 us
    pallas_call x1, Pallas kernels, kernel_shards(): call(up_kernel, [VMEM] * 16, [shape(rows, width)] + [shape(own + 8 * coar...  3.62 us
    pallas_call x1, Pallas kernels, kernel_shards(): call(coarse_kernel, [VMEM] * (8 + peers // 2), [shape(full, LANES), shape...  2.85 us
    pallas_call x1, Pallas kernels, kernel_shards(): call(functools.partial(near_kernel, edges), [VMEM] * 2 + [HBM] * 3 + [VME...  2.4 us
    pallas_call x1, Pallas kernels, kernel_shards(): call(functools.partial(edges_kernel, degree, count), [VMEM] * (1 + peers...  1.36 us
    pallas_call x1, Pallas kernels, kernel_shards(): call(functools.partial(start_kernel, count, HALO), [HBM] * 10, [shape(ful...  1.31 us
    pallas_call x1, Pallas kernels, kernel_shards(): call(far_kernel, [VMEM] * 8, [shape(full, LANES), shape(rim, LANES)])  1.3 us
  transfers between devices with their start and end apart: 15, of which 8 were waited for; matrix products, arithmetic and copies ran while one was open for 0% of the time, Pallas kernels for 12%

profile of v8, /device:TPU:0, one launch (start us, length us, event | category | flops | bytes accessed | tf_op | source)
XLA Modules:
  0.0 54.3 jit_solution(14516687438493557113)
XLA Ops:
  0.6 1.3 %shard_map.212 = (f32[512,128]{1,0:T(8,128)S(1)}, f32[16,128]{1,0:T(8,128)S(1)}, f32[8,256]{1,0:T(8,128)S(1)}, f32[272,128]{1,0:T(8,128)S(1)}, f32[256,128]{1,0:T(8,128)S(1)}) custom-call(f32[512,128]{1,0:T(8,128)} %bitcast.13, s32[8,128]{1,0:T(8,128)} %bitcast.14, s32[2,128]{1,0:T(2,128)} %bitcast.15, s32[2,128]{1,0:T(2,128)} %bitcast.16, ...), custom_call_target="tpu_custom_call" | custom-call | tf_op jit(solution)/shard_map/pallas_call | solution.py:625
  2.0 3.0 %collective-permute-start = (f32[272,128]{1,0:T(8,128)S(1)}, f32[272,128]{1,0:T(8,128)S(1)}, u32[]{:S(2)}, u32[]{:S(2)}) collective-permute-start(f32[272,128]{1,0:T(8,128)S(1)} %get-tuple-element.35), channel_id=1, source_target_pairs={{0,2},{2,0},{4,6},{6,4},{8,10},{10,8},{12,14},{14,12},{1,3},{3,1},... | collective-permute-start | bytes 417800 | tf_op jit(solution)/shard_map/ppermute | solution.py:569
  5.0 3.6 %collective-permute-start.1 = (f32[256,128]{1,0:T(8,128)S(1)}, f32[256,128]{1,0:T(8,128)S(1)}, u32[]{:S(2)}, u32[]{:S(2)}) collective-permute-start(f32[256,128]{1,0:T(8,128)S(1)} %get-tuple-element.36), channel_id=1, source_target_pairs={{0,14},{2,4},{4,2},{6,8},{8,6},{10,12},{12,10},{14,0},{1,15},{3,5}... | collective-permute-start | bytes 393224 | tf_op jit(solution)/shard_map/ppermute | solution.py:569
  8.6 2.4 %shard_map.213 = (bf16[1024,512]{1,0:T(8,128)(2,1)S(1)}, f32[1024,256]{1,0:T(8,128)S(1)}, f32[256,256]{1,0:T(8,128)S(1)}, bf16[512,256]{1,0:T(8,128)(2,1)S(1)}, bf16[512,256]{1,0:T(8,128)(2,1)S(1)}) custom-call(f32[512,128]{1,0:T(8,128)S(1)} %get-tuple-element.37.state_ref, f32[16,128]{1,0:T(8,128)S(1)} %get-tuple-element.38.ints_ref, ...), custom_call_target="tpu_custom_call" | custom-call | tf_op jit(solution)/shard_map/pallas_call | solution.py:636
  11.0 1.7 %collective-permute-done.1.diag_ref = f32[256,128]{1,0:T(8,128)S(1)} collective-permute-done((f32[256,128]{1,0:T(8,128)S(1)}, f32[256,128]{1,0:T(8,128)S(1)}, u32[]{:S(2)}, u32[]{:S(2)}) %collective-permute-start.1) | collective-permute-done | bytes 131104 | tf_op jit(solution)/shard_map/ppermute | solution.py:569
  12.7 0.0 copy-start.4
  12.7 1.3 %shard_map.214 = (f32[512,128]{1,0:T(8,128)S(1)}, f32[256,128]{1,0:T(8,128)S(1)}) custom-call(f32[272,128]{1,0:T(8,128)S(1)} %collective-permute-done.swap_ref.ints0_ref, f32[256,128]{1,0:T(8,128)S(1)} %collective-permute-done.1.diag_ref, f32[512,128]{1,0:T(8,128)S(1)} %get-tuple-element.37.state_ref, bf16[1024,512]{1,0:T(8,128)(2,1)S(1)} %get-tuple-element.40.hot_ref, ...), custom_call_target="tpu_custom_call" | custom-call | tf_op jit(solution)/shard_map/pallas_call | solution.py:643
  14.0 0.6 %collective-permute-start.2 = (f32[512,128]{1,0:T(8,128)S(1)}, f32[512,128]{1,0:T(8,128)S(1)}, u32[]{:S(2)}, u32[]{:S(2)}) collective-permute-start(f32[512,128]{1,0:T(8,128)S(1)} %get-tuple-element.45.state_ref), channel_id=1, source_target_pairs={{0,2},{2,0},{4,6},{6,4},{8,10},{10,8},{12,14},{14,12},{1,3},{3,1},... | collective-permute-start | bytes 786440 | tf_op jit(solution)/shard_map/ppermute | solution.py:569
  14.6 3.6 %collective-permute-start.3 = (f32[256,128]{1,0:T(8,128)S(1)}, f32[256,128]{1,0:T(8,128)S(1)}, u32[]{:S(2)}, u32[]{:S(2)}) collective-permute-start(f32[256,128]{1,0:T(8,128)S(1)} %get-tuple-element.46), channel_id=1, source_target_pairs={{0,12},{2,6},{4,0},{6,10},{8,4},{10,14},{12,8},{14,2},{1,13},{3,7}... | collective-permute-start | bytes 393224 | tf_op jit(solution)/shard_map/ppermute | solution.py:569
  18.2 1.1 %collective-permute-start.4 = (f32[256,128]{1,0:T(8,128)S(1)}, f32[256,128]{1,0:T(8,128)S(1)}, u32[]{:S(2)}, u32[]{:S(2)}) collective-permute-start(f32[256,128]{1,0:T(8,128)S(1)} %get-tuple-element.46), channel_id=1, source_target_pairs={{0,14},{2,4},{4,2},{6,8},{8,6},{10,12},{12,10},{14,0},{1,15},{3,5}... | collective-permute-start | bytes 393224 | tf_op jit(solution)/shard_map/ppermute | solution.py:569
  19.4 1.1 %shard_map.215 = (f32[1024,256]{1,0:T(8,128)S(1)}, f32[256,256]{1,0:T(8,128)S(1)}, bf16[256,256]{1,0:T(8,128)(2,1)S(1)}, bf16[256,256]{1,0:T(8,128)(2,1)S(1)}, b...) custom-call(f32[512,128]{1,0:T(8,128)S(1)} %get-tuple-element.45.sta, ...), custom_call_target="tpu_custom_call" | custom-call | tf_op jit(solution)/shard_map/pallas_call | solution.py:649
  20.5 0.2 collective-permute-done.3.pair_ref
  20.8 5.1 %collective-permute-done.4.diag_ref = f32[256,128]{1,0:T(8,128)S(1)} collective-permute-done((f32[256,128]{1,0:T(8,128)S(1)}, f32[256,128]{1,0:T(8,128)S(1)}, u32[]{:S(2)}, u32[]{:S(2)}) %collective-permute-start.4) | collective-permute-done | bytes 131104 | tf_op jit(solution)/shard_map/ppermute | solution.py:569
  26.0 3.6 %shard_map.216 = (f32[256,256]{1,0:T(8,128)S(1)}, f32[136,128]{1,0:T(8,128)S(1)}, f32[136,128]{1,0:T(8,128)S(1)}, f32[136,128]{1,0:T(8,128)S(1)}, f32[136,128]{1,0:T(8,128)S(1)}) custom-call(f32[512,128]{1,0:T(8,128)S(1)} %collective-permute-done.2.swap_ref, f32[256,128]{1,0:T(8,128)S(1)} %collective-permute-done.3.pair_ref, ...), custom_call_target="tpu_custom_call" | custom-call | tf_op jit(solution)/shard_map/pallas_call | solution.py:661
  29.6 0.1 collective-permute-start.5
  29.7 0.5 %collective-permute-start.6 = (f32[136,128]{1,0:T(8,128)S(1)}, f32[136,128]{1,0:T(8,128)S(1)}, u32[]{:S(2)}, u32[]{:S(2)}) collective-permute-start(f32[136,128]{1,0:T(8,128)S(1)} %get-tuple-element.58), channel_id=1, source_target_pairs={{0,8},{2,10},{4,12},{6,14},{8,0},{10,2},{12,4},{14,6},{1,9},{3,11}... | collective-permute-start | bytes 208904 | tf_op jit(solution)/shard_map/ppermute | solution.py:569
  30.2 3.8 %collective-permute-start.7 = (f32[136,128]{1,0:T(8,128)S(1)}, f32[136,128]{1,0:T(8,128)S(1)}, u32[]{:S(2)}, u32[]{:S(2)}) collective-permute-start(f32[136,128]{1,0:T(8,128)S(1)} %get-tuple-element.59), channel_id=1, source_target_pairs={{0,12},{2,14},{4,8},{6,10},{8,4},{10,6},{12,0},{14,2},{1,13},{3,15... | collective-permute-start | bytes 208904 | tf_op jit(solution)/shard_map/ppermute | solution.py:569
  34.0 1.4 %collective-permute-done.5.refs_1_ = f32[136,128]{1,0:T(8,128)S(1)} collective-permute-done((f32[136,128]{1,0:T(8,128)S(1)}, f32[136,128]{1,0:T(8,128)S(1)}, u32[]{:S(2)}, u32[]{:S(2)}) %collective-permute-start.5) | collective-permute-done | bytes 69664 | tf_op jit(solution)/shard_map/ppermute | solution.py:569
  35.4 1.8 %collective-permute-done.7.refs_3_ = f32[136,128]{1,0:T(8,128)S(1)} collective-permute-done((f32[136,128]{1,0:T(8,128)S(1)}, f32[136,128]{1,0:T(8,128)S(1)}, u32[]{:S(2)}, u32[]{:S(2)}) %collective-permute-start.7) | collective-permute-done | bytes 69664 | tf_op jit(solution)/shard_map/ppermute | solution.py:569
  37.2 0.6 %collective-permute-start.8 = (f32[128,128]{1,0:T(8,128)S(1)}, f32[128,128]{1,0:T(8,128)S(1)}, u32[]{:S(2)}, u32[]{:S(2)}) collective-permute-start(f32[128,128]{1,0:T(8,128)S(1)} %shard_map.219.refs_0_), channel_id=1, source_target_pairs={{0,4},{2,6},{4,0},{6,2},{8,12},{10,14},{12,8},{14,10},{1,5},{3,7},... | collective-permute-start | bytes 196616 | tf_op jit(solution)/shard_map/ppermute | solution.py:569
  37.9 3.2 %collective-permute-start.9 = (f32[128,128]{1,0:T(8,128)S(1)}, f32[128,128]{1,0:T(8,128)S(1)}, u32[]{:S(2)}, u32[]{:S(2)}) collective-permute-start(f32[128,128]{1,0:T(8,128)S(1)} %shard_map.219.refs_0_), channel_id=1, source_target_pairs={{0,8},{2,10},{4,12},{6,14},{8,0},{10,2},{12,4},{14,6},{1,9},{3,11}... | collective-permute-start | bytes 196616 | tf_op jit(solution)/shard_map/ppermute | solution.py:569
  41.1 0.6 %collective-permute-start.10 = (f32[128,128]{1,0:T(8,128)S(1)}, f32[128,128]{1,0:T(8,128)S(1)}, u32[]{:S(2)}, u32[]{:S(2)}) collective-permute-start(f32[128,128]{1,0:T(8,128)S(1)} %shard_map.219.refs_0_), channel_id=1, source_target_pairs={{0,12},{2,14},{4,8},{6,10},{8,4},{10,6},{12,0},{14,2},{1,13},{3,15... | collective-permute-start | bytes 196616 | tf_op jit(solution)/shard_map/ppermute | solution.py:569
  41.7 1.2 %collective-permute-start.11 = (f32[128,128]{1,0:T(8,128)S(1)}, f32[128,128]{1,0:T(8,128)S(1)}, u32[]{:S(2)}, u32[]{:S(2)}) collective-permute-start(f32[128,128]{1,0:T(8,128)S(1)} %shard_map.219.refs_0_), channel_id=1, source_target_pairs={{0,2},{2,0},{4,6},{6,4},{8,10},{10,8},{12,14},{14,12},{1,3},{3,1},... | collective-permute-start | bytes 196616 | tf_op jit(solution)/shard_map/ppermute | solution.py:569
  42.9 0.8 %collective-permute-start.12 = (f32[128,128]{1,0:T(8,128)S(1)}, f32[128,128]{1,0:T(8,128)S(1)}, u32[]{:S(2)}, u32[]{:S(2)}) collective-permute-start(f32[128,128]{1,0:T(8,128)S(1)} %collective-permute-done.8.refs_1_), channel_id=1, source_target_pairs={{0,2},{2,0},{4,6},{6,4},{8,10},{10,8},{12,14},{14,12},{1,3},{3,1},... | collective-permute-start | bytes 196616 | tf_op jit(solution)/shard_map/ppermute | solution.py:569
  43.7 0.3 collective-permute-done.9.refs_2_
  44.0 0.9 %collective-permute-start.13 = (f32[128,128]{1,0:T(8,128)S(1)}, f32[128,128]{1,0:T(8,128)S(1)}, u32[]{:S(2)}, u32[]{:S(2)}) collective-permute-start(f32[128,128]{1,0:T(8,128)S(1)} %collective-permute-done.9.refs_2_), channel_id=1, source_target_pairs={{0,2},{2,0},{4,6},{6,4},{8,10},{10,8},{12,14},{14,12},{1,3},{3,1},... | collective-permute-start | bytes 196616 | tf_op jit(solution)/shard_map/ppermute | solution.py:569
  44.9 2.2 %collective-permute-done.10.refs_3_ = f32[128,128]{1,0:T(8,128)S(1)} collective-permute-done((f32[128,128]{1,0:T(8,128)S(1)}, f32[128,128]{1,0:T(8,128)S(1)}, u32[]{:S(2)}, u32[]{:S(2)}) %collective-permute-start.10) | collective-permute-done | bytes 65568 | tf_op jit(solution)/shard_map/ppermute | solution.py:569
  47.2 0.2 shard_map.218
  47.4 1.4 %shard_map.217 = (bf16[1280,512]{1,0:T(8,128)(2,1)S(1)}, bf16[256,512]{1,0:T(8,128)(2,1)S(1)}) custom-call(f32[16,128]{1,0:T(8,128)S(1)} %get-tuple-element.38.ints_ref, f32[136,128]{1,0:T(8,128)S(1)} %get-tuple-element.56.refs_0_, f32[136,128]{1,0:T(8,128)S(1)} %collective-permute-done.5.refs_1_, f32[136,128]{1,0:T(8,128)S(1)} %collective-permute-done.6.refs_2_, ...), custom_call_target="tpu_custom_call" | custom-call | tf_op jit(solution)/shard_map/pallas_call | solution.py:678
  48.8 1.2 %shard_map.220 = (f32[1280,256]{1,0:T(8,128)S(1)}, f32[320,256]{1,0:T(8,128)S(1)}) custom-call(bf16[1280,512]{1,0:T(8,128)(2,1)S(1)} %get-tuple-element.60.hot_ref, bf16[256,512]{1,0:T(8,128)(2,1)S(1)} %get-tuple-element.61.parent_ref, bf16[1280,256]{1,0:T(8,128)(2,1)S(1)} %get-tuple-element.62.high_ref, bf16[1280,256]{1,0:T(8,128)(2,1)S(1)} %get-tuple-element.63.low_ref, ...), custom_call_target="tpu_custom_call" | custom-call | tf_op jit(solution)/shard_map/pallas_call | solution.py:690
  50.0 1.5 %collective-permute-done.14.refs_3_ = f32[128,128]{1,0:T(8,128)S(1)} collective-permute-done((f32[128,128]{1,0:T(8,128)S(1)}, f32[128,128]{1,0:T(8,128)S(1)}, u32[]{:S(2)}, u32[]{:S(2)}) %collective-permute-start.14) | collective-permute-done | bytes 65568 | tf_op jit(solution)/shard_map/ppermute | solution.py:569
  51.4 2.9 %shard_map.221 = (f32[512,128]{1,0:T(8,128)}, f32[128,128]{1,0:T(8,128)}) custom-call(f32[256,256]{1,0:T(8,128)S(1)} %get-tuple-element.55.last_ref, bf16[1280,512]{1,0:T(8,128)(2,1)S(1)} %get-tuple-element.60.hot_ref, bf16[256,512]{1,0:T(8,128)(2,1)S(1)} %get-tuple-element.61.parent_ref, f32[1280,256]{1,0:T(8,128)S(1)} %get-tuple-element.64.got_ref, ...), custom_call_target="tpu_custom_call" | custom-call | tf_op jit(solution)/shard_map/pallas_call | solution.py:695
  (30 shorter events, 0.1 us)
Async XLA Ops:
  2.0 10.7 %collective-permute-start = (f32[272,128]{1,0:T(8,128)S(1)}, f32[272,128]{1,0:T(8,128)S(1)}, u32[]{:S(2)}, u32[]{:S(2)}) collective-permute-start(f32[272,128]{1,0:T(8,128)S(1)} %get-tuple-element.35), channel_id=1, source_target_pairs={{0,2},{2,0},{4,6},{6,4},{8,10},{10,8},{12,14},{14,12},{1,3},{3,1},... | collective-permute-start | bytes 417800 | tf_op jit(solution)/shard_map/ppermute | solution.py:569
  5.0 7.7 %collective-permute-start.1 = (f32[256,128]{1,0:T(8,128)S(1)}, f32[256,128]{1,0:T(8,128)S(1)}, u32[]{:S(2)}, u32[]{:S(2)}) collective-permute-start(f32[256,128]{1,0:T(8,128)S(1)} %get-tuple-element.36), channel_id=1, source_target_pairs={{0,14},{2,4},{4,2},{6,8},{8,6},{10,12},{12,10},{14,0},{1,15},{3,5}... | collective-permute-start | bytes 393224 | tf_op jit(solution)/shard_map/ppermute | solution.py:569
  12.7 6.7 %copy-start = (f32[2,256,256]{2,1,0:T(8,128)S(1)}, f32[2,256,256]{2,1,0:T(8,128)}, u32[]{:S(2)}) copy-start(f32[2,256,256]{2,1,0:T(8,128)} %ws_ref.1) | copy-start | bytes 1572868
  12.7 6.7 %copy-start.1 = (f32[2,256,256]{2,1,0:T(8,128)S(1)}, f32[2,256,256]{2,1,0:T(8,128)}, u32[]{:S(2)}) copy-start(f32[2,256,256]{2,1,0:T(8,128)} %wr_ref.1) | copy-start | bytes 1572868
  12.7 6.7 %copy-start.2 = (f32[2,256,256]{2,1,0:T(8,128)S(1)}, f32[2,256,256]{2,1,0:T(8,128)}, u32[]{:S(2)}) copy-start(f32[2,256,256]{2,1,0:T(8,128)} %wo_ref.1) | copy-start | bytes 1572868
  12.7 6.7 %copy-start.3 = (f32[256,256]{1,0:T(8,128)S(1)}, f32[256,256]{1,0:T(8,128)}, u32[]{:S(2)}) copy-start(f32[256,256]{1,0:T(8,128)} %wi_ref.1) | copy-start | bytes 786436
  12.7 6.7 %copy-start.4 = (f32[256,256]{1,0:T(8,128)S(1)}, f32[256,256]{1,0:T(8,128)}, u32[]{:S(2)}) copy-start(f32[256,256]{1,0:T(8,128)} %wu_ref.1) | copy-start | bytes 786436
  14.0 11.9 %collective-permute-start.2 = (f32[512,128]{1,0:T(8,128)S(1)}, f32[512,128]{1,0:T(8,128)S(1)}, u32[]{:S(2)}, u32[]{:S(2)}) collective-permute-start(f32[512,128]{1,0:T(8,128)S(1)} %get-tuple-element.45.state_ref), channel_id=1, source_target_pairs={{0,2},{2,0},{4,6},{6,4},{8,10},{10,8},{12,14},{14,12},{1,3},{3,1},... | collective-permute-start | bytes 786440 | tf_op jit(solution)/shard_map/ppermute | solution.py:569
  14.6 6.1 %collective-permute-start.3 = (f32[256,128]{1,0:T(8,128)S(1)}, f32[256,128]{1,0:T(8,128)S(1)}, u32[]{:S(2)}, u32[]{:S(2)}) collective-permute-start(f32[256,128]{1,0:T(8,128)S(1)} %get-tuple-element.46), channel_id=1, source_target_pairs={{0,12},{2,6},{4,0},{6,10},{8,4},{10,14},{12,8},{14,2},{1,13},{3,7}... | collective-permute-start | bytes 393224 | tf_op jit(solution)/shard_map/ppermute | solution.py:569
  18.2 7.7 %collective-permute-start.4 = (f32[256,128]{1,0:T(8,128)S(1)}, f32[256,128]{1,0:T(8,128)S(1)}, u32[]{:S(2)}, u32[]{:S(2)}) collective-permute-start(f32[256,128]{1,0:T(8,128)S(1)} %get-tuple-element.46), channel_id=1, source_target_pairs={{0,14},{2,4},{4,2},{6,8},{8,6},{10,12},{12,10},{14,0},{1,15},{3,5}... | collective-permute-start | bytes 393224 | tf_op jit(solution)/shard_map/ppermute | solution.py:569
  25.9 11.3 %copy-start.10 = (f32[64,1,256]{2,1,0:T(1,128)S(1)}, f32[64,1,256]{2,1,0:T(1,128)}, u32[]{:S(2)}) copy-start(f32[64,1,256]{2,1,0:T(1,128)} %param.22) | copy-start | bytes 196612
  25.9 21.2 %copy-start.5 = (f32[256,256]{1,0:T(8,128)S(1)}, f32[256,256]{1,0:T(8,128)}, u32[]{:S(2)}) copy-start(f32[256,256]{1,0:T(8,128)} %cs_ref.1) | copy-start | bytes 786436
  25.9 21.2 %copy-start.6 = (f32[256,256]{1,0:T(8,128)S(1)}, f32[256,256]{1,0:T(8,128)}, u32[]{:S(2)}) copy-start(f32[256,256]{1,0:T(8,128)} %cr_ref.1) | copy-start | bytes 786436
  25.9 21.2 %copy-start.7 = (f32[256,256]{1,0:T(8,128)S(1)}, f32[256,256]{1,0:T(8,128)}, u32[]{:S(2)}) copy-start(f32[256,256]{1,0:T(8,128)} %co_ref.1) | copy-start | bytes 786436
  25.9 21.2 %copy-start.8 = (f32[256,256]{1,0:T(8,128)S(1)}, f32[256,256]{1,0:T(8,128)}, u32[]{:S(2)}) copy-start(f32[256,256]{1,0:T(8,128)} %di_ref.1) | copy-start | bytes 786436
  25.9 21.2 %copy-start.9 = (f32[256,256]{1,0:T(8,128)S(1)}, f32[256,256]{1,0:T(8,128)}, u32[]{:S(2)}) copy-start(f32[256,256]{1,0:T(8,128)} %do_ref.1) | copy-start | bytes 786436
  29.6 5.9 %collective-permute-start.5 = (f32[136,128]{1,0:T(8,128)S(1)}, f32[136,128]{1,0:T(8,128)S(1)}, u32[]{:S(2)}, u32[]{:S(2)}) collective-permute-start(f32[136,128]{1,0:T(8,128)S(1)} %get-tuple-element.57), channel_id=1, source_target_pairs={{0,4},{2,6},{4,0},{6,2},{8,12},{10,14},{12,8},{14,10},{1,5},{3,7},... | collective-permute-start | bytes 208904 | tf_op jit(solution)/shard_map/ppermute | solution.py:569
  29.7 5.8 %collective-permute-start.6 = (f32[136,128]{1,0:T(8,128)S(1)}, f32[136,128]{1,0:T(8,128)S(1)}, u32[]{:S(2)}, u32[]{:S(2)}) collective-permute-start(f32[136,128]{1,0:T(8,128)S(1)} %get-tuple-element.58), channel_id=1, source_target_pairs={{0,8},{2,10},{4,12},{6,14},{8,0},{10,2},{12,4},{14,6},{1,9},{3,11}... | collective-permute-start | bytes 208904 | tf_op jit(solution)/shard_map/ppermute | solution.py:569
  30.2 7.0 %collective-permute-start.7 = (f32[136,128]{1,0:T(8,128)S(1)}, f32[136,128]{1,0:T(8,128)S(1)}, u32[]{:S(2)}, u32[]{:S(2)}) collective-permute-start(f32[136,128]{1,0:T(8,128)S(1)} %get-tuple-element.59), channel_id=1, source_target_pairs={{0,12},{2,14},{4,8},{6,10},{8,4},{10,6},{12,0},{14,2},{1,13},{3,15... | collective-permute-start | bytes 208904 | tf_op jit(solution)/shard_map/ppermute | solution.py:569
  37.2 5.7 %collective-permute-start.8 = (f32[128,128]{1,0:T(8,128)S(1)}, f32[128,128]{1,0:T(8,128)S(1)}, u32[]{:S(2)}, u32[]{:S(2)}) collective-permute-start(f32[128,128]{1,0:T(8,128)S(1)} %shard_map.219.refs_0_), channel_id=1, source_target_pairs={{0,4},{2,6},{4,0},{6,2},{8,12},{10,14},{12,8},{14,10},{1,5},{3,7},... | collective-permute-start | bytes 196616 | tf_op jit(solution)/shard_map/ppermute | solution.py:569
  37.9 6.2 %collective-permute-start.9 = (f32[128,128]{1,0:T(8,128)S(1)}, f32[128,128]{1,0:T(8,128)S(1)}, u32[]{:S(2)}, u32[]{:S(2)}) collective-permute-start(f32[128,128]{1,0:T(8,128)S(1)} %shard_map.219.refs_0_), channel_id=1, source_target_pairs={{0,8},{2,10},{4,12},{6,14},{8,0},{10,2},{12,4},{14,6},{1,9},{3,11}... | collective-permute-start | bytes 196616 | tf_op jit(solution)/shard_map/ppermute | solution.py:569
  41.1 6.1 %collective-permute-start.10 = (f32[128,128]{1,0:T(8,128)S(1)}, f32[128,128]{1,0:T(8,128)S(1)}, u32[]{:S(2)}, u32[]{:S(2)}) collective-permute-start(f32[128,128]{1,0:T(8,128)S(1)} %shard_map.219.refs_0_), channel_id=1, source_target_pairs={{0,12},{2,14},{4,8},{6,10},{8,4},{10,6},{12,0},{14,2},{1,13},{3,15... | collective-permute-start | bytes 196616 | tf_op jit(solution)/shard_map/ppermute | solution.py:569
  41.7 8.2 %collective-permute-start.11 = (f32[128,128]{1,0:T(8,128)S(1)}, f32[128,128]{1,0:T(8,128)S(1)}, u32[]{:S(2)}, u32[]{:S(2)}) collective-permute-start(f32[128,128]{1,0:T(8,128)S(1)} %shard_map.219.refs_0_), channel_id=1, source_target_pairs={{0,2},{2,0},{4,6},{6,4},{8,10},{10,8},{12,14},{14,12},{1,3},{3,1},... | collective-permute-start | bytes 196616 | tf_op jit(solution)/shard_map/ppermute | solution.py:569
  42.9 7.1 %collective-permute-start.12 = (f32[128,128]{1,0:T(8,128)S(1)}, f32[128,128]{1,0:T(8,128)S(1)}, u32[]{:S(2)}, u32[]{:S(2)}) collective-permute-start(f32[128,128]{1,0:T(8,128)S(1)} %collective-permute-done.8.refs_1_), channel_id=1, source_target_pairs={{0,2},{2,0},{4,6},{6,4},{8,10},{10,8},{12,14},{14,12},{1,3},{3,1},... | collective-permute-start | bytes 196616 | tf_op jit(solution)/shard_map/ppermute | solution.py:569
  44.0 5.9 %collective-permute-start.13 = (f32[128,128]{1,0:T(8,128)S(1)}, f32[128,128]{1,0:T(8,128)S(1)}, u32[]{:S(2)}, u32[]{:S(2)}) collective-permute-start(f32[128,128]{1,0:T(8,128)S(1)} %collective-permute-done.9.refs_2_), channel_id=1, source_target_pairs={{0,2},{2,0},{4,6},{6,4},{8,10},{10,8},{12,14},{14,12},{1,3},{3,1},... | collective-permute-start | bytes 196616 | tf_op jit(solution)/shard_map/ppermute | solution.py:569
  47.1 4.3 %collective-permute-start.14 = (f32[128,128]{1,0:T(8,128)S(1)}, f32[128,128]{1,0:T(8,128)S(1)}, u32[]{:S(2)}, u32[]{:S(2)}) collective-permute-start(f32[128,128]{1,0:T(8,128)S(1)} %collective-permute-done.10.refs_3_), channel_id=1, source_target_pairs={{0,2},{2,0},{4,6},{6,4},{8,10},{10,8},{12,14},{14,12},{1,3},{3,1},... | collective-permute-start | bytes 196616 | tf_op jit(solution)/shard_map/ppermute | solution.py:569

commit v9 on v8

--- a/solution.py
+++ b/solution.py
@@ -168,9 +168,13 @@
     return jnp.dot(a, b, preferred_element_type=f32)
 
 
-def times(values, high, low):
-    vh, vl = halves(values)
-    return mm(vh, high) + (mm(vl, high) + mm(vh, low))
+def times(values, high, low, pieces=1):
+    size = values.shape[0] // pieces
+    done = []
+    for j in range(pieces):
+        vh, vl = halves(values[j * size : (j + 1) * size, :])
+        done.append(mm(vh, high) + (mm(vl, high) + mm(vh, low)))
+    return jnp.concatenate(done, axis=0)
 
 
 def take(one_hot, high, low):
@@ -321,7 +325,7 @@
     far = jnp.concatenate(
         [load_rows(swap_ref, rim, parts), load_rows(diag_ref, rim, parts)], axis=0
     )
-    high, low = halves(times(unit(far), *weights(high_ref, low_ref, 0)) * 0.5)
+    high, low = halves(times(unit(far), *weights(high_ref, low_ref, 0), 2) * 0.5)
     total = None
     for k in range(degree):
         part = slice(k * rows, (k + 1) * rows)
@@ -329,7 +333,7 @@
         total = gate(half) if total is None else total + gate(half)
     store_rows(
         out_full_ref,
-        load_rows(state_ref, rows, parts) + times(total, *weights(high_ref, low_ref, 1)),
+        load_rows(state_ref, rows, parts) + times(total, *weights(high_ref, low_ref, 1), 2),
         parts,
     )
     lines = out_half_ref.shape[0]
@@ -390,7 +394,7 @@
             [other, load_rows(pair_ref, rim, parts), load_rows(diag_ref, rim, parts)], axis=0
         )
     )
-    sends = halves(times(normed, *weights(high_ref, low_ref, 0)) * 0.5)
+    sends = halves(times(normed, *weights(high_ref, low_ref, 0), 2) * 0.5)
     near = []
     for src, t_ref, own_ref in (
         (sends[0], th_ref, own_high_ref), (sends[1], tl_ref, own_low_ref),
@@ -410,11 +414,11 @@
         half = into + take(hot2_ref[part, :], th_ref[...], tl_ref[...])
         total2 = gate(half) if total2 is None else total2 + gate(half)
     hidden = jnp.concatenate([load_rows(state_ref, rows, parts), other], axis=0) + times(
-        jnp.concatenate([total, total2], axis=0), *weights(high_ref, low_ref, 2)
+        jnp.concatenate([total, total2], axis=0), *weights(high_ref, low_ref, 2), 2
     )
     last_ref[...] = hidden[:rows, :]
-    act = gate((times(unit(hidden), *weights(high_ref, low_ref, 3)) + pack_ref[2:3, :]) * 0.5)
-    sums = take(select_ref[...], *halves(times(act, *weights(high_ref, low_ref, 4))))
+    act = gate((times(unit(hidden), *weights(high_ref, low_ref, 3), 2) + pack_ref[2:3, :]) * 0.5)
+    sums = take(select_ref[...], *halves(times(act, *weights(high_ref, low_ref, 4), 2)))
     size = sums.shape[0] // len(slot_refs)
     first = hot_ref.shape[0] // LANES + rows // LANES
     base = ints0_ref.shape[0] - ints_ref.shape[0]

time: 54.4 us -> 53.8 us (0.989)
  Pallas kernels: 15.4 us -> 14.7 us
where the time goes in v9:
time: 53.8 us; the launch traced here: 53.6 us
  starting transfers between devices  23.8 us (44%)
  Pallas kernels  14.7 us (27%)
  waiting for transfers between devices  14.2 us (26%)
  between operations  0.83 us (2%)
    ppermute x15, starting transfers between devices, move(): return lax.ppermute(values, 'sp', pairs)  23.8 us
    ppermute x15, waiting for transfers between devices, move(): return lax.ppermute(values, 'sp', pairs)  14.2 us
    pallas_call x1, Pallas kernels, kernel_shards(): call(up_kernel, [VMEM] * 16, [shape(rows, width)] + [shape(own + 8 * coar...  3.13 us
    pallas_call x1, Pallas kernels, kernel_shards(): call(coarse_kernel, [VMEM] * (8 + peers // 2), [shape(full, LANES), shape...  2.85 us
    pallas_call x1, Pallas kernels, kernel_shards(): call(functools.partial(near_kernel, edges), [VMEM] * 2 + [HBM] * 3 + [VME...  2.4 us
    pallas_call x1, Pallas kernels, kernel_shards(): call(functools.partial(edges_kernel, degree, count), [VMEM] * (1 + peers...  1.36 us
    pallas_call x1, Pallas kernels, kernel_shards(): call(functools.partial(start_kernel, count, HALO), [HBM] * 10, [shape(ful...  1.31 us
    pallas_call x1, Pallas kernels, kernel_shards(): call(column_kernel, [VMEM] * (4 + peers // 2), [shape(degree * (count + r...  1.16 us
  transfers between devices with their start and end apart: 15, of which 8 were waited for; matrix products, arithmetic and copies ran while one was open for 0% of the time, Pallas kernels for 12%

profile of v9, /device:TPU:0, one launch (start us, length us, event | category | flops | bytes accessed | tf_op | source)
XLA Modules:
  0.0 53.6 jit_solution(11589651701583145573)
XLA Ops:
  0.6 1.3 %shard_map.212 = (f32[512,128]{1,0:T(8,128)S(1)}, f32[16,128]{1,0:T(8,128)S(1)}, f32[8,256]{1,0:T(8,128)S(1)}, f32[272,128]{1,0:T(8,128)S(1)}, f32[256,128]{1,0:T(8,128)S(1)}) custom-call(f32[512,128]{1,0:T(8,128)} %bitcast.13, s32[8,128]{1,0:T(8,128)} %bitcast.14, s32[2,128]{1,0:T(2,128)} %bitcast.15, s32[2,128]{1,0:T(2,128)} %bitcast.16, ...), custom_call_target="tpu_custom_call" | custom-call | tf_op jit(solution)/shard_map/pallas_call | solution.py:629
  2.0 3.0 %collective-permute-start = (f32[272,128]{1,0:T(8,128)S(1)}, f32[272,128]{1,0:T(8,128)S(1)}, u32[]{:S(2)}, u32[]{:S(2)}) collective-permute-start(f32[272,128]{1,0:T(8,128)S(1)} %get-tuple-element.35), channel_id=1, source_target_pairs={{0,2},{2,0},{4,6},{6,4},{8,10},{10,8},{12,14},{14,12},{1,3},{3,1},... | collective-permute-start | bytes 417800 | tf_op jit(solution)/shard_map/ppermute | solution.py:573
  5.0 3.6 %collective-permute-start.1 = (f32[256,128]{1,0:T(8,128)S(1)}, f32[256,128]{1,0:T(8,128)S(1)}, u32[]{:S(2)}, u32[]{:S(2)}) collective-permute-start(f32[256,128]{1,0:T(8,128)S(1)} %get-tuple-element.36), channel_id=1, source_target_pairs={{0,14},{2,4},{4,2},{6,8},{8,6},{10,12},{12,10},{14,0},{1,15},{3,5}... | collective-permute-start | bytes 393224 | tf_op jit(solution)/shard_map/ppermute | solution.py:573
  8.6 2.4 %shard_map.213 = (bf16[1024,512]{1,0:T(8,128)(2,1)S(1)}, f32[1024,256]{1,0:T(8,128)S(1)}, f32[256,256]{1,0:T(8,128)S(1)}, bf16[512,256]{1,0:T(8,128)(2,1)S(1)}, bf16[512,256]{1,0:T(8,128)(2,1)S(1)}) custom-call(f32[512,128]{1,0:T(8,128)S(1)} %get-tuple-element.37.state_ref, f32[16,128]{1,0:T(8,128)S(1)} %get-tuple-element.38.ints_ref, ...), custom_call_target="tpu_custom_call" | custom-call | tf_op jit(solution)/shard_map/pallas_call | solution.py:640
  11.0 1.7 %collective-permute-done.1.diag_ref = f32[256,128]{1,0:T(8,128)S(1)} collective-permute-done((f32[256,128]{1,0:T(8,128)S(1)}, f32[256,128]{1,0:T(8,128)S(1)}, u32[]{:S(2)}, u32[]{:S(2)}) %collective-permute-start.1) | collective-permute-done | bytes 131104 | tf_op jit(solution)/shard_map/ppermute | solution.py:573
  12.7 0.0 copy-start.4
  12.7 1.1 %shard_map.214 = (f32[512,128]{1,0:T(8,128)S(1)}, f32[256,128]{1,0:T(8,128)S(1)}) custom-call(f32[272,128]{1,0:T(8,128)S(1)} %collective-permute-done.swap_ref.ints0_ref, f32[256,128]{1,0:T(8,128)S(1)} %collective-permute-done.1.diag_ref, f32[512,128]{1,0:T(8,128)S(1)} %get-tuple-element.37.state_ref, bf16[1024,512]{1,0:T(8,128)(2,1)S(1)} %get-tuple-element.40.hot_ref, ...), custom_call_target="tpu_custom_call" | custom-call | tf_op jit(solution)/shard_map/pallas_call | solution.py:647
  13.8 0.6 %collective-permute-start.2 = (f32[512,128]{1,0:T(8,128)S(1)}, f32[512,128]{1,0:T(8,128)S(1)}, u32[]{:S(2)}, u32[]{:S(2)}) collective-permute-start(f32[512,128]{1,0:T(8,128)S(1)} %get-tuple-element.45.state_ref), channel_id=1, source_target_pairs={{0,2},{2,0},{4,6},{6,4},{8,10},{10,8},{12,14},{14,12},{1,3},{3,1},... | collective-permute-start | bytes 786440 | tf_op jit(solution)/shard_map/ppermute | solution.py:573
  14.4 3.6 %collective-permute-start.3 = (f32[256,128]{1,0:T(8,128)S(1)}, f32[256,128]{1,0:T(8,128)S(1)}, u32[]{:S(2)}, u32[]{:S(2)}) collective-permute-start(f32[256,128]{1,0:T(8,128)S(1)} %get-tuple-element.46), channel_id=1, source_target_pairs={{0,12},{2,6},{4,0},{6,10},{8,4},{10,14},{12,8},{14,2},{1,13},{3,7}... | collective-permute-start | bytes 393224 | tf_op jit(solution)/shard_map/ppermute | solution.py:573
  18.1 1.1 %collective-permute-start.4 = (f32[256,128]{1,0:T(8,128)S(1)}, f32[256,128]{1,0:T(8,128)S(1)}, u32[]{:S(2)}, u32[]{:S(2)}) collective-permute-start(f32[256,128]{1,0:T(8,128)S(1)} %get-tuple-element.46), channel_id=1, source_target_pairs={{0,14},{2,4},{4,2},{6,8},{8,6},{10,12},{12,10},{14,0},{1,15},{3,5}... | collective-permute-start | bytes 393224 | tf_op jit(solution)/shard_map/ppermute | solution.py:573
  19.2 1.1 %shard_map.215 = (f32[1024,256]{1,0:T(8,128)S(1)}, f32[256,256]{1,0:T(8,128)S(1)}, bf16[256,256]{1,0:T(8,128)(2,1)S(1)}, bf16[256,256]{1,0:T(8,128)(2,1)S(1)}, b...) custom-call(f32[512,128]{1,0:T(8,128)S(1)} %get-tuple-element.45.sta, ...), custom_call_target="tpu_custom_call" | custom-call | tf_op jit(solution)/shard_map/pallas_call | solution.py:653
  20.4 0.2 collective-permute-done.3.pair_ref
  20.6 5.1 %collective-permute-done.4.diag_ref = f32[256,128]{1,0:T(8,128)S(1)} collective-permute-done((f32[256,128]{1,0:T(8,128)S(1)}, f32[256,128]{1,0:T(8,128)S(1)}, u32[]{:S(2)}, u32[]{:S(2)}) %collective-permute-start.4) | collective-permute-done | bytes 131104 | tf_op jit(solution)/shard_map/ppermute | solution.py:573
  25.8 3.1 %shard_map.216 = (f32[256,256]{1,0:T(8,128)S(1)}, f32[136,128]{1,0:T(8,128)S(1)}, f32[136,128]{1,0:T(8,128)S(1)}, f32[136,128]{1,0:T(8,128)S(1)}, f32[136,128]{1,0:T(8,128)S(1)}) custom-call(f32[512,128]{1,0:T(8,128)S(1)} %collective-permute-done.2.swap_ref, f32[256,128]{1,0:T(8,128)S(1)} %collective-permute-done.3.pair_ref, ...), custom_call_target="tpu_custom_call" | custom-call | tf_op jit(solution)/shard_map/pallas_call | solution.py:665
  28.9 0.1 collective-permute-start.5
  29.0 0.6 %collective-permute-start.6 = (f32[136,128]{1,0:T(8,128)S(1)}, f32[136,128]{1,0:T(8,128)S(1)}, u32[]{:S(2)}, u32[]{:S(2)}) collective-permute-start(f32[136,128]{1,0:T(8,128)S(1)} %get-tuple-element.58), channel_id=1, source_target_pairs={{0,8},{2,10},{4,12},{6,14},{8,0},{10,2},{12,4},{14,6},{1,9},{3,11}... | collective-permute-start | bytes 208904 | tf_op jit(solution)/shard_map/ppermute | solution.py:573
  29.6 3.8 %collective-permute-start.7 = (f32[136,128]{1,0:T(8,128)S(1)}, f32[136,128]{1,0:T(8,128)S(1)}, u32[]{:S(2)}, u32[]{:S(2)}) collective-permute-start(f32[136,128]{1,0:T(8,128)S(1)} %get-tuple-element.59), channel_id=1, source_target_pairs={{0,12},{2,14},{4,8},{6,10},{8,4},{10,6},{12,0},{14,2},{1,13},{3,15... | collective-permute-start | bytes 208904 | tf_op jit(solution)/shard_map/ppermute | solution.py:573
  33.4 1.4 %collective-permute-done.5.refs_1_ = f32[136,128]{1,0:T(8,128)S(1)} collective-permute-done((f32[136,128]{1,0:T(8,128)S(1)}, f32[136,128]{1,0:T(8,128)S(1)}, u32[]{:S(2)}, u32[]{:S(2)}) %collective-permute-start.5) | collective-permute-done | bytes 69664 | tf_op jit(solution)/shard_map/ppermute | solution.py:573
  34.8 1.8 %collective-permute-done.7.refs_3_ = f32[136,128]{1,0:T(8,128)S(1)} collective-permute-done((f32[136,128]{1,0:T(8,128)S(1)}, f32[136,128]{1,0:T(8,128)S(1)}, u32[]{:S(2)}, u32[]{:S(2)}) %collective-permute-start.7) | collective-permute-done | bytes 69664 | tf_op jit(solution)/shard_map/ppermute | solution.py:573
  36.6 0.6 %collective-permute-start.8 = (f32[128,128]{1,0:T(8,128)S(1)}, f32[128,128]{1,0:T(8,128)S(1)}, u32[]{:S(2)}, u32[]{:S(2)}) collective-permute-start(f32[128,128]{1,0:T(8,128)S(1)} %shard_map.219.refs_0_), channel_id=1, source_target_pairs={{0,4},{2,6},{4,0},{6,2},{8,12},{10,14},{12,8},{14,10},{1,5},{3,7},... | collective-permute-start | bytes 196616 | tf_op jit(solution)/shard_map/ppermute | solution.py:573
  37.2 3.2 %collective-permute-start.9 = (f32[128,128]{1,0:T(8,128)S(1)}, f32[128,128]{1,0:T(8,128)S(1)}, u32[]{:S(2)}, u32[]{:S(2)}) collective-permute-start(f32[128,128]{1,0:T(8,128)S(1)} %shard_map.219.refs_0_), channel_id=1, source_target_pairs={{0,8},{2,10},{4,12},{6,14},{8,0},{10,2},{12,4},{14,6},{1,9},{3,11}... | collective-permute-start | bytes 196616 | tf_op jit(solution)/shard_map/ppermute | solution.py:573
  40.4 0.6 %collective-permute-start.10 = (f32[128,128]{1,0:T(8,128)S(1)}, f32[128,128]{1,0:T(8,128)S(1)}, u32[]{:S(2)}, u32[]{:S(2)}) collective-permute-start(f32[128,128]{1,0:T(8,128)S(1)} %shard_map.219.refs_0_), channel_id=1, source_target_pairs={{0,12},{2,14},{4,8},{6,10},{8,4},{10,6},{12,0},{14,2},{1,13},{3,15... | collective-permute-start | bytes 196616 | tf_op jit(solution)/shard_map/ppermute | solution.py:573
  41.0 1.2 %collective-permute-start.11 = (f32[128,128]{1,0:T(8,128)S(1)}, f32[128,128]{1,0:T(8,128)S(1)}, u32[]{:S(2)}, u32[]{:S(2)}) collective-permute-start(f32[128,128]{1,0:T(8,128)S(1)} %shard_map.219.refs_0_), channel_id=1, source_target_pairs={{0,2},{2,0},{4,6},{6,4},{8,10},{10,8},{12,14},{14,12},{1,3},{3,1},... | collective-permute-start | bytes 196616 | tf_op jit(solution)/shard_map/ppermute | solution.py:573
  42.2 0.8 %collective-permute-start.12 = (f32[128,128]{1,0:T(8,128)S(1)}, f32[128,128]{1,0:T(8,128)S(1)}, u32[]{:S(2)}, u32[]{:S(2)}) collective-permute-start(f32[128,128]{1,0:T(8,128)S(1)} %collective-permute-done.8.refs_1_), channel_id=1, source_target_pairs={{0,2},{2,0},{4,6},{6,4},{8,10},{10,8},{12,14},{14,12},{1,3},{3,1},... | collective-permute-start | bytes 196616 | tf_op jit(solution)/shard_map/ppermute | solution.py:573
  43.0 0.3 collective-permute-done.9.refs_2_
  43.4 0.9 %collective-permute-start.13 = (f32[128,128]{1,0:T(8,128)S(1)}, f32[128,128]{1,0:T(8,128)S(1)}, u32[]{:S(2)}, u32[]{:S(2)}) collective-permute-start(f32[128,128]{1,0:T(8,128)S(1)} %collective-permute-done.9.refs_2_), channel_id=1, source_target_pairs={{0,2},{2,0},{4,6},{6,4},{8,10},{10,8},{12,14},{14,12},{1,3},{3,1},... | collective-permute-start | bytes 196616 | tf_op jit(solution)/shard_map/ppermute | solution.py:573
  44.3 2.2 %collective-permute-done.10.refs_3_ = f32[128,128]{1,0:T(8,128)S(1)} collective-permute-done((f32[128,128]{1,0:T(8,128)S(1)}, f32[128,128]{1,0:T(8,128)S(1)}, u32[]{:S(2)}, u32[]{:S(2)}) %collective-permute-start.10) | collective-permute-done | bytes 65568 | tf_op jit(solution)/shard_map/ppermute | solution.py:573
  46.5 0.2 shard_map.218
  46.7 1.4 %shard_map.217 = (bf16[1280,512]{1,0:T(8,128)(2,1)S(1)}, bf16[256,512]{1,0:T(8,128)(2,1)S(1)}) custom-call(f32[16,128]{1,0:T(8,128)S(1)} %get-tuple-element.38.ints_ref, f32[136,128]{1,0:T(8,128)S(1)} %get-tuple-element.56.refs_0_, f32[136,128]{1,0:T(8,128)S(1)} %collective-permute-done.5.refs_1_, f32[136,128]{1,0:T(8,128)S(1)} %collective-permute-done.6.refs_2_, ...), custom_call_target="tpu_custom_call" | custom-call | tf_op jit(solution)/shard_map/pallas_call | solution.py:682
  48.1 1.2 %shard_map.220 = (f32[1280,256]{1,0:T(8,128)S(1)}, f32[320,256]{1,0:T(8,128)S(1)}) custom-call(bf16[1280,512]{1,0:T(8,128)(2,1)S(1)} %get-tuple-element.60.hot_ref, bf16[256,512]{1,0:T(8,128)(2,1)S(1)} %get-tuple-element.61.parent_ref, bf16[1280,256]{1,0:T(8,128)(2,1)S(1)} %get-tuple-element.62.high_ref, bf16[1280,256]{1,0:T(8,128)(2,1)S(1)} %get-tuple-element.63.low_ref, ...), custom_call_target="tpu_custom_call" | custom-call | tf_op jit(solution)/shard_map/pallas_call | solution.py:694
  49.3 1.5 %collective-permute-done.14.refs_3_ = f32[128,128]{1,0:T(8,128)S(1)} collective-permute-done((f32[128,128]{1,0:T(8,128)S(1)}, f32[128,128]{1,0:T(8,128)S(1)}, u32[]{:S(2)}, u32[]{:S(2)}) %collective-permute-start.14) | collective-permute-done | bytes 65568 | tf_op jit(solution)/shard_map/ppermute | solution.py:573
  50.7 2.9 %shard_map.221 = (f32[512,128]{1,0:T(8,128)}, f32[128,128]{1,0:T(8,128)}) custom-call(f32[256,256]{1,0:T(8,128)S(1)} %get-tuple-element.55.last_ref, bf16[1280,512]{1,0:T(8,128)(2,1)S(1)} %get-tuple-element.60.hot_ref, bf16[256,512]{1,0:T(8,128)(2,1)S(1)} %get-tuple-element.61.parent_ref, f32[1280,256]{1,0:T(8,128)S(1)} %get-tuple-element.64.got_ref, ...), custom_call_target="tpu_custom_call" | custom-call | tf_op jit(solution)/shard_map/pallas_call | solution.py:699
  (30 shorter events, 0.1 us)
Async XLA Ops:
  2.0 10.7 %collective-permute-start = (f32[272,128]{1,0:T(8,128)S(1)}, f32[272,128]{1,0:T(8,128)S(1)}, u32[]{:S(2)}, u32[]{:S(2)}) collective-permute-start(f32[272,128]{1,0:T(8,128)S(1)} %get-tuple-element.35), channel_id=1, source_target_pairs={{0,2},{2,0},{4,6},{6,4},{8,10},{10,8},{12,14},{14,12},{1,3},{3,1},... | collective-permute-start | bytes 417800 | tf_op jit(solution)/shard_map/ppermute | solution.py:573
  5.0 7.7 %collective-permute-start.1 = (f32[256,128]{1,0:T(8,128)S(1)}, f32[256,128]{1,0:T(8,128)S(1)}, u32[]{:S(2)}, u32[]{:S(2)}) collective-permute-start(f32[256,128]{1,0:T(8,128)S(1)} %get-tuple-element.36), channel_id=1, source_target_pairs={{0,14},{2,4},{4,2},{6,8},{8,6},{10,12},{12,10},{14,0},{1,15},{3,5}... | collective-permute-start | bytes 393224 | tf_op jit(solution)/shard_map/ppermute | solution.py:573
  12.7 6.5 %copy-start = (f32[2,256,256]{2,1,0:T(8,128)S(1)}, f32[2,256,256]{2,1,0:T(8,128)}, u32[]{:S(2)}) copy-start(f32[2,256,256]{2,1,0:T(8,128)} %ws_ref.1) | copy-start | bytes 1572868
  12.7 6.5 %copy-start.1 = (f32[2,256,256]{2,1,0:T(8,128)S(1)}, f32[2,256,256]{2,1,0:T(8,128)}, u32[]{:S(2)}) copy-start(f32[2,256,256]{2,1,0:T(8,128)} %wr_ref.1) | copy-start | bytes 1572868
  12.7 6.5 %copy-start.2 = (f32[2,256,256]{2,1,0:T(8,128)S(1)}, f32[2,256,256]{2,1,0:T(8,128)}, u32[]{:S(2)}) copy-start(f32[2,256,256]{2,1,0:T(8,128)} %wo_ref.1) | copy-start | bytes 1572868
  12.7 6.5 %copy-start.3 = (f32[256,256]{1,0:T(8,128)S(1)}, f32[256,256]{1,0:T(8,128)}, u32[]{:S(2)}) copy-start(f32[256,256]{1,0:T(8,128)} %wi_ref.1) | copy-start | bytes 786436
  12.7 6.5 %copy-start.4 = (f32[256,256]{1,0:T(8,128)S(1)}, f32[256,256]{1,0:T(8,128)}, u32[]{:S(2)}) copy-start(f32[256,256]{1,0:T(8,128)} %wu_ref.1) | copy-start | bytes 786436
  13.8 11.9 %collective-permute-start.2 = (f32[512,128]{1,0:T(8,128)S(1)}, f32[512,128]{1,0:T(8,128)S(1)}, u32[]{:S(2)}, u32[]{:S(2)}) collective-permute-start(f32[512,128]{1,0:T(8,128)S(1)} %get-tuple-element.45.state_ref), channel_id=1, source_target_pairs={{0,2},{2,0},{4,6},{6,4},{8,10},{10,8},{12,14},{14,12},{1,3},{3,1},... | collective-permute-start | bytes 786440 | tf_op jit(solution)/shard_map/ppermute | solution.py:573
  14.4 6.1 %collective-permute-start.3 = (f32[256,128]{1,0:T(8,128)S(1)}, f32[256,128]{1,0:T(8,128)S(1)}, u32[]{:S(2)}, u32[]{:S(2)}) collective-permute-start(f32[256,128]{1,0:T(8,128)S(1)} %get-tuple-element.46), channel_id=1, source_target_pairs={{0,12},{2,6},{4,0},{6,10},{8,4},{10,14},{12,8},{14,2},{1,13},{3,7}... | collective-permute-start | bytes 393224 | tf_op jit(solution)/shard_map/ppermute | solution.py:573
  18.1 7.7 %collective-permute-start.4 = (f32[256,128]{1,0:T(8,128)S(1)}, f32[256,128]{1,0:T(8,128)S(1)}, u32[]{:S(2)}, u32[]{:S(2)}) collective-permute-start(f32[256,128]{1,0:T(8,128)S(1)} %get-tuple-element.46), channel_id=1, source_target_pairs={{0,14},{2,4},{4,2},{6,8},{8,6},{10,12},{12,10},{14,0},{1,15},{3,5}... | collective-permute-start | bytes 393224 | tf_op jit(solution)/shard_map/ppermute | solution.py:573
  25.7 10.8 %copy-start.10 = (f32[64,1,256]{2,1,0:T(1,128)S(1)}, f32[64,1,256]{2,1,0:T(1,128)}, u32[]{:S(2)}) copy-start(f32[64,1,256]{2,1,0:T(1,128)} %param.22) | copy-start | bytes 196612
  25.7 20.8 %copy-start.5 = (f32[256,256]{1,0:T(8,128)S(1)}, f32[256,256]{1,0:T(8,128)}, u32[]{:S(2)}) copy-start(f32[256,256]{1,0:T(8,128)} %cs_ref.1) | copy-start | bytes 786436
  25.7 20.8 %copy-start.6 = (f32[256,256]{1,0:T(8,128)S(1)}, f32[256,256]{1,0:T(8,128)}, u32[]{:S(2)}) copy-start(f32[256,256]{1,0:T(8,128)} %cr_ref.1) | copy-start | bytes 786436
  25.7 20.8 %copy-start.7 = (f32[256,256]{1,0:T(8,128)S(1)}, f32[256,256]{1,0:T(8,128)}, u32[]{:S(2)}) copy-start(f32[256,256]{1,0:T(8,128)} %co_ref.1) | copy-start | bytes 786436
  25.7 20.8 %copy-start.8 = (f32[256,256]{1,0:T(8,128)S(1)}, f32[256,256]{1,0:T(8,128)}, u32[]{:S(2)}) copy-start(f32[256,256]{1,0:T(8,128)} %di_ref.1) | copy-start | bytes 786436
  25.8 20.8 %copy-start.9 = (f32[256,256]{1,0:T(8,128)S(1)}, f32[256,256]{1,0:T(8,128)}, u32[]{:S(2)}) copy-start(f32[256,256]{1,0:T(8,128)} %do_ref.1) | copy-start | bytes 786436
  28.9 5.8 %collective-permute-start.5 = (f32[136,128]{1,0:T(8,128)S(1)}, f32[136,128]{1,0:T(8,128)S(1)}, u32[]{:S(2)}, u32[]{:S(2)}) collective-permute-start(f32[136,128]{1,0:T(8,128)S(1)} %get-tuple-element.57), channel_id=1, source_target_pairs={{0,4},{2,6},{4,0},{6,2},{8,12},{10,14},{12,8},{14,10},{1,5},{3,7},... | collective-permute-start | bytes 208904 | tf_op jit(solution)/shard_map/ppermute | solution.py:573
  29.0 5.8 %collective-permute-start.6 = (f32[136,128]{1,0:T(8,128)S(1)}, f32[136,128]{1,0:T(8,128)S(1)}, u32[]{:S(2)}, u32[]{:S(2)}) collective-permute-start(f32[136,128]{1,0:T(8,128)S(1)} %get-tuple-element.58), channel_id=1, source_target_pairs={{0,8},{2,10},{4,12},{6,14},{8,0},{10,2},{12,4},{14,6},{1,9},{3,11}... | collective-permute-start | bytes 208904 | tf_op jit(solution)/shard_map/ppermute | solution.py:573
  29.6 7.0 %collective-permute-start.7 = (f32[136,128]{1,0:T(8,128)S(1)}, f32[136,128]{1,0:T(8,128)S(1)}, u32[]{:S(2)}, u32[]{:S(2)}) collective-permute-start(f32[136,128]{1,0:T(8,128)S(1)} %get-tuple-element.59), channel_id=1, source_target_pairs={{0,12},{2,14},{4,8},{6,10},{8,4},{10,6},{12,0},{14,2},{1,13},{3,15... | collective-permute-start | bytes 208904 | tf_op jit(solution)/shard_map/ppermute | solution.py:573
  36.6 5.7 %collective-permute-start.8 = (f32[128,128]{1,0:T(8,128)S(1)}, f32[128,128]{1,0:T(8,128)S(1)}, u32[]{:S(2)}, u32[]{:S(2)}) collective-permute-start(f32[128,128]{1,0:T(8,128)S(1)} %shard_map.219.refs_0_), channel_id=1, source_target_pairs={{0,4},{2,6},{4,0},{6,2},{8,12},{10,14},{12,8},{14,10},{1,5},{3,7},... | collective-permute-start | bytes 196616 | tf_op jit(solution)/shard_map/ppermute | solution.py:573
  37.2 6.2 %collective-permute-start.9 = (f32[128,128]{1,0:T(8,128)S(1)}, f32[128,128]{1,0:T(8,128)S(1)}, u32[]{:S(2)}, u32[]{:S(2)}) collective-permute-start(f32[128,128]{1,0:T(8,128)S(1)} %shard_map.219.refs_0_), channel_id=1, source_target_pairs={{0,8},{2,10},{4,12},{6,14},{8,0},{10,2},{12,4},{14,6},{1,9},{3,11}... | collective-permute-start | bytes 196616 | tf_op jit(solution)/shard_map/ppermute | solution.py:573
  40.4 6.1 %collective-permute-start.10 = (f32[128,128]{1,0:T(8,128)S(1)}, f32[128,128]{1,0:T(8,128)S(1)}, u32[]{:S(2)}, u32[]{:S(2)}) collective-permute-start(f32[128,128]{1,0:T(8,128)S(1)} %shard_map.219.refs_0_), channel_id=1, source_target_pairs={{0,12},{2,14},{4,8},{6,10},{8,4},{10,6},{12,0},{14,2},{1,13},{3,15... | collective-permute-start | bytes 196616 | tf_op jit(solution)/shard_map/ppermute | solution.py:573
  41.0 8.2 %collective-permute-start.11 = (f32[128,128]{1,0:T(8,128)S(1)}, f32[128,128]{1,0:T(8,128)S(1)}, u32[]{:S(2)}, u32[]{:S(2)}) collective-permute-start(f32[128,128]{1,0:T(8,128)S(1)} %shard_map.219.refs_0_), channel_id=1, source_target_pairs={{0,2},{2,0},{4,6},{6,4},{8,10},{10,8},{12,14},{14,12},{1,3},{3,1},... | collective-permute-start | bytes 196616 | tf_op jit(solution)/shard_map/ppermute | solution.py:573
  42.2 7.1 %collective-permute-start.12 = (f32[128,128]{1,0:T(8,128)S(1)}, f32[128,128]{1,0:T(8,128)S(1)}, u32[]{:S(2)}, u32[]{:S(2)}) collective-permute-start(f32[128,128]{1,0:T(8,128)S(1)} %collective-permute-done.8.refs_1_), channel_id=1, source_target_pairs={{0,2},{2,0},{4,6},{6,4},{8,10},{10,8},{12,14},{14,12},{1,3},{3,1},... | collective-permute-start | bytes 196616 | tf_op jit(solution)/shard_map/ppermute | solution.py:573
  43.4 5.9 %collective-permute-start.13 = (f32[128,128]{1,0:T(8,128)S(1)}, f32[128,128]{1,0:T(8,128)S(1)}, u32[]{:S(2)}, u32[]{:S(2)}) collective-permute-start(f32[128,128]{1,0:T(8,128)S(1)} %collective-permute-done.9.refs_2_), channel_id=1, source_target_pairs={{0,2},{2,0},{4,6},{6,4},{8,10},{10,8},{12,14},{14,12},{1,3},{3,1},... | collective-permute-start | bytes 196616 | tf_op jit(solution)/shard_map/ppermute | solution.py:573
  46.5 4.3 %collective-permute-start.14 = (f32[128,128]{1,0:T(8,128)S(1)}, f32[128,128]{1,0:T(8,128)S(1)}, u32[]{:S(2)}, u32[]{:S(2)}) collective-permute-start(f32[128,128]{1,0:T(8,128)S(1)} %collective-permute-done.10.refs_3_), channel_id=1, source_target_pairs={{0,2},{2,0},{4,6},{6,4},{8,10},{10,8},{12,14},{14,12},{1,3},{3,1},... | collective-permute-start | bytes 196616 | tf_op jit(solution)/shard_map/ppermute | solution.py:573

commit v10 on v9

--- a/solution.py
+++ b/solution.py
@@ -443,14 +443,8 @@
     out_ref[...] = total
 
 
-def position(ids, flip, count, coarse):
-    ids = jnp.bitwise_xor(ids.astype(jnp.int32), flip)
-    slot = jnp.right_shift(ids, count.bit_length() - 1)
-    return (
-        jnp.bitwise_and(ids, count - 1)
-        + jnp.right_shift(slot, 1) * count
-        + jnp.bitwise_and(slot, 1) * (coarse // 2)
-    )
+def position(ids, flip):
+    return jnp.bitwise_xor(ids.astype(jnp.int32), flip)
 
 
 def split_kernel(cs_ref, cr_ref, co_ref, di_ref, do_ref, high_ref, low_ref):
@@ -466,17 +460,11 @@
     columns = turned(ints_ref[...])
     first = ints_ref.shape[0] // 2
     for j in range(rows // LANES):
-        column = position(columns[:, first + j : first + j + 1], flip, count, coarse).astype(f32)
+        column = position(columns[:, first + j : first + j + 1], flip).astype(f32)
         parent_ref[j * LANES : (j + 1) * LANES, :] = equal(column, coarse)
     here = coarse * degree // LANES // len(slot_refs)
-    line = here // 2
     lines = jnp.concatenate(
-        [
-            ref[ref.shape[0] - 2 * here + side * line : ref.shape[0] - 2 * here + (side + 1) * line, :]
-            for side in range(2)
-            for ref in slot_refs
-        ],
-        axis=0,
+        [ref[ref.shape[0] - 2 * here : ref.shape[0] - here, :] for ref in slot_refs], axis=0
     )
     turn_ref[...] = turned(lines)
     step = LANES // degree
@@ -484,7 +472,7 @@
     table = jnp.zeros((coarse, LANES), f32)
     each = hot_ref.shape[0] // degree
     for k in range(degree):
-        spread = position(turn_ref[pl.ds(k, step, stride=degree), :], flip, count, coarse)
+        spread = position(turn_ref[pl.ds(k, step, stride=degree), :], flip)
         column = jnp.concatenate([spread[:, j : j + 1] for j in range(lines.shape[0])], axis=0)
         hot_ref[k * each : k * each + count, :] = equal(column[:count, :].astype(f32), coarse)
         high = jnp.right_shift(column, 8).astype(f32)
@@ -676,8 +664,11 @@
     (middle,) = call(
         middle_kernel, [VMEM] * (1 + peers // 2), [shape(own, LANES)]
     )(lines(coarse_state), *arrived)
-    columns = [middle] + [move(middle, flips[j]) for j in range(1, peers // 2)]
-    across = [move(block, swap) for block in columns]
+    shift = lambda k: [(i, i ^ k) for i in range(peers)]
+    near, far = [middle], [move(middle, shift(peers // 2))]
+    for k in range(1, peers // 2):
+        near.append(move(middle, shift(k)))
+        far.append(move(far[0], shift(k)))
     degree = coarse_edges // count
     coarse_hot, parent_hot = call(
         functools.partial(edges_kernel, degree, count),
@@ -695,7 +686,7 @@
         column_kernel,
         [VMEM] * (4 + peers // 2),
         [shape(degree * (count + rows), width), shape(count + rows, width)],
-    )(coarse_hot, parent_hot, high, low, *columns)
+    )(coarse_hot, parent_hot, high, low, *near)
     fine_out, coarse_out = call(
         coarse_kernel,
         [VMEM] * (8 + peers // 2),
@@ -705,7 +696,7 @@
             pltpu.SemaphoreType.DMA((3,)),
         ],
         HBM,
-    )(hidden, coarse_hot, parent_hot, got, wanted, high, low, pack, *across)
+    )(hidden, coarse_hot, parent_hot, got, wanted, high, low, pack, *far)
     return (fine_out.reshape(fine_state.shape), coarse_out.reshape(coarse_state.shape))
 
 

time: 53.8 us -> 52.6 us (0.978)
  waiting for transfers between devices: 14.2 us -> 11.1 us
  starting transfers between devices: 23.8 us -> 25.7 us
    ppermute x15, waiting for transfers between devices: 14.2 us -> 11.1 us  [move(): return lax.ppermute(values, 'sp', pairs)]
    ppermute x15, starting transfers between devices: 23.8 us -> 25.7 us  [move(): return lax.ppermute(values, 'sp', pairs)]
  transfers between devices with their start and end apart: 15 -> 15, of which waited for: 8 -> 6; matrix products, arithmetic and copies ran while one was open for 0% -> 0% of each run, Pallas kernels for 12% -> 12%
where the time goes in v10:
time: 52.6 us; the launch traced here: 52.4 us
  starting transfers between devices  25.7 us (49%)
  Pallas kernels  14.7 us (28%)
  waiting for transfers between devices  11.1 us (21%)
  between operations  0.82 us (2%)
    ppermute x15, starting transfers between devices, move(): return lax.ppermute(values, 'sp', pairs)  25.7 us
    ppermute x15, waiting for transfers between devices, move(): return lax.ppermute(values, 'sp', pairs)  11.1 us
    pallas_call x1, Pallas kernels, kernel_shards(): call(up_kernel, [VMEM] * 16, [shape(rows, width)] + [shape(own + 8 * coar...  3.13 us
    pallas_call x1, Pallas kernels, kernel_shards(): call(coarse_kernel, [VMEM] * (8 + peers // 2), [shape(full, LANES), shape...  2.85 us
    pallas_call x1, Pallas kernels, kernel_shards(): call(functools.partial(near_kernel, edges), [VMEM] * 2 + [HBM] * 3 + [VME...  2.4 us
    pallas_call x1, Pallas kernels, kernel_shards(): call(functools.partial(edges_kernel, degree, count), [VMEM] * (1 + peers...  1.35 us
    pallas_call x1, Pallas kernels, kernel_shards(): call(functools.partial(start_kernel, count, HALO), [HBM] * 10, [shape(ful...  1.31 us
    pallas_call x1, Pallas kernels, kernel_shards(): call(column_kernel, [VMEM] * (4 + peers // 2), [shape(degree * (count + r...  1.16 us
  transfers between devices with their start and end apart: 15, of which 6 were waited for; matrix products, arithmetic and copies ran while one was open for 0% of the time, Pallas kernels for 12%

profile of v10, /device:TPU:0, one launch (start us, length us, event | category | flops | bytes accessed | tf_op | source)
XLA Modules:
  0.0 52.4 jit_solution(11643863497855804257)
XLA Ops:
  0.6 1.3 %shard_map.212 = (f32[512,128]{1,0:T(8,128)S(1)}, f32[16,128]{1,0:T(8,128)S(1)}, f32[8,256]{1,0:T(8,128)S(1)}, f32[272,128]{1,0:T(8,128)S(1)}, f32[256,128]{1,0:T(8,128)S(1)}) custom-call(f32[512,128]{1,0:T(8,128)} %bitcast.13, s32[8,128]{1,0:T(8,128)} %bitcast.14, s32[2,128]{1,0:T(2,128)} %bitcast.15, s32[2,128]{1,0:T(2,128)} %bitcast.16, ...), custom_call_target="tpu_custom_call" | custom-call | tf_op jit(solution)/shard_map/pallas_call | solution.py:617
  2.0 3.0 %collective-permute-start = (f32[272,128]{1,0:T(8,128)S(1)}, f32[272,128]{1,0:T(8,128)S(1)}, u32[]{:S(2)}, u32[]{:S(2)}) collective-permute-start(f32[272,128]{1,0:T(8,128)S(1)} %get-tuple-element.35), channel_id=1, source_target_pairs={{0,2},{2,0},{4,6},{6,4},{8,10},{10,8},{12,14},{14,12},{1,3},{3,1},... | collective-permute-start | bytes 417800 | tf_op jit(solution)/shard_map/ppermute | solution.py:561
  5.0 3.6 %collective-permute-start.1 = (f32[256,128]{1,0:T(8,128)S(1)}, f32[256,128]{1,0:T(8,128)S(1)}, u32[]{:S(2)}, u32[]{:S(2)}) collective-permute-start(f32[256,128]{1,0:T(8,128)S(1)} %get-tuple-element.36), channel_id=1, source_target_pairs={{0,14},{2,4},{4,2},{6,8},{8,6},{10,12},{12,10},{14,0},{1,15},{3,5}... | collective-permute-start | bytes 393224 | tf_op jit(solution)/shard_map/ppermute | solution.py:561
  8.6 2.4 %shard_map.213 = (bf16[1024,512]{1,0:T(8,128)(2,1)S(1)}, f32[1024,256]{1,0:T(8,128)S(1)}, f32[256,256]{1,0:T(8,128)S(1)}, bf16[512,256]{1,0:T(8,128)(2,1)S(1)}, bf16[512,256]{1,0:T(8,128)(2,1)S(1)}) custom-call(f32[512,128]{1,0:T(8,128)S(1)} %get-tuple-element.37.state_ref, f32[16,128]{1,0:T(8,128)S(1)} %get-tuple-element.38.ints_ref, ...), custom_call_target="tpu_custom_call" | custom-call | tf_op jit(solution)/shard_map/pallas_call | solution.py:628
  11.0 1.7 %collective-permute-done.1.diag_ref = f32[256,128]{1,0:T(8,128)S(1)} collective-permute-done((f32[256,128]{1,0:T(8,128)S(1)}, f32[256,128]{1,0:T(8,128)S(1)}, u32[]{:S(2)}, u32[]{:S(2)}) %collective-permute-start.1) | collective-permute-done | bytes 131104 | tf_op jit(solution)/shard_map/ppermute | solution.py:561
  12.7 0.0 copy-start.4
  12.7 1.1 %shard_map.214 = (f32[512,128]{1,0:T(8,128)S(1)}, f32[256,128]{1,0:T(8,128)S(1)}) custom-call(f32[272,128]{1,0:T(8,128)S(1)} %collective-permute-done.swap_ref.ints0_ref, f32[256,128]{1,0:T(8,128)S(1)} %collective-permute-done.1.diag_ref, f32[512,128]{1,0:T(8,128)S(1)} %get-tuple-element.37.state_ref, bf16[1024,512]{1,0:T(8,128)(2,1)S(1)} %get-tuple-element.40.hot_ref, ...), custom_call_target="tpu_custom_call" | custom-call | tf_op jit(solution)/shard_map/pallas_call | solution.py:635
  13.8 0.6 %collective-permute-start.2 = (f32[512,128]{1,0:T(8,128)S(1)}, f32[512,128]{1,0:T(8,128)S(1)}, u32[]{:S(2)}, u32[]{:S(2)}) collective-permute-start(f32[512,128]{1,0:T(8,128)S(1)} %get-tuple-element.45.state_ref), channel_id=1, source_target_pairs={{0,2},{2,0},{4,6},{6,4},{8,10},{10,8},{12,14},{14,12},{1,3},{3,1},... | collective-permute-start | bytes 786440 | tf_op jit(solution)/shard_map/ppermute | solution.py:561
  14.4 3.6 %collective-permute-start.3 = (f32[256,128]{1,0:T(8,128)S(1)}, f32[256,128]{1,0:T(8,128)S(1)}, u32[]{:S(2)}, u32[]{:S(2)}) collective-permute-start(f32[256,128]{1,0:T(8,128)S(1)} %get-tuple-element.46), channel_id=1, source_target_pairs={{0,12},{2,6},{4,0},{6,10},{8,4},{10,14},{12,8},{14,2},{1,13},{3,7}... | collective-permute-start | bytes 393224 | tf_op jit(solution)/shard_map/ppermute | solution.py:561
  18.1 1.1 %collective-permute-start.4 = (f32[256,128]{1,0:T(8,128)S(1)}, f32[256,128]{1,0:T(8,128)S(1)}, u32[]{:S(2)}, u32[]{:S(2)}) collective-permute-start(f32[256,128]{1,0:T(8,128)S(1)} %get-tuple-element.46), channel_id=1, source_target_pairs={{0,14},{2,4},{4,2},{6,8},{8,6},{10,12},{12,10},{14,0},{1,15},{3,5}... | collective-permute-start | bytes 393224 | tf_op jit(solution)/shard_map/ppermute | solution.py:561
  19.2 1.1 %shard_map.215 = (f32[1024,256]{1,0:T(8,128)S(1)}, f32[256,256]{1,0:T(8,128)S(1)}, bf16[256,256]{1,0:T(8,128)(2,1)S(1)}, bf16[256,256]{1,0:T(8,128)(2,1)S(1)}, b...) custom-call(f32[512,128]{1,0:T(8,128)S(1)} %get-tuple-element.45.sta, ...), custom_call_target="tpu_custom_call" | custom-call | tf_op jit(solution)/shard_map/pallas_call | solution.py:641
  20.4 0.2 collective-permute-done.3.pair_ref
  20.6 5.1 %collective-permute-done.4.diag_ref = f32[256,128]{1,0:T(8,128)S(1)} collective-permute-done((f32[256,128]{1,0:T(8,128)S(1)}, f32[256,128]{1,0:T(8,128)S(1)}, u32[]{:S(2)}, u32[]{:S(2)}) %collective-permute-start.4) | collective-permute-done | bytes 131104 | tf_op jit(solution)/shard_map/ppermute | solution.py:561
  25.7 0.0 copy-start.8
  25.8 0.0 copy-start.9
  25.8 3.1 %shard_map.216 = (f32[256,256]{1,0:T(8,128)S(1)}, f32[136,128]{1,0:T(8,128)S(1)}, f32[136,128]{1,0:T(8,128)S(1)}, f32[136,128]{1,0:T(8,128)S(1)}, f32[136,128]{1,0:T(8,128)S(1)}) custom-call(f32[512,128]{1,0:T(8,128)S(1)} %collective-permute-done.2.swap_ref, f32[256,128]{1,0:T(8,128)S(1)} %collective-permute-done.3.pair_ref, ...), custom_call_target="tpu_custom_call" | custom-call | tf_op jit(solution)/shard_map/pallas_call | solution.py:653
  28.9 0.1 collective-permute-start.5
  29.0 0.6 %collective-permute-start.6 = (f32[136,128]{1,0:T(8,128)S(1)}, f32[136,128]{1,0:T(8,128)S(1)}, u32[]{:S(2)}, u32[]{:S(2)}) collective-permute-start(f32[136,128]{1,0:T(8,128)S(1)} %get-tuple-element.58), channel_id=1, source_target_pairs={{0,8},{2,10},{4,12},{6,14},{8,0},{10,2},{12,4},{14,6},{1,9},{3,11}... | collective-permute-start | bytes 208904 | tf_op jit(solution)/shard_map/ppermute | solution.py:561
  29.6 3.8 %collective-permute-start.7 = (f32[136,128]{1,0:T(8,128)S(1)}, f32[136,128]{1,0:T(8,128)S(1)}, u32[]{:S(2)}, u32[]{:S(2)}) collective-permute-start(f32[136,128]{1,0:T(8,128)S(1)} %get-tuple-element.59), channel_id=1, source_target_pairs={{0,12},{2,14},{4,8},{6,10},{8,4},{10,6},{12,0},{14,2},{1,13},{3,15... | collective-permute-start | bytes 208904 | tf_op jit(solution)/shard_map/ppermute | solution.py:561
  33.4 1.4 %collective-permute-done.5.refs_1_ = f32[136,128]{1,0:T(8,128)S(1)} collective-permute-done((f32[136,128]{1,0:T(8,128)S(1)}, f32[136,128]{1,0:T(8,128)S(1)}, u32[]{:S(2)}, u32[]{:S(2)}) %collective-permute-start.5) | collective-permute-done | bytes 69664 | tf_op jit(solution)/shard_map/ppermute | solution.py:561
  34.8 1.7 %collective-permute-done.7.refs_3_ = f32[136,128]{1,0:T(8,128)S(1)} collective-permute-done((f32[136,128]{1,0:T(8,128)S(1)}, f32[136,128]{1,0:T(8,128)S(1)}, u32[]{:S(2)}, u32[]{:S(2)}) %collective-permute-start.7) | collective-permute-done | bytes 69664 | tf_op jit(solution)/shard_map/ppermute | solution.py:561
  36.5 0.5 collective-permute-start.11
  37.0 1.9 %collective-permute-start.10 = (f32[128,128]{1,0:T(8,128)S(1)}, f32[128,128]{1,0:T(8,128)S(1)}, u32[]{:S(2)}, u32[]{:S(2)}) collective-permute-start(f32[128,128]{1,0:T(8,128)S(1)} %shard_map.219.refs_0_), channel_id=1, source_target_pairs={{0,6},{2,4},{4,2},{6,0},{8,14},{10,12},{12,10},{14,8},{1,7},{3,5},... | collective-permute-start | bytes 196616 | tf_op jit(solution)/shard_map/ppermute | solution.py:561
  38.9 3.4 %collective-permute-start.8 = (f32[128,128]{1,0:T(8,128)S(1)}, f32[128,128]{1,0:T(8,128)S(1)}, u32[]{:S(2)}, u32[]{:S(2)}) collective-permute-start(f32[128,128]{1,0:T(8,128)S(1)} %shard_map.219.refs_0_), channel_id=1, source_target_pairs={{0,2},{2,0},{4,6},{6,4},{8,10},{10,8},{12,14},{14,12},{1,3},{3,1},... | collective-permute-start | bytes 196616 | tf_op jit(solution)/shard_map/ppermute | solution.py:561
  42.3 0.9 %collective-permute-start.12 = (f32[128,128]{1,0:T(8,128)S(1)}, f32[128,128]{1,0:T(8,128)S(1)}, u32[]{:S(2)}, u32[]{:S(2)}) collective-permute-start(f32[128,128]{1,0:T(8,128)S(1)} %collective-permute-done.11.refs_0_), channel_id=1, source_target_pairs={{0,2},{2,0},{4,6},{6,4},{8,10},{10,8},{12,14},{14,12},{1,3},{3,1},... | collective-permute-start | bytes 196616 | tf_op jit(solution)/shard_map/ppermute | solution.py:561
  43.3 1.1 %collective-permute-start.13 = (f32[128,128]{1,0:T(8,128)S(1)}, f32[128,128]{1,0:T(8,128)S(1)}, u32[]{:S(2)}, u32[]{:S(2)}) collective-permute-start(f32[128,128]{1,0:T(8,128)S(1)} %collective-permute-done.11.refs_0_), channel_id=1, source_target_pairs={{0,4},{2,6},{4,0},{6,2},{8,12},{10,14},{12,8},{14,10},{1,5},{3,7},... | collective-permute-start | bytes 196616 | tf_op jit(solution)/shard_map/ppermute | solution.py:561
  44.4 1.5 %collective-permute-start.14 = (f32[128,128]{1,0:T(8,128)S(1)}, f32[128,128]{1,0:T(8,128)S(1)}, u32[]{:S(2)}, u32[]{:S(2)}) collective-permute-start(f32[128,128]{1,0:T(8,128)S(1)} %collective-permute-done.11.refs_0_), channel_id=1, source_target_pairs={{0,6},{2,4},{4,2},{6,0},{8,14},{10,12},{12,10},{14,8},{1,7},{3,5},... | collective-permute-start | bytes 196616 | tf_op jit(solution)/shard_map/ppermute | solution.py:561
  45.9 0.2 shard_map.218
  46.1 1.4 %shard_map.217 = (bf16[1280,512]{1,0:T(8,128)(2,1)S(1)}, bf16[256,512]{1,0:T(8,128)(2,1)S(1)}) custom-call(f32[16,128]{1,0:T(8,128)S(1)} %get-tuple-element.38.ints_ref, f32[136,128]{1,0:T(8,128)S(1)} %get-tuple-element.56.refs_0_, f32[136,128]{1,0:T(8,128)S(1)} %collective-permute-done.5.refs_1_, f32[136,128]{1,0:T(8,128)S(1)} %collective-permute-done.6.refs_2_, ...), custom_call_target="tpu_custom_call" | custom-call | tf_op jit(solution)/shard_map/pallas_call | solution.py:673
  47.5 1.2 %shard_map.220 = (f32[1280,256]{1,0:T(8,128)S(1)}, f32[320,256]{1,0:T(8,128)S(1)}) custom-call(bf16[1280,512]{1,0:T(8,128)(2,1)S(1)} %get-tuple-element.60.hot_ref, bf16[256,512]{1,0:T(8,128)(2,1)S(1)} %get-tuple-element.61.parent_ref, bf16[1280,256]{1,0:T(8,128)(2,1)S(1)} %get-tuple-element.62.high_ref, bf16[1280,256]{1,0:T(8,128)(2,1)S(1)} %get-tuple-element.63.low_ref, ...), custom_call_target="tpu_custom_call" | custom-call | tf_op jit(solution)/shard_map/pallas_call | solution.py:685
  48.6 0.9 %collective-permute-done.14.refs_3_ = f32[128,128]{1,0:T(8,128)S(1)} collective-permute-done((f32[128,128]{1,0:T(8,128)S(1)}, f32[128,128]{1,0:T(8,128)S(1)}, u32[]{:S(2)}, u32[]{:S(2)}) %collective-permute-start.14) | collective-permute-done | bytes 65568 | tf_op jit(solution)/shard_map/ppermute | solution.py:561
  49.5 2.9 %shard_map.221 = (f32[512,128]{1,0:T(8,128)}, f32[128,128]{1,0:T(8,128)}) custom-call(f32[256,256]{1,0:T(8,128)S(1)} %get-tuple-element.55.last_ref, bf16[1280,512]{1,0:T(8,128)(2,1)S(1)} %get-tuple-element.60.hot_ref, bf16[256,512]{1,0:T(8,128)(2,1)S(1)} %get-tuple-element.61.parent_ref, f32[1280,256]{1,0:T(8,128)S(1)} %get-tuple-element.64.got_ref, ...), custom_call_target="tpu_custom_call" | custom-call | tf_op jit(solution)/shard_map/pallas_call | solution.py:690
  (30 shorter events, 0.1 us)
Async XLA Ops:
  2.0 10.7 %collective-permute-start = (f32[272,128]{1,0:T(8,128)S(1)}, f32[272,128]{1,0:T(8,128)S(1)}, u32[]{:S(2)}, u32[]{:S(2)}) collective-permute-start(f32[272,128]{1,0:T(8,128)S(1)} %get-tuple-element.35), channel_id=1, source_target_pairs={{0,2},{2,0},{4,6},{6,4},{8,10},{10,8},{12,14},{14,12},{1,3},{3,1},... | collective-permute-start | bytes 417800 | tf_op jit(solution)/shard_map/ppermute | solution.py:561
  5.0 7.7 %collective-permute-start.1 = (f32[256,128]{1,0:T(8,128)S(1)}, f32[256,128]{1,0:T(8,128)S(1)}, u32[]{:S(2)}, u32[]{:S(2)}) collective-permute-start(f32[256,128]{1,0:T(8,128)S(1)} %get-tuple-element.36), channel_id=1, source_target_pairs={{0,14},{2,4},{4,2},{6,8},{8,6},{10,12},{12,10},{14,0},{1,15},{3,5}... | collective-permute-start | bytes 393224 | tf_op jit(solution)/shard_map/ppermute | solution.py:561
  12.7 6.5 %copy-start = (f32[2,256,256]{2,1,0:T(8,128)S(1)}, f32[2,256,256]{2,1,0:T(8,128)}, u32[]{:S(2)}) copy-start(f32[2,256,256]{2,1,0:T(8,128)} %ws_ref.1) | copy-start | bytes 1572868
  12.7 6.5 %copy-start.1 = (f32[2,256,256]{2,1,0:T(8,128)S(1)}, f32[2,256,256]{2,1,0:T(8,128)}, u32[]{:S(2)}) copy-start(f32[2,256,256]{2,1,0:T(8,128)} %wr_ref.1) | copy-start | bytes 1572868
  12.7 6.5 %copy-start.2 = (f32[2,256,256]{2,1,0:T(8,128)S(1)}, f32[2,256,256]{2,1,0:T(8,128)}, u32[]{:S(2)}) copy-start(f32[2,256,256]{2,1,0:T(8,128)} %wo_ref.1) | copy-start | bytes 1572868
  12.7 6.5 %copy-start.3 = (f32[256,256]{1,0:T(8,128)S(1)}, f32[256,256]{1,0:T(8,128)}, u32[]{:S(2)}) copy-start(f32[256,256]{1,0:T(8,128)} %wi_ref.1) | copy-start | bytes 786436
  12.7 6.5 %copy-start.4 = (f32[256,256]{1,0:T(8,128)S(1)}, f32[256,256]{1,0:T(8,128)}, u32[]{:S(2)}) copy-start(f32[256,256]{1,0:T(8,128)} %wu_ref.1) | copy-start | bytes 786436
  13.8 11.9 %collective-permute-start.2 = (f32[512,128]{1,0:T(8,128)S(1)}, f32[512,128]{1,0:T(8,128)S(1)}, u32[]{:S(2)}, u32[]{:S(2)}) collective-permute-start(f32[512,128]{1,0:T(8,128)S(1)} %get-tuple-element.45.state_ref), channel_id=1, source_target_pairs={{0,2},{2,0},{4,6},{6,4},{8,10},{10,8},{12,14},{14,12},{1,3},{3,1},... | collective-permute-start | bytes 786440 | tf_op jit(solution)/shard_map/ppermute | solution.py:561
  14.4 6.1 %collective-permute-start.3 = (f32[256,128]{1,0:T(8,128)S(1)}, f32[256,128]{1,0:T(8,128)S(1)}, u32[]{:S(2)}, u32[]{:S(2)}) collective-permute-start(f32[256,128]{1,0:T(8,128)S(1)} %get-tuple-element.46), channel_id=1, source_target_pairs={{0,12},{2,6},{4,0},{6,10},{8,4},{10,14},{12,8},{14,2},{1,13},{3,7}... | collective-permute-start | bytes 393224 | tf_op jit(solution)/shard_map/ppermute | solution.py:561
  18.1 7.7 %collective-permute-start.4 = (f32[256,128]{1,0:T(8,128)S(1)}, f32[256,128]{1,0:T(8,128)S(1)}, u32[]{:S(2)}, u32[]{:S(2)}) collective-permute-start(f32[256,128]{1,0:T(8,128)S(1)} %get-tuple-element.46), channel_id=1, source_target_pairs={{0,14},{2,4},{4,2},{6,8},{8,6},{10,12},{12,10},{14,0},{1,15},{3,5}... | collective-permute-start | bytes 393224 | tf_op jit(solution)/shard_map/ppermute | solution.py:561
  25.7 10.8 %copy-start.10 = (f32[64,1,256]{2,1,0:T(1,128)S(1)}, f32[64,1,256]{2,1,0:T(1,128)}, u32[]{:S(2)}) copy-start(f32[64,1,256]{2,1,0:T(1,128)} %param.22) | copy-start | bytes 196612
  25.7 20.1 %copy-start.5 = (f32[256,256]{1,0:T(8,128)S(1)}, f32[256,256]{1,0:T(8,128)}, u32[]{:S(2)}) copy-start(f32[256,256]{1,0:T(8,128)} %cs_ref.1) | copy-start | bytes 786436
  25.7 20.1 %copy-start.6 = (f32[256,256]{1,0:T(8,128)S(1)}, f32[256,256]{1,0:T(8,128)}, u32[]{:S(2)}) copy-start(f32[256,256]{1,0:T(8,128)} %cr_ref.1) | copy-start | bytes 786436
  25.7 20.1 %copy-start.7 = (f32[256,256]{1,0:T(8,128)S(1)}, f32[256,256]{1,0:T(8,128)}, u32[]{:S(2)}) copy-start(f32[256,256]{1,0:T(8,128)} %co_ref.1) | copy-start | bytes 786436
  25.7 20.1 %copy-start.8 = (f32[256,256]{1,0:T(8,128)S(1)}, f32[256,256]{1,0:T(8,128)}, u32[]{:S(2)}) copy-start(f32[256,256]{1,0:T(8,128)} %di_ref.1) | copy-start | bytes 786436
  25.8 20.1 %copy-start.9 = (f32[256,256]{1,0:T(8,128)S(1)}, f32[256,256]{1,0:T(8,128)}, u32[]{:S(2)}) copy-start(f32[256,256]{1,0:T(8,128)} %do_ref.1) | copy-start | bytes 786436
  28.9 5.8 %collective-permute-start.5 = (f32[136,128]{1,0:T(8,128)S(1)}, f32[136,128]{1,0:T(8,128)S(1)}, u32[]{:S(2)}, u32[]{:S(2)}) collective-permute-start(f32[136,128]{1,0:T(8,128)S(1)} %get-tuple-element.57), channel_id=1, source_target_pairs={{0,4},{2,6},{4,0},{6,2},{8,12},{10,14},{12,8},{14,10},{1,5},{3,7},... | collective-permute-start | bytes 208904 | tf_op jit(solution)/shard_map/ppermute | solution.py:561
  29.0 5.8 %collective-permute-start.6 = (f32[136,128]{1,0:T(8,128)S(1)}, f32[136,128]{1,0:T(8,128)S(1)}, u32[]{:S(2)}, u32[]{:S(2)}) collective-permute-start(f32[136,128]{1,0:T(8,128)S(1)} %get-tuple-element.58), channel_id=1, source_target_pairs={{0,8},{2,10},{4,12},{6,14},{8,0},{10,2},{12,4},{14,6},{1,9},{3,11}... | collective-permute-start | bytes 208904 | tf_op jit(solution)/shard_map/ppermute | solution.py:561
  29.6 6.9 %collective-permute-start.7 = (f32[136,128]{1,0:T(8,128)S(1)}, f32[136,128]{1,0:T(8,128)S(1)}, u32[]{:S(2)}, u32[]{:S(2)}) collective-permute-start(f32[136,128]{1,0:T(8,128)S(1)} %get-tuple-element.59), channel_id=1, source_target_pairs={{0,12},{2,14},{4,8},{6,10},{8,4},{10,6},{12,0},{14,2},{1,13},{3,15... | collective-permute-start | bytes 208904 | tf_op jit(solution)/shard_map/ppermute | solution.py:561
  36.5 5.8 %collective-permute-start.11 = (f32[128,128]{1,0:T(8,128)S(1)}, f32[128,128]{1,0:T(8,128)S(1)}, u32[]{:S(2)}, u32[]{:S(2)}) collective-permute-start(f32[128,128]{1,0:T(8,128)S(1)} %shard_map.219.refs_0_), channel_id=1, source_target_pairs={{0,8},{2,10},{4,12},{6,14},{8,0},{10,2},{12,4},{14,6},{1,9},{3,11}... | collective-permute-start | bytes 196616 | tf_op jit(solution)/shard_map/ppermute | solution.py:561
  37.0 7.3 %collective-permute-start.10 = (f32[128,128]{1,0:T(8,128)S(1)}, f32[128,128]{1,0:T(8,128)S(1)}, u32[]{:S(2)}, u32[]{:S(2)}) collective-permute-start(f32[128,128]{1,0:T(8,128)S(1)} %shard_map.219.refs_0_), channel_id=1, source_target_pairs={{0,6},{2,4},{4,2},{6,0},{8,14},{10,12},{12,10},{14,8},{1,7},{3,5},... | collective-permute-start | bytes 196616 | tf_op jit(solution)/shard_map/ppermute | solution.py:561
  38.9 8.5 %collective-permute-start.8 = (f32[128,128]{1,0:T(8,128)S(1)}, f32[128,128]{1,0:T(8,128)S(1)}, u32[]{:S(2)}, u32[]{:S(2)}) collective-permute-start(f32[128,128]{1,0:T(8,128)S(1)} %shard_map.219.refs_0_), channel_id=1, source_target_pairs={{0,2},{2,0},{4,6},{6,4},{8,10},{10,8},{12,14},{14,12},{1,3},{3,1},... | collective-permute-start | bytes 196616 | tf_op jit(solution)/shard_map/ppermute | solution.py:561
  42.3 5.1 %collective-permute-start.9 = (f32[128,128]{1,0:T(8,128)S(1)}, f32[128,128]{1,0:T(8,128)S(1)}, u32[]{:S(2)}, u32[]{:S(2)}) collective-permute-start(f32[128,128]{1,0:T(8,128)S(1)} %shard_map.219.refs_0_), channel_id=1, source_target_pairs={{0,4},{2,6},{4,0},{6,2},{8,12},{10,14},{12,8},{14,10},{1,5},{3,7},... | collective-permute-start | bytes 196616 | tf_op jit(solution)/shard_map/ppermute | solution.py:561
  42.3 6.3 %collective-permute-start.12 = (f32[128,128]{1,0:T(8,128)S(1)}, f32[128,128]{1,0:T(8,128)S(1)}, u32[]{:S(2)}, u32[]{:S(2)}) collective-permute-start(f32[128,128]{1,0:T(8,128)S(1)} %collective-permute-done.11.refs_0_), channel_id=1, source_target_pairs={{0,2},{2,0},{4,6},{6,4},{8,10},{10,8},{12,14},{14,12},{1,3},{3,1},... | collective-permute-start | bytes 196616 | tf_op jit(solution)/shard_map/ppermute | solution.py:561
  43.3 5.4 %collective-permute-start.13 = (f32[128,128]{1,0:T(8,128)S(1)}, f32[128,128]{1,0:T(8,128)S(1)}, u32[]{:S(2)}, u32[]{:S(2)}) collective-permute-start(f32[128,128]{1,0:T(8,128)S(1)} %collective-permute-done.11.refs_0_), channel_id=1, source_target_pairs={{0,4},{2,6},{4,0},{6,2},{8,12},{10,14},{12,8},{14,10},{1,5},{3,7},... | collective-permute-start | bytes 196616 | tf_op jit(solution)/shard_map/ppermute | solution.py:561
  44.4 5.2 %collective-permute-start.14 = (f32[128,128]{1,0:T(8,128)S(1)}, f32[128,128]{1,0:T(8,128)S(1)}, u32[]{:S(2)}, u32[]{:S(2)}) collective-permute-start(f32[128,128]{1,0:T(8,128)S(1)} %collective-permute-done.11.refs_0_), channel_id=1, source_target_pairs={{0,6},{2,4},{4,2},{6,0},{8,14},{10,12},{12,10},{14,8},{1,7},{3,5},... | collective-permute-start | bytes 196616 | tf_op jit(solution)/shard_map/ppermute | solution.py:561

commit v11 on v10

--- a/solution.py
+++ b/solution.py
@@ -235,11 +235,9 @@
 
 
 def start_kernel(
-    count, halo, state_hbm, sender_hbm, owner_hbm, local_hbm, cowner_hbm,
-    clocal_hbm, fb_hbm, ub_hbm, cb_hbm, db_hbm,
-    state_ref, ints_ref, pack_ref, swap_ref, diag_ref,
-    sender_ref, owner_ref, local_ref, cowner_ref, clocal_ref, fb_ref, ub_ref, cb_ref, db_ref,
-    sems,
+    count, halo, rows, state_hbm, sender_hbm, owner_hbm, local_hbm, cowner_hbm,
+    clocal_hbm, ints_ref, swap_ref, diag_ref,
+    sender_ref, owner_ref, local_ref, cowner_ref, clocal_ref, sems,
 ):
     odd = place() % 2
     rim = diag_ref.shape[0]
@@ -252,20 +250,14 @@
         (local_hbm, local_ref),
         (cowner_hbm, cowner_ref),
         (clocal_hbm, clocal_ref),
-        (fb_hbm, fb_ref),
-        (ub_hbm, ub_ref),
-        (cb_hbm, cb_ref),
-        (db_hbm, db_ref),
         (state_hbm.at[mine, :], swap_ref.at[0:rim, :]),
         (state_hbm.at[away, :], diag_ref),
-        (state_hbm, state_ref),
     ]
     copies = [pltpu.make_async_copy(a, b, sems.at[j]) for j, (a, b) in enumerate(pairs)]
     for copy in copies:
         copy.start()
-    for copy in copies[:-3]:
+    for copy in copies[:-2]:
         copy.wait()
-    rows = state_hbm.shape[0] * LANES // fb_ref.shape[1]
     sender = sender_ref[...]
     before = rows + (1 - odd) * halo
     after = rows + odd * halo
@@ -283,31 +275,34 @@
     ints = jnp.concatenate(lines + [jnp.zeros((rest, LANES), f32)], axis=0)
     ints_ref[...] = ints
     swap_ref[rim:, :] = ints
-    pack_ref[...] = jnp.concatenate(
-        [fb_ref[...], ub_ref[...], cb_ref[...], db_ref[...]]
-        + [jnp.zeros((3, fb_ref.shape[1]), f32)],
-        axis=0,
-    )
-    for copy in copies[-3:]:
+    for copy in copies[-2:]:
         copy.wait()
 
 
 def near_kernel(
-    edges, state_ref, ints_ref, ws_hbm, wr_hbm, wo_hbm, pack_ref,
-    hot_ref, got_ref, into_ref, high_ref, low_ref, turn_ref, ws_ref, wr_ref, wo_ref, sems,
+    edges, ints_ref, state_hbm, ws_hbm, wr_hbm, wo_hbm, fb_hbm, ub_hbm, cb_hbm, db_hbm,
+    hot_ref, got_ref, into_ref, high_ref, low_ref, state_ref, pack_ref,
+    turn_ref, ws_ref, wr_ref, wo_ref, fb_ref, ub_ref, cb_ref, db_ref, sems,
 ):
     rows, width = into_ref.shape
     parts = width // LANES
-    pairs = ((ws_hbm, ws_ref), (wr_hbm, wr_ref), (wo_hbm, wo_ref))
-    copies = [
-        pltpu.make_async_copy(a.at[0], b, sems.at[j]) for j, (a, b) in enumerate(pairs)
-    ]
+    pairs = (
+        (state_hbm, state_ref), (ws_hbm.at[0], ws_ref), (wr_hbm.at[0], wr_ref),
+        (wo_hbm.at[0], wo_ref), (fb_hbm, fb_ref), (ub_hbm, ub_ref), (cb_hbm, cb_ref),
+        (db_hbm, db_ref),
+    )
+    copies = [pltpu.make_async_copy(a, b, sems.at[j]) for j, (a, b) in enumerate(pairs)]
     for copy in copies:
         copy.start()
     edge_hot(hot_ref, turn_ref, ints_ref[: edges // LANES, :], edges // rows, rows)
-    normed = unit(load_rows(state_ref, rows, parts))
     for copy in copies:
         copy.wait()
+    pack_ref[...] = jnp.concatenate(
+        [fb_ref[...], ub_ref[...], cb_ref[...], db_ref[...]]
+        + [jnp.zeros((3, width), f32)],
+        axis=0,
+    )
+    normed = unit(load_rows(state_ref, rows, parts))
     split_into(high_ref, low_ref, ws_ref[...], wo_ref[...])
     into_ref[...] = (times(normed, *halves(wr_ref[...])) + pack_ref[0:1, :]) * 0.5
     high, low = halves(times(normed, *weights(high_ref, low_ref, 0)) * 0.5)
@@ -612,26 +607,28 @@
 
     small_args = [
         lines(fine_senders), lines(up_owner), lines(up_local), lines(coarse_owner),
-        lines(coarse_local), fine_bias, row(up_bias), row(coarse_bias), row(down_bias),
+        lines(coarse_local),
     ]
-    state, ints, pack, out_swap, out_diag = call(
-        functools.partial(start_kernel, count, HALO),
-        [HBM] * 10,
-        [
-            shape(full, LANES), shape(16, LANES), shape(8, width), shape(rim + 16, LANES),
-            shape(rim, LANES),
-        ],
-        [small(x) for x in small_args] + [pltpu.SemaphoreType.DMA((12,))],
+    biases = [fine_bias, row(up_bias), row(coarse_bias), row(down_bias)]
+    ints, out_swap, out_diag = call(
+        functools.partial(start_kernel, count, HALO, rows),
+        [HBM] * 6,
+        [shape(16, LANES), shape(rim + 16, LANES), shape(rim, LANES)],
+        [small(x) for x in small_args] + [pltpu.SemaphoreType.DMA((7,))],
     )(*here(lines(fine_state), *small_args))
     swap0 = move(out_swap, swap)
     diag0 = move(out_diag, diag)
-    hot, got, into, high, low = call(
+    hot, got, into, high, low, state, pack = call(
         functools.partial(near_kernel, edges),
-        [VMEM] * 2 + [HBM] * 3 + [VMEM],
+        [VMEM] + [HBM] * 8,
         [hot_shape, shape(edges, width), shape(rows, width)]
-        + [shape(2 * size, width, kind=bf16)] * 2,
-        [turn] + [pltpu.VMEM((size, width), f32)] * 3 + [pltpu.SemaphoreType.DMA((3,))],
-    )(state, ints, *here(fine_w_send, fine_w_recv, fine_w_out), pack)
+        + [shape(2 * size, width, kind=bf16)] * 2
+        + [shape(full, LANES), shape(8, width)],
+        [turn]
+        + [pltpu.VMEM((size, width), f32)] * 3
+        + [small(x) for x in biases]
+        + [pltpu.SemaphoreType.DMA((8,))],
+    )(ints, *here(lines(fine_state), fine_w_send, fine_w_recv, fine_w_out, *biases))
     state, out_half = call(
         far_kernel, [VMEM] * 8, [shape(full, LANES), shape(rim, LANES)]
     )(swap0, diag0, state, hot, got, into, high, low)

time: 52.6 us -> 52.4 us (level)
  no operation moved by 1% of the time
where the time goes in v11:
time: 52.4 us; the launch traced here: 52.2 us
  starting transfers between devices  25.7 us (49%)
  Pallas kernels  14.4 us (27%)
  waiting for transfers between devices  11.2 us (21%)
  between operations  0.82 us (2%)
    ppermute x15, starting transfers between devices, move(): return lax.ppermute(values, 'sp', pairs)  25.7 us
    ppermute x15, waiting for transfers between devices, move(): return lax.ppermute(values, 'sp', pairs)  11.2 us
    pallas_call x1, Pallas kernels, kernel_shards(): call(up_kernel, [VMEM] * 16, [shape(rows, width)] + [shape(own + 8 * coar...  3.16 us
    pallas_call x1, Pallas kernels, kernel_shards(): call(coarse_kernel, [VMEM] * (8 + peers // 2), [shape(full, LANES), shape...  2.85 us
    pallas_call x1, Pallas kernels, kernel_shards(): call(functools.partial(near_kernel, edges), [VMEM] + [HBM] * 8, [hot_shap...  2.26 us
    pallas_call x1, Pallas kernels, kernel_shards(): call(functools.partial(edges_kernel, degree, count), [VMEM] * (1 + peers...  1.35 us
    pallas_call x1, Pallas kernels, kernel_shards(): call(column_kernel, [VMEM] * (4 + peers // 2), [shape(degree * (count + r...  1.16 us
    pallas_call x1, Pallas kernels, kernel_shards(): call(functools.partial(near2_kernel, edges, count), [VMEM] * 10, [shape(e...  1.15 us
  transfers between devices with their start and end apart: 15, of which 6 were waited for; matrix products, arithmetic and copies ran while one was open for 0% of the time, Pallas kernels for 12%

profile of v11, /device:TPU:0, one launch (start us, length us, event | category | flops | bytes accessed | tf_op | source)
XLA Modules:
  0.0 52.2 jit_solution(1224863912773614687)
XLA Ops:
  0.6 1.1 %shard_map.212 = (f32[16,128]{1,0:T(8,128)S(1)}, f32[272,128]{1,0:T(8,128)S(1)}, f32[256,128]{1,0:T(8,128)S(1)}) custom-call(f32[512,128]{1,0:T(8,128)} %bitcast.13, s32[8,128]{1,0:T(8,128)} %bitcast.15, s32[2,128]{1,0:T(2,128)} %bitcast.16, s32[2,128]{1,0:T(2,128)} %bitcast.17, s32[2,128]{1,0:T(2,128)} %bitcast.18, s32[2,128]{1,0:T(2,128)} %bitcast.19), custom_call_target="tpu_custom_call" | custom-call | tf_op jit(solution)/shard_map/pallas_call | solution.py:613
  1.7 3.0 %collective-permute-start = (f32[272,128]{1,0:T(8,128)S(1)}, f32[272,128]{1,0:T(8,128)S(1)}, u32[]{:S(2)}, u32[]{:S(2)}) collective-permute-start(f32[272,128]{1,0:T(8,128)S(1)} %get-tuple-element.35), channel_id=1, source_target_pairs={{0,2},{2,0},{4,6},{6,4},{8,10},{10,8},{12,14},{14,12},{1,3},{3,1},... | collective-permute-start | bytes 417800 | tf_op jit(solution)/shard_map/ppermute | solution.py:556
  4.8 3.6 %collective-permute-start.1 = (f32[256,128]{1,0:T(8,128)S(1)}, f32[256,128]{1,0:T(8,128)S(1)}, u32[]{:S(2)}, u32[]{:S(2)}) collective-permute-start(f32[256,128]{1,0:T(8,128)S(1)} %get-tuple-element.36), channel_id=1, source_target_pairs={{0,14},{2,4},{4,2},{6,8},{8,6},{10,12},{12,10},{14,0},{1,15},{3,5}... | collective-permute-start | bytes 393224 | tf_op jit(solution)/shard_map/ppermute | solution.py:556
  8.4 2.3 %shard_map.213 = (bf16[1024,512]{1,0:T(8,128)(2,1)S(1)}, f32[1024,256]{1,0:T(8,128)S(1)}, f32[256,256]{1,0:T(8,128)S(1)}, bf16[512,256]{1,0:T(8,128)(2,1)S(1)}, ...) custom-call(f32[16,128]{1,0:T(8,128)S(1)} %get-tuple-element.37.ints_ref, ...), custom_call_target="tpu_custom_call" | custom-call | tf_op jit(solution)/shard_map/pallas_call | solution.py:621
  10.6 1.8 %collective-permute-done.1.diag_ref = f32[256,128]{1,0:T(8,128)S(1)} collective-permute-done((f32[256,128]{1,0:T(8,128)S(1)}, f32[256,128]{1,0:T(8,128)S(1)}, u32[]{:S(2)}, u32[]{:S(2)}) %collective-permute-start.1) | collective-permute-done | bytes 131104 | tf_op jit(solution)/shard_map/ppermute | solution.py:556
  12.5 0.0 copy-start.3
  12.5 0.0 copy-start.4
  12.5 1.1 %shard_map.214 = (f32[512,128]{1,0:T(8,128)S(1)}, f32[256,128]{1,0:T(8,128)S(1)}) custom-call(f32[272,128]{1,0:T(8,128)S(1)} %collective-permute-done.swap_ref.ints0_ref, f32[256,128]{1,0:T(8,128)S(1)} %collective-permute-done.1.diag_ref, f32[512,128]{1,0:T(8,128)S(1)} %get-tuple-element.38.state_ref, bf16[1024,512]{1,0:T(8,128)(2,1)S(1)} %get-tuple-element.39.hot_ref, ...), custom_call_target="tpu_custom_call" | custom-call | tf_op jit(solution)/shard_map/pallas_call | solution.py:632
  13.6 0.6 %collective-permute-start.2 = (f32[512,128]{1,0:T(8,128)S(1)}, f32[512,128]{1,0:T(8,128)S(1)}, u32[]{:S(2)}, u32[]{:S(2)}) collective-permute-start(f32[512,128]{1,0:T(8,128)S(1)} %get-tuple-element.44.state_ref), channel_id=1, source_target_pairs={{0,2},{2,0},{4,6},{6,4},{8,10},{10,8},{12,14},{14,12},{1,3},{3,1},... | collective-permute-start | bytes 786440 | tf_op jit(solution)/shard_map/ppermute | solution.py:556
  14.2 3.6 %collective-permute-start.3 = (f32[256,128]{1,0:T(8,128)S(1)}, f32[256,128]{1,0:T(8,128)S(1)}, u32[]{:S(2)}, u32[]{:S(2)}) collective-permute-start(f32[256,128]{1,0:T(8,128)S(1)} %get-tuple-element.45), channel_id=1, source_target_pairs={{0,12},{2,6},{4,0},{6,10},{8,4},{10,14},{12,8},{14,2},{1,13},{3,7}... | collective-permute-start | bytes 393224 | tf_op jit(solution)/shard_map/ppermute | solution.py:556
  17.8 1.1 %collective-permute-start.4 = (f32[256,128]{1,0:T(8,128)S(1)}, f32[256,128]{1,0:T(8,128)S(1)}, u32[]{:S(2)}, u32[]{:S(2)}) collective-permute-start(f32[256,128]{1,0:T(8,128)S(1)} %get-tuple-element.45), channel_id=1, source_target_pairs={{0,14},{2,4},{4,2},{6,8},{8,6},{10,12},{12,10},{14,0},{1,15},{3,5}... | collective-permute-start | bytes 393224 | tf_op jit(solution)/shard_map/ppermute | solution.py:556
  19.0 1.1 %shard_map.215 = (f32[1024,256]{1,0:T(8,128)S(1)}, f32[256,256]{1,0:T(8,128)S(1)}, bf16[256,256]{1,0:T(8,128)(2,1)S(1)}, bf16[256,256]{1,0:T(8,128)(2,1)S(1)}, b...) custom-call(f32[512,128]{1,0:T(8,128)S(1)} %get-tuple-element.44.sta, ...), custom_call_target="tpu_custom_call" | custom-call | tf_op jit(solution)/shard_map/pallas_call | solution.py:638
  20.1 0.2 collective-permute-done.3.pair_ref
  20.4 5.1 %collective-permute-done.4.diag_ref = f32[256,128]{1,0:T(8,128)S(1)} collective-permute-done((f32[256,128]{1,0:T(8,128)S(1)}, f32[256,128]{1,0:T(8,128)S(1)}, u32[]{:S(2)}, u32[]{:S(2)}) %collective-permute-start.4) | collective-permute-done | bytes 131104 | tf_op jit(solution)/shard_map/ppermute | solution.py:556
  25.5 0.0 copy-start.7
  25.6 3.2 %shard_map.216 = (f32[256,256]{1,0:T(8,128)S(1)}, f32[136,128]{1,0:T(8,128)S(1)}, f32[136,128]{1,0:T(8,128)S(1)}, f32[136,128]{1,0:T(8,128)S(1)}, f32[136,128]{1,0:T(8,128)S(1)}) custom-call(f32[512,128]{1,0:T(8,128)S(1)} %collective-permute-done.2.swap_ref, f32[256,128]{1,0:T(8,128)S(1)} %collective-permute-done.3.pair_ref, ...), custom_call_target="tpu_custom_call" | custom-call | tf_op jit(solution)/shard_map/pallas_call | solution.py:650
  28.7 0.1 collective-permute-start.5
  28.8 0.6 %collective-permute-start.6 = (f32[136,128]{1,0:T(8,128)S(1)}, f32[136,128]{1,0:T(8,128)S(1)}, u32[]{:S(2)}, u32[]{:S(2)}) collective-permute-start(f32[136,128]{1,0:T(8,128)S(1)} %get-tuple-element.58), channel_id=1, source_target_pairs={{0,8},{2,10},{4,12},{6,14},{8,0},{10,2},{12,4},{14,6},{1,9},{3,11}... | collective-permute-start | bytes 208904 | tf_op jit(solution)/shard_map/ppermute | solution.py:556
  29.4 3.8 %collective-permute-start.7 = (f32[136,128]{1,0:T(8,128)S(1)}, f32[136,128]{1,0:T(8,128)S(1)}, u32[]{:S(2)}, u32[]{:S(2)}) collective-permute-start(f32[136,128]{1,0:T(8,128)S(1)} %get-tuple-element.59), channel_id=1, source_target_pairs={{0,12},{2,14},{4,8},{6,10},{8,4},{10,6},{12,0},{14,2},{1,13},{3,15... | collective-permute-start | bytes 208904 | tf_op jit(solution)/shard_map/ppermute | solution.py:556
  33.2 1.4 %collective-permute-done.5.refs_1_ = f32[136,128]{1,0:T(8,128)S(1)} collective-permute-done((f32[136,128]{1,0:T(8,128)S(1)}, f32[136,128]{1,0:T(8,128)S(1)}, u32[]{:S(2)}, u32[]{:S(2)}) %collective-permute-start.5) | collective-permute-done | bytes 69664 | tf_op jit(solution)/shard_map/ppermute | solution.py:556
  34.6 1.7 %collective-permute-done.7.refs_3_ = f32[136,128]{1,0:T(8,128)S(1)} collective-permute-done((f32[136,128]{1,0:T(8,128)S(1)}, f32[136,128]{1,0:T(8,128)S(1)}, u32[]{:S(2)}, u32[]{:S(2)}) %collective-permute-start.7) | collective-permute-done | bytes 69664 | tf_op jit(solution)/shard_map/ppermute | solution.py:556
  36.3 0.5 collective-permute-start.11
  36.9 1.9 %collective-permute-start.10 = (f32[128,128]{1,0:T(8,128)S(1)}, f32[128,128]{1,0:T(8,128)S(1)}, u32[]{:S(2)}, u32[]{:S(2)}) collective-permute-start(f32[128,128]{1,0:T(8,128)S(1)} %shard_map.219.refs_0_), channel_id=1, source_target_pairs={{0,6},{2,4},{4,2},{6,0},{8,14},{10,12},{12,10},{14,8},{1,7},{3,5},... | collective-permute-start | bytes 196616 | tf_op jit(solution)/shard_map/ppermute | solution.py:556
  38.8 3.4 %collective-permute-start.8 = (f32[128,128]{1,0:T(8,128)S(1)}, f32[128,128]{1,0:T(8,128)S(1)}, u32[]{:S(2)}, u32[]{:S(2)}) collective-permute-start(f32[128,128]{1,0:T(8,128)S(1)} %shard_map.219.refs_0_), channel_id=1, source_target_pairs={{0,2},{2,0},{4,6},{6,4},{8,10},{10,8},{12,14},{14,12},{1,3},{3,1},... | collective-permute-start | bytes 196616 | tf_op jit(solution)/shard_map/ppermute | solution.py:556
  42.2 0.9 %collective-permute-start.12 = (f32[128,128]{1,0:T(8,128)S(1)}, f32[128,128]{1,0:T(8,128)S(1)}, u32[]{:S(2)}, u32[]{:S(2)}) collective-permute-start(f32[128,128]{1,0:T(8,128)S(1)} %collective-permute-done.11.refs_0_), channel_id=1, source_target_pairs={{0,2},{2,0},{4,6},{6,4},{8,10},{10,8},{12,14},{14,12},{1,3},{3,1},... | collective-permute-start | bytes 196616 | tf_op jit(solution)/shard_map/ppermute | solution.py:556
  43.1 1.1 %collective-permute-start.13 = (f32[128,128]{1,0:T(8,128)S(1)}, f32[128,128]{1,0:T(8,128)S(1)}, u32[]{:S(2)}, u32[]{:S(2)}) collective-permute-start(f32[128,128]{1,0:T(8,128)S(1)} %collective-permute-done.11.refs_0_), channel_id=1, source_target_pairs={{0,4},{2,6},{4,0},{6,2},{8,12},{10,14},{12,8},{14,10},{1,5},{3,7},... | collective-permute-start | bytes 196616 | tf_op jit(solution)/shard_map/ppermute | solution.py:556
  44.2 1.5 %collective-permute-start.14 = (f32[128,128]{1,0:T(8,128)S(1)}, f32[128,128]{1,0:T(8,128)S(1)}, u32[]{:S(2)}, u32[]{:S(2)}) collective-permute-start(f32[128,128]{1,0:T(8,128)S(1)} %collective-permute-done.11.refs_0_), channel_id=1, source_target_pairs={{0,6},{2,4},{4,2},{6,0},{8,14},{10,12},{12,10},{14,8},{1,7},{3,5},... | collective-permute-start | bytes 196616 | tf_op jit(solution)/shard_map/ppermute | solution.py:556
  45.7 0.2 shard_map.218
  45.9 1.4 %shard_map.217 = (bf16[1280,512]{1,0:T(8,128)(2,1)S(1)}, bf16[256,512]{1,0:T(8,128)(2,1)S(1)}) custom-call(f32[16,128]{1,0:T(8,128)S(1)} %get-tuple-element.37.ints_ref, f32[136,128]{1,0:T(8,128)S(1)} %get-tuple-element.56.refs_0_, f32[136,128]{1,0:T(8,128)S(1)} %collective-permute-done.5.refs_1_, f32[136,128]{1,0:T(8,128)S(1)} %collective-permute-done.6.refs_2_, ...), custom_call_target="tpu_custom_call" | custom-call | tf_op jit(solution)/shard_map/pallas_call | solution.py:670
  47.3 1.2 %shard_map.220 = (f32[1280,256]{1,0:T(8,128)S(1)}, f32[320,256]{1,0:T(8,128)S(1)}) custom-call(bf16[1280,512]{1,0:T(8,128)(2,1)S(1)} %get-tuple-element.60.hot_ref, bf16[256,512]{1,0:T(8,128)(2,1)S(1)} %get-tuple-element.61.parent_ref, bf16[1280,256]{1,0:T(8,128)(2,1)S(1)} %get-tuple-element.62.high_ref, bf16[1280,256]{1,0:T(8,128)(2,1)S(1)} %get-tuple-element.63.low_ref, ...), custom_call_target="tpu_custom_call" | custom-call | tf_op jit(solution)/shard_map/pallas_call | solution.py:682
  48.5 0.9 %collective-permute-done.14.refs_3_ = f32[128,128]{1,0:T(8,128)S(1)} collective-permute-done((f32[128,128]{1,0:T(8,128)S(1)}, f32[128,128]{1,0:T(8,128)S(1)}, u32[]{:S(2)}, u32[]{:S(2)}) %collective-permute-start.14) | collective-permute-done | bytes 65568 | tf_op jit(solution)/shard_map/ppermute | solution.py:556
  49.4 2.9 %shard_map.221 = (f32[512,128]{1,0:T(8,128)}, f32[128,128]{1,0:T(8,128)}) custom-call(f32[256,256]{1,0:T(8,128)S(1)} %get-tuple-element.55.last_ref, bf16[1280,512]{1,0:T(8,128)(2,1)S(1)} %get-tuple-element.60.hot_ref, bf16[256,512]{1,0:T(8,128)(2,1)S(1)} %get-tuple-element.61.parent_ref, f32[1280,256]{1,0:T(8,128)S(1)} %get-tuple-element.64.got_ref, ...), custom_call_target="tpu_custom_call" | custom-call | tf_op jit(solution)/shard_map/pallas_call | solution.py:687
  (30 shorter events, 0.1 us)
Async XLA Ops:
  1.7 10.7 %collective-permute-start = (f32[272,128]{1,0:T(8,128)S(1)}, f32[272,128]{1,0:T(8,128)S(1)}, u32[]{:S(2)}, u32[]{:S(2)}) collective-permute-start(f32[272,128]{1,0:T(8,128)S(1)} %get-tuple-element.35), channel_id=1, source_target_pairs={{0,2},{2,0},{4,6},{6,4},{8,10},{10,8},{12,14},{14,12},{1,3},{3,1},... | collective-permute-start | bytes 417800 | tf_op jit(solution)/shard_map/ppermute | solution.py:556
  4.8 7.7 %collective-permute-start.1 = (f32[256,128]{1,0:T(8,128)S(1)}, f32[256,128]{1,0:T(8,128)S(1)}, u32[]{:S(2)}, u32[]{:S(2)}) collective-permute-start(f32[256,128]{1,0:T(8,128)S(1)} %get-tuple-element.36), channel_id=1, source_target_pairs={{0,14},{2,4},{4,2},{6,8},{8,6},{10,12},{12,10},{14,0},{1,15},{3,5}... | collective-permute-start | bytes 393224 | tf_op jit(solution)/shard_map/ppermute | solution.py:556
  12.4 6.5 %copy-start = (f32[2,256,256]{2,1,0:T(8,128)S(1)}, f32[2,256,256]{2,1,0:T(8,128)}, u32[]{:S(2)}) copy-start(f32[2,256,256]{2,1,0:T(8,128)} %ws_ref.1) | copy-start | bytes 1572868
  12.5 6.5 %copy-start.1 = (f32[2,256,256]{2,1,0:T(8,128)S(1)}, f32[2,256,256]{2,1,0:T(8,128)}, u32[]{:S(2)}) copy-start(f32[2,256,256]{2,1,0:T(8,128)} %wr_ref.1) | copy-start | bytes 1572868
  12.5 6.5 %copy-start.2 = (f32[2,256,256]{2,1,0:T(8,128)S(1)}, f32[2,256,256]{2,1,0:T(8,128)}, u32[]{:S(2)}) copy-start(f32[2,256,256]{2,1,0:T(8,128)} %wo_ref.1) | copy-start | bytes 1572868
  12.5 6.5 %copy-start.3 = (f32[256,256]{1,0:T(8,128)S(1)}, f32[256,256]{1,0:T(8,128)}, u32[]{:S(2)}) copy-start(f32[256,256]{1,0:T(8,128)} %wi_ref.1) | copy-start | bytes 786436
  12.5 6.5 %copy-start.4 = (f32[256,256]{1,0:T(8,128)S(1)}, f32[256,256]{1,0:T(8,128)}, u32[]{:S(2)}) copy-start(f32[256,256]{1,0:T(8,128)} %wu_ref.1) | copy-start | bytes 786436
  13.6 11.9 %collective-permute-start.2 = (f32[512,128]{1,0:T(8,128)S(1)}, f32[512,128]{1,0:T(8,128)S(1)}, u32[]{:S(2)}, u32[]{:S(2)}) collective-permute-start(f32[512,128]{1,0:T(8,128)S(1)} %get-tuple-element.44.state_ref), channel_id=1, source_target_pairs={{0,2},{2,0},{4,6},{6,4},{8,10},{10,8},{12,14},{14,12},{1,3},{3,1},... | collective-permute-start | bytes 786440 | tf_op jit(solution)/shard_map/ppermute | solution.py:556
  14.2 6.1 %collective-permute-start.3 = (f32[256,128]{1,0:T(8,128)S(1)}, f32[256,128]{1,0:T(8,128)S(1)}, u32[]{:S(2)}, u32[]{:S(2)}) collective-permute-start(f32[256,128]{1,0:T(8,128)S(1)} %get-tuple-element.45), channel_id=1, source_target_pairs={{0,12},{2,6},{4,0},{6,10},{8,4},{10,14},{12,8},{14,2},{1,13},{3,7}... | collective-permute-start | bytes 393224 | tf_op jit(solution)/shard_map/ppermute | solution.py:556
  17.8 7.7 %collective-permute-start.4 = (f32[256,128]{1,0:T(8,128)S(1)}, f32[256,128]{1,0:T(8,128)S(1)}, u32[]{:S(2)}, u32[]{:S(2)}) collective-permute-start(f32[256,128]{1,0:T(8,128)S(1)} %get-tuple-element.45), channel_id=1, source_target_pairs={{0,14},{2,4},{4,2},{6,8},{8,6},{10,12},{12,10},{14,0},{1,15},{3,5}... | collective-permute-start | bytes 393224 | tf_op jit(solution)/shard_map/ppermute | solution.py:556
  25.5 10.8 %copy-start.10 = (f32[64,1,256]{2,1,0:T(1,128)S(1)}, f32[64,1,256]{2,1,0:T(1,128)}, u32[]{:S(2)}) copy-start(f32[64,1,256]{2,1,0:T(1,128)} %param.22) | copy-start | bytes 196612
  25.5 20.1 %copy-start.5 = (f32[256,256]{1,0:T(8,128)S(1)}, f32[256,256]{1,0:T(8,128)}, u32[]{:S(2)}) copy-start(f32[256,256]{1,0:T(8,128)} %cs_ref.1) | copy-start | bytes 786436
  25.5 20.1 %copy-start.6 = (f32[256,256]{1,0:T(8,128)S(1)}, f32[256,256]{1,0:T(8,128)}, u32[]{:S(2)}) copy-start(f32[256,256]{1,0:T(8,128)} %cr_ref.1) | copy-start | bytes 786436
  25.5 20.1 %copy-start.7 = (f32[256,256]{1,0:T(8,128)S(1)}, f32[256,256]{1,0:T(8,128)}, u32[]{:S(2)}) copy-start(f32[256,256]{1,0:T(8,128)} %co_ref.1) | copy-start | bytes 786436
  25.5 20.1 %copy-start.8 = (f32[256,256]{1,0:T(8,128)S(1)}, f32[256,256]{1,0:T(8,128)}, u32[]{:S(2)}) copy-start(f32[256,256]{1,0:T(8,128)} %di_ref.1) | copy-start | bytes 786436
  25.5 20.1 %copy-start.9 = (f32[256,256]{1,0:T(8,128)S(1)}, f32[256,256]{1,0:T(8,128)}, u32[]{:S(2)}) copy-start(f32[256,256]{1,0:T(8,128)} %do_ref.1) | copy-start | bytes 786436
  28.7 5.9 %collective-permute-start.5 = (f32[136,128]{1,0:T(8,128)S(1)}, f32[136,128]{1,0:T(8,128)S(1)}, u32[]{:S(2)}, u32[]{:S(2)}) collective-permute-start(f32[136,128]{1,0:T(8,128)S(1)} %get-tuple-element.57), channel_id=1, source_target_pairs={{0,4},{2,6},{4,0},{6,2},{8,12},{10,14},{12,8},{14,10},{1,5},{3,7},... | collective-permute-start | bytes 208904 | tf_op jit(solution)/shard_map/ppermute | solution.py:556
  28.8 5.8 %collective-permute-start.6 = (f32[136,128]{1,0:T(8,128)S(1)}, f32[136,128]{1,0:T(8,128)S(1)}, u32[]{:S(2)}, u32[]{:S(2)}) collective-permute-start(f32[136,128]{1,0:T(8,128)S(1)} %get-tuple-element.58), channel_id=1, source_target_pairs={{0,8},{2,10},{4,12},{6,14},{8,0},{10,2},{12,4},{14,6},{1,9},{3,11}... | collective-permute-start | bytes 208904 | tf_op jit(solution)/shard_map/ppermute | solution.py:556
  29.4 6.9 %collective-permute-start.7 = (f32[136,128]{1,0:T(8,128)S(1)}, f32[136,128]{1,0:T(8,128)S(1)}, u32[]{:S(2)}, u32[]{:S(2)}) collective-permute-start(f32[136,128]{1,0:T(8,128)S(1)} %get-tuple-element.59), channel_id=1, source_target_pairs={{0,12},{2,14},{4,8},{6,10},{8,4},{10,6},{12,0},{14,2},{1,13},{3,15... | collective-permute-start | bytes 208904 | tf_op jit(solution)/shard_map/ppermute | solution.py:556
  36.3 5.8 %collective-permute-start.11 = (f32[128,128]{1,0:T(8,128)S(1)}, f32[128,128]{1,0:T(8,128)S(1)}, u32[]{:S(2)}, u32[]{:S(2)}) collective-permute-start(f32[128,128]{1,0:T(8,128)S(1)} %shard_map.219.refs_0_), channel_id=1, source_target_pairs={{0,8},{2,10},{4,12},{6,14},{8,0},{10,2},{12,4},{14,6},{1,9},{3,11}... | collective-permute-start | bytes 196616 | tf_op jit(solution)/shard_map/ppermute | solution.py:556
  36.9 7.3 %collective-permute-start.10 = (f32[128,128]{1,0:T(8,128)S(1)}, f32[128,128]{1,0:T(8,128)S(1)}, u32[]{:S(2)}, u32[]{:S(2)}) collective-permute-start(f32[128,128]{1,0:T(8,128)S(1)} %shard_map.219.refs_0_), channel_id=1, source_target_pairs={{0,6},{2,4},{4,2},{6,0},{8,14},{10,12},{12,10},{14,8},{1,7},{3,5},... | collective-permute-start | bytes 196616 | tf_op jit(solution)/shard_map/ppermute | solution.py:556
  38.8 8.5 %collective-permute-start.8 = (f32[128,128]{1,0:T(8,128)S(1)}, f32[128,128]{1,0:T(8,128)S(1)}, u32[]{:S(2)}, u32[]{:S(2)}) collective-permute-start(f32[128,128]{1,0:T(8,128)S(1)} %shard_map.219.refs_0_), channel_id=1, source_target_pairs={{0,2},{2,0},{4,6},{6,4},{8,10},{10,8},{12,14},{14,12},{1,3},{3,1},... | collective-permute-start | bytes 196616 | tf_op jit(solution)/shard_map/ppermute | solution.py:556
  42.2 5.1 %collective-permute-start.9 = (f32[128,128]{1,0:T(8,128)S(1)}, f32[128,128]{1,0:T(8,128)S(1)}, u32[]{:S(2)}, u32[]{:S(2)}) collective-permute-start(f32[128,128]{1,0:T(8,128)S(1)} %shard_map.219.refs_0_), channel_id=1, source_target_pairs={{0,4},{2,6},{4,0},{6,2},{8,12},{10,14},{12,8},{14,10},{1,5},{3,7},... | collective-permute-start | bytes 196616 | tf_op jit(solution)/shard_map/ppermute | solution.py:556
  42.2 6.3 %collective-permute-start.12 = (f32[128,128]{1,0:T(8,128)S(1)}, f32[128,128]{1,0:T(8,128)S(1)}, u32[]{:S(2)}, u32[]{:S(2)}) collective-permute-start(f32[128,128]{1,0:T(8,128)S(1)} %collective-permute-done.11.refs_0_), channel_id=1, source_target_pairs={{0,2},{2,0},{4,6},{6,4},{8,10},{10,8},{12,14},{14,12},{1,3},{3,1},... | collective-permute-start | bytes 196616 | tf_op jit(solution)/shard_map/ppermute | solution.py:556
  43.1 5.4 %collective-permute-start.13 = (f32[128,128]{1,0:T(8,128)S(1)}, f32[128,128]{1,0:T(8,128)S(1)}, u32[]{:S(2)}, u32[]{:S(2)}) collective-permute-start(f32[128,128]{1,0:T(8,128)S(1)} %collective-permute-done.11.refs_0_), channel_id=1, source_target_pairs={{0,4},{2,6},{4,0},{6,2},{8,12},{10,14},{12,8},{14,10},{1,5},{3,7},... | collective-permute-start | bytes 196616 | tf_op jit(solution)/shard_map/ppermute | solution.py:556
  44.2 5.2 %collective-permute-start.14 = (f32[128,128]{1,0:T(8,128)S(1)}, f32[128,128]{1,0:T(8,128)S(1)}, u32[]{:S(2)}, u32[]{:S(2)}) collective-permute-start(f32[128,128]{1,0:T(8,128)S(1)} %collective-permute-done.11.refs_0_), channel_id=1, source_target_pairs={{0,6},{2,4},{4,2},{6,0},{8,14},{10,12},{12,10},{14,8},{1,7},{3,5},... | collective-permute-start | bytes 196616 | tf_op jit(solution)/shard_map/ppermute | solution.py:556

commit v12 on v10

--- a/solution.py
+++ b/solution.py
@@ -311,7 +311,7 @@
     split_into(high_ref, low_ref, ws_ref[...], wo_ref[...])
     into_ref[...] = (times(normed, *halves(wr_ref[...])) + pack_ref[0:1, :]) * 0.5
     high, low = halves(times(normed, *weights(high_ref, low_ref, 0)) * 0.5)
-    got_ref[...] = take(hot_ref[:, :rows], high, low)
+    got_ref[...] = take(hot_ref[:, :rows], high, low) + jnp.tile(into_ref[...], (edges // rows, 1))
 
 
 def far_kernel(
@@ -329,7 +329,7 @@
     total = None
     for k in range(degree):
         part = slice(k * rows, (k + 1) * rows)
-        half = got_ref[part, :] + into_ref[...] + take(hot_ref[part, rows:], high, low)
+        half = got_ref[part, :] + take(hot_ref[part, rows:], high, low)
         total = gate(half) if total is None else total + gate(half)
     store_rows(
         out_full_ref,
@@ -358,7 +358,7 @@
     high, low = halves(times(normed, *weights(high_ref, low_ref, 0)) * 0.5)
     own_high_ref[...] = high
     own_low_ref[...] = low
-    got_ref[...] = take(hot_ref[:, :rows], high, low)
+    got_ref[...] = take(hot_ref[:, :rows], high, low) + jnp.tile(into_ref[...], (edges // rows, 1))
     first = ints0_ref.shape[0] - ints_ref.shape[0]
     edge_hot(hot2_ref, turn_ref, ints0_ref[first : first + senders, :], edges // rows, rows)
     flip = place() * count
@@ -409,7 +409,7 @@
     total, total2 = None, None
     for k in range(degree):
         part = slice(k * rows, (k + 1) * rows)
-        half = got_ref[part, :] + into_ref[...] + take(hot_ref[part, rows:], *near)
+        half = got_ref[part, :] + take(hot_ref[part, rows:], *near)
         total = gate(half) if total is None else total + gate(half)
         half = into + take(hot2_ref[part, :], th_ref[...], tl_ref[...])
         total2 = gate(half) if total2 is None else total2 + gate(half)

time: 52.6 us -> 52.5 us (level)
  no operation moved by 1% of the time
where the time goes in v12:
time: 52.5 us; the launch traced here: 52.4 us
  starting transfers between devices  25.7 us (49%)
  Pallas kernels  14.7 us (28%)
  waiting for transfers between devices  11.1 us (21%)
  between operations  0.82 us (2%)
    ppermute x15, starting transfers between devices, move(): return lax.ppermute(values, 'sp', pairs)  25.7 us
    ppermute x15, waiting for transfers between devices, move(): return lax.ppermute(values, 'sp', pairs)  11.1 us
    pallas_call x1, Pallas kernels, kernel_shards(): call(up_kernel, [VMEM] * 16, [shape(rows, width)] + [shape(own + 8 * coar...  3.1 us
    pallas_call x1, Pallas kernels, kernel_shards(): call(coarse_kernel, [VMEM] * (8 + peers // 2), [shape(full, LANES), shape...  2.85 us
    pallas_call x1, Pallas kernels, kernel_shards(): call(functools.partial(near_kernel, edges), [VMEM] * 2 + [HBM] * 3 + [VME...  2.4 us
    pallas_call x1, Pallas kernels, kernel_shards(): call(functools.partial(edges_kernel, degree, count), [VMEM] * (1 + peers...  1.35 us
    pallas_call x1, Pallas kernels, kernel_shards(): call(functools.partial(start_kernel, count, HALO), [HBM] * 10, [shape(ful...  1.31 us
    pallas_call x1, Pallas kernels, kernel_shards(): call(functools.partial(near2_kernel, edges, count), [VMEM] * 10, [shape(e...  1.16 us
  transfers between devices with their start and end apart: 15, of which 6 were waited for; matrix products, arithmetic and copies ran while one was open for 0% of the time, Pallas kernels for 12%

profile of v12, /device:TPU:0, one launch (start us, length us, event | category | flops | bytes accessed | tf_op | source)
XLA Modules:
  0.0 52.4 jit_solution(11253755967977246897)
XLA Ops:
  0.6 1.3 %shard_map.212 = (f32[512,128]{1,0:T(8,128)S(1)}, f32[16,128]{1,0:T(8,128)S(1)}, f32[8,256]{1,0:T(8,128)S(1)}, f32[272,128]{1,0:T(8,128)S(1)}, f32[256,128]{1,0:T(8,128)S(1)}) custom-call(f32[512,128]{1,0:T(8,128)} %bitcast.13, s32[8,128]{1,0:T(8,128)} %bitcast.14, s32[2,128]{1,0:T(2,128)} %bitcast.15, s32[2,128]{1,0:T(2,128)} %bitcast.16, ...), custom_call_target="tpu_custom_call" | custom-call | tf_op jit(solution)/shard_map/pallas_call | solution.py:617
  2.0 3.0 %collective-permute-start = (f32[272,128]{1,0:T(8,128)S(1)}, f32[272,128]{1,0:T(8,128)S(1)}, u32[]{:S(2)}, u32[]{:S(2)}) collective-permute-start(f32[272,128]{1,0:T(8,128)S(1)} %get-tuple-element.35), channel_id=1, source_target_pairs={{0,2},{2,0},{4,6},{6,4},{8,10},{10,8},{12,14},{14,12},{1,3},{3,1},... | collective-permute-start | bytes 417800 | tf_op jit(solution)/shard_map/ppermute | solution.py:561
  5.0 3.6 %collective-permute-start.1 = (f32[256,128]{1,0:T(8,128)S(1)}, f32[256,128]{1,0:T(8,128)S(1)}, u32[]{:S(2)}, u32[]{:S(2)}) collective-permute-start(f32[256,128]{1,0:T(8,128)S(1)} %get-tuple-element.36), channel_id=1, source_target_pairs={{0,14},{2,4},{4,2},{6,8},{8,6},{10,12},{12,10},{14,0},{1,15},{3,5}... | collective-permute-start | bytes 393224 | tf_op jit(solution)/shard_map/ppermute | solution.py:561
  8.6 2.4 %shard_map.213 = (bf16[1024,512]{1,0:T(8,128)(2,1)S(1)}, f32[1024,256]{1,0:T(8,128)S(1)}, f32[256,256]{1,0:T(8,128)S(1)}, bf16[512,256]{1,0:T(8,128)(2,1)S(1)}, bf16[512,256]{1,0:T(8,128)(2,1)S(1)}) custom-call(f32[512,128]{1,0:T(8,128)S(1)} %get-tuple-element.37.state_ref, f32[16,128]{1,0:T(8,128)S(1)} %get-tuple-element.38.ints_ref, ...), custom_call_target="tpu_custom_call" | custom-call | tf_op jit(solution)/shard_map/pallas_call | solution.py:628
  11.0 1.7 %collective-permute-done.1.diag_ref = f32[256,128]{1,0:T(8,128)S(1)} collective-permute-done((f32[256,128]{1,0:T(8,128)S(1)}, f32[256,128]{1,0:T(8,128)S(1)}, u32[]{:S(2)}, u32[]{:S(2)}) %collective-permute-start.1) | collective-permute-done | bytes 131104 | tf_op jit(solution)/shard_map/ppermute | solution.py:561
  12.7 0.0 copy-start.4
  12.7 1.1 %shard_map.214 = (f32[512,128]{1,0:T(8,128)S(1)}, f32[256,128]{1,0:T(8,128)S(1)}) custom-call(f32[272,128]{1,0:T(8,128)S(1)} %collective-permute-done.swap_ref.ints0_ref, f32[256,128]{1,0:T(8,128)S(1)} %collective-permute-done.1.diag_ref, f32[512,128]{1,0:T(8,128)S(1)} %get-tuple-element.37.state_ref, bf16[1024,512]{1,0:T(8,128)(2,1)S(1)} %get-tuple-element.40.hot_ref, ...), custom_call_target="tpu_custom_call" | custom-call | tf_op jit(solution)/shard_map/pallas_call | solution.py:635
  13.8 0.6 %collective-permute-start.2 = (f32[512,128]{1,0:T(8,128)S(1)}, f32[512,128]{1,0:T(8,128)S(1)}, u32[]{:S(2)}, u32[]{:S(2)}) collective-permute-start(f32[512,128]{1,0:T(8,128)S(1)} %get-tuple-element.45.state_ref), channel_id=1, source_target_pairs={{0,2},{2,0},{4,6},{6,4},{8,10},{10,8},{12,14},{14,12},{1,3},{3,1},... | collective-permute-start | bytes 786440 | tf_op jit(solution)/shard_map/ppermute | solution.py:561
  14.4 3.6 %collective-permute-start.3 = (f32[256,128]{1,0:T(8,128)S(1)}, f32[256,128]{1,0:T(8,128)S(1)}, u32[]{:S(2)}, u32[]{:S(2)}) collective-permute-start(f32[256,128]{1,0:T(8,128)S(1)} %get-tuple-element.46), channel_id=1, source_target_pairs={{0,12},{2,6},{4,0},{6,10},{8,4},{10,14},{12,8},{14,2},{1,13},{3,7}... | collective-permute-start | bytes 393224 | tf_op jit(solution)/shard_map/ppermute | solution.py:561
  18.0 1.1 %collective-permute-start.4 = (f32[256,128]{1,0:T(8,128)S(1)}, f32[256,128]{1,0:T(8,128)S(1)}, u32[]{:S(2)}, u32[]{:S(2)}) collective-permute-start(f32[256,128]{1,0:T(8,128)S(1)} %get-tuple-element.46), channel_id=1, source_target_pairs={{0,14},{2,4},{4,2},{6,8},{8,6},{10,12},{12,10},{14,0},{1,15},{3,5}... | collective-permute-start | bytes 393224 | tf_op jit(solution)/shard_map/ppermute | solution.py:561
  19.2 1.2 %shard_map.215 = (f32[1024,256]{1,0:T(8,128)S(1)}, f32[256,256]{1,0:T(8,128)S(1)}, bf16[256,256]{1,0:T(8,128)(2,1)S(1)}, bf16[256,256]{1,0:T(8,128)(2,1)S(1)}, b...) custom-call(f32[512,128]{1,0:T(8,128)S(1)} %get-tuple-element.45.sta, ...), custom_call_target="tpu_custom_call" | custom-call | tf_op jit(solution)/shard_map/pallas_call | solution.py:641
  20.4 0.2 collective-permute-done.3.pair_ref
  20.6 5.1 %collective-permute-done.4.diag_ref = f32[256,128]{1,0:T(8,128)S(1)} collective-permute-done((f32[256,128]{1,0:T(8,128)S(1)}, f32[256,128]{1,0:T(8,128)S(1)}, u32[]{:S(2)}, u32[]{:S(2)}) %collective-permute-start.4) | collective-permute-done | bytes 131104 | tf_op jit(solution)/shard_map/ppermute | solution.py:561
  25.7 0.0 copy-start.7
  25.7 0.0 copy-start.8
  25.8 3.1 %shard_map.216 = (f32[256,256]{1,0:T(8,128)S(1)}, f32[136,128]{1,0:T(8,128)S(1)}, f32[136,128]{1,0:T(8,128)S(1)}, f32[136,128]{1,0:T(8,128)S(1)}, f32[136,128]{1,0:T(8,128)S(1)}) custom-call(f32[512,128]{1,0:T(8,128)S(1)} %collective-permute-done.2.swap_ref, f32[256,128]{1,0:T(8,128)S(1)} %collective-permute-done.3.pair_ref, ...), custom_call_target="tpu_custom_call" | custom-call | tf_op jit(solution)/shard_map/pallas_call | solution.py:653
  28.9 0.1 collective-permute-start.5
  28.9 0.6 %collective-permute-start.6 = (f32[136,128]{1,0:T(8,128)S(1)}, f32[136,128]{1,0:T(8,128)S(1)}, u32[]{:S(2)}, u32[]{:S(2)}) collective-permute-start(f32[136,128]{1,0:T(8,128)S(1)} %get-tuple-element.58), channel_id=1, source_target_pairs={{0,8},{2,10},{4,12},{6,14},{8,0},{10,2},{12,4},{14,6},{1,9},{3,11}... | collective-permute-start | bytes 208904 | tf_op jit(solution)/shard_map/ppermute | solution.py:561
  29.5 3.8 %collective-permute-start.7 = (f32[136,128]{1,0:T(8,128)S(1)}, f32[136,128]{1,0:T(8,128)S(1)}, u32[]{:S(2)}, u32[]{:S(2)}) collective-permute-start(f32[136,128]{1,0:T(8,128)S(1)} %get-tuple-element.59), channel_id=1, source_target_pairs={{0,12},{2,14},{4,8},{6,10},{8,4},{10,6},{12,0},{14,2},{1,13},{3,15... | collective-permute-start | bytes 208904 | tf_op jit(solution)/shard_map/ppermute | solution.py:561
  33.3 1.4 %collective-permute-done.5.refs_1_ = f32[136,128]{1,0:T(8,128)S(1)} collective-permute-done((f32[136,128]{1,0:T(8,128)S(1)}, f32[136,128]{1,0:T(8,128)S(1)}, u32[]{:S(2)}, u32[]{:S(2)}) %collective-permute-start.5) | collective-permute-done | bytes 69664 | tf_op jit(solution)/shard_map/ppermute | solution.py:561
  34.7 1.7 %collective-permute-done.7.refs_3_ = f32[136,128]{1,0:T(8,128)S(1)} collective-permute-done((f32[136,128]{1,0:T(8,128)S(1)}, f32[136,128]{1,0:T(8,128)S(1)}, u32[]{:S(2)}, u32[]{:S(2)}) %collective-permute-start.7) | collective-permute-done | bytes 69664 | tf_op jit(solution)/shard_map/ppermute | solution.py:561
  36.5 0.5 collective-permute-start.11
  37.0 1.9 %collective-permute-start.10 = (f32[128,128]{1,0:T(8,128)S(1)}, f32[128,128]{1,0:T(8,128)S(1)}, u32[]{:S(2)}, u32[]{:S(2)}) collective-permute-start(f32[128,128]{1,0:T(8,128)S(1)} %shard_map.219.refs_0_), channel_id=1, source_target_pairs={{0,6},{2,4},{4,2},{6,0},{8,14},{10,12},{12,10},{14,8},{1,7},{3,5},... | collective-permute-start | bytes 196616 | tf_op jit(solution)/shard_map/ppermute | solution.py:561
  38.9 3.4 %collective-permute-start.8 = (f32[128,128]{1,0:T(8,128)S(1)}, f32[128,128]{1,0:T(8,128)S(1)}, u32[]{:S(2)}, u32[]{:S(2)}) collective-permute-start(f32[128,128]{1,0:T(8,128)S(1)} %shard_map.219.refs_0_), channel_id=1, source_target_pairs={{0,2},{2,0},{4,6},{6,4},{8,10},{10,8},{12,14},{14,12},{1,3},{3,1},... | collective-permute-start | bytes 196616 | tf_op jit(solution)/shard_map/ppermute | solution.py:561
  42.3 0.9 %collective-permute-start.12 = (f32[128,128]{1,0:T(8,128)S(1)}, f32[128,128]{1,0:T(8,128)S(1)}, u32[]{:S(2)}, u32[]{:S(2)}) collective-permute-start(f32[128,128]{1,0:T(8,128)S(1)} %collective-permute-done.11.refs_0_), channel_id=1, source_target_pairs={{0,2},{2,0},{4,6},{6,4},{8,10},{10,8},{12,14},{14,12},{1,3},{3,1},... | collective-permute-start | bytes 196616 | tf_op jit(solution)/shard_map/ppermute | solution.py:561
  43.2 1.1 %collective-permute-start.13 = (f32[128,128]{1,0:T(8,128)S(1)}, f32[128,128]{1,0:T(8,128)S(1)}, u32[]{:S(2)}, u32[]{:S(2)}) collective-permute-start(f32[128,128]{1,0:T(8,128)S(1)} %collective-permute-done.11.refs_0_), channel_id=1, source_target_pairs={{0,4},{2,6},{4,0},{6,2},{8,12},{10,14},{12,8},{14,10},{1,5},{3,7},... | collective-permute-start | bytes 196616 | tf_op jit(solution)/shard_map/ppermute | solution.py:561
  44.3 1.5 %collective-permute-start.14 = (f32[128,128]{1,0:T(8,128)S(1)}, f32[128,128]{1,0:T(8,128)S(1)}, u32[]{:S(2)}, u32[]{:S(2)}) collective-permute-start(f32[128,128]{1,0:T(8,128)S(1)} %collective-permute-done.11.refs_0_), channel_id=1, source_target_pairs={{0,6},{2,4},{4,2},{6,0},{8,14},{10,12},{12,10},{14,8},{1,7},{3,5},... | collective-permute-start | bytes 196616 | tf_op jit(solution)/shard_map/ppermute | solution.py:561
  45.8 0.2 shard_map.218
  46.0 1.4 %shard_map.217 = (bf16[1280,512]{1,0:T(8,128)(2,1)S(1)}, bf16[256,512]{1,0:T(8,128)(2,1)S(1)}) custom-call(f32[16,128]{1,0:T(8,128)S(1)} %get-tuple-element.38.ints_ref, f32[136,128]{1,0:T(8,128)S(1)} %get-tuple-element.56.refs_0_, f32[136,128]{1,0:T(8,128)S(1)} %collective-permute-done.5.refs_1_, f32[136,128]{1,0:T(8,128)S(1)} %collective-permute-done.6.refs_2_, ...), custom_call_target="tpu_custom_call" | custom-call | tf_op jit(solution)/shard_map/pallas_call | solution.py:673
  47.4 1.2 %shard_map.220 = (f32[1280,256]{1,0:T(8,128)S(1)}, f32[320,256]{1,0:T(8,128)S(1)}) custom-call(bf16[1280,512]{1,0:T(8,128)(2,1)S(1)} %get-tuple-element.60.hot_ref, bf16[256,512]{1,0:T(8,128)(2,1)S(1)} %get-tuple-element.61.parent_ref, bf16[1280,256]{1,0:T(8,128)(2,1)S(1)} %get-tuple-element.62.high_ref, bf16[1280,256]{1,0:T(8,128)(2,1)S(1)} %get-tuple-element.63.low_ref, ...), custom_call_target="tpu_custom_call" | custom-call | tf_op jit(solution)/shard_map/pallas_call | solution.py:685
  48.6 0.9 %collective-permute-done.14.refs_3_ = f32[128,128]{1,0:T(8,128)S(1)} collective-permute-done((f32[128,128]{1,0:T(8,128)S(1)}, f32[128,128]{1,0:T(8,128)S(1)}, u32[]{:S(2)}, u32[]{:S(2)}) %collective-permute-start.14) | collective-permute-done | bytes 65568 | tf_op jit(solution)/shard_map/ppermute | solution.py:561
  49.5 2.9 %shard_map.221 = (f32[512,128]{1,0:T(8,128)}, f32[128,128]{1,0:T(8,128)}) custom-call(f32[256,256]{1,0:T(8,128)S(1)} %get-tuple-element.55.last_ref, bf16[1280,512]{1,0:T(8,128)(2,1)S(1)} %get-tuple-element.60.hot_ref, bf16[256,512]{1,0:T(8,128)(2,1)S(1)} %get-tuple-element.61.parent_ref, f32[1280,256]{1,0:T(8,128)S(1)} %get-tuple-element.64.got_ref, ...), custom_call_target="tpu_custom_call" | custom-call | tf_op jit(solution)/shard_map/pallas_call | solution.py:690
  (30 shorter events, 0.1 us)
Async XLA Ops:
  2.0 10.7 %collective-permute-start = (f32[272,128]{1,0:T(8,128)S(1)}, f32[272,128]{1,0:T(8,128)S(1)}, u32[]{:S(2)}, u32[]{:S(2)}) collective-permute-start(f32[272,128]{1,0:T(8,128)S(1)} %get-tuple-element.35), channel_id=1, source_target_pairs={{0,2},{2,0},{4,6},{6,4},{8,10},{10,8},{12,14},{14,12},{1,3},{3,1},... | collective-permute-start | bytes 417800 | tf_op jit(solution)/shard_map/ppermute | solution.py:561
  5.0 7.7 %collective-permute-start.1 = (f32[256,128]{1,0:T(8,128)S(1)}, f32[256,128]{1,0:T(8,128)S(1)}, u32[]{:S(2)}, u32[]{:S(2)}) collective-permute-start(f32[256,128]{1,0:T(8,128)S(1)} %get-tuple-element.36), channel_id=1, source_target_pairs={{0,14},{2,4},{4,2},{6,8},{8,6},{10,12},{12,10},{14,0},{1,15},{3,5}... | collective-permute-start | bytes 393224 | tf_op jit(solution)/shard_map/ppermute | solution.py:561
  12.7 6.5 %copy-start = (f32[2,256,256]{2,1,0:T(8,128)S(1)}, f32[2,256,256]{2,1,0:T(8,128)}, u32[]{:S(2)}) copy-start(f32[2,256,256]{2,1,0:T(8,128)} %ws_ref.1) | copy-start | bytes 1572868
  12.7 6.5 %copy-start.1 = (f32[2,256,256]{2,1,0:T(8,128)S(1)}, f32[2,256,256]{2,1,0:T(8,128)}, u32[]{:S(2)}) copy-start(f32[2,256,256]{2,1,0:T(8,128)} %wr_ref.1) | copy-start | bytes 1572868
  12.7 6.5 %copy-start.2 = (f32[2,256,256]{2,1,0:T(8,128)S(1)}, f32[2,256,256]{2,1,0:T(8,128)}, u32[]{:S(2)}) copy-start(f32[2,256,256]{2,1,0:T(8,128)} %wo_ref.1) | copy-start | bytes 1572868
  12.7 6.5 %copy-start.3 = (f32[256,256]{1,0:T(8,128)S(1)}, f32[256,256]{1,0:T(8,128)}, u32[]{:S(2)}) copy-start(f32[256,256]{1,0:T(8,128)} %wi_ref.1) | copy-start | bytes 786436
  12.7 6.5 %copy-start.4 = (f32[256,256]{1,0:T(8,128)S(1)}, f32[256,256]{1,0:T(8,128)}, u32[]{:S(2)}) copy-start(f32[256,256]{1,0:T(8,128)} %wu_ref.1) | copy-start | bytes 786436
  13.8 11.9 %collective-permute-start.2 = (f32[512,128]{1,0:T(8,128)S(1)}, f32[512,128]{1,0:T(8,128)S(1)}, u32[]{:S(2)}, u32[]{:S(2)}) collective-permute-start(f32[512,128]{1,0:T(8,128)S(1)} %get-tuple-element.45.state_ref), channel_id=1, source_target_pairs={{0,2},{2,0},{4,6},{6,4},{8,10},{10,8},{12,14},{14,12},{1,3},{3,1},... | collective-permute-start | bytes 786440 | tf_op jit(solution)/shard_map/ppermute | solution.py:561
  14.4 6.1 %collective-permute-start.3 = (f32[256,128]{1,0:T(8,128)S(1)}, f32[256,128]{1,0:T(8,128)S(1)}, u32[]{:S(2)}, u32[]{:S(2)}) collective-permute-start(f32[256,128]{1,0:T(8,128)S(1)} %get-tuple-element.46), channel_id=1, source_target_pairs={{0,12},{2,6},{4,0},{6,10},{8,4},{10,14},{12,8},{14,2},{1,13},{3,7}... | collective-permute-start | bytes 393224 | tf_op jit(solution)/shard_map/ppermute | solution.py:561
  18.0 7.7 %collective-permute-start.4 = (f32[256,128]{1,0:T(8,128)S(1)}, f32[256,128]{1,0:T(8,128)S(1)}, u32[]{:S(2)}, u32[]{:S(2)}) collective-permute-start(f32[256,128]{1,0:T(8,128)S(1)} %get-tuple-element.46), channel_id=1, source_target_pairs={{0,14},{2,4},{4,2},{6,8},{8,6},{10,12},{12,10},{14,0},{1,15},{3,5}... | collective-permute-start | bytes 393224 | tf_op jit(solution)/shard_map/ppermute | solution.py:561
  25.7 10.7 %copy-start.10 = (f32[64,1,256]{2,1,0:T(1,128)S(1)}, f32[64,1,256]{2,1,0:T(1,128)}, u32[]{:S(2)}) copy-start(f32[64,1,256]{2,1,0:T(1,128)} %param.22) | copy-start | bytes 196612
  25.7 20.1 %copy-start.5 = (f32[256,256]{1,0:T(8,128)S(1)}, f32[256,256]{1,0:T(8,128)}, u32[]{:S(2)}) copy-start(f32[256,256]{1,0:T(8,128)} %cs_ref.1) | copy-start | bytes 786436
  25.7 20.1 %copy-start.6 = (f32[256,256]{1,0:T(8,128)S(1)}, f32[256,256]{1,0:T(8,128)}, u32[]{:S(2)}) copy-start(f32[256,256]{1,0:T(8,128)} %cr_ref.1) | copy-start | bytes 786436
  25.7 20.1 %copy-start.7 = (f32[256,256]{1,0:T(8,128)S(1)}, f32[256,256]{1,0:T(8,128)}, u32[]{:S(2)}) copy-start(f32[256,256]{1,0:T(8,128)} %co_ref.1) | copy-start | bytes 786436
  25.7 20.1 %copy-start.8 = (f32[256,256]{1,0:T(8,128)S(1)}, f32[256,256]{1,0:T(8,128)}, u32[]{:S(2)}) copy-start(f32[256,256]{1,0:T(8,128)} %di_ref.1) | copy-start | bytes 786436
  25.7 20.1 %copy-start.9 = (f32[256,256]{1,0:T(8,128)S(1)}, f32[256,256]{1,0:T(8,128)}, u32[]{:S(2)}) copy-start(f32[256,256]{1,0:T(8,128)} %do_ref.1) | copy-start | bytes 786436
  28.9 5.9 %collective-permute-start.5 = (f32[136,128]{1,0:T(8,128)S(1)}, f32[136,128]{1,0:T(8,128)S(1)}, u32[]{:S(2)}, u32[]{:S(2)}) collective-permute-start(f32[136,128]{1,0:T(8,128)S(1)} %get-tuple-element.57), channel_id=1, source_target_pairs={{0,4},{2,6},{4,0},{6,2},{8,12},{10,14},{12,8},{14,10},{1,5},{3,7},... | collective-permute-start | bytes 208904 | tf_op jit(solution)/shard_map/ppermute | solution.py:561
  28.9 5.8 %collective-permute-start.6 = (f32[136,128]{1,0:T(8,128)S(1)}, f32[136,128]{1,0:T(8,128)S(1)}, u32[]{:S(2)}, u32[]{:S(2)}) collective-permute-start(f32[136,128]{1,0:T(8,128)S(1)} %get-tuple-element.58), channel_id=1, source_target_pairs={{0,8},{2,10},{4,12},{6,14},{8,0},{10,2},{12,4},{14,6},{1,9},{3,11}... | collective-permute-start | bytes 208904 | tf_op jit(solution)/shard_map/ppermute | solution.py:561
  29.5 6.9 %collective-permute-start.7 = (f32[136,128]{1,0:T(8,128)S(1)}, f32[136,128]{1,0:T(8,128)S(1)}, u32[]{:S(2)}, u32[]{:S(2)}) collective-permute-start(f32[136,128]{1,0:T(8,128)S(1)} %get-tuple-element.59), channel_id=1, source_target_pairs={{0,12},{2,14},{4,8},{6,10},{8,4},{10,6},{12,0},{14,2},{1,13},{3,15... | collective-permute-start | bytes 208904 | tf_op jit(solution)/shard_map/ppermute | solution.py:561
  36.5 5.8 %collective-permute-start.11 = (f32[128,128]{1,0:T(8,128)S(1)}, f32[128,128]{1,0:T(8,128)S(1)}, u32[]{:S(2)}, u32[]{:S(2)}) collective-permute-start(f32[128,128]{1,0:T(8,128)S(1)} %shard_map.219.refs_0_), channel_id=1, source_target_pairs={{0,8},{2,10},{4,12},{6,14},{8,0},{10,2},{12,4},{14,6},{1,9},{3,11}... | collective-permute-start | bytes 196616 | tf_op jit(solution)/shard_map/ppermute | solution.py:561
  37.0 7.3 %collective-permute-start.10 = (f32[128,128]{1,0:T(8,128)S(1)}, f32[128,128]{1,0:T(8,128)S(1)}, u32[]{:S(2)}, u32[]{:S(2)}) collective-permute-start(f32[128,128]{1,0:T(8,128)S(1)} %shard_map.219.refs_0_), channel_id=1, source_target_pairs={{0,6},{2,4},{4,2},{6,0},{8,14},{10,12},{12,10},{14,8},{1,7},{3,5},... | collective-permute-start | bytes 196616 | tf_op jit(solution)/shard_map/ppermute | solution.py:561
  38.9 8.5 %collective-permute-start.8 = (f32[128,128]{1,0:T(8,128)S(1)}, f32[128,128]{1,0:T(8,128)S(1)}, u32[]{:S(2)}, u32[]{:S(2)}) collective-permute-start(f32[128,128]{1,0:T(8,128)S(1)} %shard_map.219.refs_0_), channel_id=1, source_target_pairs={{0,2},{2,0},{4,6},{6,4},{8,10},{10,8},{12,14},{14,12},{1,3},{3,1},... | collective-permute-start | bytes 196616 | tf_op jit(solution)/shard_map/ppermute | solution.py:561
  42.3 5.1 %collective-permute-start.9 = (f32[128,128]{1,0:T(8,128)S(1)}, f32[128,128]{1,0:T(8,128)S(1)}, u32[]{:S(2)}, u32[]{:S(2)}) collective-permute-start(f32[128,128]{1,0:T(8,128)S(1)} %shard_map.219.refs_0_), channel_id=1, source_target_pairs={{0,4},{2,6},{4,0},{6,2},{8,12},{10,14},{12,8},{14,10},{1,5},{3,7},... | collective-permute-start | bytes 196616 | tf_op jit(solution)/shard_map/ppermute | solution.py:561
  42.3 6.3 %collective-permute-start.12 = (f32[128,128]{1,0:T(8,128)S(1)}, f32[128,128]{1,0:T(8,128)S(1)}, u32[]{:S(2)}, u32[]{:S(2)}) collective-permute-start(f32[128,128]{1,0:T(8,128)S(1)} %collective-permute-done.11.refs_0_), channel_id=1, source_target_pairs={{0,2},{2,0},{4,6},{6,4},{8,10},{10,8},{12,14},{14,12},{1,3},{3,1},... | collective-permute-start | bytes 196616 | tf_op jit(solution)/shard_map/ppermute | solution.py:561
  43.2 5.4 %collective-permute-start.13 = (f32[128,128]{1,0:T(8,128)S(1)}, f32[128,128]{1,0:T(8,128)S(1)}, u32[]{:S(2)}, u32[]{:S(2)}) collective-permute-start(f32[128,128]{1,0:T(8,128)S(1)} %collective-permute-done.11.refs_0_), channel_id=1, source_target_pairs={{0,4},{2,6},{4,0},{6,2},{8,12},{10,14},{12,8},{14,10},{1,5},{3,7},... | collective-permute-start | bytes 196616 | tf_op jit(solution)/shard_map/ppermute | solution.py:561
  44.3 5.2 %collective-permute-start.14 = (f32[128,128]{1,0:T(8,128)S(1)}, f32[128,128]{1,0:T(8,128)S(1)}, u32[]{:S(2)}, u32[]{:S(2)}) collective-permute-start(f32[128,128]{1,0:T(8,128)S(1)} %collective-permute-done.11.refs_0_), channel_id=1, source_target_pairs={{0,6},{2,4},{4,2},{6,0},{8,14},{10,12},{12,10},{14,8},{1,7},{3,5},... | collective-permute-start | bytes 196616 | tf_op jit(solution)/shard_map/ppermute | solution.py:561
